TPU v7x, 32 devices: a whole 2x2x4 slice. The times are simulated.
32 devices in a mesh: seq: 8 (over z, y), dp: 4 (over x, core).
Axes of the slice: x: 2, y: 2, z: 4, core: 2. Of those that a mesh axis runs over, the one named last changes fastest.
Arguments:
- inputs: bfloat16 [8, 1024, 1024], P('dp', 'seq'), may hold values from -6 to 6
- first_values: bfloat16 [8, 1024, 1024], P('dp', 'seq'), may hold values from -6 to 6
- teacher_states: bfloat16 [8, 1024, 1024], P('dp', 'seq'), may hold values from -6 to 6
- out_cotangent: bfloat16 [8, 1024, 1024], P('dp', 'seq'), may hold values from -6 to 6
- token_valid: int32 [8, 1024], P('dp', 'seq'), may hold values from 0 to 1, as said below
- attn_gain: bfloat16 [1024], P(('seq', 'dp')), may hold values from 0.5 to 1.5
- w_query: bfloat16 [1024, 1024], P(('seq', 'dp')), may hold values from -0.1875 to 0.1875
- w_key: bfloat16 [1024, 1024], P(('seq', 'dp')), may hold values from -0.1875 to 0.1875
- w_value: bfloat16 [1024, 1024], P(('seq', 'dp')), may hold values from -0.1875 to 0.1875
- w_output: bfloat16 [1024, 1024], P(('seq', 'dp')), may hold values from -3 to 3
- mlp_gain: bfloat16 [1024], P(('seq', 'dp')), may hold values from 0.5 to 1.5
- w_gate: bfloat16 [1024, 2816], P(('seq', 'dp')), may hold values from -0.1875 to 0.1875
- w_up: bfloat16 [1024, 2816], P(('seq', 'dp')), may hold values from -0.1875 to 0.1875
- w_down: bfloat16 [2816, 1024], P(('seq', 'dp')), may hold values from -0.109375 to 0.109375
Outputs:
- output: float32 [8, 1024, 1024], P('dp', 'seq')
- loss_value: float32 [], replicated
- grad_inputs: float32 [8, 1024, 1024], P('dp', 'seq')
- grad_first_values: float32 [8, 1024, 1024], P('dp', 'seq')
- grad_attn_gain: float32 [1024], P(('seq', 'dp'))
- grad_query: float32 [1024, 1024], P(('seq', 'dp'))
- grad_key: float32 [1024, 1024], P(('seq', 'dp'))
- grad_value: float32 [1024, 1024], P(('seq', 'dp'))
- grad_output: float32 [1024, 1024], P(('seq', 'dp'))
- grad_mlp_gain: float32 [1024], P(('seq', 'dp'))
- grad_gate: float32 [1024, 2816], P(('seq', 'dp'))
- grad_up: float32 [1024, 2816], P(('seq', 'dp'))
- grad_down: float32 [2816, 1024], P(('seq', 'dp'))
Inputs may be any that keep to these rules, and one draw needn't show every extreme that they name: `token_valid`: 1 marks a token that counts in the loss; the last position of every sequence is 1.
All inputs are finite; a program needn't handle non-finite values.
Results may differ from a plain program's by a relative error of at most 0.018.
Values may be sent and summed in bfloat16 or wider, within the bound.
No kernel may reach another device: no remote copies, remote signals or barrier semaphores. Data moves between devices by JAX's collectives and lax.ppermute only.
A program may use at most 256 MiB of HBM per device.

v0:
```python
import jax
import jax.numpy as jnp
from jax import lax
from jax.sharding import PartitionSpec as P

HEAD_DIM = 64
BLOCK = 256
MB = 2


EPSILON = 1e-06
THETA = 10000.0
MASKED = -1000000000.0
SCALE = 0.125


def rotary_tables(positions, head_dim):
    half_dim = head_dim // 2
    frequency = THETA ** (-(jnp.arange(half_dim, dtype=jnp.float32) * 2.0 / head_dim))
    angles = positions[:, None] * frequency[None, :]
    return (jnp.cos(angles), jnp.sin(angles))


def rotate(values, cosines, sines):
    half_dim = values.shape[-1] // 2
    first_half = values[..., :half_dim]
    second_half = values[..., half_dim:]
    cos_rows = cosines[:, None, :]
    sin_rows = sines[:, None, :]
    return jnp.concatenate(
        [
            first_half * cos_rows - second_half * sin_rows,
            second_half * cos_rows + first_half * sin_rows,
        ],
        axis=-1,
    )


def rotate_back(grads_in, cosines, sines):
    half_dim = grads_in.shape[-1] // 2
    first_half = grads_in[..., :half_dim]
    second_half = grads_in[..., half_dim:]
    cos_rows = cosines[:, None, :]
    sin_rows = sines[:, None, :]
    return jnp.concatenate(
        [
            first_half * cos_rows + second_half * sin_rows,
            second_half * cos_rows - first_half * sin_rows,
        ],
        axis=-1,
    )


def weight_grad(left, right):
    return lax.dot_general(
        left, right, (((0,), (0,)), ((), ())), preferred_element_type=jnp.float32
    )


def input_grad(left, weight):
    return lax.dot_general(
        left, weight, (((1,), (1,)), ((), ())), preferred_element_type=jnp.float32
    )


def masked_scores(query_part, key_part, allowed):
    scores = (
        jnp.einsum("sqhd,skhd->shqk", query_part, key_part, preferred_element_type=jnp.float32)
        * SCALE
    )
    return jnp.where(allowed[None, None], scores, MASKED)


def attend_forward(queries, key_rows, value_rows, allowed):
    head_count = queries.shape[2]
    head_span = 4
    pieces = []
    totals = []
    for head_start in range(0, head_count, head_span):
        query_part = queries[:, :, head_start : head_start + head_span]
        key_part = key_rows[:, :, head_start : head_start + head_span]
        value_part = value_rows[:, :, head_start : head_start + head_span]
        scores = masked_scores(query_part, key_part, allowed)
        row_top = jnp.max(scores, axis=-1, keepdims=True)
        log_total = row_top + jnp.log(jnp.sum(jnp.exp(scores - row_top), axis=-1, keepdims=True))
        probabilities = jnp.exp(scores - log_total).astype(jnp.bfloat16)
        pieces.append(
            jnp.einsum(
                "shqk,skhd->sqhd", probabilities, value_part, preferred_element_type=jnp.float32
            )
        )
        totals.append(log_total)
    return (jnp.concatenate(pieces, axis=2), totals)


def attend_backward(queries, key_rows, value_rows, grad_att, totals, allowed):
    head_count = queries.shape[2]
    head_span = 4
    query_grads = []
    key_grads = []
    value_grads = []
    inner_sums = []
    for group_index, head_start in enumerate(range(0, head_count, head_span)):
        query_part = queries[:, :, head_start : head_start + head_span]
        key_part = key_rows[:, :, head_start : head_start + head_span]
        value_part = value_rows[:, :, head_start : head_start + head_span]
        grad_part = grad_att[:, :, head_start : head_start + head_span]
        scores = masked_scores(query_part, key_part, allowed)
        probabilities = jnp.exp(scores - totals[group_index])
        grad_probs = jnp.einsum(
            "sqhd,skhd->shqk", grad_part, value_part, preferred_element_type=jnp.float32
        )
        inner_sum = jnp.sum(probabilities * grad_probs, axis=-1, keepdims=True)
        inner_sums.append(inner_sum)
        grad_scores = (probabilities * (grad_probs - inner_sum)).astype(jnp.bfloat16)
        query_grads.append(
            jnp.einsum("shqk,skhd->sqhd", grad_scores, key_part, preferred_element_type=jnp.float32)
            * SCALE
        )
        key_grads.append(
            jnp.einsum(
                "shqk,sqhd->skhd", grad_scores, query_part, preferred_element_type=jnp.float32
            )
            * SCALE
        )
        value_grads.append(
            jnp.einsum(
                "shqk,sqhd->skhd",
                probabilities.astype(jnp.bfloat16),
                grad_part,
                preferred_element_type=jnp.float32,
            )
        )
    query_grad = jnp.concatenate(query_grads, axis=2)
    return (
        query_grad,
        (jnp.concatenate(key_grads, axis=2), jnp.concatenate(value_grads, axis=2)),
        inner_sums,
    )


def on_device(
    inputs,
    first_values,
    teacher_states,
    out_cotangent,
    token_valid,
    attn_gain,
    w_query,
    w_key,
    w_value,
    w_output,
    mlp_gain,
    w_gate,
    w_up,
    w_down,
):
    shards = (attn_gain, w_query, w_key, w_value, w_output, mlp_gain, w_gate, w_up, w_down)
    local_len = inputs.shape[1]
    model_width = inputs.shape[2]
    head_count = model_width // HEAD_DIM
    length = local_len * lax.axis_size("seq")
    per_batch = inputs.shape[0] // MB
    valid_float = token_valid.astype(jnp.float32)
    valid_total = lax.psum(jnp.sum(valid_float), ("seq", "dp"))
    positions = lax.axis_index("seq") * local_len + jnp.arange(local_len, dtype=jnp.int32)
    cosines, sines = rotary_tables(positions.astype(jnp.float32), HEAD_DIM)
    allowed = (jnp.arange(length, dtype=jnp.int32) // BLOCK)[None, :] <= (positions // BLOCK)[
        :, None
    ]
    kept_normed = []
    kept_query = []
    kept_key = []
    kept_mixed = []
    kept_att = []
    kept_branch = []
    kept_mlp = []
    kept_gate = []
    kept_up = []
    kept_gain_a = []
    kept_gain_m = []
    kept_act = []
    kept_down = []
    loss_local = jnp.zeros((), jnp.float32)
    result_list = []
    grad_in_list = []
    grad_first_list = []
    for micro_batch in range(MB):
        row_lo = micro_batch * per_batch
        gathered = (
            lax.all_gather(shards[0], ("seq", "dp"), axis=0, tiled=True),
            lax.all_gather(shards[1], ("seq", "dp"), axis=0, tiled=True),
            lax.all_gather(shards[2], ("seq", "dp"), axis=0, tiled=True),
            lax.all_gather(shards[3], ("seq", "dp"), axis=0, tiled=True),
            lax.all_gather(shards[4], ("seq", "dp"), axis=0, tiled=True),
            lax.all_gather(shards[5], ("seq", "dp"), axis=0, tiled=True),
            lax.all_gather(shards[6], ("seq", "dp"), axis=0, tiled=True),
            lax.all_gather(shards[7], ("seq", "dp"), axis=0, tiled=True),
            lax.all_gather(shards[8], ("seq", "dp"), axis=0, tiled=True),
        )
        gain_a, query_w, key_w, value_w, output_w, gain_m, gate_w, up_w, down_w = gathered
        x_rows = inputs[row_lo : row_lo + per_batch].astype(jnp.float32).reshape(-1, model_width)
        first_rows = (
            first_values[row_lo : row_lo + per_batch].astype(jnp.float32).reshape(-1, model_width)
        )
        inv_rms_a = lax.rsqrt(jnp.mean(x_rows * x_rows, axis=-1, keepdims=True) + EPSILON)
        scaled_a = x_rows * inv_rms_a
        normed = (scaled_a * gain_a.astype(jnp.float32)).astype(jnp.bfloat16)
        head_shape = (per_batch, local_len, head_count, HEAD_DIM)
        queries = rotate(
            jnp.dot(normed, query_w, preferred_element_type=jnp.float32).reshape(head_shape),
            cosines,
            sines,
        ).astype(jnp.bfloat16)
        keys_own = rotate(
            jnp.dot(normed, key_w, preferred_element_type=jnp.float32).reshape(head_shape),
            cosines,
            sines,
        ).astype(jnp.bfloat16)
        mixed = (
            0.5 * jnp.dot(normed, value_w, preferred_element_type=jnp.float32) + 0.5 * first_rows
        ).astype(jnp.bfloat16)
        keys_all, values_all = (
            lax.all_gather(
                keys_own.reshape(per_batch, local_len, model_width), "seq", axis=1, tiled=True
            ),
            lax.all_gather(
                mixed.reshape(per_batch, local_len, model_width), "seq", axis=1, tiled=True
            ),
        )
        full_heads = (per_batch, length, head_count, HEAD_DIM)
        keys_all = keys_all.reshape(full_heads)
        values_all = values_all.reshape(full_heads)
        attended, totals = attend_forward(queries, keys_all, values_all, allowed)
        att_low = attended.reshape(-1, model_width).astype(jnp.bfloat16)
        hidden_in = x_rows + jnp.dot(att_low, output_w, preferred_element_type=jnp.float32)
        inv_rms_m = lax.rsqrt(jnp.mean(hidden_in * hidden_in, axis=-1, keepdims=True) + EPSILON)
        scaled_m = hidden_in * inv_rms_m
        normed_mlp = (scaled_m * gain_m.astype(jnp.float32)).astype(jnp.bfloat16)
        gate_pre = jnp.dot(normed_mlp, gate_w, preferred_element_type=jnp.float32)
        up_part = jnp.dot(normed_mlp, up_w, preferred_element_type=jnp.float32)
        gate_sigmoid = jax.nn.sigmoid(gate_pre)
        swish_value = gate_pre * gate_sigmoid
        activated = (swish_value * up_part).astype(jnp.bfloat16)
        result = hidden_in + jnp.dot(activated, down_w, preferred_element_type=jnp.float32)
        result_list.append(result.reshape(per_batch, local_len, model_width))
        teacher_rows = (
            teacher_states[row_lo : row_lo + per_batch].astype(jnp.float32).reshape(-1, model_width)
        )
        valid_rows = valid_float[row_lo : row_lo + per_batch].reshape(-1, 1)
        residual_err = result - teacher_rows
        loss_local = loss_local + jnp.sum(
            valid_rows[:, 0] * jnp.mean(residual_err * residual_err, axis=-1)
        )
        grad_out = (
            out_cotangent[row_lo : row_lo + per_batch].astype(jnp.float32).reshape(-1, model_width)
            + 2.0 / model_width * valid_rows * residual_err / valid_total
        )
        back_weights = (
            lax.all_gather(shards[0], ("seq", "dp"), axis=0, tiled=True),
            lax.all_gather(shards[1], ("seq", "dp"), axis=0, tiled=True),
            lax.all_gather(shards[2], ("seq", "dp"), axis=0, tiled=True),
            lax.all_gather(shards[3], ("seq", "dp"), axis=0, tiled=True),
            lax.all_gather(shards[4], ("seq", "dp"), axis=0, tiled=True),
            lax.all_gather(shards[5], ("seq", "dp"), axis=0, tiled=True),
            lax.all_gather(shards[6], ("seq", "dp"), axis=0, tiled=True),
            lax.all_gather(shards[7], ("seq", "dp"), axis=0, tiled=True),
            lax.all_gather(shards[8], ("seq", "dp"), axis=0, tiled=True),
        )
        gain_a, query_w, key_w, value_w, output_w, gain_m, gate_w, up_w, down_w = back_weights
        grad_down_in = grad_out.astype(jnp.bfloat16)
        kept_act.append(activated)
        kept_down.append(grad_down_in)
        grad_act = input_grad(grad_down_in, down_w)
        swish_slope = gate_sigmoid * (1.0 + gate_pre * (1.0 - gate_sigmoid))
        grad_gate_in = (grad_act * up_part * swish_slope).astype(jnp.bfloat16)
        grad_up_in = (grad_act * swish_value).astype(jnp.bfloat16)
        kept_mlp.append(normed_mlp)
        kept_gate.append(grad_gate_in)
        kept_up.append(grad_up_in)
        grad_norm_m = input_grad(grad_gate_in, gate_w) + input_grad(grad_up_in, up_w)
        kept_gain_m.append(grad_norm_m * scaled_m)
        scaled_grad_m = grad_norm_m * gain_m.astype(jnp.float32)
        grad_hidden = grad_out + inv_rms_m * (
            scaled_grad_m - scaled_m * jnp.mean(scaled_grad_m * scaled_m, axis=-1, keepdims=True)
        )
        grad_branch = grad_hidden.astype(jnp.bfloat16)
        kept_att.append(att_low)
        kept_branch.append(grad_branch)
        grad_att = input_grad(grad_branch, output_w).astype(jnp.bfloat16).reshape(head_shape)
        query_grad, kv_parts, inner_sums = attend_backward(
            queries, keys_all, values_all, grad_att, totals, allowed
        )
        key_grad_all, value_grad_all = kv_parts
        key_grad, value_grad = (
            lax.psum_scatter(
                key_grad_all.reshape(per_batch, length, model_width).astype(jnp.bfloat16),
                "seq",
                scatter_dimension=1,
                tiled=True,
            ).astype(jnp.float32),
            lax.psum_scatter(
                value_grad_all.reshape(per_batch, length, model_width).astype(jnp.bfloat16),
                "seq",
                scatter_dimension=1,
                tiled=True,
            ).astype(jnp.float32),
        )
        grad_query_in = (
            rotate_back(query_grad, cosines, sines).astype(jnp.bfloat16).reshape(-1, model_width)
        )
        grad_key_in = (
            rotate_back(key_grad.reshape(head_shape), cosines, sines)
            .astype(jnp.bfloat16)
            .reshape(-1, model_width)
        )
        grad_mixed = value_grad.reshape(-1, model_width).astype(jnp.bfloat16)
        grad_first_list.append(
            (0.5 * grad_mixed.astype(jnp.float32)).reshape(per_batch, local_len, model_width)
        )
        kept_normed.append(normed)
        kept_query.append(grad_query_in)
        kept_key.append(grad_key_in)
        kept_mixed.append(grad_mixed)
        grad_norm_a = (
            input_grad(grad_query_in, query_w)
            + input_grad(grad_key_in, key_w)
            + 0.5 * input_grad(grad_mixed, value_w)
        )
        kept_gain_a.append(grad_norm_a * scaled_a)
        scaled_grad_a = grad_norm_a * gain_a.astype(jnp.float32)
        grad_in = grad_hidden + inv_rms_a * (
            scaled_grad_a - scaled_a * jnp.mean(scaled_grad_a * scaled_a, axis=-1, keepdims=True)
        )
        grad_in_list.append(grad_in.reshape(per_batch, local_len, model_width))
    loss_value = lax.psum(loss_local, ("seq", "dp")) / valid_total
    normed_all = jnp.concatenate(kept_normed, axis=0)
    query_all_g = jnp.concatenate(kept_query, axis=0)
    key_all_g = jnp.concatenate(kept_key, axis=0)
    mixed_all_g = jnp.concatenate(kept_mixed, axis=0)
    att_all = jnp.concatenate(kept_att, axis=0)
    branch_all = jnp.concatenate(kept_branch, axis=0)
    mlp_all = jnp.concatenate(kept_mlp, axis=0)
    gate_all = jnp.concatenate(kept_gate, axis=0)
    up_all = jnp.concatenate(kept_up, axis=0)
    gain_terms_a = jnp.concatenate(kept_gain_a, axis=0)
    gain_terms_m = jnp.concatenate(kept_gain_m, axis=0)
    act_all = jnp.concatenate(kept_act, axis=0)
    down_all = jnp.concatenate(kept_down, axis=0)
    gain_col_a = jnp.sum(gain_terms_a, axis=0)[:, None]
    gain_col_m = jnp.sum(gain_terms_m, axis=0)[:, None]
    owned = lax.psum_scatter(
        jnp.concatenate(
            [
                weight_grad(normed_all, query_all_g),
                weight_grad(normed_all, key_all_g),
                0.5 * weight_grad(normed_all, mixed_all_g),
                weight_grad(att_all, branch_all),
                weight_grad(mlp_all, gate_all),
                weight_grad(mlp_all, up_all),
                gain_col_a,
                gain_col_m,
            ],
            axis=1,
        ),
        ("seq", "dp"),
        scatter_dimension=0,
        tiled=True,
    )
    owned_down = lax.psum_scatter(
        weight_grad(act_all, down_all), ("seq", "dp"), scatter_dimension=0, tiled=True
    )
    ff_width = w_gate.shape[1]
    offset = 0
    grad_query = owned[:, offset : offset + model_width]
    offset = offset + model_width
    grad_key = owned[:, offset : offset + model_width]
    offset = offset + model_width
    grad_value = owned[:, offset : offset + model_width]
    offset = offset + model_width
    grad_output = owned[:, offset : offset + model_width]
    offset = offset + model_width
    grad_gate = owned[:, offset : offset + ff_width]
    offset = offset + ff_width
    grad_up = owned[:, offset : offset + ff_width]
    offset = offset + ff_width
    grad_attn_gain = owned[:, offset]
    grad_mlp_gain = owned[:, offset + 1]
    return (
        jnp.concatenate(result_list, axis=0),
        loss_value,
        jnp.concatenate(grad_in_list, axis=0),
        jnp.concatenate(grad_first_list, axis=0),
        grad_attn_gain,
        grad_query,
        grad_key,
        grad_value,
        grad_output,
        grad_mlp_gain,
        grad_gate,
        grad_up,
        owned_down,
    )


def solution(mesh):
    placed = (
        P("dp", "seq", None),
        P("dp", "seq", None),
        P("dp", "seq", None),
        P("dp", "seq", None),
        P("dp", "seq"),
        P(("seq", "dp")),
        P(("seq", "dp"), None),
        P(("seq", "dp"), None),
        P(("seq", "dp"), None),
        P(("seq", "dp"), None),
        P(("seq", "dp")),
        P(("seq", "dp"), None),
        P(("seq", "dp"), None),
        P(("seq", "dp"), None),
    )
    return jax.shard_map(
        on_device,
        mesh=mesh,
        in_specs=placed,
        out_specs=(
            P("dp", "seq", None),
            P(),
            P("dp", "seq", None),
            P("dp", "seq", None),
            P(("seq", "dp")),
            P(("seq", "dp"), None),
            P(("seq", "dp"), None),
            P(("seq", "dp"), None),
            P(("seq", "dp"), None),
            P(("seq", "dp")),
            P(("seq", "dp"), None),
            P(("seq", "dp"), None),
            P(("seq", "dp"), None),
        ),
        check_vma=False,
    )
```

profile of v0, /device:TPU:8, one launch (start us, length us, event | category | flops | bytes accessed | tf_op | source)
XLA Modules:
  0.0 1682.1 jit_solution(7669823449581622395)
XLA Ops:
  11.1 40.9 %all-reduce.3 = (bf16[1024]{0:T(1024)(128)(2,1)S(1)}, bf16[1024]{0:T(1024)(128)(2,1)S(1)}) all-reduce(bf16[1024]{0:T(1024)(128)(2,1)S(1)} %dynamic-update-slice, bf16[1024]{0:T(1024)(128)(2,1)S(1)} %dynamic-update-slice.1), channel_id=1, replica_groups=mesh['seq'=8,'dp'=4] {'seq','dp'}, use_global_device_ids=true, to_apply=%add | all-reduce | flops 2048 | bytes 8192
  54.6 13.0 all-gather.14.cloned.1.call-done
  67.6 2.9 fusion.50
  72.6 53.1 %all-gather.18.cloned.1.call-done = bf16[1024,1024]{1,0:T(8,128)(2,1)} async-done(((bf16[32,1024]{1,0:T(8,128)(2,1)}), bf16[1024,1024]{1,0:T(8,128)(2,1)}) %all-gather.18.cloned.1.call-update) | async-done | bytes 2097168 | tf_op jit(solution)/shard_map/all_gather | solution.py:193
  125.7 2.9 copy.67
  128.6 55.3 %all-gather.16.cloned.1.call-done = bf16[1024,1024]{1,0:T(8,128)(2,1)} async-done(((bf16[32,1024]{1,0:T(8,128)(2,1)}), bf16[1024,1024]{1,0:T(8,128)(2,1)}) %all-gather.16.cloned.1.call-update) | async-done | bytes 2097168 | tf_op jit(solution)/shard_map/all_gather | solution.py:192
  183.8 4.0 copy.66
  198.7 36.8 %all-gather.32.cloned.1.call-done = bf16[1024,1024]{1,0:T(8,128)(2,1)} async-done(((bf16[128,1024]{1,0:T(8,128)(2,1)}), bf16[1024,1024]{1,0:T(8,128)(2,1)}) %all-gather.32.cloned.1.call-update) | async-done | bytes 2097168 | tf_op jit(solution)/shard_map/all_gather | solution.py:227
  235.5 3.9 copy.65
  239.4 46.4 %all-gather.34.cloned.1.call-done = bf16[1024,1024]{1,0:T(8,128)(2,1)} async-done(((bf16[128,1024]{1,0:T(8,128)(2,1)}), bf16[1024,1024]{1,0:T(8,128)(2,1)}) %all-gather.34.cloned.1.call-update) | async-done | bytes 2097168 | tf_op jit(solution)/shard_map/all_gather | solution.py:227
  285.8 4.2 copy.68
  290.0 46.0 %all-gather.30.cloned.1.call-done = bf16[1,1024,1024]{1,2,0:T(8,128)(2,1)} async-done(((bf16[1,128,1024]{1,2,0:T(8,128)(2,1)}), bf16[1,1024,1024]{1,2,0:T(8,128)(2,1)}) %all-gather.30.cloned.1.call-update) | async-done | bytes 2097168 | tf_op jit(solution)/shard_map/all_gather | solution.py:224
  345.3 42.7 %all-gather.20.cloned.1.call-done = bf16[1,1024,1024]{1,2,0:T(8,128)(2,1)} async-done(((bf16[1,128,1024]{1,2,0:T(8,128)(2,1)}), bf16[1,1024,1024]{1,2,0:T(8,128)(2,1)}) %all-gather.20.cloned.1.call-update) | async-done | bytes 2097168 | tf_op jit(solution)/shard_map/all_gather | solution.py:224
  397.0 49.4 %all-gather.22.cloned.1.call-done = bf16[1024,1024]{1,0:T(8,128)(2,1)} async-done(((bf16[32,1024]{1,0:T(8,128)(2,1)}), bf16[1024,1024]{1,0:T(8,128)(2,1)}) %all-gather.22.cloned.1.call-update) | async-done | bytes 2097168 | tf_op jit(solution)/shard_map/all_gather | solution.py:195
  450.3 66.6 %all-gather.24.cloned.1.call-done = bf16[1024,2816]{1,0:T(8,128)(2,1)} async-done(((bf16[32,2816]{1,0:T(8,128)(2,1)}), bf16[1024,2816]{1,0:T(8,128)(2,1)}) %all-gather.24.cloned.1.call-update) | async-done | bytes 5767184 | tf_op jit(solution)/shard_map/all_gather | solution.py:197
  516.9 17.4 %fusion.206 = f32[128,2816]{1,0:T(8,128)} fusion(bf16[128,1024]{1,0:T(8,128)(2,1)S(1)} %get-tuple-element.87, bf16[1024,2816]{1,0:T(8,128)(2,1)} %all-gather.24.cloned.1.call-done), kind=kOutput, calls=%fused_computation.408 | convolution fusion | flops 738197504 | bytes 7471104 | tf_op jit(solution)/shard_map/dot_general | solution.py:240
  536.4 49.5 %all-gather.26.cloned.1.call-done = bf16[1024,2816]{1,0:T(8,128)(2,1)} async-done(((bf16[32,2816]{1,0:T(8,128)(2,1)}), bf16[1024,2816]{1,0:T(8,128)(2,1)}) %all-gather.26.cloned.1.call-update) | async-done | bytes 5767184 | tf_op jit(solution)/shard_map/all_gather | solution.py:198
  585.8 5.7 multiply_convert_fusion.12
  594.1 60.9 %all-gather.28.cloned.1.call-done = bf16[2816,1024]{1,0:T(8,128)(2,1)} async-done(((bf16[88,1024]{1,0:T(8,128)(2,1)}), bf16[2816,1024]{1,0:T(8,128)(2,1)}) %all-gather.28.cloned.1.call-update) | async-done | bytes 5767184 | tf_op jit(solution)/shard_map/all_gather | solution.py:199
  655.0 4.0 convolution_add_fusion.9
  664.3 38.1 %all-reduce.2 = (f32[]{:T(128)}, f32[]{:T(128)}) all-reduce(f32[]{:T(128)S(6)} %add.256, f32[]{:T(128)} %convert_reduce_fusion), channel_id=1, replica_groups=mesh['seq'=8,'dp'=4] {'seq','dp'}, use_global_device_ids=true, to_apply=%region_24.25 | all-reduce | flops 2 | bytes 16 | tf_op jit(solution)/shard_map/psum | solution.py:336
  702.4 2.8 fusion.192
  705.3 6.0 multiply_convert_fusion.8
  719.8 2.7 multiply_reduce_fusion.9
  728.9 2.5 multiply_reduce_fusion.4
  743.6 10.8 copy.82
  754.5 4.3 copy.91
  758.9 3.2 convolution_convert_fusion.8
  777.3 10.9 copy.84
  788.1 4.5 copy.90
  797.7 2.6 copy.72
  807.6 4.1 copy.70
  823.8 2.7 fusion.111
  826.5 6.0 fusion.12
  832.5 6.0 fusion.8
  840.5 57.4 %reduce-scatter.21.cloned.1.call-done = bf16[128,1024]{1,0:T(8,128)(2,1)} async-done(((bf16[1024,1024]{1,0:T(8,128)(2,1)}), bf16[128,1024]{1,0:T(8,128)(2,1)}) %reduce-scatter.21.cloned.1.call-update) | async-done | bytes 262160
  900.6 2.8 fusion.104
  903.4 2.8 fusion.100
  911.9 56.1 %reduce-scatter.13.cloned.1.call-done = bf16[1,128,1024]{2,1,0:T(8,128)(2,1)} async-done(((bf16[1,1024,1024]{2,1,0:T(8,128)(2,1)}), bf16[1,128,1024]{2,1,0:T(8,128)(2,1)}) %reduce-scatter.13.cloned.1.call-update) | async-done | bytes 262160 | tf_op jit(solution)/shard_map/reduce_scatter | solution.py:302
  968.1 2.8 fusion.46
  970.8 67.6 %reduce-scatter.11.cloned.1.call-done = bf16[1,128,1024]{2,1,0:T(8,128)(2,1)} async-done(((bf16[1,1024,1024]{2,1,0:T(8,128)(2,1)}), bf16[1,128,1024]{2,1,0:T(8,128)(2,1)}) %reduce-scatter.11.cloned.1.call-update) | async-done | bytes 262160 | tf_op jit(solution)/shard_map/reduce_scatter | solution.py:302
  1038.4 3.0 fusion.86
  1041.6 3.9 convolution_multiply_fusion
  1045.5 5.4 copy.75
  1050.9 42.6 %concatenate.165 = f32[1024,9730]{1,0:T(8,128)} concatenate(f32[1024,1024]{1,0:T(8,128)} %fusion.100, f32[1024,1024]{1,0:T(8,128)} %fusion.104, f32[1024,1024]{1,0:T(8,128)} %copy.75, f32[1024,1024]{1,0:T(8,128)} %fusion.111, f32[1024,2816]{1,0:T(8,128)} %fusion.8, f32[1024,2816]{1,0:T(8,128)} %fusion.12, f32[1024,1]{1,0:T(8,128)S(1)} %copy.77, f32[1024,1]{1,0:T(8,128)S(1)} %copy-done.99), dimensions={1} | concatenate | bytes 79708160 | tf_op jit(solution)/shard_map/concatenate | solution.py:353
  1095.0 6.5 fusion.16
  1107.3 412.1 %reduce-scatter.15.cloned.1.call-done = f32[32,9730]{1,0:T(8,128)} async-done(((f32[1024,9730]{1,0:T(8,128)}), f32[32,9730]{1,0:T(8,128)}) %reduce-scatter.15.cloned.1.call-update) | async-done | bytes 1245456 | tf_op jit(solution)/shard_map/reduce_scatter | solution.py:352
  1524.8 149.4 %reduce-scatter.17.cloned.1.call-done = f32[88,1024]{1,0:T(8,128)} async-done(((f32[2816,1024]{1,0:T(8,128)}), f32[88,1024]{1,0:T(8,128)}) %reduce-scatter.17.cloned.1.call-update) | async-done | bytes 360464 | tf_op jit(solution)/shard_map/reduce_scatter | solution.py:370
  (505 shorter events, 137.2 us)
Async XLA Ops:
  7.2 60.4 %all-gather.14.cloned.1.call-start = ((), (), s32[]{:S(2)}) async-start(), calls=%async_computation.6 | async-start | bytes 2162688 | tf_op jit(solution)/shard_map/all_gather | solution.py:194
  7.9 117.8 %all-gather.18.cloned.1.call-start = ((), (), s32[]{:S(2)}) async-start(), calls=%async_computation.8 | async-start | bytes 2162688 | tf_op jit(solution)/shard_map/all_gather | solution.py:193
  8.7 175.2 %all-gather.16.cloned.1.call-start = ((), (), s32[]{:S(2)}) async-start(), calls=%async_computation.7 | async-start | bytes 2162688 | tf_op jit(solution)/shard_map/all_gather | solution.py:192
  9.4 226.1 %all-gather.32.cloned.1.call-start = ((), (), s32[]{:S(2)}) async-start(), calls=%async_computation.19 | async-start | bytes 2359296 | tf_op jit(solution)/shard_map/all_gather | solution.py:227
  53.3 136.2 %copy-start.135 = (f32[128]{0:T(128)}, f32[128]{0:T(128)S(1)}, u32[]{:S(2)}) copy-start(f32[128]{0:T(128)S(1)} %get-tuple-element.136) | copy-start | bytes 1540
  53.3 137.7 %copy-start.137 = (f32[128]{0:T(128)}, f32[128]{0:T(128)S(1)}, u32[]{:S(2)}) copy-start(f32[128]{0:T(128)S(1)} %get-tuple-element.137) | copy-start | bytes 1540
  53.3 17.3 %copy-start.114 = (bf16[2,128,1024]{2,1,0:T(8,128)(2,1)S(1)}, bf16[2,128,1024]{2,1,0:T(8,128)(2,1)}, u32[]{:S(2)}) copy-start(bf16[2,128,1024]{2,1,0:T(8,128)(2,1)} %param.15) | copy-start | bytes 1572868
  54.6 17.1 %copy-start.64 = (bf16[128,1024]{1,0:T(8,128)(2,1)}, bf16[128,1024]{1,0:T(8,128)(2,1)S(1)}, u32[]{:S(2)}) copy-start(bf16[128,1024]{1,0:T(8,128)(2,1)S(1)} %get-tuple-element.71) | copy-start | bytes 786436
  54.6 17.1 %copy-start.66 = (bf16[128,1024]{1,0:T(8,128)(2,1)}, bf16[128,1024]{1,0:T(8,128)(2,1)S(1)}, u32[]{:S(2)}) copy-start(bf16[128,1024]{1,0:T(8,128)(2,1)S(1)} %get-tuple-element.72) | copy-start | bytes 786436
  70.5 215.3 %all-gather.34.cloned.1.call-start = ((), (), s32[]{:S(2)}) async-start(), calls=%async_computation.20 | async-start | bytes 2359296 | tf_op jit(solution)/shard_map/all_gather | solution.py:227
  71.8 264.3 %all-gather.30.cloned.1.call-start = ((), (), s32[]{:S(2)}) async-start(), calls=%async_computation.14 | async-start | bytes 2359296 | tf_op jit(solution)/shard_map/all_gather | solution.py:224
  192.2 200.5 %copy-start.57 = (bf16[1,128,16,32]{1,3,2,0:T(8,128)(2,1)}, bf16[1,128,16,32]{1,3,2,0:T(8,128)(2,1)S(1)}, u32[]{:S(2)}) copy-start(bf16[1,128,16,32]{1,3,2,0:T(8,128)(2,1)S(1)} %get-tuple-element.84) | copy-start | bytes 393220
  193.0 195.0 %all-gather.20.cloned.1.call-start = ((), (), s32[]{:S(2)}) async-start(), calls=%async_computation.9 | async-start | bytes 2359296 | tf_op jit(solution)/shard_map/all_gather | solution.py:224
  193.8 252.7 %all-gather.22.cloned.1.call-start = ((), (), s32[]{:S(2)}) async-start(), calls=%async_computation.10 | async-start | bytes 2162688 | tf_op jit(solution)/shard_map/all_gather | solution.py:195
  194.5 322.4 %all-gather.24.cloned.1.call-start = ((), (), s32[]{:S(2)}) async-start(), calls=%async_computation.11 | async-start | bytes 5947392 | tf_op jit(solution)/shard_map/all_gather | solution.py:197
  195.2 390.6 %all-gather.26.cloned.1.call-start = ((), (), s32[]{:S(2)}) async-start(), calls=%async_computation.12 | async-start | bytes 5947392 | tf_op jit(solution)/shard_map/all_gather | solution.py:198
  195.8 459.1 %all-gather.28.cloned.1.call-start = ((), (), s32[]{:S(2)}) async-start(), calls=%async_computation.13 | async-start | bytes 5947392 | tf_op jit(solution)/shard_map/all_gather | solution.py:199
  196.6 641.9 %reduce-scatter.19.cloned.1.call-start = ((), (), s32[]{:S(2)}) async-start(), calls=%async_computation.21 | async-start | bytes 2359296
  198.1 138.0 %copy-start.111 = (bf16[128,4,64]{0,2,1:T(8,128)(2,1)}, bf16[128,4,64]{0,2,1:T(8,128)(2,1)S(1)}, u32[]{:S(2)}) copy-start(bf16[128,4,64]{0,2,1:T(8,128)(2,1)S(1)} %fusion.159) | copy-start | bytes 196612
  345.3 101.1 %copy-start.92 = (bf16[1,128,16,64]{1,3,2,0:T(8,128)(2,1)}, bf16[1,128,16,64]{1,3,2,0:T(8,128)(2,1)S(1)}, u32[]{:S(2)}) copy-start(bf16[1,128,16,64]{1,3,2,0:T(8,128)(2,1)S(1)} %pad_maximum_fusion.16) | copy-start | bytes 786436
  397.0 52.3 %copy-start.94 = (bf16[1,128,16,64]{1,3,2,0:T(8,128)(2,1)}, bf16[1,128,16,64]{1,3,2,0:T(8,128)(2,1)S(1)}, u32[]{:S(2)}) copy-start(bf16[1,128,16,64]{1,3,2,0:T(8,128)(2,1)S(1)} %pad_maximum_fusion.14) | copy-start | bytes 786436
  450.3 135.5 %copy-start.70 = (bf16[128,1024]{1,0:T(8,128)(2,1)}, bf16[128,1024]{1,0:T(8,128)(2,1)S(1)}, u32[]{:S(2)}) copy-start(bf16[128,1024]{1,0:T(8,128)(2,1)S(1)} %get-tuple-element.88) | copy-start | bytes 786436
  450.3 141.2 %copy-start.68 = (bf16[128,1024]{1,0:T(8,128)(2,1)}, bf16[128,1024]{1,0:T(8,128)(2,1)S(1)}, u32[]{:S(2)}) copy-start(bf16[128,1024]{1,0:T(8,128)(2,1)S(1)} %get-tuple-element.87) | copy-start | bytes 786436
  516.9 17.4 %copy-start = (bf16[1024,2816]{1,0:T(8,128)(2,1)S(1)}, bf16[1024,2816]{1,0:T(8,128)(2,1)}, u32[]{:S(2)}) copy-start(bf16[1024,2816]{1,0:T(8,128)(2,1)} %all-gather.24.cloned.1.call-done) | copy-start | bytes 17301508
  585.8 5.7 copy-start.26
  585.8 5.7 copy-start.104
  702.4 8.9 slice-start
  702.4 10.9 slice-start.4
  705.2 6.1 copy-start.109
  705.2 8.1 copy-start.107
  705.2 6.1 slice-start.1
  705.3 8.1 slice-start.5
  705.3 8.1 copy-start.149
  711.3 6.4 copy-start.75
  711.3 6.3 slice-start.2
  758.8 139.1 %reduce-scatter.21.cloned.1.call-start = ((), (), s32[]{:S(2)}) async-start(), calls=%async_computation.22 | async-start | bytes 2359296
  792.6 175.4 %reduce-scatter.13.cloned.1.call-start = ((), (), s32[]{:S(2)}) async-start(), calls=%async_computation.16 | async-start | bytes 2359296 | tf_op jit(solution)/shard_map/reduce_scatter | solution.py:302
  800.4 238.0 %reduce-scatter.11.cloned.1.call-start = ((), (), s32[]{:S(2)}) async-start(), calls=%async_computation.15 | async-start | bytes 2359296 | tf_op jit(solution)/shard_map/reduce_scatter | solution.py:302
  807.6 5.7 copy-start.44
  822.4 697.0 %reduce-scatter.15.cloned.1.call-start = ((), (), s32[]{:S(2)}) async-start(), calls=%async_computation.17 | async-start | bytes 41631744 | tf_op jit(solution)/shard_map/reduce_scatter | solution.py:352
  826.5 6.0 copy-start.78
  826.5 6.0 copy-start.80
  839.7 59.9 %copy-start.116 = (f32[128,32]{0,1:T(8,128)S(1)}, f32[128,32]{0,1:T(8,128)}, u32[]{:S(2)}) copy-start(f32[128,32]{0,1:T(8,128)} %get-tuple-element.91) | copy-start | bytes 49156
  839.7 59.9 %copy-start.118 = (f32[128,32]{0,1:T(8,128)S(1)}, f32[128,32]{0,1:T(8,128)}, u32[]{:S(2)}) copy-start(f32[128,32]{0,1:T(8,128)} %get-tuple-element.92) | copy-start | bytes 49156
  910.3 57.8 %copy-start.25 = (bf16[1024,1024]{1,0:T(8,128)(2,1)S(1)}, bf16[1024,1024]{1,0:T(8,128)(2,1)}, u32[]{:S(2)}) copy-start(bf16[1024,1024]{1,0:T(8,128)(2,1)} %all-gather.14.cloned.1.call-done) | copy-start | bytes 6291460
  911.9 126.5 %copy-start.136 = (f32[128]{0:T(128)S(1)}, f32[128]{0:T(128)}, u32[]{:S(2)}) copy-start(f32[128]{0:T(128)} %copy-done.135) | copy-start | bytes 1540
  911.9 126.5 %copy-start.138 = (f32[128]{0:T(128)S(1)}, f32[128]{0:T(128)}, u32[]{:S(2)}) copy-start(f32[128]{0:T(128)} %copy-done.137) | copy-start | bytes 1540
  1093.6 580.6 %reduce-scatter.17.cloned.1.call-start = ((), (), s32[]{:S(2)}) async-start(), calls=%async_computation.18 | async-start | bytes 11894784 | tf_op jit(solution)/shard_map/reduce_scatter | solution.py:370
  (125 other events, 286.0 us)
Sparse Core Ops, SparseCore 0:
  10.9 56.6 all-gather.13
  70.5 55.2 all-gather.17
  128.6 55.2 all-gather.15
  186.4 49.0 all-gather.31
  238.0 47.7 all-gather.33
  288.3 47.7 all-gather.29
  338.7 49.2 all-gather.19
  390.8 55.5 all-gather.21
  449.3 67.5 all-gather.23
  519.5 66.2 all-gather.25
  588.7 66.2 all-gather.27
  758.9 69.1 reduce-scatter.18
  831.6 66.1 reduce-scatter.20
  901.2 66.7 reduce-scatter.12
  971.4 66.9 reduce-scatter.10
  1093.7 425.6 reduce-scatter.14
  1522.2 151.8 reduce-scatter.16
where the time goes:
time: 1700 us; the launch traced here: 1680 us
  waiting for transfers between devices  1270 us (75%)
  matrix products  145 us (9%)
  local copies, waits for them, and re-layouts  138 us (8%)
  blocking collectives  79 us (5%)
  other arithmetic  32.3 us (2%)
  between operations  20.1 us (1%)
    reduce_scatter x1, waiting for transfers between devices, on_device(): lax.psum_scatter(jnp.concatenate([weight_grad(normed_all, query_all_g), w...  412 us
    reduce_scatter x1, waiting for transfers between devices, on_device(): lax.psum_scatter(weight_grad(act_all, down_all), ('seq', 'dp'), scatter_d...  149 us
    reduce_scatter x2, waiting for transfers between devices, on_device(): lax.psum_scatter(value_grad_all.reshape(per_batch, length, model_width).a...  124 us
    all_gather x2, waiting for transfers between devices, on_device(): lax.all_gather(keys_own.reshape(per_batch, local_len, model_width), 'seq'...  88.7 us
    all_gather x2, waiting for transfers between devices, on_device(): lax.all_gather(mixed.reshape(per_batch, local_len, model_width), 'seq', a...  83.2 us
    all_gather x1, waiting for transfers between devices, on_device(): lax.all_gather(shards[6], ('seq', 'dp'), axis=0, tiled=True)  66.6 us
    unnamed x19, waiting for transfers between devices  62.2 us
    all_gather x1, waiting for transfers between devices, on_device(): lax.all_gather(shards[8], ('seq', 'dp'), axis=0, tiled=True)  60.9 us
  transfers between devices with their start and end apart: 17, of which 16 were waited for; matrix products, arithmetic and copies ran while one was open for 11% of the time, Pallas kernels for 0%

commit v1 on v0

v1 whole, which is shorter than its diff:
```python
import functools

import jax
import jax.numpy as jnp
from jax import lax
from jax.experimental import pallas as pl
from jax.experimental.pallas import tpu as pltpu
from jax.sharding import Mesh
from jax.sharding import PartitionSpec as P

HEAD_DIM = 64
BLOCK = 256
PAIR = 2 * HEAD_DIM

EPSILON = 1e-06
THETA = 10000.0
SCALE = 0.125
ALL = ("z", "y", "x", "c")
SEQ = ("z", "y")
F32 = jnp.float32
BF16 = jnp.bfloat16


def rotary_tables(positions):
    lane = jnp.arange(PAIR, dtype=jnp.int32)
    half = HEAD_DIM // 2
    index = (lane % half).astype(F32)
    frequency = THETA ** (-(index * 2.0 / HEAD_DIM))
    angles = positions.astype(F32)[:, None] * frequency[None, :]
    sign = jnp.where(lane % HEAD_DIM < half, -1.0, 1.0)[None, :]
    return jnp.cos(angles), jnp.sin(angles) * sign


def partner(values):
    half = HEAD_DIM // 2
    lane = lax.broadcasted_iota(jnp.int32, values.shape, values.ndim - 1)
    first = lane % HEAD_DIM < half
    width = values.shape[-1]
    return jnp.where(
        first,
        pltpu.roll(values, width - half, values.ndim - 1),
        pltpu.roll(values, half, values.ndim - 1),
    )


def dot_t(left, right):
    return lax.dot_general(left, right, (((1,), (1,)), ((), ())), preferred_element_type=F32)


def t_dot(left, right):
    return lax.dot_general(left, right, (((0,), (0,)), ((), ())), preferred_element_type=F32)


def dot(left, right):
    return jnp.dot(left, right, preferred_element_type=F32)


def attend_forward_kernel(qkv_ref, out_ref, total_ref):
    parts, _, _, rows, _ = qkv_ref.shape
    per_block = BLOCK // rows
    blocks = parts // per_block
    for head in range(2):
        lanes = pl.ds(head * HEAD_DIM, HEAD_DIM)
        for block in range(blocks):
            lo, hi = block * per_block, (block + 1) * per_block
            query = qkv_ref[lo:hi, 0, 0, :, lanes].reshape(BLOCK, HEAD_DIM)
            keys = qkv_ref[0:hi, 1, 0, :, lanes].reshape(hi * rows, HEAD_DIM)
            values = qkv_ref[0:hi, 2, 0, :, lanes].reshape(hi * rows, HEAD_DIM)
            scores = dot_t(keys, query) * SCALE
            top = jnp.max(scores, axis=0, keepdims=True)
            total = top + jnp.log(jnp.sum(jnp.exp(scores - top), axis=0, keepdims=True))
            probs = jnp.exp(scores - total).astype(BF16)
            mixed = t_dot(values, probs)
            out_ref[lo:hi, 0, :, lanes] = mixed.T.astype(BF16).reshape(per_block, rows, HEAD_DIM)
            total_ref[0, head, block : block + 1, :] = total


def attend_backward_kernel(qkv_ref, grad_ref, total_ref, cos_ref, sin_ref, out_ref, dk_acc, dv_acc):
    parts, _, _, rows, _ = qkv_ref.shape
    per_block = BLOCK // rows
    blocks = parts // per_block
    dk_acc[...] = jnp.zeros_like(dk_acc)
    dv_acc[...] = jnp.zeros_like(dv_acc)
    for block in range(blocks):
        lo, hi = block * per_block, (block + 1) * per_block
        keys_n = hi * rows
        dq_parts = []
        for head in range(2):
            lanes = pl.ds(head * HEAD_DIM, HEAD_DIM)
            query = qkv_ref[lo:hi, 0, 0, :, lanes].reshape(BLOCK, HEAD_DIM)
            grad = grad_ref[lo:hi, 0, :, lanes].reshape(BLOCK, HEAD_DIM)
            keys = qkv_ref[0:hi, 1, 0, :, lanes].reshape(keys_n, HEAD_DIM)
            values = qkv_ref[0:hi, 2, 0, :, lanes].reshape(keys_n, HEAD_DIM)
            scores = dot_t(keys, query) * SCALE
            probs = jnp.exp(scores - total_ref[0, head, block : block + 1, :])
            grad_probs = dot_t(values, grad)
            inner = jnp.sum(probs * grad_probs, axis=0, keepdims=True)
            grad_scores = (probs * (grad_probs - inner)).astype(BF16)
            dk_acc[0:keys_n, lanes] += dot(grad_scores, query) * SCALE
            dv_acc[0:keys_n, lanes] += dot(probs.astype(BF16), grad)
            dq_parts.append(t_dot(keys, grad_scores).T * SCALE)
        dq = jnp.concatenate(dq_parts, axis=1)
        cos = cos_ref[block * BLOCK : (block + 1) * BLOCK, :]
        sin = sin_ref[block * BLOCK : (block + 1) * BLOCK, :]
        dq = (dq * cos - partner(dq) * sin).astype(BF16)
        out_ref[lo:hi, 0, 0, :, :] = dq.reshape(per_block, rows, PAIR)
    dk = dk_acc[...]
    dk = (dk * cos_ref[...] - partner(dk) * sin_ref[...]).astype(BF16)
    out_ref[:, 1, 0, :, :] = dk.reshape(parts, rows, PAIR)
    out_ref[:, 2, 0, :, :] = dv_acc[...].astype(BF16).reshape(parts, rows, PAIR)


VMEM_LIMIT = 60 * 1024 * 1024


def attend_forward(qkv):
    parts, _, units, rows, _ = qkv.shape
    blocks = parts * rows // BLOCK
    return pl.pallas_call(
        attend_forward_kernel,
        grid=(units,),
        in_specs=[pl.BlockSpec((parts, 3, 1, rows, PAIR), lambda u: (0, 0, u, 0, 0))],
        out_specs=[
            pl.BlockSpec((parts, 1, rows, PAIR), lambda u: (0, u, 0, 0)),
            pl.BlockSpec((1, 2, blocks, BLOCK), lambda u: (u, 0, 0, 0)),
        ],
        out_shape=[
            jax.ShapeDtypeStruct((parts, units, rows, PAIR), BF16),
            jax.ShapeDtypeStruct((units, 2, blocks, BLOCK), F32),
        ],
        compiler_params=pltpu.CompilerParams(vmem_limit_bytes=VMEM_LIMIT),
        name="attend_forward",
    )(qkv)


def attend_backward(qkv, grad_att, totals, cos, sin):
    parts, _, units, rows, _ = qkv.shape
    length = parts * rows
    blocks = length // BLOCK
    return pl.pallas_call(
        attend_backward_kernel,
        grid=(units,),
        in_specs=[
            pl.BlockSpec((parts, 3, 1, rows, PAIR), lambda u: (0, 0, u, 0, 0)),
            pl.BlockSpec((parts, 1, rows, PAIR), lambda u: (0, u, 0, 0)),
            pl.BlockSpec((1, 2, blocks, BLOCK), lambda u: (u, 0, 0, 0)),
            pl.BlockSpec((length, PAIR), lambda u: (0, 0)),
            pl.BlockSpec((length, PAIR), lambda u: (0, 0)),
        ],
        out_specs=pl.BlockSpec((parts, 3, 1, rows, PAIR), lambda u: (0, 0, u, 0, 0)),
        out_shape=jax.ShapeDtypeStruct((parts, 3, units, rows, PAIR), BF16),
        scratch_shapes=[pltpu.VMEM((length, PAIR), F32), pltpu.VMEM((length, PAIR), F32)],
        compiler_params=pltpu.CompilerParams(vmem_limit_bytes=VMEM_LIMIT),
        name="attend_backward",
    )(qkv, grad_att, totals, cos, sin)


def swap(array, name, distance):
    size = lax.axis_size(name)
    return lax.ppermute(array, name, [(i, i ^ distance) for i in range(size)])


def arrange(pieces, at):
    bit = 1
    while bit < len(pieces):
        odd = (at & bit) != 0
        pieces = [jnp.where(odd, pieces[j ^ bit], pieces[j]) for j in range(len(pieces))]
        bit *= 2
    return pieces


def gather_rows(shard, order):
    value = shard
    held = []
    for name in order:
        at = lax.axis_index(name)
        pieces = [value] + [swap(value, name, k) for k in range(1, lax.axis_size(name))]
        held.append(name)
        held.sort(key=ALL.index)
        value = jnp.stack(arrange(pieces, at), axis=held.index(name))
    return value.reshape(-1, shard.shape[1])


def stage_rows(rows, order):
    sizes = [lax.axis_size(name) for name in order]
    per = rows // functools.reduce(lambda a, b: a * b, sizes)
    index = lax.broadcasted_iota(jnp.int32, (rows, 1), 0)
    left, inner = index // per, index % per
    place = {}
    for name, size in zip(reversed(order), reversed(sizes)):
        place[name] = (left % size) ^ lax.axis_index(name)
        left = left // size
    device = jnp.zeros_like(index)
    for name in ALL:
        device = device * lax.axis_size(name) + place[name]
    return device * per + inner


def reduce_staged(partial, order):
    columns = partial.shape[1]
    value = partial
    for stage, name in enumerate(order):
        size = lax.axis_size(name)
        value = value.reshape(size, -1, columns)
        received = [swap(value[k], name, k) for k in range(1, size)]
        total = value[0].astype(F32)
        for piece in received:
            total = total + piece.astype(F32)
        value = total if stage == len(order) - 1 else total.astype(BF16)
    return value


def params():
    return pltpu.CompilerParams(vmem_limit_bytes=VMEM_LIMIT)


def project_kernel(x_ref, first_ref, gain_ref, cos_ref, sin_ref, wq_ref, wk_ref, wv_ref, normed_ref, out_ref):
    @pl.when(pl.program_id(0) == 0)
    def _():
        x = x_ref[...].astype(F32)
        inv = lax.rsqrt(jnp.mean(x * x, axis=-1, keepdims=True) + EPSILON)
        normed_ref[...] = (x * inv * gain_ref[...]).astype(BF16)

    normed = normed_ref[...]
    width = wq_ref.shape[1]
    copies = normed.shape[0] // cos_ref.shape[0]
    cos = jnp.concatenate([jnp.concatenate([cos_ref[...]] * copies, 0)] * (width // PAIR), 1)
    sin = jnp.concatenate([jnp.concatenate([sin_ref[...]] * copies, 0)] * (width // PAIR), 1)
    query = dot(normed, wq_ref[...])
    query = (query * cos + partner(query) * sin).astype(BF16)
    key = dot(normed, wk_ref[...])
    key = (key * cos + partner(key) * sin).astype(BF16)
    mixed = (0.5 * dot(normed, wv_ref[...]) + 0.5 * first_ref[...].astype(F32)).astype(BF16)
    _, groups, _, units, rows, _ = out_ref.shape
    for kind, value in enumerate((query, key, mixed)):
        for pair in range(width // PAIR):
            piece = value[:, pair * PAIR : (pair + 1) * PAIR]
            out_ref[pair, :, kind] = piece.reshape(groups, units, rows, PAIR)


def project(x, first, gain, cos, sin, weights, groups, units):
    tokens, width = x.shape
    local_len = tokens // (groups * units)
    pairs = width // PAIR
    wide = 2 * PAIR
    steps = width // wide
    return pl.pallas_call(
        project_kernel,
        grid=(steps,),
        in_specs=[
            pl.BlockSpec((tokens, width), lambda j: (0, 0)),
            pl.BlockSpec((tokens, wide), lambda j: (0, j)),
            pl.BlockSpec((1, width), lambda j: (0, 0)),
            pl.BlockSpec((local_len, PAIR), lambda j: (0, 0)),
            pl.BlockSpec((local_len, PAIR), lambda j: (0, 0)),
            pl.BlockSpec((width, wide), lambda j: (0, j)),
            pl.BlockSpec((width, wide), lambda j: (0, steps + j)),
            pl.BlockSpec((width, wide), lambda j: (0, 2 * steps + j)),
        ],
        out_specs=[
            pl.BlockSpec((tokens, width), lambda j: (0, 0)),
            pl.BlockSpec((2, groups, 3, units, local_len, PAIR), lambda j: (j, 0, 0, 0, 0, 0)),
        ],
        out_shape=[
            jax.ShapeDtypeStruct((tokens, width), BF16),
            jax.ShapeDtypeStruct((pairs, groups, 3, units, local_len, PAIR), BF16),
        ],
        compiler_params=params(),
        name="project",
    )(x, first, gain, cos, sin, weights, weights, weights)


def join_kernel(x_ref, heads_ref, weight_ref, gain_ref, att_ref, hidden_ref, scaled_ref, inv_ref, normed_ref):
    pairs = heads_ref.shape[0]
    tokens = x_ref.shape[0]
    for pair in range(pairs):
        att_ref[:, pair * PAIR : (pair + 1) * PAIR] = heads_ref[pair].reshape(tokens, PAIR)
    hidden = x_ref[...].astype(F32) + dot(att_ref[...], weight_ref[...])
    inv = lax.rsqrt(jnp.mean(hidden * hidden, axis=-1, keepdims=True) + EPSILON)
    scaled = hidden * inv
    hidden_ref[...] = hidden
    scaled_ref[...] = scaled
    inv_ref[...] = jnp.broadcast_to(inv, inv_ref.shape)
    normed_ref[...] = (scaled * gain_ref[...]).astype(BF16)


def join(x, heads, weight, gain):
    tokens, width = x.shape
    return pl.pallas_call(
        join_kernel,
        out_shape=[
            jax.ShapeDtypeStruct((tokens, width), BF16),
            jax.ShapeDtypeStruct((tokens, width), F32),
            jax.ShapeDtypeStruct((tokens, width), F32),
            jax.ShapeDtypeStruct((tokens, PAIR), F32),
            jax.ShapeDtypeStruct((tokens, width), BF16),
        ],
        compiler_params=params(),
        name="join",
    )(x, heads, weight, gain)


def split_kernel(grad_ref, weight_ref, out_ref):
    value = dot_t(grad_ref[...], weight_ref[...]).astype(BF16)
    pairs, groups, _, units, rows, _ = out_ref.shape
    for pair in range(pairs):
        out_ref[pair, :, 0] = value[:, pair * PAIR : (pair + 1) * PAIR].reshape(groups, units, rows, PAIR)


def split(grad, weight, groups, units):
    tokens, width = grad.shape
    return pl.pallas_call(
        split_kernel,
        out_shape=jax.ShapeDtypeStruct(
            (width // PAIR, groups, 1, units, tokens // (groups * units), PAIR), BF16
        ),
        compiler_params=params(),
        name="split",
    )(grad, weight)


def picker(place, width):
    lane = lax.broadcasted_iota(jnp.int32, (place.shape[0], width), 1)
    return jnp.where(lane == place, 1.0, 0.0).astype(BF16)


def staged_kernel(left_ref, right_ref, place_ref, out_ref, turned):
    @pl.when(pl.program_id(0) == 0)
    def _():
        pick = picker(place_ref[...], left_ref.shape[1])
        turned[...] = dot_t(pick, left_ref[...]).astype(BF16)

    out_ref[...] = dot(turned[...], right_ref[...]).astype(BF16)


def staged_grad(left, right, place):
    tokens, width = left.shape
    columns = right.shape[1]
    wide = 2 * PAIR
    return pl.pallas_call(
        staged_kernel,
        grid=(columns // wide,),
        in_specs=[
            pl.BlockSpec((tokens, width), lambda j: (0, 0)),
            pl.BlockSpec((tokens, wide), lambda j: (0, j)),
            pl.BlockSpec((width, 1), lambda j: (0, 0)),
        ],
        out_specs=pl.BlockSpec((width, wide), lambda j: (0, j)),
        out_shape=jax.ShapeDtypeStruct((width, columns), BF16),
        scratch_shapes=[pltpu.VMEM((width, tokens), BF16)],
        compiler_params=params(),
        name="staged_grad",
    )(left, right, place)


def last_kernel(
    heads_ref, normed_ref, x_ref, gain_ref, wq_ref, wk_ref, wv_ref, grad_hidden_ref, gain_m_ref, loss_ref, place_b_ref,
    place_c_ref, grad_in_ref, first_ref, out_b_ref, out_c_ref, grads,
):
    pairs = heads_ref.shape[0]
    tokens, width = x_ref.shape
    for kind in range(3):
        for pair in range(pairs):
            grads[kind, :, pair * PAIR : (pair + 1) * PAIR] = heads_ref[pair, :, kind].reshape(tokens, PAIR)
    first_ref[...] = 0.5 * grads[2].astype(F32)
    grad_norm = (
        dot_t(grads[0], wq_ref[...]) + dot_t(grads[1], wk_ref[...]) + 0.5 * dot_t(grads[2], wv_ref[...])
    )
    x = x_ref[...].astype(F32)
    inv = lax.rsqrt(jnp.mean(x * x, axis=-1, keepdims=True) + EPSILON)
    scaled = x * inv
    gain_part = jnp.sum(grad_norm * scaled, axis=0, keepdims=True)
    scaled_grad = grad_norm * gain_ref[...]
    grad_in_ref[...] = grad_hidden_ref[...] + inv * (
        scaled_grad - scaled * jnp.mean(scaled_grad * scaled, axis=-1, keepdims=True)
    )
    half = width // 2
    pick_b = picker(place_b_ref[...], width)
    turned = dot_t(pick_b, normed_ref[...]).astype(BF16)
    out_b_ref[:, :width] = dot(turned, grads[0]).astype(BF16)
    out_b_ref[:, width : width + half] = (0.5 * dot(turned, grads[2, :, :half])).astype(BF16)
    pick_c = picker(place_c_ref[...], width)
    turned = dot_t(pick_c, normed_ref[...]).astype(BF16)
    out_c_ref[:, :width] = dot(turned, grads[1]).astype(BF16)
    out_c_ref[:, width : width + half] = (0.5 * dot(turned, grads[2, :, half:])).astype(BF16)
    row = lax.broadcasted_iota(jnp.int32, (PAIR, width), 0)
    extra = jnp.where(row == 0, gain_part, jnp.where(row == 1, gain_m_ref[...], loss_ref[...]))
    out_c_ref[:, width + half :] = dot_t(pick_c, extra.astype(BF16)).astype(BF16)


def last(heads, normed, x, gain, weights, grad_hidden, gain_m_part, loss_rows, place_b, place_c):
    tokens, width = x.shape
    whole = lambda *shape: pl.BlockSpec(shape, lambda i: (0,) * len(shape))
    half = width // 2
    return pl.pallas_call(
        last_kernel,
        grid=(1,),
        in_specs=[
            whole(*heads.shape),
            whole(tokens, width),
            whole(tokens, width),
            whole(1, width),
            pl.BlockSpec((width, width), lambda i: (0, 0)),
            pl.BlockSpec((width, width), lambda i: (0, 1)),
            pl.BlockSpec((width, width), lambda i: (0, 2)),
            whole(tokens, width),
            whole(1, width),
            whole(PAIR, 1),
            whole(width, 1),
            whole(width, 1),
        ],
        out_specs=[
            whole(tokens, width),
            whole(tokens, width),
            whole(width, width + half),
            whole(width, width + half + PAIR),
        ],
        out_shape=[
            jax.ShapeDtypeStruct((tokens, width), F32),
            jax.ShapeDtypeStruct((tokens, width), F32),
            jax.ShapeDtypeStruct((width, width + half), BF16),
            jax.ShapeDtypeStruct((width, width + half + PAIR), BF16),
        ],
        scratch_shapes=[pltpu.VMEM((3, tokens, width), BF16)],
        compiler_params=params(),
        name="last",
    )(heads, normed, x, gain, weights, weights, weights, grad_hidden, gain_m_part, loss_rows, place_b, place_c)


STAGES_B = ("c", "y", "x", "z")
STAGES_C = ("c", "x", "y", "z")


def on_device(
    inputs,
    first_values,
    teacher_states,
    out_cotangent,
    token_valid,
    attn_gain,
    w_query,
    w_key,
    w_value,
    w_output,
    mlp_gain,
    w_gate,
    w_up,
    w_down,
):
    batch, local_len, width = inputs.shape
    seqs = lax.axis_size(SEQ)
    devices = lax.axis_size(ALL)
    tokens = batch * local_len
    length = local_len * seqs
    pairs = width // PAIR
    own_rows = w_query.shape[0]
    own_down = w_down.shape[0]
    groups = seqs // pairs
    units = batch // groups

    valid_float = token_valid.astype(F32)
    count = jnp.sum(token_valid)
    extra = jnp.stack(
        [
            attn_gain,
            mlp_gain,
            jnp.full((own_rows,), count // 256, jnp.int32).astype(BF16),
            jnp.full((own_rows,), count % 256, jnp.int32).astype(BF16),
        ],
        axis=1,
    )
    extra = jnp.pad(extra, ((0, 0), (0, PAIR - 4)))
    first_w = lax.all_gather(
        jnp.concatenate([w_query, w_key, w_value, extra], axis=1), ALL, axis=0, tiled=True
    )
    gate_w = gather_rows(w_gate, ("z", "x", "y", "c"))
    up_w = gather_rows(w_up, ("z", "y", "x", "c"))
    rest_w = lax.all_gather(jnp.concatenate([w_down, w_output], axis=0), ALL, axis=0)
    down_w = rest_w[:, :own_down].reshape(-1, width)
    output_w = rest_w[:, own_down:].reshape(-1, width)

    extra_all = first_w[:, 3 * width :].astype(F32).T
    gain_a = extra_all[0:1, :]
    gain_m = extra_all[1:2, :]
    valid_total = jnp.sum(extra_all[2] * 256.0 + extra_all[3]) / own_rows

    cos_all, sin_all = rotary_tables(jnp.arange(length, dtype=jnp.int32))
    here = lax.axis_index(SEQ) * local_len
    cos = lax.dynamic_slice_in_dim(cos_all, here, local_len, 0)
    sin = lax.dynamic_slice_in_dim(sin_all, here, local_len, 0)
    place_b = stage_rows(width, STAGES_B)
    place_c = stage_rows(width, STAGES_C)

    x_low = inputs.reshape(tokens, width)
    normed, packed = project(
        x_low, first_values.reshape(tokens, width), gain_a, cos, sin, first_w, groups, units
    )

    def exchange(array, kinds):
        array = array.reshape(seqs, kinds, units, local_len, PAIR)
        return lax.all_to_all(array, SEQ, split_axis=0, concat_axis=0, tiled=True)

    def by_pair(array):
        return array.reshape(pairs, groups, array.shape[1], units, local_len, PAIR)

    qkv = exchange(packed, 3)
    attended, totals = attend_forward(qkv)
    att_heads = by_pair(exchange(attended, 1))

    att_low, hidden_in, scaled_m, inv_wide, normed_mlp = join(
        x_low, att_heads.reshape(pairs, groups, units, local_len, PAIR), output_w, gain_m
    )
    inv_rms_m = inv_wide[:, :1]
    gate_pre = dot(normed_mlp, gate_w)
    up_part = dot(normed_mlp, up_w)
    gate_sigmoid = jax.nn.sigmoid(gate_pre)
    swish_value = gate_pre * gate_sigmoid
    activated = (swish_value * up_part).astype(BF16)
    result = hidden_in + dot(activated, down_w)
    residual_err = result - teacher_states.astype(F32).reshape(tokens, width)
    valid_rows = valid_float.reshape(tokens, 1)
    token_loss = valid_rows * jnp.mean(residual_err * residual_err, axis=-1, keepdims=True)
    grad_out = (
        out_cotangent.astype(F32).reshape(tokens, width)
        + 2.0 / width * valid_rows * residual_err / valid_total
    )

    grad_down_in = grad_out.astype(BF16)
    grad_act = dot_t(grad_down_in, down_w)
    swish_slope = gate_sigmoid * (1.0 + gate_pre * (1.0 - gate_sigmoid))
    grad_gate_in = (grad_act * up_part * swish_slope).astype(BF16)
    grad_up_in = (grad_act * swish_value).astype(BF16)
    grad_norm_m = dot_t(grad_gate_in, gate_w) + dot_t(grad_up_in, up_w)
    gain_part_m = jnp.sum(grad_norm_m * scaled_m, axis=0, keepdims=True)
    scaled_grad_m = grad_norm_m * gain_m
    grad_hidden = grad_out + inv_rms_m * (
        scaled_grad_m - scaled_m * jnp.mean(scaled_grad_m * scaled_m, axis=-1, keepdims=True)
    )
    grad_branch = grad_hidden.astype(BF16)
    grad_heads = exchange(split(grad_branch, output_w, groups, units), 1)

    down_part = t_dot(activated, grad_down_in).astype(BF16).reshape(devices, own_down, width)
    output_part = t_dot(att_low, grad_branch).astype(BF16).reshape(devices, own_rows, width)
    owned_rest = lax.psum_scatter(
        jnp.concatenate([down_part, output_part], axis=1), ALL, scatter_dimension=0, tiled=True
    )[0].astype(F32)
    owned_gate = reduce_staged(staged_grad(normed_mlp, grad_gate_in, place_b), STAGES_B)
    owned_up = reduce_staged(staged_grad(normed_mlp, grad_up_in, place_c), STAGES_C)

    grad_qkv = attend_backward(qkv, grad_heads[:, 0], totals, cos_all, sin_all)
    grad_qkv = by_pair(exchange(grad_qkv, 3))

    loss_rows = jnp.sum(token_loss.reshape(-1, 64), axis=0)
    loss_rows = jnp.concatenate([jnp.zeros((PAIR - 64,), F32), loss_rows])[:, None]
    grad_in, grad_first, part_b, part_c = last(
        grad_qkv, normed, x_low, gain_a, first_w, grad_hidden, gain_part_m, loss_rows, place_b, place_c
    )
    owned_b = reduce_staged(part_b, STAGES_B)
    owned_c = reduce_staged(part_c, STAGES_C)
    half = width // 2
    owned_tail = owned_c[:, width + half :]
    loss_value = jnp.sum(owned_tail[0, PAIR - 64 :]) / valid_total
    return (
        result.reshape(batch, local_len, width),
        loss_value,
        grad_in.reshape(batch, local_len, width),
        grad_first.reshape(batch, local_len, width),
        owned_tail[:, 0],
        owned_b[:, :width],
        owned_c[:, :width],
        jnp.concatenate([owned_b[:, width:], owned_c[:, width : width + half]], axis=1),
        owned_rest[own_down:],
        owned_tail[:, 1],
        owned_gate,
        owned_up,
        owned_rest[:own_down],
    )


def solution(mesh):
    seqs, dps = mesh.devices.shape
    fine = Mesh(mesh.devices.reshape(seqs // 2, 2, dps // 2, 2), ALL)
    tokens = P(("x", "c"), SEQ, None)
    rows = P(ALL, None)
    gain = P(ALL)
    return jax.shard_map(
        on_device,
        mesh=fine,
        in_specs=(
            tokens, tokens, tokens, tokens, P(("x", "c"), SEQ), gain, rows, rows, rows, rows, gain, rows, rows, rows,
        ),
        out_specs=(
            tokens, P(), tokens, tokens, gain, rows, rows, rows, rows, gain, rows, rows, rows,
        ),
        check_vma=False,
    )
```

time: 1700 us -> 544 us (0.32)
  waiting for transfers between devices: 1270 us -> 235 us
  matrix products: 145 us -> 26.3 us
  local copies, waits for them, and re-layouts: 138 us -> 41 us
  blocking collectives: 79 us -> 0 us
  starting transfers between devices: 0.85 us -> 75.3 us
  Pallas kernels: 0 us -> 72.6 us
  other arithmetic: 32.3 us -> 64.7 us
    reduce_scatter x4 -> x1, waiting for transfers between devices: 685 us -> 7.87 us  [on_device(): lax.psum_scatter(jnp.concatenate([down_part, output_part], axis=1), ALL,...]
    all_gather x11 -> x2, waiting for transfers between devices: 519 us -> 0.02 us  [the longest x1 0.02 us: on_device(): lax.all_gather(jnp.concatenate([w_down, w_output], axis=0), ALL, axis=0)]
    ppermute x0 -> x36, waiting for transfers between devices: none -> 165 us  [swap(): return lax.ppermute(array, name, [(i, i ^ distance) for i in range(size)])]
    dot_general x83 -> x8, matrix products: 145 us -> 26.3 us  [the longest x3 10.9 us: dot_t(): lax.dot_general(left, right, (((1,), (1,)), ((), ())), preferred_element_...]
    pallas_call x0 -> x8, Pallas kernels: none -> 72.6 us  [the longest x2 20.6 us: staged_grad(): pl.pallas_call(staged_kernel, grid=(columns // wide,), in_specs=[pl.Block...]
    unnamed x19 -> x3, waiting for transfers between devices: 62.2 us -> 0.05 us
    all_to_all x0 -> x4, waiting for transfers between devices: none -> 61.8 us  [exchange(): return lax.all_to_all(array, SEQ, split_axis=0, concat_axis=0, tiled=True)]
    unnamed x324 -> x72, local copies, waits for them, and re-layouts: 58.3 us -> 7.43 us
  transfers between devices with their start and end apart: 17 -> 43, of which waited for: 16 -> 26; matrix products, arithmetic and copies ran while one was open for 11% -> 19% of each run, Pallas kernels for 0% -> 11%
where the time goes in v1:
time: 544 us; the launch traced here: 535 us
  waiting for transfers between devices  235 us (43%)
  starting transfers between devices  75.3 us (14%)
  Pallas kernels  72.6 us (13%)
  other arithmetic  64.7 us (12%)
  local copies, waits for them, and re-layouts  41 us (8%)
  matrix products  26.3 us (5%)
  between operations  19.7 us (4%)
    ppermute x36, waiting for transfers between devices, swap(): return lax.ppermute(array, name, [(i, i ^ distance) for i in range(size)])  165 us
    all_to_all x4, waiting for transfers between devices, exchange(): return lax.all_to_all(array, SEQ, split_axis=0, concat_axis=0, tiled=True)  61.8 us
    ppermute x36, starting transfers between devices, swap(): return lax.ppermute(array, name, [(i, i ^ distance) for i in range(size)])  49.2 us
    another operation x15, other arithmetic, gather_rows(): value = jnp.stack(arrange(pieces, at), axis=held.index(name))  27.4 us
    all_to_all x4, starting transfers between devices, exchange(): return lax.all_to_all(array, SEQ, split_axis=0, concat_axis=0, tiled=True)  25.6 us
    pallas_call x2, Pallas kernels, staged_grad(): pl.pallas_call(staged_kernel, grid=(columns // wide,), in_specs=[pl.Block...  20.6 us
    pallas_call x1, Pallas kernels, attend_backward(): pl.pallas_call(attend_backward_kernel, grid=(units,), in_specs=[pl.BlockS...  14.2 us
    slice x16, local copies, waits for them, and re-layouts, reduce_staged(): received = [swap(value[k], name, k) for k in range(1, size)]  13.4 us
  transfers between devices with their start and end apart: 43, of which 26 were waited for; matrix products, arithmetic and copies ran while one was open for 19% of the time, Pallas kernels for 11%

profile of v1, /device:TPU:8, one launch (start us, length us, event | category | flops | bytes accessed | tf_op | source)
XLA Modules:
  0.0 534.5 jit_solution(17474277654010241186)
XLA Ops:
  21.8 12.3 %collective-permute-done.1 = bf16[32,2816]{1,0:T(8,128)(2,1)S(1)} collective-permute-done((bf16[32,2816]{1,0:T(8,128)(2,1)}, bf16[32,2816]{1,0:T(8,128)(2,1)S(1)}, u32[]{:S(2)}, u32[]{:S(2)}) %collective-permute-start.1) | collective-permute-done | bytes 180256 | tf_op jit(solution)/shard_map/ppermute | solution.py:160
  34.0 3.5 collective-permute-start.8
  37.5 9.0 %collective-permute-done = bf16[32,2816]{1,0:T(8,128)(2,1)S(1)} collective-permute-done((bf16[32,2816]{1,0:T(8,128)(2,1)}, bf16[32,2816]{1,0:T(8,128)(2,1)S(1)}, u32[]{:S(2)}, u32[]{:S(2)}) %collective-permute-start) | collective-permute-done | bytes 180256 | tf_op jit(solution)/shard_map/ppermute | solution.py:160
  46.5 3.4 collective-permute-done.7
  49.9 9.6 %collective-permute-done.6 = bf16[32,2816]{1,0:T(8,128)(2,1)S(1)} collective-permute-done((bf16[32,2816]{1,0:T(8,128)(2,1)}, bf16[32,2816]{1,0:T(8,128)(2,1)S(1)}, u32[]{:S(2)}, u32[]{:S(2)}) %collective-permute-start.6) | collective-permute-done | bytes 180256 | tf_op jit(solution)/shard_map/ppermute | solution.py:160
  65.6 19.9 %collective-permute-done.3 = bf16[4,32,2816]{2,1,0:T(8,128)(2,1)} collective-permute-done((bf16[4,32,2816]{2,1,0:T(8,128)(2,1)S(1)}, bf16[4,32,2816]{2,1,0:T(8,128)(2,1)}, u32[]{:S(2)}, u32[]{:S(2)}) %collective-permute-start.3) | collective-permute-done | bytes 720928 | tf_op jit(solution)/shard_map/ppermute | solution.py:160
  93.9 32.0 %collective-permute-done.4 = bf16[4,2,32,2816]{3,2,1,0:T(8,128)(2,1)} collective-permute-done((bf16[4,2,32,2816]{3,2,1,0:T(8,128)(2,1)}, bf16[4,2,32,2816]{3,2,1,0:T(8,128)(2,1)}, u32[]{:S(2)}, u32[]{:S(2)}) %collective-permute-start.4) | collective-permute-done | bytes 1441824 | tf_op jit(solution)/shard_map/ppermute | solution.py:160
  139.8 6.7 %project.1 = (bf16[256,1024]{1,0:T(8,128)(2,1)}, bf16[8,1,3,2,128,128]{5,4,3,2,1,0:T(8,128)(2,1)}) custom-call(bf16[256,1024]{1,0:T(8,128)(2,1)} %bitcast.121, bf16[256,1024]{1,0:T(8,128)(2,1)} %bitcast.127, f32[1,1024]{1,0:T(1,128)} %copy.59.gain_ref, f32[128,128]{1,0:T(8,128)} %constant_dynamic-slice_fusion.1.cos_ref, ...), custom_call_target="tpu_custom_call" | custom-call | tf_op jit(solution)/shard_map/project/pallas_call | solution.py:247
  146.6 6.7 %all-to-all-start = ((bf16[8,3,2,128,128]{4,3,2,1,0:T(8,128)(2,1)}), bf16[8,3,2,128,128]{4,3,2,1,0:T(8,128)(2,1)S(1)}, u32[]{:S(2)}, u32[]{:S(2)}) async-start(bf16[8,3,2,128,128]{4,3,2,1,0:T(8,128)(2,1)} %bitcast.126), calls=%async_computation | async-start | bytes 3145728 | tf_op jit(solution)/shard_map/all_to_all | solution.py:501
  155.6 5.3 select_bitcast_fusion.3
  161.6 4.1 select_bitcast_fusion.1
  165.6 42.3 %all-to-all-done.qkv_ref = bf16[8,3,2,128,128]{4,3,2,1,0:T(8,128)(2,1)S(1)} async-done(((bf16[8,3,2,128,128]{4,3,2,1,0:T(8,128)(2,1)}), bf16[8,3,2,128,128]{4,3,2,1,0:T(8,128)(2,1)S(1)}, u32[]{:S(2)}, u32[]{:S(2)}) %all-to-all-start) | async-done | bytes 1572896 | tf_op jit(solution)/shard_map/all_to_all | solution.py:501
  209.1 11.4 %attend_forward.1 = (bf16[8,2,128,128]{3,2,1,0:T(8,128)(2,1)}, f32[2,2,4,256]{3,2,1,0:T(4,128)}) custom-call(bf16[8,3,2,128,128]{4,3,2,1,0:T(8,128)(2,1)} %copy-done), custom_call_target="tpu_custom_call" | custom-call | tf_op jit(solution)/shard_map/attend_forward/pallas_call | solution.py:119
  220.5 7.4 %all-to-all-start.1 = ((bf16[8,1,2,128,128]{4,3,2,1,0:T(8,128)(2,1)}), bf16[8,1,2,128,128]{4,3,2,1,0:T(8,128)(2,1)S(1)}, u32[]{:S(2)}, u32[]{:S(2)}) async-start(bf16[8,1,2,128,128]{4,3,2,1,0:T(8,128)(2,1)} %bitcast.128), calls=%async_computation.1 | async-start | bytes 1048576 | tf_op jit(solution)/shard_map/all_to_all | solution.py:501
  231.2 3.4 copy.66
  243.6 5.8 %slice.284 = bf16[32,88,1024]{2,1,0:T(8,128)(2,1)} slice(bf16[32,120,1024]{2,1,0:T(8,128)(2,1)} %bitcast.108), slice={[0:32], [0:88], [0:1024]} | slice | bytes 11534336 | tf_op jit(solution)/shard_map/slice | solution.py:479
  250.2 4.4 join.1
  254.6 4.6 fusion.40
  264.2 4.0 multiply_convert_fusion.1
  268.2 10.2 %staged_grad.3 = bf16[1024,2816]{1,0:T(8,128)(2,1)} custom-call(bf16[256,1024]{1,0:T(8,128)(2,1)} %get-tuple-element.29.left_ref, bf16[256,2816]{1,0:T(8,128)(2,1)} %get-tuple-element.48.right_ref, s32[1024,1]{1,0:T(8,128)} %get-tuple-element.95.place_c_ref.place_ref), custom_call_target="tpu_custom_call" | custom-call | tf_op jit(solution)/shard_map/staged_grad/pallas_call | solution.py:340
  278.4 3.6 slice.322
  282.0 10.4 %staged_grad.2 = bf16[1024,2816]{1,0:T(8,128)(2,1)} custom-call(bf16[256,1024]{1,0:T(8,128)(2,1)} %get-tuple-element.29.left_ref, bf16[256,2816]{1,0:T(8,128)(2,1)} %get-tuple-element.47.right_ref, s32[1024,1]{1,0:T(8,128)} %get-tuple-element.96.place_b_ref.place_ref), custom_call_target="tpu_custom_call" | custom-call | tf_op jit(solution)/shard_map/staged_grad/pallas_call | solution.py:340
  292.4 3.8 slice.312
  296.7 4.5 fusion.41
  305.2 3.3 split.1
  308.5 6.0 %all-to-all-start.2 = ((bf16[8,1,2,128,128]{4,3,2,1,0:T(8,128)(2,1)}), bf16[8,1,2,128,128]{4,3,2,1,0:T(8,128)(2,1)S(1)}, u32[]{:S(2)}, u32[]{:S(2)}) async-start(bf16[8,1,2,128,128]{4,3,2,1,0:T(8,128)(2,1)} %bitcast.125), calls=%async_computation.2 | async-start | bytes 1048576 | tf_op jit(solution)/shard_map/all_to_all | solution.py:501
  314.7 4.2 convolution_convert_fusion
  318.9 9.0 %all-to-all-done.2 = bf16[8,1,2,128,128]{4,3,2,1,0:T(8,128)(2,1)S(1)} async-done(((bf16[8,1,2,128,128]{4,3,2,1,0:T(8,128)(2,1)}), bf16[8,1,2,128,128]{4,3,2,1,0:T(8,128)(2,1)S(1)}, u32[]{:S(2)}, u32[]{:S(2)}) %all-to-all-start.2) | async-done | bytes 524320 | tf_op jit(solution)/shard_map/all_to_all | solution.py:501
  328.7 14.2 %attend_backward.1 = bf16[8,3,2,128,128]{4,3,2,1,0:T(8,128)(2,1)} custom-call(bf16[8,3,2,128,128]{4,3,2,1,0:T(8,128)(2,1)} %copy-done, bf16[8,2,128,128]{3,2,1,0:T(8,128)(2,1)} %bitcast.124, f32[2,2,4,256]{3,2,1,0:T(4,128)} %get-tuple-element.32.total_ref, f32[1024,128]{1,0:T(8,128)} %copy-done.14, f32[1024,128]{1,0:T(8,128)} %copy-done.13), custom_call_target="tpu_custom_call" | custom-call | tf_op jit(solution)/shard_map/attend_backward/pallas_call | solution.py:140
  342.8 5.5 %all-to-all-start.3 = ((bf16[8,3,2,128,128]{4,3,2,1,0:T(8,128)(2,1)}), bf16[8,3,2,128,128]{4,3,2,1,0:T(8,128)(2,1)}, u32[]{:S(2)}, u32[]{:S(2)}) async-start(bf16[8,3,2,128,128]{4,3,2,1,0:T(8,128)(2,1)} %attend_backward.1), calls=%async_computation.3 | async-start | bytes 3145728 | tf_op jit(solution)/shard_map/all_to_all | solution.py:501
  350.8 3.5 add_convert_fusion
  363.6 7.4 %pad_maximum_fusion = bf16[32,120,1024]{2,1,0:T(8,128)(2,1)} fusion(bf16[32,32,1024]{2,1,0:T(8,128)(2,1)} %bitcast.106, bf16[32,88,1024]{2,1,0:T(8,128)(2,1)} %bitcast.101), kind=kLoop, calls=%fused_computation | loop fusion | flops 15728640 | bytes 15728640 | tf_op jit(solution)/shard_map/concatenate | solution.py:545
  371.1 10.5 %all-to-all-done.3 = bf16[8,3,2,128,128]{4,3,2,1,0:T(8,128)(2,1)} async-done(((bf16[8,3,2,128,128]{4,3,2,1,0:T(8,128)(2,1)}), bf16[8,3,2,128,128]{4,3,2,1,0:T(8,128)(2,1)}, u32[]{:S(2)}, u32[]{:S(2)}) %all-to-all-start.3) | async-done | bytes 1572896 | tf_op jit(solution)/shard_map/all_to_all | solution.py:501
  381.6 12.0 %last.1 = (f32[256,1024]{1,0:T(8,128)}, f32[256,1024]{1,0:T(8,128)}, bf16[1024,1536]{1,0:T(8,128)(2,1)}, bf16[1024,1664]{1,0:T(8,128)(2,1)}) custom-call(bf16[8,1,3,2,128,128]{5,4,3,2,1,0:T(8,128)(2,1)} %bitcast.42.heads_ref, bf16[256,1024]{1,0:T(8,128)(2,1)} %get-tuple-element.33.normed_ref, bf16[256,1024]{1,0:T(8,128)(2,1)} %bitcast.123, ...), custom_call_target="tpu_custom_call" | custom-call | tf_op jit(solution)/shard_map/last/pallas_call | solution.py:395
  407.0 10.6 %collective-permute-done.32 = bf16[128,2816]{1,0:T(8,128)(2,1)S(1)} collective-permute-done((bf16[128,2816]{1,0:T(8,128)(2,1)S(1)}, bf16[128,2816]{1,0:T(8,128)(2,1)S(1)}, u32[]{:S(2)}, u32[]{:S(2)}) %collective-permute-start.32) | collective-permute-done | bytes 720928 | tf_op jit(solution)/shard_map/ppermute | solution.py:160
  417.8 3.4 collective-permute-start.33
  424.3 4.4 collective-permute-done.33
  428.8 4.0 collective-permute-start.27
  432.7 9.2 %collective-permute-done.35 = bf16[32,2816]{1,0:T(8,128)(2,1)S(1)} collective-permute-done((bf16[32,2816]{1,0:T(8,128)(2,1)S(1)}, bf16[32,2816]{1,0:T(8,128)(2,1)S(1)}, u32[]{:S(2)}, u32[]{:S(2)}) %collective-permute-start.35) | collective-permute-done | bytes 180256 | tf_op jit(solution)/shard_map/ppermute | solution.py:160
  443.4 14.9 %collective-permute-done.34 = bf16[32,2816]{1,0:T(8,128)(2,1)S(1)} collective-permute-done((bf16[32,2816]{1,0:T(8,128)(2,1)S(1)}, bf16[32,2816]{1,0:T(8,128)(2,1)S(1)}, u32[]{:S(2)}, u32[]{:S(2)}) %collective-permute-start.34) | collective-permute-done | bytes 180256 | tf_op jit(solution)/shard_map/ppermute | solution.py:160
  458.3 4.2 collective-permute-start.28
  466.3 5.8 %collective-permute-done.29 = bf16[32,2816]{1,0:T(8,128)(2,1)S(1)} collective-permute-done((bf16[32,2816]{1,0:T(8,128)(2,1)S(1)}, bf16[32,2816]{1,0:T(8,128)(2,1)S(1)}, u32[]{:S(2)}, u32[]{:S(2)}) %collective-permute-start.29) | collective-permute-done | bytes 180256 | tf_op jit(solution)/shard_map/ppermute | solution.py:160
  477.0 8.6 %collective-permute-done.13 = bf16[256,1664]{1,0:T(8,128)(2,1)S(1)} collective-permute-done((bf16[256,1664]{1,0:T(8,128)(2,1)S(1)}, bf16[256,1664]{1,0:T(8,128)(2,1)S(1)}, u32[]{:S(2)}, u32[]{:S(2)}) %collective-permute-start.13) | collective-permute-done | bytes 852000 | tf_op jit(solution)/shard_map/ppermute | solution.py:160
  487.1 3.7 collective-permute-done.20
  492.1 3.3 collective-permute-start.22
  500.0 5.4 %collective-permute-done.22 = bf16[32,1536]{1,0:T(8,128)(2,1)S(1)} collective-permute-done((bf16[32,1536]{1,0:T(8,128)(2,1)S(1)}, bf16[32,1536]{1,0:T(8,128)(2,1)S(1)}, u32[]{:S(2)}, u32[]{:S(2)}) %collective-permute-start.22) | collective-permute-done | bytes 98336 | tf_op jit(solution)/shard_map/ppermute | solution.py:160
  506.2 5.2 collective-permute-done.17
  516.4 7.9 %reduce-scatter.2.cloned.1.call-done = bf16[1,120,1024]{2,1,0:T(8,128)(2,1)} async-done(((bf16[32,120,1024]{2,1,0:T(8,128)(2,1)}), bf16[1,120,1024]{2,1,0:T(8,128)(2,1)}) %reduce-scatter.2.cloned.1.call-update) | async-done | bytes 245776 | tf_op jit(solution)/shard_map/reduce_scatter | solution.py:544
  (221 shorter events, 120.5 us)
Async XLA Ops:
  7.2 128.9 %all-gather.4.cloned.1.call-start = ((), (), s32[]{:S(2)}) async-start(), calls=%async_computation.5 | async-start | bytes 6758400 | tf_op jit(solution)/shard_map/all_gather | solution.py:473
  13.9 226.5 %all-gather.6.cloned.1.call-start = ((), (), s32[]{:S(2)}) async-start(), calls=%async_computation.7 | async-start | bytes 8110080 | tf_op jit(solution)/shard_map/all_gather | solution.py:478
  15.6 18.4 %collective-permute-start.1 = (bf16[32,2816]{1,0:T(8,128)(2,1)}, bf16[32,2816]{1,0:T(8,128)(2,1)S(1)}, u32[]{:S(2)}, u32[]{:S(2)}) collective-permute-start(bf16[32,2816]{1,0:T(8,128)(2,1)} %param.25), channel_id=1, source_target_pairs={{0,16},{8,24},{16,0},{24,8},{1,17},{9,25},{17,1},{25,9},{2,18},{10... | collective-permute-start | bytes 540680 | tf_op jit(solution)/shard_map/ppermute | solution.py:160
  18.3 28.3 %collective-permute-start = (bf16[32,2816]{1,0:T(8,128)(2,1)}, bf16[32,2816]{1,0:T(8,128)(2,1)S(1)}, u32[]{:S(2)}, u32[]{:S(2)}) collective-permute-start(bf16[32,2816]{1,0:T(8,128)(2,1)} %param.25), channel_id=1, source_target_pairs={{0,24},{8,16},{16,8},{24,0},{1,25},{9,17},{17,9},{25,1},{2,26},{10... | collective-permute-start | bytes 540680 | tf_op jit(solution)/shard_map/ppermute | solution.py:160
  18.3 28.3 %collective-permute-start.2 = (bf16[32,2816]{1,0:T(8,128)(2,1)}, bf16[32,2816]{1,0:T(8,128)(2,1)S(1)}, u32[]{:S(2)}, u32[]{:S(2)}) collective-permute-start(bf16[32,2816]{1,0:T(8,128)(2,1)} %param.25), channel_id=1, source_target_pairs={{0,8},{8,0},{16,24},{24,16},{1,9},{9,1},{17,25},{25,17},{2,10},{10... | collective-permute-start | bytes 540680 | tf_op jit(solution)/shard_map/ppermute | solution.py:160
  20.1 29.9 %collective-permute-start.7 = (bf16[32,2816]{1,0:T(8,128)(2,1)}, bf16[32,2816]{1,0:T(8,128)(2,1)S(1)}, u32[]{:S(2)}, u32[]{:S(2)}) collective-permute-start(bf16[32,2816]{1,0:T(8,128)(2,1)} %param.26), channel_id=1, source_target_pairs={{0,16},{8,24},{16,0},{24,8},{1,17},{9,25},{17,1},{25,9},{2,18},{10... | collective-permute-start | bytes 540680 | tf_op jit(solution)/shard_map/ppermute | solution.py:160
  21.8 37.7 %collective-permute-start.6 = (bf16[32,2816]{1,0:T(8,128)(2,1)}, bf16[32,2816]{1,0:T(8,128)(2,1)S(1)}, u32[]{:S(2)}, u32[]{:S(2)}) collective-permute-start(bf16[32,2816]{1,0:T(8,128)(2,1)} %param.26), channel_id=1, source_target_pairs={{0,24},{8,16},{16,8},{24,0},{1,25},{9,17},{17,9},{25,1},{2,26},{10... | collective-permute-start | bytes 540680 | tf_op jit(solution)/shard_map/ppermute | solution.py:160
  34.0 25.5 %collective-permute-start.8 = (bf16[32,2816]{1,0:T(8,128)(2,1)}, bf16[32,2816]{1,0:T(8,128)(2,1)S(1)}, u32[]{:S(2)}, u32[]{:S(2)}) collective-permute-start(bf16[32,2816]{1,0:T(8,128)(2,1)} %param.26), channel_id=1, source_target_pairs={{0,8},{8,0},{16,24},{24,16},{1,9},{9,1},{17,25},{25,17},{2,10},{10... | collective-permute-start | bytes 540680 | tf_op jit(solution)/shard_map/ppermute | solution.py:160
  60.7 24.8 %collective-permute-start.3 = (bf16[4,32,2816]{2,1,0:T(8,128)(2,1)S(1)}, bf16[4,32,2816]{2,1,0:T(8,128)(2,1)}, u32[]{:S(2)}, u32[]{:S(2)}) collective-permute-start(bf16[4,32,2816]{2,1,0:T(8,128)(2,1)S(1)} %pad_maximum_fusion.7), channel_id=1, source_target_pairs={{0,2},{2,0},{1,3},{3,1},{4,6},{6,4},{5,7},{7,5},{8,10},{10,8},{9,1... | collective-permute-start | bytes 2162696 | tf_op jit(solution)/shard_map/ppermute | solution.py:160
  63.7 28.7 %collective-permute-start.9 = (bf16[4,32,2816]{2,1,0:T(8,128)(2,1)}, bf16[4,32,2816]{2,1,0:T(8,128)(2,1)}, u32[]{:S(2)}, u32[]{:S(2)}) collective-permute-start(bf16[4,32,2816]{2,1,0:T(8,128)(2,1)} %pad_maximum_fusion.8), channel_id=1, source_target_pairs={{0,4},{4,0},{1,5},{5,1},{2,6},{6,2},{3,7},{7,3},{8,12},{12,8},{9,1... | collective-permute-start | bytes 2162696 | tf_op jit(solution)/shard_map/ppermute | solution.py:160
  88.0 37.9 %collective-permute-start.4 = (bf16[4,2,32,2816]{3,2,1,0:T(8,128)(2,1)}, bf16[4,2,32,2816]{3,2,1,0:T(8,128)(2,1)}, u32[]{:S(2)}, u32[]{:S(2)}) collective-permute-start(bf16[4,2,32,2816]{3,2,1,0:T(8,128)(2,1)} %pad_maximum_fusion.5), channel_id=1, source_target_pairs={{0,4},{4,0},{1,5},{5,1},{2,6},{6,2},{3,7},{7,3},{8,12},{12,8},{9,1... | collective-permute-start | bytes 4325384 | tf_op jit(solution)/shard_map/ppermute | solution.py:160
  93.8 35.7 %collective-permute-start.10 = (bf16[4,2,32,2816]{3,2,0,1:T(8,128)(2,1)S(1)}, bf16[4,2,32,2816]{3,2,0,1:T(8,128)(2,1)S(1)}, u32[]{:S(2)}, u32[]{:S(2)}) collective-permute-start(bf16[4,2,32,2816]{3,2,0,1:T(8,128)(2,1)S(1)} %pad_maximum_fusion.6), channel_id=1, source_target_pairs={{0,2},{2,0},{1,3},{3,1},{4,6},{6,4},{5,7},{7,5},{8,10},{10,8},{9,1... | collective-permute-start | bytes 4325384 | tf_op jit(solution)/shard_map/ppermute | solution.py:160
  129.5 26.1 %collective-permute-start.5 = (bf16[4,2,2,32,2816]{4,3,2,1,0:T(8,128)(2,1)}, bf16[4,2,2,32,2816]{4,3,2,1,0:T(8,128)(2,1)}, u32[]{:S(2)}, u32[]{:S(2)}) collective-permute-start(bf16[4,2,2,32,2816]{4,3,2,1,0:T(8,128)(2,1)} %pad_maximum_fusion.3), channel_id=1, source_target_pairs={{0,1},{1,0},{2,3},{3,2},{4,5},{5,4},{6,7},{7,6},{8,9},{9,8},{10,11... | collective-permute-start | bytes 8650760 | tf_op jit(solution)/shard_map/ppermute | solution.py:160
  132.2 28.7 %collective-permute-start.11 = (bf16[4,2,2,32,2816]{4,3,0,1,2:T(8,128)(2,1)}, bf16[4,2,2,32,2816]{4,3,0,1,2:T(8,128)(2,1)}, u32[]{:S(2)}, u32[]{:S(2)}) collective-permute-start(bf16[4,2,2,32,2816]{4,3,0,1,2:T(8,128)(2,1)} %pad_maximum_fusion.4), channel_id=1, source_target_pairs={{0,1},{1,0},{2,3},{3,2},{4,5},{5,4},{6,7},{7,6},{8,9},{9,8},{10,11... | collective-permute-start | bytes 8650760 | tf_op jit(solution)/shard_map/ppermute | solution.py:160
  134.6 11.9 %copy-start.13 = (f32[1024,128]{1,0:T(8,128)}, f32[1024,128]{1,0:T(8,128)S(1)}, u32[]{:S(2)}) copy-start(f32[1024,128]{1,0:T(8,128)S(1)} %get-tuple-element.85.sin_ref) | copy-start | bytes 1572868
  146.6 61.4 %all-to-all-start = ((bf16[8,3,2,128,128]{4,3,2,1,0:T(8,128)(2,1)}), bf16[8,3,2,128,128]{4,3,2,1,0:T(8,128)(2,1)S(1)}, u32[]{:S(2)}, u32[]{:S(2)}) async-start(bf16[8,3,2,128,128]{4,3,2,1,0:T(8,128)(2,1)} %bitcast.126), calls=%async_computation | async-start | bytes 3145728 | tf_op jit(solution)/shard_map/all_to_all | solution.py:501
  220.5 28.8 %all-to-all-start.1 = ((bf16[8,1,2,128,128]{4,3,2,1,0:T(8,128)(2,1)}), bf16[8,1,2,128,128]{4,3,2,1,0:T(8,128)(2,1)S(1)}, u32[]{:S(2)}, u32[]{:S(2)}) async-start(bf16[8,1,2,128,128]{4,3,2,1,0:T(8,128)(2,1)} %bitcast.128), calls=%async_computation.1 | async-start | bytes 1048576 | tf_op jit(solution)/shard_map/all_to_all | solution.py:501
  250.1 9.1 %slice-start.4 = ((s8[5767168]{0:T(1024)(128)(4,1)}), s8[1572864]{0:T(1024)(128)(4,1)S(1)}, s32[]{:S(2)}) async-start(s8[5767168]{0:T(1024)(128)(4,1)} %bitcast.114), calls=%async_computation.12 | async-start | bytes 3145728
  282.0 68.8 %collective-permute-start.30 = (bf16[512,2816]{1,0:T(8,128)(2,1)}, bf16[512,2816]{1,0:T(8,128)(2,1)}, u32[]{:S(2)}, u32[]{:S(2)}) collective-permute-start(bf16[512,2816]{1,0:T(8,128)(2,1)} %slice.322), channel_id=1, source_target_pairs={{0,1},{1,0},{2,3},{3,2},{4,5},{5,4},{6,7},{7,6},{8,9},{9,8},{10,11... | collective-permute-start | bytes 8650760 | tf_op jit(solution)/shard_map/ppermute | solution.py:160
  296.2 59.6 %collective-permute-start.24 = (bf16[512,2816]{1,0:T(8,128)(2,1)}, bf16[512,2816]{1,0:T(8,128)(2,1)}, u32[]{:S(2)}, u32[]{:S(2)}) collective-permute-start(bf16[512,2816]{1,0:T(8,128)(2,1)} %slice.312), channel_id=1, source_target_pairs={{0,1},{1,0},{2,3},{3,2},{4,5},{5,4},{6,7},{7,6},{8,9},{9,8},{10,11... | collective-permute-start | bytes 8650760 | tf_op jit(solution)/shard_map/ppermute | solution.py:160
  308.5 19.3 %all-to-all-start.2 = ((bf16[8,1,2,128,128]{4,3,2,1,0:T(8,128)(2,1)}), bf16[8,1,2,128,128]{4,3,2,1,0:T(8,128)(2,1)S(1)}, u32[]{:S(2)}, u32[]{:S(2)}) async-start(bf16[8,1,2,128,128]{4,3,2,1,0:T(8,128)(2,1)} %bitcast.125), calls=%async_computation.2 | async-start | bytes 1048576 | tf_op jit(solution)/shard_map/all_to_all | solution.py:501
  328.7 20.0 %copy-start.10 = (bf16[256,1024]{1,0:T(8,128)(2,1)S(1)}, bf16[256,1024]{1,0:T(8,128)(2,1)}, u32[]{:S(2)}) copy-start(bf16[256,1024]{1,0:T(8,128)(2,1)} %get-tuple-element.45.grad_ref) | copy-start | bytes 1572868
  328.7 20.0 %copy-start.22 = (bf16[256,1024]{1,0:T(8,128)(2,1)S(1)}, bf16[256,1024]{1,0:T(8,128)(2,1)}, u32[]{:S(2)}) copy-start(bf16[256,1024]{1,0:T(8,128)(2,1)} %get-tuple-element.38) | copy-start | bytes 1572868
  342.8 38.8 %all-to-all-start.3 = ((bf16[8,3,2,128,128]{4,3,2,1,0:T(8,128)(2,1)}), bf16[8,3,2,128,128]{4,3,2,1,0:T(8,128)(2,1)}, u32[]{:S(2)}, u32[]{:S(2)}) async-start(bf16[8,3,2,128,128]{4,3,2,1,0:T(8,128)(2,1)} %attend_backward.1), calls=%async_computation.3 | async-start | bytes 3145728 | tf_op jit(solution)/shard_map/all_to_all | solution.py:501
  348.3 176.0 %reduce-scatter.2.cloned.1.call-start = ((), (), s32[]{:S(2)}) async-start(), calls=%async_computation.6 | async-start | bytes 8110080 | tf_op jit(solution)/shard_map/reduce_scatter | solution.py:544
  355.4 42.1 %collective-permute-start.31 = (bf16[256,2816]{1,0:T(8,128)(2,1)}, bf16[256,2816]{1,0:T(8,128)(2,1)}, u32[]{:S(2)}, u32[]{:S(2)}) collective-permute-start(bf16[256,2816]{1,0:T(8,128)(2,1)} %slice.324), channel_id=1, source_target_pairs={{0,2},{2,0},{1,3},{3,1},{4,6},{6,4},{5,7},{7,5},{8,10},{10,8},{9,1... | collective-permute-start | bytes 4325384 | tf_op jit(solution)/shard_map/ppermute | solution.py:160
  361.3 40.8 %collective-permute-start.25 = (bf16[256,2816]{1,0:T(8,128)(2,1)}, bf16[256,2816]{1,0:T(8,128)(2,1)}, u32[]{:S(2)}, u32[]{:S(2)}) collective-permute-start(bf16[256,2816]{1,0:T(8,128)(2,1)} %slice.314), channel_id=1, source_target_pairs={{0,4},{4,0},{1,5},{5,1},{2,6},{6,2},{3,7},{7,3},{8,12},{12,8},{9,1... | collective-permute-start | bytes 4325384 | tf_op jit(solution)/shard_map/ppermute | solution.py:160
  395.2 68.1 %collective-permute-start.18 = (bf16[512,1536]{1,0:T(8,128)(2,1)S(1)}, bf16[512,1536]{1,0:T(8,128)(2,1)S(1)}, u32[]{:S(2)}, u32[]{:S(2)}) collective-permute-start(bf16[512,1536]{1,0:T(8,128)(2,1)S(1)} %slice.242), channel_id=1, source_target_pairs={{0,1},{1,0},{2,3},{3,2},{4,5},{5,4},{6,7},{7,6},{8,9},{9,8},{10,11... | collective-permute-start | bytes 4718600 | tf_op jit(solution)/shard_map/ppermute | solution.py:160
  396.9 68.6 %collective-permute-start.12 = (bf16[512,1664]{1,0:T(8,128)(2,1)S(1)}, bf16[512,1664]{1,0:T(8,128)(2,1)S(1)}, u32[]{:S(2)}, u32[]{:S(2)}) collective-permute-start(bf16[512,1664]{1,0:T(8,128)(2,1)S(1)} %slice.230), channel_id=1, source_target_pairs={{0,1},{1,0},{2,3},{3,2},{4,5},{5,4},{6,7},{7,6},{8,9},{9,8},{10,11... | collective-permute-start | bytes 5111816 | tf_op jit(solution)/shard_map/ppermute | solution.py:160
  399.6 18.0 %collective-permute-start.32 = (bf16[128,2816]{1,0:T(8,128)(2,1)S(1)}, bf16[128,2816]{1,0:T(8,128)(2,1)S(1)}, u32[]{:S(2)}, u32[]{:S(2)}) collective-permute-start(bf16[128,2816]{1,0:T(8,128)(2,1)S(1)} %slice.326), channel_id=1, source_target_pairs={{0,4},{4,0},{1,5},{5,1},{2,6},{6,2},{3,7},{7,3},{8,12},{12,8},{9,1... | collective-permute-start | bytes 2162696 | tf_op jit(solution)/shard_map/ppermute | solution.py:160
  404.0 17.8 %collective-permute-start.26 = (bf16[128,2816]{1,0:T(8,128)(2,1)S(1)}, bf16[128,2816]{1,0:T(8,128)(2,1)S(1)}, u32[]{:S(2)}, u32[]{:S(2)}) collective-permute-start(bf16[128,2816]{1,0:T(8,128)(2,1)S(1)} %slice.316), channel_id=1, source_target_pairs={{0,2},{2,0},{1,3},{3,1},{4,6},{6,4},{5,7},{7,5},{8,10},{10,8},{9,1... | collective-permute-start | bytes 2162696 | tf_op jit(solution)/shard_map/ppermute | solution.py:160
  417.7 45.6 %copy-start.12 = (bf16[1024,1536]{1,0:T(8,128)(2,1)S(1)}, bf16[1024,1536]{1,0:T(8,128)(2,1)}, u32[]{:S(2)}) copy-start(bf16[1024,1536]{1,0:T(8,128)(2,1)} %get-tuple-element.37) | copy-start | bytes 9437188
  417.8 11.0 %collective-permute-start.33 = (bf16[32,2816]{1,0:T(8,128)(2,1)S(1)}, bf16[32,2816]{1,0:T(8,128)(2,1)S(1)}, u32[]{:S(2)}, u32[]{:S(2)}) collective-permute-start(bf16[32,2816]{1,0:T(8,128)(2,1)S(1)} %get-tuple-element.63), channel_id=1, source_target_pairs={{0,8},{8,0},{16,24},{24,16},{1,9},{9,1},{17,25},{25,17},{2,10},{10... | collective-permute-start | bytes 540680 | tf_op jit(solution)/shard_map/ppermute | solution.py:160
  421.2 20.7 %collective-permute-start.35 = (bf16[32,2816]{1,0:T(8,128)(2,1)S(1)}, bf16[32,2816]{1,0:T(8,128)(2,1)S(1)}, u32[]{:S(2)}, u32[]{:S(2)}) collective-permute-start(bf16[32,2816]{1,0:T(8,128)(2,1)S(1)} %get-tuple-element.64), channel_id=1, source_target_pairs={{0,24},{8,16},{16,8},{24,0},{1,25},{9,17},{17,9},{25,1},{2,26},{10... | collective-permute-start | bytes 540680 | tf_op jit(solution)/shard_map/ppermute | solution.py:160
  421.8 36.5 %collective-permute-start.34 = (bf16[32,2816]{1,0:T(8,128)(2,1)S(1)}, bf16[32,2816]{1,0:T(8,128)(2,1)S(1)}, u32[]{:S(2)}, u32[]{:S(2)}) collective-permute-start(bf16[32,2816]{1,0:T(8,128)(2,1)S(1)} %get-tuple-element.65), channel_id=1, source_target_pairs={{0,16},{8,24},{16,0},{24,8},{1,17},{9,25},{17,1},{25,9},{2,18},{10... | collective-permute-start | bytes 540680 | tf_op jit(solution)/shard_map/ppermute | solution.py:160
  428.8 37.5 %collective-permute-start.27 = (bf16[32,2816]{1,0:T(8,128)(2,1)S(1)}, bf16[32,2816]{1,0:T(8,128)(2,1)S(1)}, u32[]{:S(2)}, u32[]{:S(2)}) collective-permute-start(bf16[32,2816]{1,0:T(8,128)(2,1)S(1)} %get-tuple-element.66), channel_id=1, source_target_pairs={{0,8},{8,0},{16,24},{24,16},{1,9},{9,1},{17,25},{25,17},{2,10},{10... | collective-permute-start | bytes 540680 | tf_op jit(solution)/shard_map/ppermute | solution.py:160
  441.9 30.1 %collective-permute-start.29 = (bf16[32,2816]{1,0:T(8,128)(2,1)S(1)}, bf16[32,2816]{1,0:T(8,128)(2,1)S(1)}, u32[]{:S(2)}, u32[]{:S(2)}) collective-permute-start(bf16[32,2816]{1,0:T(8,128)(2,1)S(1)} %get-tuple-element.67), channel_id=1, source_target_pairs={{0,24},{8,16},{16,8},{24,0},{1,25},{9,17},{17,9},{25,1},{2,26},{10... | collective-permute-start | bytes 540680 | tf_op jit(solution)/shard_map/ppermute | solution.py:160
  458.3 14.3 %collective-permute-start.28 = (bf16[32,2816]{1,0:T(8,128)(2,1)S(1)}, bf16[32,2816]{1,0:T(8,128)(2,1)S(1)}, u32[]{:S(2)}, u32[]{:S(2)}) collective-permute-start(bf16[32,2816]{1,0:T(8,128)(2,1)S(1)} %get-tuple-element.68), channel_id=1, source_target_pairs={{0,16},{8,24},{16,0},{24,8},{1,17},{9,25},{17,1},{25,9},{2,18},{10... | collective-permute-start | bytes 540680 | tf_op jit(solution)/shard_map/ppermute | solution.py:160
  463.8 12.9 %collective-permute-start.19 = (bf16[256,1536]{1,0:T(8,128)(2,1)S(1)}, bf16[256,1536]{1,0:T(8,128)(2,1)S(1)}, u32[]{:S(2)}, u32[]{:S(2)}) collective-permute-start(bf16[256,1536]{1,0:T(8,128)(2,1)S(1)} %slice.298), channel_id=1, source_target_pairs={{0,4},{4,0},{1,5},{5,1},{2,6},{6,2},{3,7},{7,3},{8,12},{12,8},{9,1... | collective-permute-start | bytes 2359304 | tf_op jit(solution)/shard_map/ppermute | solution.py:160
  466.2 19.5 %collective-permute-start.13 = (bf16[256,1664]{1,0:T(8,128)(2,1)S(1)}, bf16[256,1664]{1,0:T(8,128)(2,1)S(1)}, u32[]{:S(2)}, u32[]{:S(2)}) collective-permute-start(bf16[256,1664]{1,0:T(8,128)(2,1)S(1)} %slice.288), channel_id=1, source_target_pairs={{0,2},{2,0},{1,3},{3,1},{4,6},{6,4},{5,7},{7,5},{8,10},{10,8},{9,1... | collective-permute-start | bytes 2555912 | tf_op jit(solution)/shard_map/ppermute | solution.py:160
  476.9 13.9 %collective-permute-start.20 = (bf16[128,1536]{1,0:T(8,128)(2,1)S(1)}, bf16[128,1536]{1,0:T(8,128)(2,1)S(1)}, u32[]{:S(2)}, u32[]{:S(2)}) collective-permute-start(bf16[128,1536]{1,0:T(8,128)(2,1)S(1)} %slice.300), channel_id=1, source_target_pairs={{0,2},{2,0},{1,3},{3,1},{4,6},{6,4},{5,7},{7,5},{8,10},{10,8},{9,1... | collective-permute-start | bytes 1179656 | tf_op jit(solution)/shard_map/ppermute | solution.py:160
  485.9 9.5 %collective-permute-start.14 = (bf16[128,1664]{1,0:T(8,128)(2,1)S(1)}, bf16[128,1664]{1,0:T(8,128)(2,1)S(1)}, u32[]{:S(2)}, u32[]{:S(2)}) collective-permute-start(bf16[128,1664]{1,0:T(8,128)(2,1)S(1)} %slice.290), channel_id=1, source_target_pairs={{0,4},{4,0},{1,5},{5,1},{2,6},{6,2},{3,7},{7,3},{8,12},{12,8},{9,1... | collective-permute-start | bytes 1277960 | tf_op jit(solution)/shard_map/ppermute | solution.py:160
  491.0 7.7 %collective-permute-start.21 = (bf16[32,1536]{1,0:T(8,128)(2,1)S(1)}, bf16[32,1536]{1,0:T(8,128)(2,1)S(1)}, u32[]{:S(2)}, u32[]{:S(2)}) collective-permute-start(bf16[32,1536]{1,0:T(8,128)(2,1)S(1)} %get-tuple-element.82), channel_id=1, source_target_pairs={{0,8},{8,0},{16,24},{24,16},{1,9},{9,1},{17,25},{25,17},{2,10},{10... | collective-permute-start | bytes 294920 | tf_op jit(solution)/shard_map/ppermute | solution.py:160
  491.1 9.0 %collective-permute-start.23 = (bf16[32,1536]{1,0:T(8,128)(2,1)S(1)}, bf16[32,1536]{1,0:T(8,128)(2,1)S(1)}, u32[]{:S(2)}, u32[]{:S(2)}) collective-permute-start(bf16[32,1536]{1,0:T(8,128)(2,1)S(1)} %get-tuple-element.83), channel_id=1, source_target_pairs={{0,24},{8,16},{16,8},{24,0},{1,25},{9,17},{17,9},{25,1},{2,26},{10... | collective-permute-start | bytes 294920 | tf_op jit(solution)/shard_map/ppermute | solution.py:160
  492.1 13.3 %collective-permute-start.22 = (bf16[32,1536]{1,0:T(8,128)(2,1)S(1)}, bf16[32,1536]{1,0:T(8,128)(2,1)S(1)}, u32[]{:S(2)}, u32[]{:S(2)}) collective-permute-start(bf16[32,1536]{1,0:T(8,128)(2,1)S(1)} %get-tuple-element.84), channel_id=1, source_target_pairs={{0,16},{8,24},{16,0},{24,8},{1,17},{9,25},{17,1},{25,9},{2,18},{10... | collective-permute-start | bytes 294920 | tf_op jit(solution)/shard_map/ppermute | solution.py:160
  495.6 10.6 %collective-permute-start.15 = (bf16[32,1664]{1,0:T(8,128)(2,1)S(1)}, bf16[32,1664]{1,0:T(8,128)(2,1)S(1)}, u32[]{:S(2)}, u32[]{:S(2)}) collective-permute-start(bf16[32,1664]{1,0:T(8,128)(2,1)S(1)} %get-tuple-element.79), channel_id=1, source_target_pairs={{0,8},{8,0},{16,24},{24,16},{1,9},{9,1},{17,25},{25,17},{2,10},{10... | collective-permute-start | bytes 319496 | tf_op jit(solution)/shard_map/ppermute | solution.py:160
  495.7 15.7 %collective-permute-start.17 = (bf16[32,1664]{1,0:T(8,128)(2,1)S(1)}, bf16[32,1664]{1,0:T(8,128)(2,1)S(1)}, u32[]{:S(2)}, u32[]{:S(2)}) collective-permute-start(bf16[32,1664]{1,0:T(8,128)(2,1)S(1)} %get-tuple-element.80), channel_id=1, source_target_pairs={{0,24},{8,16},{16,8},{24,0},{1,25},{9,17},{17,9},{25,1},{2,26},{10... | collective-permute-start | bytes 319496 | tf_op jit(solution)/shard_map/ppermute | solution.py:160
  498.7 14.3 %collective-permute-start.16 = (bf16[32,1664]{1,0:T(8,128)(2,1)S(1)}, bf16[32,1664]{1,0:T(8,128)(2,1)S(1)}, u32[]{:S(2)}, u32[]{:S(2)}) collective-permute-start(bf16[32,1664]{1,0:T(8,128)(2,1)S(1)} %get-tuple-element.81), channel_id=1, source_target_pairs={{0,16},{8,24},{16,0},{24,8},{1,17},{9,25},{17,1},{25,9},{2,18},{10... | collective-permute-start | bytes 319496 | tf_op jit(solution)/shard_map/ppermute | solution.py:160
  (31 other events, 114.7 us)
Sparse Core Ops, SparseCore 0:
  14.0 89.5 all-gather.3
  107.1 95.3 all-gather.5
  371.2 153.0 reduce-scatter.1

commit v2 on v1

v2 whole, which is shorter than its diff:
```python
import functools

import jax
import jax.numpy as jnp
from jax import lax
from jax.experimental import pallas as pl
from jax.experimental.pallas import tpu as pltpu
from jax.sharding import Mesh
from jax.sharding import PartitionSpec as P

HEAD_DIM = 64
BLOCK = 256
PAIR = 2 * HEAD_DIM

EPSILON = 1e-06
THETA = 10000.0
SCALE = 0.125
ALL = ("z", "y", "x", "c")
SEQ = ("z", "y")
F32 = jnp.float32
BF16 = jnp.bfloat16


def rotary_tables(positions):
    lane = jnp.arange(PAIR, dtype=jnp.int32)
    half = HEAD_DIM // 2
    index = (lane % half).astype(F32)
    frequency = THETA ** (-(index * 2.0 / HEAD_DIM))
    angles = positions.astype(F32)[:, None] * frequency[None, :]
    sign = jnp.where(lane % HEAD_DIM < half, -1.0, 1.0)[None, :]
    return jnp.cos(angles), jnp.sin(angles) * sign


def partner(values):
    half = HEAD_DIM // 2
    lane = lax.broadcasted_iota(jnp.int32, values.shape, values.ndim - 1)
    first = lane % HEAD_DIM < half
    width = values.shape[-1]
    return jnp.where(
        first,
        pltpu.roll(values, width - half, values.ndim - 1),
        pltpu.roll(values, half, values.ndim - 1),
    )


def dot_t(left, right):
    return lax.dot_general(left, right, (((1,), (1,)), ((), ())), preferred_element_type=F32)


def t_dot(left, right):
    return lax.dot_general(left, right, (((0,), (0,)), ((), ())), preferred_element_type=F32)


def dot(left, right):
    return jnp.dot(left, right, preferred_element_type=F32)


def attend_forward_kernel(qkv_ref, out_ref, total_ref):
    parts, _, _, rows, _ = qkv_ref.shape
    per_block = BLOCK // rows
    blocks = parts // per_block
    for head in range(2):
        lanes = pl.ds(head * HEAD_DIM, HEAD_DIM)
        for block in range(blocks):
            lo, hi = block * per_block, (block + 1) * per_block
            query = qkv_ref[lo:hi, 0, 0, :, lanes].reshape(BLOCK, HEAD_DIM)
            keys = qkv_ref[0:hi, 1, 0, :, lanes].reshape(hi * rows, HEAD_DIM)
            values = qkv_ref[0:hi, 2, 0, :, lanes].reshape(hi * rows, HEAD_DIM)
            scores = dot_t(keys, query) * SCALE
            top = jnp.max(scores, axis=0, keepdims=True)
            total = top + jnp.log(jnp.sum(jnp.exp(scores - top), axis=0, keepdims=True))
            probs = jnp.exp(scores - total).astype(BF16)
            mixed = t_dot(values, probs)
            out_ref[lo:hi, 0, :, lanes] = mixed.T.astype(BF16).reshape(per_block, rows, HEAD_DIM)
            total_ref[0, head, block : block + 1, :] = total


def attend_backward_kernel(qkv_ref, grad_ref, total_ref, cos_ref, sin_ref, out_ref, dk_acc, dv_acc):
    parts, _, _, rows, _ = qkv_ref.shape
    per_block = BLOCK // rows
    blocks = parts // per_block
    dk_acc[...] = jnp.zeros_like(dk_acc)
    dv_acc[...] = jnp.zeros_like(dv_acc)
    for block in range(blocks):
        lo, hi = block * per_block, (block + 1) * per_block
        keys_n = hi * rows
        dq_parts = []
        for head in range(2):
            lanes = pl.ds(head * HEAD_DIM, HEAD_DIM)
            query = qkv_ref[lo:hi, 0, 0, :, lanes].reshape(BLOCK, HEAD_DIM)
            grad = grad_ref[lo:hi, 0, :, lanes].reshape(BLOCK, HEAD_DIM)
            keys = qkv_ref[0:hi, 1, 0, :, lanes].reshape(keys_n, HEAD_DIM)
            values = qkv_ref[0:hi, 2, 0, :, lanes].reshape(keys_n, HEAD_DIM)
            scores = dot_t(keys, query) * SCALE
            probs = jnp.exp(scores - total_ref[0, head, block : block + 1, :])
            grad_probs = dot_t(values, grad)
            inner = jnp.sum(probs * grad_probs, axis=0, keepdims=True)
            grad_scores = (probs * (grad_probs - inner)).astype(BF16)
            dk_acc[0:keys_n, lanes] += dot(grad_scores, query) * SCALE
            dv_acc[0:keys_n, lanes] += dot(probs.astype(BF16), grad)
            dq_parts.append(t_dot(keys, grad_scores).T * SCALE)
        dq = jnp.concatenate(dq_parts, axis=1)
        cos = cos_ref[block * BLOCK : (block + 1) * BLOCK, :]
        sin = sin_ref[block * BLOCK : (block + 1) * BLOCK, :]
        dq = (dq * cos - partner(dq) * sin).astype(BF16)
        out_ref[lo:hi, 0, 0, :, :] = dq.reshape(per_block, rows, PAIR)
    dk = dk_acc[...]
    dk = (dk * cos_ref[...] - partner(dk) * sin_ref[...]).astype(BF16)
    out_ref[:, 1, 0, :, :] = dk.reshape(parts, rows, PAIR)
    out_ref[:, 2, 0, :, :] = dv_acc[...].astype(BF16).reshape(parts, rows, PAIR)


VMEM_LIMIT = 60 * 1024 * 1024


def attend_backward(qkv, grad_att, totals, cos, sin):
    parts, _, units, rows, _ = qkv.shape
    length = parts * rows
    blocks = length // BLOCK
    return pl.pallas_call(
        attend_backward_kernel,
        grid=(units,),
        in_specs=[
            pl.BlockSpec((parts, 3, 1, rows, PAIR), lambda u: (0, 0, u, 0, 0)),
            pl.BlockSpec((parts, 1, rows, PAIR), lambda u: (0, u, 0, 0)),
            pl.BlockSpec((1, 2, blocks, BLOCK), lambda u: (u, 0, 0, 0)),
            pl.BlockSpec((length, PAIR), lambda u: (0, 0)),
            pl.BlockSpec((length, PAIR), lambda u: (0, 0)),
        ],
        out_specs=pl.BlockSpec((parts, 3, 1, rows, PAIR), lambda u: (0, 0, u, 0, 0)),
        out_shape=jax.ShapeDtypeStruct((parts, 3, units, rows, PAIR), BF16),
        scratch_shapes=[pltpu.VMEM((length, PAIR), F32), pltpu.VMEM((length, PAIR), F32)],
        compiler_params=pltpu.CompilerParams(vmem_limit_bytes=VMEM_LIMIT),
        name="attend_backward",
    )(qkv, grad_att, totals, cos, sin)


def swap(array, name, distance):
    size = lax.axis_size(name)
    return lax.ppermute(array, name, [(i, i ^ distance) for i in range(size)])


def arrange(pieces, at):
    bit = 1
    while bit < len(pieces):
        odd = (at & bit) != 0
        pieces = [jnp.where(odd, pieces[j ^ bit], pieces[j]) for j in range(len(pieces))]
        bit *= 2
    return pieces


def gather_rows(shard, order):
    value = shard
    held = []
    for name in order:
        at = lax.axis_index(name)
        pieces = [value] + [swap(value, name, k) for k in range(1, lax.axis_size(name))]
        held.append(name)
        held.sort(key=ALL.index)
        value = jnp.stack(arrange(pieces, at), axis=held.index(name))
    return value.reshape(-1, shard.shape[1])


def stage_rows(rows, order, relative=ALL):
    sizes = [lax.axis_size(name) for name in order]
    per = rows // functools.reduce(lambda a, b: a * b, sizes)
    index = lax.broadcasted_iota(jnp.int32, (rows, 1), 0)
    left, inner = index // per, index % per
    place = {}
    for name, size in zip(reversed(order), reversed(sizes)):
        place[name] = left % size
        if name in relative:
            place[name] = place[name] ^ lax.axis_index(name)
        left = left // size
    device = jnp.zeros_like(index)
    for name in ALL:
        device = device * lax.axis_size(name) + place[name]
    return device * per + inner


def reduce_staged(sent, kept, order):
    columns = kept.shape[1]
    value = kept.astype(F32) + swap(sent, order[0], 1).astype(F32)
    for name in order[1:]:
        size = lax.axis_size(name)
        value = value.astype(BF16).reshape(size, -1, columns)
        received = [swap(value[k], name, k) for k in range(1, size)]
        value = value[0].astype(F32)
        for piece in received:
            value = value + piece.astype(F32)
    return value


def params():
    return pltpu.CompilerParams(vmem_limit_bytes=VMEM_LIMIT)


def front_kernel(
    x_ref, first_ref, gain_ref, cos_ref, sin_ref, weight_ref, normed_ref, qkv_ref, att_ref, total_ref
):
    parts, _, rows, width = x_ref.shape
    per_block = BLOCK // rows
    blocks = parts // per_block
    gain = gain_ref[...]
    for block in range(blocks):
        lo, hi = block * per_block, (block + 1) * per_block
        x = x_ref[lo:hi, 0].reshape(BLOCK, width).astype(F32)
        inv = lax.rsqrt(jnp.mean(x * x, axis=-1, keepdims=True) + EPSILON)
        normed = (x * inv * gain).astype(BF16)
        normed_ref[lo:hi, 0] = normed.reshape(per_block, rows, width)
        cos = cos_ref[block * BLOCK : (block + 1) * BLOCK, :]
        sin = sin_ref[block * BLOCK : (block + 1) * BLOCK, :]
        for kind in range(2):
            value = dot(normed, weight_ref[kind])
            value = (value * cos + partner(value) * sin).astype(BF16)
            qkv_ref[lo:hi, kind, 0] = value.reshape(per_block, rows, PAIR)
        first = first_ref[lo:hi, 0].reshape(BLOCK, PAIR).astype(F32)
        mixed = (0.5 * dot(normed, weight_ref[2]) + 0.5 * first).astype(BF16)
        qkv_ref[lo:hi, 2, 0] = mixed.reshape(per_block, rows, PAIR)
    attend_forward_kernel(qkv_ref, att_ref, total_ref)


def front(x, first, gain, cos, sin, weights):
    parts, units, rows, width = x.shape
    length = parts * rows
    blocks = length // BLOCK
    return pl.pallas_call(
        front_kernel,
        grid=(units,),
        in_specs=[
            pl.BlockSpec((parts, 1, rows, width), lambda u: (0, u, 0, 0)),
            pl.BlockSpec((parts, 1, rows, PAIR), lambda u: (0, u, 0, 0)),
            pl.BlockSpec((1, width), lambda u: (0, 0)),
            pl.BlockSpec((length, PAIR), lambda u: (0, 0)),
            pl.BlockSpec((length, PAIR), lambda u: (0, 0)),
            pl.BlockSpec((3, width, PAIR), lambda u: (0, 0, 0)),
        ],
        out_specs=[
            pl.BlockSpec((parts, 1, rows, width), lambda u: (0, u, 0, 0)),
            pl.BlockSpec((parts, 3, 1, rows, PAIR), lambda u: (0, 0, u, 0, 0)),
            pl.BlockSpec((parts, 1, rows, PAIR), lambda u: (0, u, 0, 0)),
            pl.BlockSpec((1, 2, blocks, BLOCK), lambda u: (u, 0, 0, 0)),
        ],
        out_shape=[
            jax.ShapeDtypeStruct((parts, units, rows, width), BF16),
            jax.ShapeDtypeStruct((parts, 3, units, rows, PAIR), BF16),
            jax.ShapeDtypeStruct((parts, units, rows, PAIR), BF16),
            jax.ShapeDtypeStruct((units, 2, blocks, BLOCK), F32),
        ],
        compiler_params=params(),
        name="front",
    )(x, first, gain, cos, sin, weights)


def join_kernel(
    x_ref, heads_ref, weight_ref, gain_ref, pick_b_ref, pick_c_ref,
    att_ref, hidden_ref, scaled_ref, inv_ref, normed_ref, turned_b_ref, turned_c_ref,
):
    pairs = heads_ref.shape[0]
    tokens = x_ref.shape[0]
    for pair in range(pairs):
        att_ref[:, pair * PAIR : (pair + 1) * PAIR] = heads_ref[pair].reshape(tokens, PAIR)
    hidden = x_ref[...].astype(F32) + dot(att_ref[...], weight_ref[...])
    inv = lax.rsqrt(jnp.mean(hidden * hidden, axis=-1, keepdims=True) + EPSILON)
    scaled = hidden * inv
    hidden_ref[...] = hidden
    scaled_ref[...] = scaled
    inv_ref[...] = jnp.broadcast_to(inv, inv_ref.shape)
    normed = (scaled * gain_ref[...]).astype(BF16)
    normed_ref[...] = normed
    turned_b_ref[...] = dot_t(pick_b_ref[...], normed).astype(BF16)
    turned_c_ref[...] = dot_t(pick_c_ref[...], normed).astype(BF16)


def join(x, heads, weight, gain, pick_b, pick_c):
    tokens, width = x.shape
    return pl.pallas_call(
        join_kernel,
        out_shape=[
            jax.ShapeDtypeStruct((tokens, width), BF16),
            jax.ShapeDtypeStruct((tokens, width), F32),
            jax.ShapeDtypeStruct((tokens, width), F32),
            jax.ShapeDtypeStruct((tokens, PAIR), F32),
            jax.ShapeDtypeStruct((tokens, width), BF16),
            jax.ShapeDtypeStruct((width, tokens), BF16),
            jax.ShapeDtypeStruct((width, tokens), BF16),
        ],
        compiler_params=params(),
        name="join",
    )(x, heads, weight, gain, pick_b, pick_c)


def split_kernel(grad_ref, weight_ref, out_ref):
    value = dot_t(grad_ref[...], weight_ref[...]).astype(BF16)
    pairs, groups, _, units, rows, _ = out_ref.shape
    for pair in range(pairs):
        out_ref[pair, :, 0] = value[:, pair * PAIR : (pair + 1) * PAIR].reshape(groups, units, rows, PAIR)


def split(grad, weight, groups, units):
    tokens, width = grad.shape
    return pl.pallas_call(
        split_kernel,
        out_shape=jax.ShapeDtypeStruct(
            (width // PAIR, groups, 1, units, tokens // (groups * units), PAIR), BF16
        ),
        compiler_params=params(),
        name="split",
    )(grad, weight)


def picker(place, width):
    lane = lax.broadcasted_iota(jnp.int32, (place.shape[0], width), 1)
    return jnp.where(lane == place, 1.0, 0.0).astype(BF16)


def head_grads_kernel(normed_ref, grads_ref, loss_ref, pick_ref, out_ref, turned):
    unit = pl.program_id(0)
    parts, _, rows, width = normed_ref.shape
    normed = normed_ref[...].reshape(parts * rows, width)
    for kind in range(3):
        grad = grads_ref[:, kind, 0].reshape(parts * rows, PAIR)
        value = t_dot(grad, normed)
        if kind == 2:
            value = 0.5 * value
        at = pl.ds(kind * PAIR, PAIR)
        turned[at, :] = jnp.where(unit == 0, value, turned[at, :] + value)

    @pl.when(unit == pl.num_programs(0) - 1)
    def _():
        out_ref[:, : 3 * PAIR] = dot_t(pick_ref[...], turned[...].astype(BF16)).astype(BF16)
        out_ref[:, 3 * PAIR :] = jnp.broadcast_to(loss_ref[...], (width, PAIR)).astype(BF16)


def head_grads(normed, grads, loss_row, pick):
    parts, units, rows, width = normed.shape
    return pl.pallas_call(
        head_grads_kernel,
        grid=(units,),
        in_specs=[
            pl.BlockSpec((parts, 1, rows, width), lambda u: (0, u, 0, 0)),
            pl.BlockSpec((parts, 3, 1, rows, PAIR), lambda u: (0, 0, u, 0, 0)),
            pl.BlockSpec((1, PAIR), lambda u: (0, 0)),
            pl.BlockSpec((width, width), lambda u: (0, 0)),
        ],
        out_specs=pl.BlockSpec((width, 4 * PAIR), lambda u: (0, 0)),
        out_shape=jax.ShapeDtypeStruct((width, 4 * PAIR), BF16),
        scratch_shapes=[pltpu.VMEM((3 * PAIR, width), F32)],
        compiler_params=params(),
        name="head_grads",
    )(normed, grads, loss_row, pick)


def last_kernel(heads_ref, x_ref, gain_ref, weight_ref, grad_hidden_ref, grad_in_ref, first_ref, grads):
    pairs = heads_ref.shape[0]
    tokens, width = x_ref.shape
    for kind in range(3):
        for pair in range(pairs):
            at = kind * width + pair * PAIR
            piece = heads_ref[pair, :, kind].reshape(tokens, PAIR)
            if kind == 2:
                half = 0.5 * piece.astype(F32)
                first_ref[:, pair * PAIR : (pair + 1) * PAIR] = half
                piece = half.astype(BF16)
            grads[:, at : at + PAIR] = piece
    grad_norm = dot_t(grads[...], weight_ref[...])
    x = x_ref[...].astype(F32)
    inv = lax.rsqrt(jnp.mean(x * x, axis=-1, keepdims=True) + EPSILON)
    scaled = x * inv
    scaled_grad = grad_norm * gain_ref[...]
    grad_in_ref[...] = grad_hidden_ref[...] + inv * (
        scaled_grad - scaled * jnp.mean(scaled_grad * scaled, axis=-1, keepdims=True)
    )


def last(heads, x, gain, weights, grad_hidden):
    tokens, width = x.shape
    return pl.pallas_call(
        last_kernel,
        out_shape=[
            jax.ShapeDtypeStruct((tokens, width), F32),
            jax.ShapeDtypeStruct((tokens, width), F32),
        ],
        scratch_shapes=[pltpu.VMEM((tokens, 3 * width), BF16)],
        compiler_params=params(),
        name="last",
    )(heads, x, gain, weights, grad_hidden)


STAGES_B = ("c", "y", "x", "z")
STAGES_C = ("c", "x", "y", "z")
STAGES_H = ("c", "x", "z", "y")


def on_device(
    inputs,
    first_values,
    teacher_states,
    out_cotangent,
    token_valid,
    attn_gain,
    w_query,
    w_key,
    w_value,
    w_output,
    mlp_gain,
    w_gate,
    w_up,
    w_down,
):
    batch, local_len, width = inputs.shape
    seqs = lax.axis_size(SEQ)
    devices = lax.axis_size(ALL)
    tokens = batch * local_len
    length = local_len * seqs
    pairs = width // PAIR
    own_rows = w_query.shape[0]
    own_down = w_down.shape[0]
    hidden = w_gate.shape[1]
    groups = seqs // pairs
    units = batch // groups
    my_group = lax.axis_index(SEQ) % groups

    def gather_positions(value):
        for name in ("z", "y"):
            pieces = [value] + [swap(value, name, k) for k in range(1, lax.axis_size(name))]
            value = jnp.stack(arrange(pieces, lax.axis_index(name)), axis=-3)
        return value.reshape(seqs, local_len, width)

    x_all = jnp.stack([gather_positions(inputs[b]) for b in range(batch)], axis=1)
    x_all = lax.dynamic_slice_in_dim(x_all, my_group * units, units, 1)

    valid_float = token_valid.astype(F32)
    count = jnp.sum(token_valid)
    extra = jnp.stack(
        [
            attn_gain,
            mlp_gain,
            jnp.full((own_rows,), count // 256, jnp.int32).astype(BF16),
            jnp.full((own_rows,), count % 256, jnp.int32).astype(BF16),
        ],
        axis=1,
    )
    extra = jnp.pad(extra, ((0, 0), (0, PAIR - 4)))
    columns = jnp.stack([w_query, w_key, w_value]).reshape(3, own_rows, pairs, PAIR)
    columns = jnp.concatenate(
        [columns, jnp.broadcast_to(extra[None, :, None, :], (1, own_rows, pairs, PAIR))]
    )
    columns = columns.transpose(2, 0, 1, 3).reshape(pairs, 1, 4 * own_rows, PAIR)
    columns = jnp.broadcast_to(columns, (pairs, groups, 4 * own_rows, PAIR))
    firsts = first_values.reshape(groups, units, local_len, pairs, PAIR)
    firsts = firsts.transpose(3, 0, 1, 2, 4).reshape(pairs, groups, units * local_len, PAIR)
    parcel = jnp.concatenate([columns, firsts], axis=2).reshape(seqs, -1, PAIR)
    parcel = lax.all_to_all(parcel, SEQ, split_axis=0, concat_axis=0, tiled=True)
    first_all = parcel[:, 4 * own_rows :].reshape(seqs, units, local_len, PAIR)
    head_w = parcel[:, : 4 * own_rows].reshape(seqs, 4, own_rows, PAIR).transpose(1, 0, 2, 3)
    for at, name in ((2, "x"), (3, "c")):
        pieces = [head_w] + [swap(head_w, name, k) for k in range(1, lax.axis_size(name))]
        head_w = jnp.stack(arrange(pieces, lax.axis_index(name)), axis=at)
    head_w = head_w.reshape(4, width, PAIR)
    extra_all = head_w[3].astype(F32).T
    gain_a = extra_all[0:1, :]
    gain_m = extra_all[1:2, :]
    valid_total = jnp.sum(extra_all[2] * 256.0 + extra_all[3]) / own_rows

    mlp_w = lax.all_gather(jnp.concatenate([w_gate, w_up, w_output], axis=1), ALL, axis=0, tiled=True)
    down_w = gather_rows(w_down, ("z", "y", "x", "c"))
    attn_w = lax.all_gather(jnp.concatenate([w_query, w_key, w_value], axis=1), ALL, axis=0, tiled=True)
    gate_w = mlp_w[:, :hidden]
    up_w = mlp_w[:, hidden : 2 * hidden]
    output_w = mlp_w[:, 2 * hidden :]

    cos_all, sin_all = rotary_tables(jnp.arange(length, dtype=jnp.int32))
    pick_b = picker(stage_rows(width, STAGES_B), width)
    pick_c = picker(stage_rows(width, STAGES_C), width)
    pick_h = picker(stage_rows(width, STAGES_H, ("c", "x")), width)

    normed_all, qkv, attended, totals = front(x_all, first_all, gain_a, cos_all, sin_all, head_w[:3])

    def exchange(array):
        return lax.all_to_all(array, SEQ, split_axis=0, concat_axis=0, tiled=True)

    att_heads = exchange(attended).reshape(pairs, groups, units, local_len, PAIR)
    x_low = inputs.reshape(tokens, width)
    att_low, hidden_in, scaled_m, inv_wide, normed_mlp, turned_b, turned_c = join(
        x_low, att_heads, output_w, gain_m, pick_b, pick_c
    )
    inv_rms_m = inv_wide[:, :1]
    gate_pre = dot(normed_mlp, gate_w)
    up_part = dot(normed_mlp, up_w)
    gate_sigmoid = jax.nn.sigmoid(gate_pre)
    swish_value = gate_pre * gate_sigmoid
    activated = (swish_value * up_part).astype(BF16)
    result = hidden_in + dot(activated, down_w)
    residual_err = result - teacher_states.astype(F32).reshape(tokens, width)
    valid_rows = valid_float.reshape(tokens, 1)
    token_loss = valid_rows * jnp.mean(residual_err * residual_err, axis=-1, keepdims=True)
    grad_out = (
        out_cotangent.astype(F32).reshape(tokens, width)
        + 2.0 / width * valid_rows * residual_err / valid_total
    )

    grad_down_in = grad_out.astype(BF16)
    grad_act = dot_t(grad_down_in, down_w)
    swish_slope = gate_sigmoid * (1.0 + gate_pre * (1.0 - gate_sigmoid))
    grad_gate_in = (grad_act * up_part * swish_slope).astype(BF16)
    grad_up_in = (grad_act * swish_value).astype(BF16)
    half = width // 2
    gate_sent = dot(turned_b[half:], grad_gate_in).astype(BF16)
    up_sent = dot(turned_c[half:], grad_up_in).astype(BF16)
    gate_kept = dot(turned_b[:half], grad_gate_in)
    up_kept = dot(turned_c[:half], grad_up_in)
    owned_gate = reduce_staged(gate_sent, gate_kept, STAGES_B)
    owned_up = reduce_staged(up_sent, up_kept, STAGES_C)
    grad_norm_m = dot_t(grad_gate_in, gate_w) + dot_t(grad_up_in, up_w)
    scaled_grad_m = grad_norm_m * gain_m
    grad_hidden = grad_out + inv_rms_m * (
        scaled_grad_m - scaled_m * jnp.mean(scaled_grad_m * scaled_m, axis=-1, keepdims=True)
    )
    grad_branch = grad_hidden.astype(BF16)
    grad_heads = split(grad_branch, output_w, groups, units)
    grad_heads = exchange(grad_heads.reshape(seqs, units, local_len, PAIR))

    down_part = t_dot(activated, grad_down_in).astype(BF16).reshape(devices, own_down, width)
    output_part = t_dot(att_low, grad_branch).astype(BF16).reshape(devices, own_rows, width)
    owned_rest = lax.psum_scatter(
        jnp.concatenate([down_part, output_part], axis=1), ALL, scatter_dimension=0, tiled=True
    )[0].astype(F32)

    grad_qkv = attend_backward(qkv, grad_heads, totals, cos_all, sin_all)
    grad_own = exchange(grad_qkv).reshape(pairs, groups, 3, units, local_len, PAIR)

    loss_row = jnp.sum(token_loss.reshape(-1, PAIR), axis=0)[None, :]
    value = head_grads(normed_all, grad_qkv, loss_row, pick_h)
    for name in ("c", "x"):
        size = lax.axis_size(name)
        value = value.reshape(size, -1, 4 * PAIR)
        received = [swap(value[k], name, k) for k in range(1, size)]
        value = value[0].astype(F32)
        for piece in received:
            value = value + piece.astype(F32)
        value = value.astype(BF16)
    value = exchange(value.reshape(seqs, own_rows, 4 * PAIR))
    loss_value = jnp.sum(value[:, 0, 3 * PAIR :].astype(F32)) / valid_total
    value = value[:, :, : 3 * PAIR].reshape(pairs, groups, own_rows, 3, PAIR).astype(F32).sum(1)
    owned_qkv = value.transpose(2, 1, 0, 3).reshape(3, own_rows, width)

    grad_in, grad_first = last(grad_own, x_low, gain_a, attn_w, grad_hidden)

    gain_grad_a = (
        jnp.sum(w_query.astype(F32) * owned_qkv[0], axis=1)
        + jnp.sum(w_key.astype(F32) * owned_qkv[1], axis=1)
        + jnp.sum(w_value.astype(F32) * owned_qkv[2], axis=1)
    ) / attn_gain.astype(F32)
    gain_grad_m = (
        jnp.sum(w_gate.astype(F32) * owned_gate, axis=1) + jnp.sum(w_up.astype(F32) * owned_up, axis=1)
    ) / mlp_gain.astype(F32)
    return (
        result.reshape(batch, local_len, width),
        loss_value,
        grad_in.reshape(batch, local_len, width),
        grad_first.reshape(batch, local_len, width),
        gain_grad_a,
        owned_qkv[0],
        owned_qkv[1],
        owned_qkv[2],
        owned_rest[own_down:],
        gain_grad_m,
        owned_gate,
        owned_up,
        owned_rest[:own_down],
    )


def solution(mesh):
    seqs, dps = mesh.devices.shape
    fine = Mesh(mesh.devices.reshape(seqs // 2, 2, dps // 2, 2), ALL)
    tokens = P(("x", "c"), SEQ, None)
    rows = P(ALL, None)
    gain = P(ALL)
    return jax.shard_map(
        on_device,
        mesh=fine,
        in_specs=(
            tokens, tokens, tokens, tokens, P(("x", "c"), SEQ), gain, rows, rows, rows, rows, gain, rows, rows, rows,
        ),
        out_specs=(
            tokens, P(), tokens, tokens, gain, rows, rows, rows, rows, gain, rows, rows, rows,
        ),
        check_vma=False,
    )
```

time: 544 us -> 504 us (0.926); the launches traced: 535 us -> 500 us
  matrix products: 26.3 us -> 44.5 us
  Pallas kernels: 72.6 us -> 55.7 us
  local copies, waits for them, and re-layouts: 41 us -> 24.2 us
  starting transfers between devices: 75.3 us -> 61.2 us
  blocking collectives: 0 us -> 13.6 us
  waiting for transfers between devices: 235 us -> 223 us
  other arithmetic: 64.7 us -> 58.3 us
    all_to_all x4 -> x3, waiting for transfers between devices: 61.8 us -> 31.9 us  [exchange(): return lax.all_to_all(array, SEQ, split_axis=0, concat_axis=0, tiled=True)]
    ppermute x36 -> x30, waiting for transfers between devices: 165 us -> 191 us  [swap(): return lax.ppermute(array, name, [(i, i ^ distance) for i in range(size)])]
    pallas_call x5 -> x3, Pallas kernels: 50.7 us -> 31.6 us  [the longest x1 17.9 us: front(): pl.pallas_call(front_kernel, grid=(units,), in_specs=[pl.BlockSpec((parts...]
    dot_general x3 -> x7, matrix products: 9.16 us -> 27.8 us  [dot(): return jnp.dot(left, right, preferred_element_type=F32)]
    another operation x15 -> x8, other arithmetic: 27.4 us -> 11.7 us  [gather_rows(): value = jnp.stack(arrange(pieces, at), axis=held.index(name))]
    all_to_all x0 -> x1, blocking collectives: none -> 13.6 us  [exchange(): return lax.all_to_all(array, SEQ, split_axis=0, concat_axis=0, tiled=True)]
    ppermute x36 -> x30, starting transfers between devices: 49.2 us -> 36.7 us  [swap(): return lax.ppermute(array, name, [(i, i ^ distance) for i in range(size)])]
    slice x16 -> x6, local copies, waits for them, and re-layouts: 13.4 us -> 2.57 us  [reduce_staged(): received = [swap(value[k], name, k) for k in range(1, size)]]
  transfers between devices with their start and end apart: 43 -> 37, of which waited for: 26 -> 19; matrix products, arithmetic and copies ran while one was open for 19% -> 24% of each run, Pallas kernels for 11% -> 11%
where the time goes in v2:
time: 504 us; the launch traced here: 500 us
  waiting for transfers between devices  223 us (44%)
  starting transfers between devices  61.2 us (12%)
  other arithmetic  58.3 us (12%)
  Pallas kernels  55.7 us (11%)
  matrix products  44.5 us (9%)
  local copies, waits for them, and re-layouts  24.2 us (5%)
  between operations  20 us (4%)
  blocking collectives  13.6 us (3%)
    ppermute x30, waiting for transfers between devices, swap(): return lax.ppermute(array, name, [(i, i ^ distance) for i in range(size)])  191 us
    ppermute x30, starting transfers between devices, swap(): return lax.ppermute(array, name, [(i, i ^ distance) for i in range(size)])  36.7 us
    all_to_all x3, waiting for transfers between devices, exchange(): return lax.all_to_all(array, SEQ, split_axis=0, concat_axis=0, tiled=True)  31.9 us
    dot_general x7, matrix products, dot(): return jnp.dot(left, right, preferred_element_type=F32)  27.8 us
    pallas_call x1, Pallas kernels, front(): pl.pallas_call(front_kernel, grid=(units,), in_specs=[pl.BlockSpec((parts...  17.9 us
    all_to_all x3, starting transfers between devices, exchange(): return lax.all_to_all(array, SEQ, split_axis=0, concat_axis=0, tiled=True)  16.6 us
    pallas_call x1, Pallas kernels, attend_backward(): pl.pallas_call(attend_backward_kernel, grid=(units,), in_specs=[pl.BlockS...  14.3 us
    all_to_all x1, blocking collectives, exchange(): return lax.all_to_all(array, SEQ, split_axis=0, concat_axis=0, tiled=True)  13.6 us
  transfers between devices with their start and end apart: 37, of which 19 were waited for; matrix products, arithmetic and copies ran while one was open for 24% of the time, Pallas kernels for 11%

profile of v2, /device:TPU:8, one launch (start us, length us, event | category | flops | bytes accessed | tf_op | source)
XLA Modules:
  0.0 500.1 jit_solution(7616487024147461605)
XLA Ops:
  13.4 13.0 %collective-permute-done.10 = bf16[88,1024]{1,0:T(8,128)(2,1)S(1)} collective-permute-done((bf16[88,1024]{1,0:T(8,128)(2,1)}, bf16[88,1024]{1,0:T(8,128)(2,1)S(1)}, u32[]{:S(2)}, u32[]{:S(2)}) %collective-permute-start.10) | collective-permute-done | bytes 180256 | tf_op jit(solution)/shard_map/ppermute | solution.py:140
  26.4 9.1 %collective-permute-done.11 = bf16[88,1024]{1,0:T(8,128)(2,1)S(1)} collective-permute-done((bf16[88,1024]{1,0:T(8,128)(2,1)}, bf16[88,1024]{1,0:T(8,128)(2,1)S(1)}, u32[]{:S(2)}, u32[]{:S(2)}) %collective-permute-start.11) | collective-permute-done | bytes 180256 | tf_op jit(solution)/shard_map/ppermute | solution.py:140
  39.5 4.3 collective-permute-start.1
  50.6 6.6 %collective-permute-done.13 = bf16[4,88,1024]{2,1,0:T(8,128)(2,1)S(1)} collective-permute-done((bf16[4,88,1024]{2,1,0:T(8,128)(2,1)S(1)}, bf16[4,88,1024]{2,1,0:T(8,128)(2,1)S(1)}, u32[]{:S(2)}, u32[]{:S(2)}) %collective-permute-start.13) | collective-permute-done | bytes 720928 | tf_op jit(solution)/shard_map/ppermute | solution.py:140
  61.9 7.8 %all-to-all-start = ((bf16[8,384,128]{2,1,0:T(8,128)(2,1)}), bf16[8,384,128]{2,1,0:T(8,128)(2,1)}, u32[]{:S(2)}, u32[]{:S(2)}) async-start(bf16[8,384,128]{2,1,0:T(8,128)(2,1)} %maximum_bitcast_fusion), calls=%async_computation | async-start | bytes 1572864 | tf_op jit(solution)/shard_map/all_to_all | solution.py:454
  69.7 3.3 collective-permute-done
  73.0 25.4 %collective-permute-done.1 = bf16[128,1024]{1,0:T(8,128)(2,1)} collective-permute-done((bf16[128,1024]{1,0:T(8,128)(2,1)}, bf16[128,1024]{1,0:T(8,128)(2,1)}, u32[]{:S(2)}, u32[]{:S(2)}) %collective-permute-start.1) | collective-permute-done | bytes 262176 | tf_op jit(solution)/shard_map/ppermute | solution.py:140
  101.1 15.3 %collective-permute-done.4 = bf16[128,1024]{1,0:T(8,128)(2,1)} collective-permute-done((bf16[128,1024]{1,0:T(8,128)(2,1)}, bf16[128,1024]{1,0:T(8,128)(2,1)}, u32[]{:S(2)}, u32[]{:S(2)}) %collective-permute-start.4) | collective-permute-done | bytes 262176 | tf_op jit(solution)/shard_map/ppermute | solution.py:140
  116.4 37.7 %collective-permute-done.5 = bf16[128,1024]{1,0:T(8,128)(2,1)S(1)} collective-permute-done((bf16[128,1024]{1,0:T(8,128)(2,1)}, bf16[128,1024]{1,0:T(8,128)(2,1)S(1)}, u32[]{:S(2)}, u32[]{:S(2)}) %collective-permute-start.5) | collective-permute-done | bytes 262176 | tf_op jit(solution)/shard_map/ppermute | solution.py:140
  164.3 3.1 fusion.15
  171.6 12.4 %collective-permute-done.3 = bf16[4,128,1024]{2,1,0:T(8,128)(2,1)} collective-permute-done((bf16[4,128,1024]{2,1,0:T(8,128)(2,1)}, bf16[4,128,1024]{2,1,0:T(8,128)(2,1)}, u32[]{:S(2)}, u32[]{:S(2)}) %collective-permute-start.3) | collective-permute-done | bytes 1048608 | tf_op jit(solution)/shard_map/ppermute | solution.py:140
  184.0 14.0 %collective-permute-done.7 = bf16[4,128,1024]{2,1,0:T(8,128)(2,1)} collective-permute-done((bf16[4,128,1024]{2,1,0:T(8,128)(2,1)}, bf16[4,128,1024]{2,1,0:T(8,128)(2,1)}, u32[]{:S(2)}, u32[]{:S(2)}) %collective-permute-start.7) | collective-permute-done | bytes 1048608 | tf_op jit(solution)/shard_map/ppermute | solution.py:140
  198.1 2.2 select_bitcast_fusion.5
  201.5 2.4 pad_maximum_fusion.2.x_ref
  210.1 17.9 %front.1 = (bf16[8,2,128,1024]{3,2,1,0:T(8,128)(2,1)}, bf16[8,3,2,128,128]{4,3,2,1,0:T(8,128)(2,1)}, bf16[8,2,128,128]{3,2,1,0:T(8,128)(2,1)}, f32[2,2,4,256]{3,2,1,0:T(4,128)}) custom-call(bf16[8,2,128,1024]{3,2,1,0:T(8,128)(2,1)} %pad_maximum_fusion.2.x_ref, bf16[8,2,128,128]{3,2,1,0:T(8,128)(2,1)} %bitcast.188, f32[1,1024]{1,0:T(1,128)} %get-tuple-element.90.gain_ref, ...), custom_call_target="tpu_custom_call" | custom-call | tf_op jit(solution)/shard_map/front/pallas_call | solution.py:227
  228.0 6.3 %all-to-all-start.1 = ((bf16[8,2,128,128]{3,2,1,0:T(8,128)(2,1)}), bf16[8,2,128,128]{3,2,1,0:T(8,128)(2,1)S(1)}, u32[]{:S(2)}, u32[]{:S(2)}) async-start(bf16[8,2,128,128]{3,2,1,0:T(8,128)(2,1)} %get-tuple-element.26), calls=%async_computation.1 | async-start | bytes 1048576 | tf_op jit(solution)/shard_map/all_to_all | solution.py:481
  234.9 2.4 select_bitcast_fusion.1
  237.3 3.0 pad_maximum_fusion.1
  240.3 3.1 slice.222.weight_ref
  243.4 4.7 all-to-all-done.1
  248.9 6.2 %join.1 = (bf16[256,1024]{1,0:T(8,128)(2,1)}, f32[256,1024]{1,0:T(8,128)}, f32[256,1024]{1,0:T(8,128)}, f32[256,128]{1,0:T(8,128)}, bf16[256,1024]{1,0:T(8,128)(...) custom-call(bf16[256,1024]{1,0:T(8,128)(2,1)} %bitcast.173, bf16[8,1,2,128,128]{4,3,2,1,0:T(8,128)(2,1)} %bitcast.183, ...), custom_call_target="tpu_custom_call" | custom-call | tf_op jit(solution)/shard_map/join/pallas_call | solution.py:277
  256.2 4.6 fusion.6
  260.8 7.0 %multiply_convert_fusion.2 = (bf16[256,2816]{1,0:T(8,128)(2,1)S(1)}, f32[256,2816]{1,0:T(8,128)}) fusion(f32[256,2816]{1,0:T(8,128)S(1)} %fusion.6, bf16[256,1024]{1,0:T(8,128)(2,1)S(1)} %copy-done.43, bf16[1024,6656]{1,0:T(8,128)(2,1)} %all-gather.3.cloned.1.call-done), kind=kOutput, calls=%fused_computation.29 | convolution fusion | flops 1480720384 | bytes 13500416 | tf_op jit(solution)/shard_map/dot_general | solution.py:55
  267.9 3.4 multiply_reduce_fusion
  271.3 5.5 %multiply_convert_fusion.1 = (bf16[256,2816]{1,0:T(8,128)(2,1)S(1)}, bf16[256,2816]{1,0:T(8,128)(2,1)S(1)}) fusion(f32[256,2816]{1,0:T(8,128)} %copy-done.44, f32[256,2816]{1,0:T(8,128)} %get-tuple-element.102, bf16[2816,1024]{1,0:T(8,128)(2,1)S(1)} %bitcast.181, f32[256,1024]{1,0:T(8,128)S(1)} %get-tuple-element.62), kind=kOutput, calls=%fused_computation.26 | convolution fusion | flops 1486028800 | bytes 15466496 | tf_op jit(solution)/shard_map/dot_general | solution.py:47
  282.2 3.5 split.1
  285.8 4.9 all-to-all-start.2
  292.5 5.9 %convolution_convert_fusion = bf16[2816,1024]{1,0:T(8,128)(2,1)} fusion(bf16[256,2816]{1,0:T(8,128)(2,1)} %copy-done.10, f32[256,1024]{1,0:T(8,128)} %copy-done.9), kind=kOutput, calls=%fused_computation.4 | convolution fusion | flops 1479540736 | bytes 8257536 | tf_op jit(solution)/shard_map/dot_general | solution.py:51
  298.4 6.9 %pad_maximum_fusion = bf16[32,120,1024]{2,1,0:T(8,128)(2,1)} fusion(bf16[32,32,1024]{2,1,0:T(8,128)(2,1)S(1)} %bitcast.175, bf16[32,88,1024]{2,1,0:T(8,128)(2,1)} %bitcast.172), kind=kLoop, calls=%fused_computation | loop fusion | flops 15728640 | bytes 15728640 | tf_op jit(solution)/shard_map/concatenate | solution.py:527
  305.3 2.4 convolution_convert_fusion.1
  310.9 14.3 %attend_backward.1.grads_ref = bf16[8,3,2,128,128]{4,3,2,1,0:T(8,128)(2,1)} custom-call(bf16[8,3,2,128,128]{4,3,2,1,0:T(8,128)(2,1)} %get-tuple-element.30.qkv_ref, bf16[8,2,128,128]{3,2,1,0:T(8,128)(2,1)} %copy-done.17, f32[2,2,4,256]{3,2,1,0:T(4,128)} %get-tuple-element.33.total_ref, f32[1024,128]{1,0:T(8,128)} %get-tuple-element.100.cos_ref, ...), custom_call_target="tpu_custom_call" | custom-call | tf_op jit(solution)/shard_map/attend_backward/pallas_call | solution.py:120
  325.1 7.1 %head_grads.1 = bf16[1024,512]{1,0:T(8,128)(2,1)} custom-call(bf16[8,2,128,1024]{3,2,1,0:T(8,128)(2,1)} %get-tuple-element.29.normed_ref, bf16[8,3,2,128,128]{4,3,2,1,0:T(8,128)(2,1)} %attend_backward.1.grads_ref, f32[1,128]{1,0:T(1,128)} %bitcast.208, bf16[1024,1024]{1,0:T(8,128)(2,1)} %select_convert_fusion.pick_ref), custom_call_target="tpu_custom_call" | custom-call | tf_op jit(solution)/shard_map/head_grads/pallas_call | solution.py:337
  333.9 4.0 convolution_convert_fusion.2
  339.6 7.3 %collective-permute-done.17 = bf16[256,512]{1,0:T(8,128)(2,1)S(1)} collective-permute-done((bf16[256,512]{1,0:T(8,128)(2,1)S(1)}, bf16[256,512]{1,0:T(8,128)(2,1)S(1)}, u32[]{:S(2)}, u32[]{:S(2)}) %collective-permute-start.17) | collective-permute-done | bytes 262176 | tf_op jit(solution)/shard_map/ppermute | solution.py:140
  346.9 13.6 %all_to_all.25 = bf16[8,32,512]{2,1,0:T(8,128)(2,1)S(1)} all-to-all(bf16[8,32,512]{2,1,0:T(8,128)(2,1)S(1)} %bitcast.190), channel_id=1, replica_groups=mesh['z'=4,'y'=2,'x'=2,'c'=2] {'z','y'}, dimensions={0} | all-to-all | bytes 524288 | tf_op jit(solution)/shard_map/all_to_all | solution.py:481
  360.6 5.4 %all-to-all-start.4 = ((bf16[8,3,2,128,128]{4,3,2,1,0:T(8,128)(2,1)}), bf16[8,3,2,128,128]{4,3,2,1,0:T(8,128)(2,1)}, u32[]{:S(2)}, u32[]{:S(2)}) async-start(bf16[8,3,2,128,128]{4,3,2,1,0:T(8,128)(2,1)} %attend_backward.1.grads_ref), calls=%async_computation.4 | async-start | bytes 3145728 | tf_op jit(solution)/shard_map/all_to_all | solution.py:481
  370.5 3.2 add_convert_fusion
  380.1 3.2 add_convert_fusion.1
  389.6 27.2 %all-to-all-done.4 = bf16[8,3,2,128,128]{4,3,2,1,0:T(8,128)(2,1)} async-done(((bf16[8,3,2,128,128]{4,3,2,1,0:T(8,128)(2,1)}), bf16[8,3,2,128,128]{4,3,2,1,0:T(8,128)(2,1)}, u32[]{:S(2)}, u32[]{:S(2)}) %all-to-all-start.4) | async-done | bytes 1572896 | tf_op jit(solution)/shard_map/all_to_all | solution.py:481
  416.8 6.7 %last.1 = (f32[256,1024]{1,0:T(8,128)}, f32[256,1024]{1,0:T(8,128)}) custom-call(bf16[8,1,3,2,128,128]{5,4,3,2,1,0:T(8,128)(2,1)} %bitcast.59.heads_ref, bf16[256,1024]{1,0:T(8,128)(2,1)} %bitcast.174, f32[1,1024]{1,0:T(1,128)} %get-tuple-element.90.gain_ref, bf16[1024,3072]{1,0:T(8,128)(2,1)} %all-gather.5.cloned.1.call-done.weight_ref, ...), custom_call_target="tpu_custom_call" | custom-call | tf_op jit(solution)/shard_map/last/pallas_call | solution.py:378
  427.2 4.0 collective-permute-done.19
  433.2 15.5 %collective-permute-done.26 = bf16[128,2816]{1,0:T(8,128)(2,1)S(1)} collective-permute-done((bf16[128,2816]{1,0:T(8,128)(2,1)S(1)}, bf16[128,2816]{1,0:T(8,128)(2,1)S(1)}, u32[]{:S(2)}, u32[]{:S(2)}) %collective-permute-start.26) | collective-permute-done | bytes 720928 | tf_op jit(solution)/shard_map/ppermute | solution.py:140
  449.2 2.4 collective-permute-start.28
  455.8 4.7 collective-permute-done.27
  460.5 4.4 collective-permute-start.23
  464.9 2.9 collective-permute-done.28
  467.8 14.1 %collective-permute-done.29 = bf16[32,2816]{1,0:T(8,128)(2,1)S(1)} collective-permute-done((bf16[32,2816]{1,0:T(8,128)(2,1)S(1)}, bf16[32,2816]{1,0:T(8,128)(2,1)S(1)}, u32[]{:S(2)}, u32[]{:S(2)}) %collective-permute-start.29) | collective-permute-done | bytes 180256 | tf_op jit(solution)/shard_map/ppermute | solution.py:140
  483.8 4.5 collective-permute-done.23
  (246 shorter events, 91.4 us)
Async XLA Ops:
  7.2 31.5 %copy-start.2 = (bf16[2,128,1024]{2,1,0:T(8,128)(2,1)S(1)}, bf16[2,128,1024]{2,1,0:T(8,128)(2,1)}, u32[]{:S(2)}) copy-start(bf16[2,128,1024]{2,1,0:T(8,128)(2,1)} %param.14) | copy-start | bytes 1572868
  7.2 38.7 %copy-start.26 = (bf16[32,1024]{1,0:T(8,128)(2,1)S(1)}, bf16[32,1024]{1,0:T(8,128)(2,1)}, u32[]{:S(2)}) copy-start(bf16[32,1024]{1,0:T(8,128)(2,1)} %param.20) | copy-start | bytes 196612
  7.2 38.7 %copy-start.25 = (bf16[32,1024]{1,0:T(8,128)(2,1)S(1)}, bf16[32,1024]{1,0:T(8,128)(2,1)}, u32[]{:S(2)}) copy-start(bf16[32,1024]{1,0:T(8,128)(2,1)} %param.21) | copy-start | bytes 196612
  7.2 38.7 %copy-start.27 = (bf16[32,1024]{1,0:T(8,128)(2,1)S(1)}, bf16[32,1024]{1,0:T(8,128)(2,1)}, u32[]{:S(2)}) copy-start(bf16[32,1024]{1,0:T(8,128)(2,1)} %param.22) | copy-start | bytes 196612
  7.2 39.4 %copy-start.33 = (s32[2,128]{1,0:T(2,128)S(1)}, s32[2,128]{1,0:T(2,128)}, u32[]{:S(2)}) copy-start(s32[2,128]{1,0:T(2,128)} %param.18) | copy-start | bytes 3076
  7.2 42.8 %copy-start.34 = (bf16[32]{0:T(256)(128)(2,1)S(1)}, bf16[32]{0:T(256)(128)(2,1)}, u32[]{:S(2)}) copy-start(bf16[32]{0:T(256)(128)(2,1)} %param.19) | copy-start | bytes 196
  7.2 42.8 %copy-start.35 = (bf16[32]{0:T(256)(128)(2,1)S(1)}, bf16[32]{0:T(256)(128)(2,1)}, u32[]{:S(2)}) copy-start(bf16[32]{0:T(256)(128)(2,1)} %param.24) | copy-start | bytes 196
  7.3 233.1 %all-gather.3.cloned.1.call-start = ((), (), s32[]{:S(2)}) async-start(), calls=%async_computation.6 | async-start | bytes 14057472 | tf_op jit(solution)/shard_map/all_gather | solution.py:466
  9.2 41.2 %copy-start.31 = (bf16[2,128,1024]{2,1,0:T(8,128)(2,1)S(1)}, bf16[2,128,1024]{2,1,0:T(8,128)(2,1)}, u32[]{:S(2)}) copy-start(bf16[2,128,1024]{2,1,0:T(8,128)(2,1)} %param.15) | copy-start | bytes 1572868
  9.2 380.4 %all-gather.5.cloned.1.call-start = ((), (), s32[]{:S(2)}) async-start(), calls=%async_computation.7 | async-start | bytes 6488064 | tf_op jit(solution)/shard_map/all_gather | solution.py:468
  9.3 17.1 %collective-permute-start.10 = (bf16[88,1024]{1,0:T(8,128)(2,1)}, bf16[88,1024]{1,0:T(8,128)(2,1)S(1)}, u32[]{:S(2)}, u32[]{:S(2)}) collective-permute-start(bf16[88,1024]{1,0:T(8,128)(2,1)} %param.27), channel_id=1, source_target_pairs={{0,24},{8,16},{16,8},{24,0},{1,25},{9,17},{17,9},{25,1},{2,26},{10... | collective-permute-start | bytes 540680 | tf_op jit(solution)/shard_map/ppermute | solution.py:140
  10.9 24.6 %collective-permute-start.11 = (bf16[88,1024]{1,0:T(8,128)(2,1)}, bf16[88,1024]{1,0:T(8,128)(2,1)S(1)}, u32[]{:S(2)}, u32[]{:S(2)}) collective-permute-start(bf16[88,1024]{1,0:T(8,128)(2,1)} %param.27), channel_id=1, source_target_pairs={{0,16},{8,24},{16,0},{24,8},{1,17},{9,25},{17,1},{25,9},{2,18},{10... | collective-permute-start | bytes 540680 | tf_op jit(solution)/shard_map/ppermute | solution.py:140
  12.0 23.6 %collective-permute-start.12 = (bf16[88,1024]{1,0:T(8,128)(2,1)}, bf16[88,1024]{1,0:T(8,128)(2,1)S(1)}, u32[]{:S(2)}, u32[]{:S(2)}) collective-permute-start(bf16[88,1024]{1,0:T(8,128)(2,1)} %param.27), channel_id=1, source_target_pairs={{0,8},{8,0},{16,24},{24,16},{1,9},{9,1},{17,25},{25,17},{2,10},{10... | collective-permute-start | bytes 540680 | tf_op jit(solution)/shard_map/ppermute | solution.py:140
  36.6 20.5 %collective-permute-start.13 = (bf16[4,88,1024]{2,1,0:T(8,128)(2,1)S(1)}, bf16[4,88,1024]{2,1,0:T(8,128)(2,1)S(1)}, u32[]{:S(2)}, u32[]{:S(2)}) collective-permute-start(bf16[4,88,1024]{2,1,0:T(8,128)(2,1)S(1)} %pad_maximum_fusion.10), channel_id=1, source_target_pairs={{0,4},{4,0},{1,5},{5,1},{2,6},{6,2},{3,7},{7,3},{8,12},{12,8},{9,1... | collective-permute-start | bytes 2162696 | tf_op jit(solution)/shard_map/ppermute | solution.py:140
  39.5 33.5 %collective-permute-start = (bf16[128,1024]{1,0:T(8,128)(2,1)}, bf16[128,1024]{1,0:T(8,128)(2,1)}, u32[]{:S(2)}, u32[]{:S(2)}) collective-permute-start(bf16[128,1024]{1,0:T(8,128)(2,1)} %get-tuple-element.97), channel_id=1, source_target_pairs={{0,24},{8,16},{16,8},{24,0},{1,25},{9,17},{17,9},{25,1},{2,26},{10... | collective-permute-start | bytes 786440 | tf_op jit(solution)/shard_map/ppermute | solution.py:140
  39.5 58.9 %collective-permute-start.1 = (bf16[128,1024]{1,0:T(8,128)(2,1)}, bf16[128,1024]{1,0:T(8,128)(2,1)}, u32[]{:S(2)}, u32[]{:S(2)}) collective-permute-start(bf16[128,1024]{1,0:T(8,128)(2,1)} %get-tuple-element.97), channel_id=1, source_target_pairs={{0,16},{8,24},{16,0},{24,8},{1,17},{9,25},{17,1},{25,9},{2,18},{10... | collective-permute-start | bytes 786440 | tf_op jit(solution)/shard_map/ppermute | solution.py:140
  43.8 57.3 %collective-permute-start.2 = (bf16[128,1024]{1,0:T(8,128)(2,1)}, bf16[128,1024]{1,0:T(8,128)(2,1)}, u32[]{:S(2)}, u32[]{:S(2)}) collective-permute-start(bf16[128,1024]{1,0:T(8,128)(2,1)} %get-tuple-element.97), channel_id=1, source_target_pairs={{0,8},{8,0},{16,24},{24,16},{1,9},{9,1},{17,25},{25,17},{2,10},{10... | collective-permute-start | bytes 786440 | tf_op jit(solution)/shard_map/ppermute | solution.py:140
  44.4 72.0 %collective-permute-start.4 = (bf16[128,1024]{1,0:T(8,128)(2,1)}, bf16[128,1024]{1,0:T(8,128)(2,1)}, u32[]{:S(2)}, u32[]{:S(2)}) collective-permute-start(bf16[128,1024]{1,0:T(8,128)(2,1)} %get-tuple-element.98), channel_id=1, source_target_pairs={{0,24},{8,16},{16,8},{24,0},{1,25},{9,17},{17,9},{25,1},{2,26},{10... | collective-permute-start | bytes 786440 | tf_op jit(solution)/shard_map/ppermute | solution.py:140
  59.4 101.0 %collective-permute-start.14 = (bf16[4,2,88,1024]{3,2,1,0:T(8,128)(2,1)}, bf16[4,2,88,1024]{3,2,1,0:T(8,128)(2,1)}, u32[]{:S(2)}, u32[]{:S(2)}) collective-permute-start(bf16[4,2,88,1024]{3,2,1,0:T(8,128)(2,1)} %pad_maximum_fusion.6), channel_id=1, source_target_pairs={{0,2},{2,0},{1,3},{3,1},{4,6},{6,4},{5,7},{7,5},{8,10},{10,8},{9,1... | collective-permute-start | bytes 4325384 | tf_op jit(solution)/shard_map/ppermute | solution.py:140
  61.9 107.2 %all-to-all-start = ((bf16[8,384,128]{2,1,0:T(8,128)(2,1)}), bf16[8,384,128]{2,1,0:T(8,128)(2,1)}, u32[]{:S(2)}, u32[]{:S(2)}) async-start(bf16[8,384,128]{2,1,0:T(8,128)(2,1)} %maximum_bitcast_fusion), calls=%async_computation | async-start | bytes 1572864 | tf_op jit(solution)/shard_map/all_to_all | solution.py:454
  73.0 81.0 %collective-permute-start.5 = (bf16[128,1024]{1,0:T(8,128)(2,1)}, bf16[128,1024]{1,0:T(8,128)(2,1)S(1)}, u32[]{:S(2)}, u32[]{:S(2)}) collective-permute-start(bf16[128,1024]{1,0:T(8,128)(2,1)} %get-tuple-element.98), channel_id=1, source_target_pairs={{0,16},{8,24},{16,0},{24,8},{1,17},{9,25},{17,1},{25,9},{2,18},{10... | collective-permute-start | bytes 786440 | tf_op jit(solution)/shard_map/ppermute | solution.py:140
  98.4 55.7 %collective-permute-start.6 = (bf16[128,1024]{1,0:T(8,128)(2,1)}, bf16[128,1024]{1,0:T(8,128)(2,1)S(1)}, u32[]{:S(2)}, u32[]{:S(2)}) collective-permute-start(bf16[128,1024]{1,0:T(8,128)(2,1)} %get-tuple-element.98), channel_id=1, source_target_pairs={{0,8},{8,0},{16,24},{24,16},{1,9},{9,1},{17,25},{25,17},{2,10},{10... | collective-permute-start | bytes 786440 | tf_op jit(solution)/shard_map/ppermute | solution.py:140
  156.7 27.3 %collective-permute-start.3 = (bf16[4,128,1024]{2,1,0:T(8,128)(2,1)}, bf16[4,128,1024]{2,1,0:T(8,128)(2,1)}, u32[]{:S(2)}, u32[]{:S(2)}) collective-permute-start(bf16[4,128,1024]{2,1,0:T(8,128)(2,1)} %pad_maximum_fusion.7), channel_id=1, source_target_pairs={{0,4},{4,0},{1,5},{5,1},{2,6},{6,2},{3,7},{7,3},{8,12},{12,8},{9,1... | collective-permute-start | bytes 3145736 | tf_op jit(solution)/shard_map/ppermute | solution.py:140
  157.9 40.1 %collective-permute-start.7 = (bf16[4,128,1024]{2,1,0:T(8,128)(2,1)}, bf16[4,128,1024]{2,1,0:T(8,128)(2,1)}, u32[]{:S(2)}, u32[]{:S(2)}) collective-permute-start(bf16[4,128,1024]{2,1,0:T(8,128)(2,1)} %pad_maximum_fusion.8), channel_id=1, source_target_pairs={{0,4},{4,0},{1,5},{5,1},{2,6},{6,2},{3,7},{7,3},{8,12},{12,8},{9,1... | collective-permute-start | bytes 3145736 | tf_op jit(solution)/shard_map/ppermute | solution.py:140
  164.3 70.6 %collective-permute-start.15 = (bf16[4,2,2,88,1024]{4,3,2,1,0:T(8,128)(2,1)}, bf16[4,2,2,88,1024]{4,3,2,1,0:T(8,128)(2,1)}, u32[]{:S(2)}, u32[]{:S(2)}) collective-permute-start(bf16[4,2,2,88,1024]{4,3,2,1,0:T(8,128)(2,1)} %pad_maximum_fusion.3), channel_id=1, source_target_pairs={{0,1},{1,0},{2,3},{3,2},{4,5},{5,4},{6,7},{7,6},{8,9},{9,8},{10,11... | collective-permute-start | bytes 8650760 | tf_op jit(solution)/shard_map/ppermute | solution.py:140
  170.1 30.3 %collective-permute-start.8 = (bf16[4,8,32,128]{3,2,0,1:T(8,128)(2,1)S(1)}, bf16[4,8,32,128]{3,2,0,1:T(8,128)(2,1)S(1)}, u32[]{:S(2)}, u32[]{:S(2)}) collective-permute-start(bf16[4,8,32,128]{3,2,0,1:T(8,128)(2,1)S(1)} %bitcast.191), channel_id=1, source_target_pairs={{0,2},{2,0},{1,3},{3,1},{4,6},{6,4},{5,7},{7,5},{8,10},{10,8},{9,1... | collective-permute-start | bytes 786440 | tf_op jit(solution)/shard_map/ppermute | solution.py:140
  200.4 5.3 %collective-permute-start.9 = (bf16[4,8,2,32,128]{4,3,0,1,2:T(8,128)(2,1)S(1)}, bf16[4,8,2,32,128]{4,3,0,1,2:T(8,128)(2,1)S(1)}, u32[]{:S(2)}, u32[]{:S(2)}) collective-permute-start(bf16[4,8,2,32,128]{4,3,0,1,2:T(8,128)(2,1)S(1)} %pad_maximum_fusion.11), channel_id=1, source_target_pairs={{0,1},{1,0},{2,3},{3,2},{4,5},{5,4},{6,7},{7,6},{8,9},{9,8},{10,11... | collective-permute-start | bytes 1572872 | tf_op jit(solution)/shard_map/ppermute | solution.py:140
  228.0 20.2 %all-to-all-start.1 = ((bf16[8,2,128,128]{3,2,1,0:T(8,128)(2,1)}), bf16[8,2,128,128]{3,2,1,0:T(8,128)(2,1)S(1)}, u32[]{:S(2)}, u32[]{:S(2)}) async-start(bf16[8,2,128,128]{3,2,1,0:T(8,128)(2,1)} %get-tuple-element.26), calls=%async_computation.1 | async-start | bytes 1048576 | tf_op jit(solution)/shard_map/all_to_all | solution.py:481
  285.8 24.3 %all-to-all-start.2 = ((bf16[8,2,128,128]{3,2,1,0:T(8,128)(2,1)}), bf16[8,2,128,128]{3,2,1,0:T(8,128)(2,1)S(1)}, u32[]{:S(2)}, u32[]{:S(2)}) async-start(bf16[8,2,128,128]{3,2,1,0:T(8,128)(2,1)} %bitcast.187), calls=%async_computation.2 | async-start | bytes 1048576 | tf_op jit(solution)/shard_map/all_to_all | solution.py:481
  290.7 199.1 %reduce-scatter.2.cloned.1.call-start = ((), (), s32[]{:S(2)}) async-start(), calls=%async_computation.8 | async-start | bytes 8110080 | tf_op jit(solution)/shard_map/reduce_scatter | solution.py:526
  307.7 62.8 %collective-permute-start.24 = (bf16[512,2816]{1,0:T(8,128)(2,1)S(1)}, bf16[512,2816]{1,0:T(8,128)(2,1)}, u32[]{:S(2)}, u32[]{:S(2)}) collective-permute-start(bf16[512,2816]{1,0:T(8,128)(2,1)S(1)} %convolution_convert_fusion.1), channel_id=1, source_target_pairs={{0,1},{1,0},{2,3},{3,2},{4,5},{5,4},{6,7},{7,6},{8,9},{9,8},{10,11... | collective-permute-start | bytes 8650760 | tf_op jit(solution)/shard_map/ppermute | solution.py:140
  333.3 4.6 collective-permute-start.16
  337.9 42.2 %collective-permute-start.18 = (bf16[512,2816]{1,0:T(8,128)(2,1)}, bf16[512,2816]{1,0:T(8,128)(2,1)}, u32[]{:S(2)}, u32[]{:S(2)}) collective-permute-start(bf16[512,2816]{1,0:T(8,128)(2,1)} %convolution_convert_fusion.2), channel_id=1, source_target_pairs={{0,1},{1,0},{2,3},{3,2},{4,5},{5,4},{6,7},{7,6},{8,9},{9,8},{10,11... | collective-permute-start | bytes 8650760 | tf_op jit(solution)/shard_map/ppermute | solution.py:140
  338.1 8.7 %collective-permute-start.17 = (bf16[256,512]{1,0:T(8,128)(2,1)S(1)}, bf16[256,512]{1,0:T(8,128)(2,1)S(1)}, u32[]{:S(2)}, u32[]{:S(2)}) collective-permute-start(bf16[256,512]{1,0:T(8,128)(2,1)S(1)} %slice.231), channel_id=1, source_target_pairs={{0,2},{2,0},{1,3},{3,1},{4,6},{6,4},{5,7},{7,5},{8,10},{10,8},{9,1... | collective-permute-start | bytes 786440 | tf_op jit(solution)/shard_map/ppermute | solution.py:140
  360.6 56.2 %all-to-all-start.4 = ((bf16[8,3,2,128,128]{4,3,2,1,0:T(8,128)(2,1)}), bf16[8,3,2,128,128]{4,3,2,1,0:T(8,128)(2,1)}, u32[]{:S(2)}, u32[]{:S(2)}) async-start(bf16[8,3,2,128,128]{4,3,2,1,0:T(8,128)(2,1)} %attend_backward.1.grads_ref), calls=%async_computation.4 | async-start | bytes 3145728 | tf_op jit(solution)/shard_map/all_to_all | solution.py:481
  375.0 48.5 %collective-permute-start.25 = (bf16[256,2816]{1,0:T(8,128)(2,1)}, bf16[256,2816]{1,0:T(8,128)(2,1)}, u32[]{:S(2)}, u32[]{:S(2)}) collective-permute-start(bf16[256,2816]{1,0:T(8,128)(2,1)} %slice.247), channel_id=1, source_target_pairs={{0,2},{2,0},{1,3},{3,1},{4,6},{6,4},{5,7},{7,5},{8,10},{10,8},{9,1... | collective-permute-start | bytes 4325384 | tf_op jit(solution)/shard_map/ppermute | solution.py:140
  386.1 45.1 %collective-permute-start.19 = (bf16[256,2816]{1,0:T(8,128)(2,1)}, bf16[256,2816]{1,0:T(8,128)(2,1)}, u32[]{:S(2)}, u32[]{:S(2)}) collective-permute-start(bf16[256,2816]{1,0:T(8,128)(2,1)} %slice.239), channel_id=1, source_target_pairs={{0,4},{4,0},{1,5},{5,1},{2,6},{6,2},{3,7},{7,3},{8,12},{12,8},{9,1... | collective-permute-start | bytes 4325384 | tf_op jit(solution)/shard_map/ppermute | solution.py:140
  425.4 23.3 %collective-permute-start.26 = (bf16[128,2816]{1,0:T(8,128)(2,1)S(1)}, bf16[128,2816]{1,0:T(8,128)(2,1)S(1)}, u32[]{:S(2)}, u32[]{:S(2)}) collective-permute-start(bf16[128,2816]{1,0:T(8,128)(2,1)S(1)} %slice.249), channel_id=1, source_target_pairs={{0,4},{4,0},{1,5},{5,1},{2,6},{6,2},{3,7},{7,3},{8,12},{12,8},{9,1... | collective-permute-start | bytes 2162696 | tf_op jit(solution)/shard_map/ppermute | solution.py:140
  433.0 48.9 %copy-start.23 = (bf16[32,2816]{1,0:T(8,128)(2,1)S(1)}, bf16[32,2816]{1,0:T(8,128)(2,1)}, u32[]{:S(2)}) copy-start(bf16[32,2816]{1,0:T(8,128)(2,1)} %param.26) | copy-start | bytes 540676
  433.0 19.5 %collective-permute-start.20 = (bf16[128,2816]{1,0:T(8,128)(2,1)S(1)}, bf16[128,2816]{1,0:T(8,128)(2,1)S(1)}, u32[]{:S(2)}, u32[]{:S(2)}) collective-permute-start(bf16[128,2816]{1,0:T(8,128)(2,1)S(1)} %slice.241), channel_id=1, source_target_pairs={{0,2},{2,0},{1,3},{3,1},{4,6},{6,4},{5,7},{7,5},{8,10},{10,8},{9,1... | collective-permute-start | bytes 2162696 | tf_op jit(solution)/shard_map/ppermute | solution.py:140
  448.8 39.4 %copy-start.24 = (bf16[32,2816]{1,0:T(8,128)(2,1)S(1)}, bf16[32,2816]{1,0:T(8,128)(2,1)}, u32[]{:S(2)}) copy-start(bf16[32,2816]{1,0:T(8,128)(2,1)} %param.25) | copy-start | bytes 540676
  448.9 11.6 %collective-permute-start.27 = (bf16[32,2816]{1,0:T(8,128)(2,1)S(1)}, bf16[32,2816]{1,0:T(8,128)(2,1)S(1)}, u32[]{:S(2)}, u32[]{:S(2)}) collective-permute-start(bf16[32,2816]{1,0:T(8,128)(2,1)S(1)} %get-tuple-element.75), channel_id=1, source_target_pairs={{0,8},{8,0},{16,24},{24,16},{1,9},{9,1},{17,25},{25,17},{2,10},{10... | collective-permute-start | bytes 540680 | tf_op jit(solution)/shard_map/ppermute | solution.py:140
  449.2 18.6 %collective-permute-start.28 = (bf16[32,2816]{1,0:T(8,128)(2,1)S(1)}, bf16[32,2816]{1,0:T(8,128)(2,1)S(1)}, u32[]{:S(2)}, u32[]{:S(2)}) collective-permute-start(bf16[32,2816]{1,0:T(8,128)(2,1)S(1)} %get-tuple-element.77), channel_id=1, source_target_pairs={{0,16},{8,24},{16,0},{24,8},{1,17},{9,25},{17,1},{25,9},{2,18},{10... | collective-permute-start | bytes 540680 | tf_op jit(solution)/shard_map/ppermute | solution.py:140
  451.6 37.6 %copy-start.36 = (bf16[32]{0:T(256)(128)(2,1)S(1)}, bf16[32]{0:T(256)(128)(2,1)}, u32[]{:S(2)}) copy-start(bf16[32]{0:T(256)(128)(2,1)} %param.24) | copy-start | bytes 196
  451.6 30.2 %collective-permute-start.29 = (bf16[32,2816]{1,0:T(8,128)(2,1)S(1)}, bf16[32,2816]{1,0:T(8,128)(2,1)S(1)}, u32[]{:S(2)}, u32[]{:S(2)}) collective-permute-start(bf16[32,2816]{1,0:T(8,128)(2,1)S(1)} %get-tuple-element.76), channel_id=1, source_target_pairs={{0,24},{8,16},{16,8},{24,0},{1,25},{9,17},{17,9},{25,1},{2,26},{10... | collective-permute-start | bytes 540680 | tf_op jit(solution)/shard_map/ppermute | solution.py:140
  452.7 30.1 %collective-permute-start.21 = (bf16[32,2816]{1,0:T(8,128)(2,1)S(1)}, bf16[32,2816]{1,0:T(8,128)(2,1)S(1)}, u32[]{:S(2)}, u32[]{:S(2)}) collective-permute-start(bf16[32,2816]{1,0:T(8,128)(2,1)S(1)} %get-tuple-element.78), channel_id=1, source_target_pairs={{0,8},{8,0},{16,24},{24,16},{1,9},{9,1},{17,25},{25,17},{2,10},{10... | collective-permute-start | bytes 540680 | tf_op jit(solution)/shard_map/ppermute | solution.py:140
  453.9 29.9 %collective-permute-start.22 = (bf16[32,2816]{1,0:T(8,128)(2,1)S(1)}, bf16[32,2816]{1,0:T(8,128)(2,1)S(1)}, u32[]{:S(2)}, u32[]{:S(2)}) collective-permute-start(bf16[32,2816]{1,0:T(8,128)(2,1)S(1)} %get-tuple-element.80), channel_id=1, source_target_pairs={{0,16},{8,24},{16,0},{24,8},{1,17},{9,25},{17,1},{25,9},{2,18},{10... | collective-permute-start | bytes 540680 | tf_op jit(solution)/shard_map/ppermute | solution.py:140
  460.5 27.8 %collective-permute-start.23 = (bf16[32,2816]{1,0:T(8,128)(2,1)S(1)}, bf16[32,2816]{1,0:T(8,128)(2,1)S(1)}, u32[]{:S(2)}, u32[]{:S(2)}) collective-permute-start(bf16[32,2816]{1,0:T(8,128)(2,1)S(1)} %get-tuple-element.79), channel_id=1, source_target_pairs={{0,24},{8,16},{16,8},{24,0},{1,25},{9,17},{17,9},{25,1},{2,26},{10... | collective-permute-start | bytes 540680 | tf_op jit(solution)/shard_map/ppermute | solution.py:140
  (40 other events, 195.0 us)
Sparse Core Ops, SparseCore 0:
  10.9 143.1 all-gather.2
  156.9 74.0 all-gather.4
  305.4 166.4 reduce-scatter.1

commit v3 on v2

v3 whole, which is shorter than its diff:
```python
import functools

import jax
import jax.numpy as jnp
from jax import lax
from jax.experimental import pallas as pl
from jax.experimental.pallas import tpu as pltpu
from jax.sharding import Mesh
from jax.sharding import PartitionSpec as P

HEAD_DIM = 64
BLOCK = 256
PAIR = 2 * HEAD_DIM

EPSILON = 1e-06
THETA = 10000.0
SCALE = 0.125
ALL = ("z", "y", "x", "c")
SEQ = ("z", "y")
F32 = jnp.float32
BF16 = jnp.bfloat16


def rotary_tables(positions):
    lane = jnp.arange(PAIR, dtype=jnp.int32)
    half = HEAD_DIM // 2
    index = (lane % half).astype(F32)
    frequency = THETA ** (-(index * 2.0 / HEAD_DIM))
    angles = positions.astype(F32)[:, None] * frequency[None, :]
    sign = jnp.where(lane % HEAD_DIM < half, -1.0, 1.0)[None, :]
    return jnp.cos(angles), jnp.sin(angles) * sign


def partner(values):
    half = HEAD_DIM // 2
    lane = lax.broadcasted_iota(jnp.int32, values.shape, values.ndim - 1)
    first = lane % HEAD_DIM < half
    width = values.shape[-1]
    return jnp.where(
        first,
        pltpu.roll(values, width - half, values.ndim - 1),
        pltpu.roll(values, half, values.ndim - 1),
    )


def dot_t(left, right):
    return lax.dot_general(left, right, (((1,), (1,)), ((), ())), preferred_element_type=F32)


def t_dot(left, right):
    return lax.dot_general(left, right, (((0,), (0,)), ((), ())), preferred_element_type=F32)


def dot(left, right):
    return jnp.dot(left, right, preferred_element_type=F32)


def attend_forward_kernel(qkv_ref, out_ref, total_ref):
    parts, _, _, rows, _ = qkv_ref.shape
    per_block = BLOCK // rows
    blocks = parts // per_block
    for head in range(2):
        lanes = pl.ds(head * HEAD_DIM, HEAD_DIM)
        for block in range(blocks):
            lo, hi = block * per_block, (block + 1) * per_block
            query = qkv_ref[lo:hi, 0, 0, :, lanes].reshape(BLOCK, HEAD_DIM)
            keys = qkv_ref[0:hi, 1, 0, :, lanes].reshape(hi * rows, HEAD_DIM)
            values = qkv_ref[0:hi, 2, 0, :, lanes].reshape(hi * rows, HEAD_DIM)
            scores = dot_t(keys, query) * SCALE
            top = jnp.max(scores, axis=0, keepdims=True)
            total = top + jnp.log(jnp.sum(jnp.exp(scores - top), axis=0, keepdims=True))
            probs = jnp.exp(scores - total).astype(BF16)
            mixed = t_dot(values, probs)
            out_ref[lo:hi, 0, :, lanes] = mixed.T.astype(BF16).reshape(per_block, rows, HEAD_DIM)
            total_ref[0, head, block : block + 1, :] = total


def attend_backward_kernel(qkv_ref, grad_ref, total_ref, cos_ref, sin_ref, out_ref, dk_acc, dv_acc):
    parts, _, _, rows, _ = qkv_ref.shape
    per_block = BLOCK // rows
    blocks = parts // per_block
    dk_acc[...] = jnp.zeros_like(dk_acc)
    dv_acc[...] = jnp.zeros_like(dv_acc)
    for block in range(blocks):
        lo, hi = block * per_block, (block + 1) * per_block
        keys_n = hi * rows
        dq_parts = []
        for head in range(2):
            lanes = pl.ds(head * HEAD_DIM, HEAD_DIM)
            query = qkv_ref[lo:hi, 0, 0, :, lanes].reshape(BLOCK, HEAD_DIM)
            grad = grad_ref[lo:hi, 0, :, lanes].reshape(BLOCK, HEAD_DIM)
            keys = qkv_ref[0:hi, 1, 0, :, lanes].reshape(keys_n, HEAD_DIM)
            values = qkv_ref[0:hi, 2, 0, :, lanes].reshape(keys_n, HEAD_DIM)
            scores = dot_t(keys, query) * SCALE
            probs = jnp.exp(scores - total_ref[0, head, block : block + 1, :])
            grad_probs = dot_t(values, grad)
            inner = jnp.sum(probs * grad_probs, axis=0, keepdims=True)
            grad_scores = (probs * (grad_probs - inner)).astype(BF16)
            dk_acc[0:keys_n, lanes] += dot(grad_scores, query) * SCALE
            dv_acc[0:keys_n, lanes] += dot(probs.astype(BF16), grad)
            dq_parts.append(t_dot(keys, grad_scores).T * SCALE)
        dq = jnp.concatenate(dq_parts, axis=1)
        cos = cos_ref[block * BLOCK : (block + 1) * BLOCK, :]
        sin = sin_ref[block * BLOCK : (block + 1) * BLOCK, :]
        dq = (dq * cos - partner(dq) * sin).astype(BF16)
        out_ref[lo:hi, 0, 0, :, :] = dq.reshape(per_block, rows, PAIR)
    dk = dk_acc[...]
    dk = (dk * cos_ref[...] - partner(dk) * sin_ref[...]).astype(BF16)
    out_ref[:, 1, 0, :, :] = dk.reshape(parts, rows, PAIR)
    out_ref[:, 2, 0, :, :] = dv_acc[...].astype(BF16).reshape(parts, rows, PAIR)


VMEM_LIMIT = 60 * 1024 * 1024


def attend_backward(qkv, grad_att, totals, cos, sin):
    parts, _, units, rows, _ = qkv.shape
    length = parts * rows
    blocks = length // BLOCK
    return pl.pallas_call(
        attend_backward_kernel,
        grid=(units,),
        in_specs=[
            pl.BlockSpec((parts, 3, 1, rows, PAIR), lambda u: (0, 0, u, 0, 0)),
            pl.BlockSpec((parts, 1, rows, PAIR), lambda u: (0, u, 0, 0)),
            pl.BlockSpec((1, 2, blocks, BLOCK), lambda u: (u, 0, 0, 0)),
            pl.BlockSpec((length, PAIR), lambda u: (0, 0)),
            pl.BlockSpec((length, PAIR), lambda u: (0, 0)),
        ],
        out_specs=pl.BlockSpec((parts, 3, 1, rows, PAIR), lambda u: (0, 0, u, 0, 0)),
        out_shape=jax.ShapeDtypeStruct((parts, 3, units, rows, PAIR), BF16),
        scratch_shapes=[pltpu.VMEM((length, PAIR), F32), pltpu.VMEM((length, PAIR), F32)],
        compiler_params=pltpu.CompilerParams(vmem_limit_bytes=VMEM_LIMIT),
        name="attend_backward",
    )(qkv, grad_att, totals, cos, sin)


def swap(array, name, distance):
    size = lax.axis_size(name)
    return lax.ppermute(array, name, [(i, i ^ distance) for i in range(size)])


def pick(array, index, axis):
    return lax.dynamic_index_in_dim(array, index, axis, keepdims=False)


def arrange(pieces, at):
    bit = 1
    while bit < len(pieces):
        odd = (at & bit) != 0
        pieces = [jnp.where(odd, pieces[j ^ bit], pieces[j]) for j in range(len(pieces))]
        bit *= 2
    return pieces


def stage_rows(rows, order, relative=ALL):
    sizes = [lax.axis_size(name) for name in order]
    per = rows // functools.reduce(lambda a, b: a * b, sizes)
    index = lax.broadcasted_iota(jnp.int32, (rows, 1), 0)
    left, inner = index // per, index % per
    place = {}
    for name, size in zip(reversed(order), reversed(sizes)):
        place[name] = left % size
        if name in relative:
            place[name] = place[name] ^ lax.axis_index(name)
        left = left // size
    device = jnp.zeros_like(index)
    for name in ALL:
        device = device * lax.axis_size(name) + place[name]
    return device * per + inner


def add_stage(value, name):
    size = lax.axis_size(name)
    value = value.astype(BF16).reshape(size, -1, value.shape[1])
    received = [swap(value[k], name, k) for k in range(1, size)]
    value = value[0].astype(F32)
    for piece in received:
        value = value + piece.astype(F32)
    return value


def together(*values):
    return lax.optimization_barrier(values)


def params():
    return pltpu.CompilerParams(vmem_limit_bytes=VMEM_LIMIT)


def front_kernel(
    x_ref, first_ref, gain_ref, cos_ref, sin_ref, weight_ref, normed_ref, qkv_ref, att_ref, total_ref
):
    parts, rows, width = x_ref.shape
    per_block = BLOCK // rows
    blocks = parts // per_block
    gain = gain_ref[...]
    for block in range(blocks):
        lo, hi = block * per_block, (block + 1) * per_block

        @pl.when(pl.program_id(0) == 0)
        def _(lo=lo, hi=hi):
            x = x_ref[lo:hi].reshape(BLOCK, width).astype(F32)
            inv = lax.rsqrt(jnp.mean(x * x, axis=-1, keepdims=True) + EPSILON)
            normed_ref[lo:hi] = (x * inv * gain).astype(BF16).reshape(per_block, rows, width)

        normed = normed_ref[lo:hi].reshape(BLOCK, width)
        cos = cos_ref[block * BLOCK : (block + 1) * BLOCK, :]
        sin = sin_ref[block * BLOCK : (block + 1) * BLOCK, :]
        for kind in range(2):
            value = dot(normed, weight_ref[kind])
            value = (value * cos + partner(value) * sin).astype(BF16)
            qkv_ref[lo:hi, kind, 0] = value.reshape(per_block, rows, PAIR)
        first = first_ref[lo:hi, 0].reshape(BLOCK, PAIR).astype(F32)
        mixed = (0.5 * dot(normed, weight_ref[2]) + 0.5 * first).astype(BF16)
        qkv_ref[lo:hi, 2, 0] = mixed.reshape(per_block, rows, PAIR)
    attend_forward_kernel(qkv_ref, att_ref, total_ref)


def front(x, first, gain, cos, sin, weights):
    parts, rows, width = x.shape
    units = first.shape[1]
    length = parts * rows
    blocks = length // BLOCK
    return pl.pallas_call(
        front_kernel,
        grid=(units,),
        in_specs=[
            pl.BlockSpec((parts, rows, width), lambda u: (0, 0, 0)),
            pl.BlockSpec((parts, 1, rows, PAIR), lambda u: (0, u, 0, 0)),
            pl.BlockSpec((1, width), lambda u: (0, 0)),
            pl.BlockSpec((length, PAIR), lambda u: (0, 0)),
            pl.BlockSpec((length, PAIR), lambda u: (0, 0)),
            pl.BlockSpec((3, width, PAIR), lambda u: (u, 0, 0)),
        ],
        out_specs=[
            pl.BlockSpec((parts, rows, width), lambda u: (0, 0, 0)),
            pl.BlockSpec((parts, 3, 1, rows, PAIR), lambda u: (0, 0, u, 0, 0)),
            pl.BlockSpec((parts, 1, rows, PAIR), lambda u: (0, u, 0, 0)),
            pl.BlockSpec((1, 2, blocks, BLOCK), lambda u: (u, 0, 0, 0)),
        ],
        out_shape=[
            jax.ShapeDtypeStruct((parts, rows, width), BF16),
            jax.ShapeDtypeStruct((parts, 3, units, rows, PAIR), BF16),
            jax.ShapeDtypeStruct((parts, units, rows, PAIR), BF16),
            jax.ShapeDtypeStruct((units, 2, blocks, BLOCK), F32),
        ],
        compiler_params=params(),
        name="front",
    )(x, first, gain, cos, sin, weights)


def sections(weight_ref):
    outer, parts, rows, columns = weight_ref.shape
    return [weight_ref[:, part].reshape(outer * rows, columns) for part in range(parts)]


def dot_sections(left, weight_ref):
    parts = sections(weight_ref)
    wide = left.shape[1] // len(parts)
    total = dot(left[:, :wide], parts[0])
    for at in range(1, len(parts)):
        total = total + dot(left[:, at * wide : (at + 1) * wide], parts[at])
    return total


def dot_t_sections(left, weight_ref):
    return jnp.concatenate([dot_t(left, part) for part in sections(weight_ref)], axis=1)


def forward_kernel(
    x_ref, heads_ref, gain_ref, teacher_ref, cotangent_ref, valid_ref, rate_ref, wo_ref, wg_ref, wu_ref, wd_ref,
    att_ref, hidden_ref, normed_ref, gate_ref, up_ref, act_ref, result_ref, grad_ref, grad_low_ref, loss_ref,
):
    step = pl.program_id(0)
    tokens, width = x_ref.shape

    @pl.when(step == 0)
    def _():
        for pair in range(width // PAIR):
            at, unit = divmod(pair, heads_ref.shape[2])
            att_ref[:, pair * PAIR : (pair + 1) * PAIR] = heads_ref[at, :, unit].reshape(tokens, PAIR)
        hidden = x_ref[...].astype(F32) + dot_sections(att_ref[...], wo_ref)
        inv = lax.rsqrt(jnp.mean(hidden * hidden, axis=-1, keepdims=True) + EPSILON)
        hidden_ref[...] = hidden
        result_ref[...] = hidden
        normed_ref[...] = (hidden * inv * gain_ref[...]).astype(BF16)

    gate = dot_sections(normed_ref[...], wg_ref)
    up = dot_sections(normed_ref[...], wu_ref)
    act = (gate * jax.nn.sigmoid(gate) * up).astype(BF16)
    gate_ref[...] = gate
    up_ref[...] = up
    act_ref[...] = act
    result_ref[...] += dot(act, sections(wd_ref)[0])

    @pl.when(step == pl.num_programs(0) - 1)
    def _():
        error = result_ref[...] - teacher_ref[...].astype(F32)
        valid = valid_ref[...]
        grad = cotangent_ref[...].astype(F32) + rate_ref[0:1, 0:1] * valid * error
        grad_ref[...] = grad
        grad_low_ref[...] = grad.astype(BF16)
        losses = jnp.sum(error * error * (valid / width), axis=0, keepdims=True)
        total = losses[:, :PAIR]
        for at in range(PAIR, width, PAIR):
            total = total + losses[:, at : at + PAIR]
        loss_ref[...] = total


def weight_specs(width, parts, gate_out, rest):
    outer, sides, rows, _ = rest.shape
    wide = outer * rows
    per = width // wide
    whole = (outer, sides, rows)
    return wide, [
        pl.BlockSpec(whole + (width,), lambda j: (0, 0, 0, parts)),
        pl.BlockSpec(whole + (wide,), lambda j: (0, 0, 0, j)),
        pl.BlockSpec(whole + (wide,), lambda j: (0, 0, 0, 3 * per + j)),
        pl.BlockSpec((outer, 1, rows, width), lambda j: (0, j % per, 0, 3 + parts + j // per)),
    ], (gate_out, gate_out, rest, rest)


def still(*shape):
    return pl.BlockSpec(shape, lambda j: (0,) * len(shape))


def mlp_forward(x, heads, gain, teacher, cotangent, valid, rate, gate_out, rest):
    tokens, width = x.shape
    parts = gate_out.shape[3] // width - 1
    wide, specs, weights = weight_specs(width, parts, gate_out, rest)
    moving = pl.BlockSpec((tokens, wide), lambda j: (0, j))
    whole = still(tokens, width)
    hidden = (tokens, parts * width)
    return pl.pallas_call(
        forward_kernel,
        grid=(parts * width // wide,),
        in_specs=[whole, still(*heads.shape), still(1, width), whole, whole, still(tokens, 1), still(1, PAIR)]
        + specs,
        out_specs=[whole, whole, whole, moving, moving, moving, whole, whole, whole, still(1, PAIR)],
        out_shape=[
            jax.ShapeDtypeStruct((tokens, width), BF16),
            jax.ShapeDtypeStruct((tokens, width), F32),
            jax.ShapeDtypeStruct((tokens, width), BF16),
            jax.ShapeDtypeStruct(hidden, F32),
            jax.ShapeDtypeStruct(hidden, F32),
            jax.ShapeDtypeStruct(hidden, BF16),
            jax.ShapeDtypeStruct((tokens, width), F32),
            jax.ShapeDtypeStruct((tokens, width), F32),
            jax.ShapeDtypeStruct((tokens, width), BF16),
            jax.ShapeDtypeStruct((1, PAIR), F32),
        ],
        compiler_params=params(),
        name="mlp_forward",
    )(x, heads, gain, teacher, cotangent, valid, rate, *weights)


def backward_kernel(
    grad_ref, grad_low_ref, hidden_ref, gain_ref, gate_ref, up_ref, wo_ref, wg_ref, wu_ref, wd_ref,
    grads_ref, grad_hidden_ref, branch_ref, heads_ref, total,
):
    step = pl.program_id(0)
    wide = gate_ref.shape[1]
    gate = gate_ref[...]
    up = up_ref[...]
    sigmoid = jax.nn.sigmoid(gate)
    grad_act = dot_t(grad_low_ref[...], sections(wd_ref)[0])
    grad_gate = (grad_act * up * (sigmoid * (1.0 + gate * (1.0 - sigmoid)))).astype(BF16)
    grad_up = (grad_act * (gate * sigmoid)).astype(BF16)
    grads_ref[:, :wide] = grad_gate
    grads_ref[:, wide:] = grad_up
    value = dot_t_sections(grad_gate, wg_ref) + dot_t_sections(grad_up, wu_ref)

    @pl.when(step == 0)
    def _():
        total[...] = value

    @pl.when(step > 0)
    def _():
        total[...] += value

    @pl.when(step == pl.num_programs(0) - 1)
    def _():
        hidden = hidden_ref[...]
        inv = lax.rsqrt(jnp.mean(hidden * hidden, axis=-1, keepdims=True) + EPSILON)
        scaled = hidden * inv
        scaled_grad = total[...] * gain_ref[...]
        grad = grad_ref[...] + inv * (
            scaled_grad - scaled * jnp.mean(scaled_grad * scaled, axis=-1, keepdims=True)
        )
        grad_hidden_ref[...] = grad
        branch = grad.astype(BF16)
        branch_ref[...] = branch
        value = dot_t_sections(branch, wo_ref).astype(BF16)
        _, batch, units, rows, _ = heads_ref.shape
        for pair in range(value.shape[1] // PAIR):
            at, unit = divmod(pair, units)
            heads_ref[at, :, unit] = value[:, pair * PAIR : (pair + 1) * PAIR].reshape(batch, rows, PAIR)


def mlp_backward(grad, grad_low, hidden, gain, gate, up, gate_out, rest, heads):
    tokens, width = grad.shape
    parts = gate_out.shape[3] // width - 1
    wide, specs, weights = weight_specs(width, parts, gate_out, rest)
    moving = pl.BlockSpec((tokens, wide), lambda j: (0, j))
    whole = still(tokens, width)
    return pl.pallas_call(
        backward_kernel,
        grid=(parts * width // wide,),
        in_specs=[whole, whole, whole, still(1, width), moving, moving] + specs,
        out_specs=[pl.BlockSpec((tokens, 2 * wide), lambda j: (0, j)), whole, whole, still(*heads)],
        out_shape=[
            jax.ShapeDtypeStruct((tokens, 2 * parts * width), BF16),
            jax.ShapeDtypeStruct((tokens, width), F32),
            jax.ShapeDtypeStruct((tokens, width), BF16),
            jax.ShapeDtypeStruct(heads, BF16),
        ],
        scratch_shapes=[pltpu.VMEM((tokens, width), F32)],
        compiler_params=params(),
        name="mlp_backward",
    )(grad, grad_low, hidden, gain, gate, up, *weights)


def picker(place, width):
    lane = lax.broadcasted_iota(jnp.int32, (place.shape[0], width), 1)
    return jnp.where(lane == place, 1.0, 0.0).astype(BF16)


def head_grads_kernel(normed_ref, grads_ref, loss_ref, pick_ref, out_ref, turned):
    parts, kinds, units, rows, _ = grads_ref.shape
    width = normed_ref.shape[2]
    normed = normed_ref[...].reshape(parts * rows, width)
    for unit in range(units):
        for kind in range(kinds):
            value = t_dot(grads_ref[:, kind, unit].reshape(parts * rows, PAIR), normed)
            if kind == 2:
                value = 0.5 * value
            at = (unit * kinds + kind) * PAIR
            turned[at : at + PAIR, :] = value.astype(BF16)
    columns = turned.shape[0]
    out_ref[:, :columns] = dot_t(pick_ref[...], turned[...]).astype(BF16)
    out_ref[:, columns:] = jnp.broadcast_to(loss_ref[...], (width, PAIR)).astype(BF16)


def head_grads(normed, grads, loss_row, pick):
    width = normed.shape[2]
    columns = 3 * grads.shape[2] * PAIR
    return pl.pallas_call(
        head_grads_kernel,
        out_shape=jax.ShapeDtypeStruct((width, columns + PAIR), BF16),
        scratch_shapes=[pltpu.VMEM((columns, width), BF16)],
        compiler_params=params(),
        name="head_grads",
    )(normed, grads, loss_row, pick)


def last_kernel(heads_ref, x_ref, gain_ref, weight_ref, grad_hidden_ref, grad_in_ref, first_ref, grads):
    tokens, width = x_ref.shape
    for kind in range(3):
        for pair in range(width // PAIR):
            at = kind * width + pair * PAIR
            place, unit = divmod(pair, heads_ref.shape[3])
            piece = heads_ref[place, :, kind, unit].reshape(tokens, PAIR)
            if kind == 2:
                half = 0.5 * piece.astype(F32)
                first_ref[:, pair * PAIR : (pair + 1) * PAIR] = half
                piece = half.astype(BF16)
            grads[:, at : at + PAIR] = piece
    grad_norm = dot_t_sections(grads[...], weight_ref)
    x = x_ref[...].astype(F32)
    inv = lax.rsqrt(jnp.mean(x * x, axis=-1, keepdims=True) + EPSILON)
    scaled = x * inv
    scaled_grad = grad_norm * gain_ref[...]
    grad_in_ref[...] = grad_hidden_ref[...] + inv * (
        scaled_grad - scaled * jnp.mean(scaled_grad * scaled, axis=-1, keepdims=True)
    )


def last(heads, x, gain, weights, grad_hidden):
    tokens, width = x.shape
    return pl.pallas_call(
        last_kernel,
        grid=(1,),
        in_specs=[
            still(*heads.shape),
            still(tokens, width),
            still(1, width),
            pl.BlockSpec(weights.shape[:3] + (3 * width,), lambda j: (0, 0, 0, 0)),
            still(tokens, width),
        ],
        out_specs=[still(tokens, width), still(tokens, width)],
        out_shape=[
            jax.ShapeDtypeStruct((tokens, width), F32),
            jax.ShapeDtypeStruct((tokens, width), F32),
        ],
        scratch_shapes=[pltpu.VMEM((tokens, 3 * width), BF16)],
        compiler_params=params(),
        name="last",
    )(heads, x, gain, weights, grad_hidden)


STAGES_NATIVE = ("c", "y", "x", "z")
STAGES_OUTPUT = ("c", "z", "y", "x")
STAGES_HEADS = ("c", "x", "y", "z")


def on_device(
    inputs,
    first_values,
    teacher_states,
    out_cotangent,
    token_valid,
    attn_gain,
    w_query,
    w_key,
    w_value,
    w_output,
    mlp_gain,
    w_gate,
    w_up,
    w_down,
):
    batch, local_len, width = inputs.shape
    seqs = lax.axis_size(SEQ)
    tokens = batch * local_len
    length = local_len * seqs
    pairs = width // PAIR
    own_rows = w_query.shape[0]
    own_down = w_down.shape[0]
    zs = lax.axis_size("z")
    units = pairs // zs
    mine = lax.axis_index("y")

    valid_float = token_valid.astype(F32)
    count = jnp.sum(token_valid)
    extra = jnp.stack(
        [
            attn_gain,
            mlp_gain,
            jnp.full((own_rows,), count // 256, jnp.int32).astype(BF16),
            jnp.full((own_rows,), count % 256, jnp.int32).astype(BF16),
        ],
        axis=1,
    )
    extra = jnp.pad(extra, ((0, 0), (0, PAIR - 4)))
    columns = jnp.stack([w_query, w_key, w_value]).reshape(3, own_rows, zs, units, PAIR)
    columns = columns.transpose(2, 3, 0, 1, 4).reshape(zs, 3 * units, own_rows, PAIR)
    columns = jnp.concatenate(
        [columns, jnp.broadcast_to(extra[None, None], (zs, 1, own_rows, PAIR))], axis=1
    )
    blocks = 3 * units + 1
    columns = jnp.broadcast_to(
        columns.reshape(zs, 1, blocks * own_rows, PAIR), (zs, batch, blocks * own_rows, PAIR)
    )
    firsts = first_values.reshape(batch, local_len, zs, units, PAIR).transpose(2, 0, 3, 1, 4)
    firsts = firsts.reshape(zs, batch, units * local_len, PAIR)
    parcel = jnp.concatenate([columns, firsts], axis=2).reshape(seqs, -1, PAIR)

    hidden_parts = -(-own_down // own_rows)
    padded = hidden_parts * own_rows - own_down

    def pack_columns(weight):
        weight = jnp.pad(weight.reshape(own_rows, -1, own_down), ((0, 0), (0, 0), (0, padded)))
        weight = weight.reshape(own_rows, -1, hidden_parts, own_rows)
        return weight.transpose(0, 2, 1, 3).reshape(own_rows, hidden_parts * width)

    def unpack_columns(grad):
        grad = grad.reshape(own_rows, hidden_parts, -1, own_rows).transpose(0, 2, 1, 3)
        return grad.reshape(own_rows, -1, hidden_parts * own_rows)[:, :, :own_down].reshape(own_rows, -1)

    down_rows = jnp.pad(w_down, ((0, padded), (0, 0))).reshape(hidden_parts, own_rows, width)
    down_rows = down_rows.transpose(1, 0, 2).reshape(own_rows, hidden_parts * width)
    def along_z(rows):
        pieces = [rows] + [swap(rows, "z", k) for k in range(1, zs)]
        return jnp.stack(arrange(pieces, lax.axis_index("z")), axis=0)

    def across(rows):
        rows = lax.all_gather(rows, ("y", "x", "c"), axis=0)
        if own_rows % 16:
            rows = rows.transpose(1, 0, 2, 3).reshape(1, width // BLOCK, BLOCK, rows.shape[3])
        return rows

    gate_out = along_z(jnp.concatenate([pack_columns(w_gate), w_output], axis=1))
    rest = jnp.concatenate([w_query, w_key, w_value, pack_columns(w_up), down_rows], axis=1)
    gate_out, rest, parcel = together(gate_out, rest, parcel)
    gate_out = across(gate_out)
    rest = along_z(rest)
    parcel = lax.all_to_all(parcel, SEQ, split_axis=0, concat_axis=0, tiled=True)
    rest, x_own, x_sent = together(rest, pick(inputs, mine, 0), pick(inputs, 1 - mine, 0))
    rest = across(rest)
    pieces = arrange([x_own, swap(x_sent, "y", 1)], mine)
    x_all = along_z(jnp.stack(pieces, axis=0)).reshape(seqs, local_len, width)

    first_all = parcel[:, blocks * own_rows :].reshape(seqs, units, local_len, PAIR)
    head_w = parcel[:, : blocks * own_rows].reshape(seqs, blocks, own_rows, PAIR).transpose(1, 0, 2, 3)
    for at, name in ((2, "x"), (3, "c")):
        pieces = [head_w] + [swap(head_w, name, k) for k in range(1, lax.axis_size(name))]
        head_w = jnp.stack(arrange(pieces, lax.axis_index(name)), axis=at)
    head_w = head_w.reshape(blocks, width, PAIR)
    extra_all = head_w[blocks - 1].astype(F32).T
    gain_a = extra_all[0:1, :]
    gain_m = extra_all[1:2, :]
    valid_total = jnp.sum(extra_all[2] * 256.0 + extra_all[3]) / own_rows

    cos_all, sin_all = rotary_tables(jnp.arange(length, dtype=jnp.int32))
    pick_native = picker(stage_rows(width, STAGES_NATIVE, ("c", "z")), width)
    pick_output = picker(stage_rows(width, STAGES_OUTPUT), width)
    pick_heads = picker(stage_rows(width, STAGES_HEADS, ("c", "x", "y")), width)

    normed_all, qkv, attended, totals = front(x_all, first_all, gain_a, cos_all, sin_all, head_w)

    def exchange(array):
        return lax.all_to_all(array, SEQ, split_axis=0, concat_axis=0, tiled=True)

    att_heads = exchange(attended).reshape(zs, batch, units, local_len, PAIR)
    x_low = inputs.reshape(tokens, width)
    rate = jnp.full((1, PAIR), 2.0 / width, F32) / valid_total
    att_low, hidden_in, normed_mlp, gate, up, activated, result, grad_out, grad_down_in, loss_row = mlp_forward(
        x_low,
        att_heads,
        gain_m,
        teacher_states.reshape(tokens, width),
        out_cotangent.reshape(tokens, width),
        valid_float.reshape(tokens, 1),
        rate,
        gate_out,
        rest,
    )

    half = width // 2
    turned = [
        dot_t(pick_native, activated[:, p * width : (p + 1) * width]).astype(BF16).reshape(-1, own_rows, tokens)
        for p in range(hidden_parts)
    ]
    turned_act = jnp.stack(turned, axis=1).reshape(hidden_parts * width, tokens)
    cut = hidden_parts * half
    down_sent = swap(dot(turned_act[cut:], grad_down_in).astype(BF16), "c", 1)
    down_sum = (dot(turned_act[:cut], grad_down_in) + down_sent.astype(F32)).astype(BF16)
    down_sum, grad_down_in = together(down_sum, grad_down_in)

    def over_yx(value):
        value = value.reshape(2 * lax.axis_size("x"), -1, value.shape[1])
        value = lax.psum_scatter(value, ("y", "x"), scatter_dimension=0, tiled=True)
        return lax.optimization_barrier(value)[0]

    down_sum = over_yx(down_sum)
    grads, grad_hidden, grad_branch, grad_heads = mlp_backward(
        grad_out, grad_down_in, hidden_in, gain_m, gate, up, gate_out, rest, att_heads.shape
    )
    grad_heads = exchange(grad_heads.reshape(seqs, units, local_len, PAIR))
    turned_mlp = dot_t(pick_native, normed_mlp).astype(BF16)
    mlp_sent = swap(dot(turned_mlp[half:], grads).astype(BF16), "c", 1)
    mlp_sum = (dot(turned_mlp[:half], grads) + mlp_sent.astype(F32)).astype(BF16)

    turned_att = dot_t(pick_output, att_low).astype(BF16)
    out_sent = swap(dot(turned_att[half:], grad_branch).astype(BF16), "c", 1)
    out_sum = (dot(turned_att[:half], grad_branch) + out_sent.astype(F32)).astype(BF16)

    grad_heads, mlp_sum, out_sum = together(grad_heads, mlp_sum, out_sum)
    mlp_sum = over_yx(mlp_sum)
    out_sum = add_stage(out_sum, "z").astype(BF16)

    grad_qkv = attend_backward(qkv, grad_heads, totals, cos_all, sin_all)
    grad_own = exchange(grad_qkv).reshape(zs, batch, 3, units, local_len, PAIR)

    value = head_grads(normed_all, grad_qkv, loss_row, pick_heads)
    for name in ("c", "x", "y"):
        value = add_stage(value, name)
    value, grad_own, down_sum, out_sum = together(value.astype(BF16), grad_own, down_sum, out_sum)
    owned_down = add_stage(down_sum, "z")[:own_down]
    owned_output = add_stage(add_stage(out_sum, "y"), "x")
    mlp_sum = add_stage(mlp_sum, "z")
    value = value.reshape(zs, own_rows, value.shape[1])
    value = lax.all_to_all(value, "z", split_axis=0, concat_axis=0, tiled=True)
    columns = 3 * units * PAIR
    loss_value = jnp.sum(value[:, 0, columns:].astype(F32)) / valid_total
    value = value[:, :, :columns].reshape(zs, own_rows, units, 3, PAIR).astype(F32)
    owned_qkv = value.transpose(3, 1, 0, 2, 4).reshape(3, own_rows, width)

    grad_in, grad_first = last(grad_own, x_low, gain_a, rest, grad_hidden)

    gain_grad_a = (
        jnp.sum(w_query.astype(F32) * owned_qkv[0], axis=1)
        + jnp.sum(w_key.astype(F32) * owned_qkv[1], axis=1)
        + jnp.sum(w_value.astype(F32) * owned_qkv[2], axis=1)
    ) / attn_gain.astype(F32)
    mlp_sum = mlp_sum.reshape(own_rows, -1, 2, BLOCK)
    owned_gate = unpack_columns(mlp_sum[:, :, 0])
    owned_up = unpack_columns(mlp_sum[:, :, 1])
    gain_grad_m = (
        jnp.sum(w_gate.astype(F32) * owned_gate, axis=1) + jnp.sum(w_up.astype(F32) * owned_up, axis=1)
    ) / mlp_gain.astype(F32)
    return (
        result.reshape(batch, local_len, width),
        loss_value,
        grad_in.reshape(batch, local_len, width),
        grad_first.reshape(batch, local_len, width),
        gain_grad_a,
        owned_qkv[0],
        owned_qkv[1],
        owned_qkv[2],
        owned_output,
        gain_grad_m,
        owned_gate,
        owned_up,
        owned_down,
    )


def solution(mesh):
    seqs, dps = mesh.devices.shape
    fine = Mesh(mesh.devices.reshape(seqs // 2, 2, dps // 2, 2), ALL)
    tokens = P(("x", "c"), SEQ, None)
    rows = P(ALL, None)
    gain = P(ALL)
    return jax.shard_map(
        on_device,
        mesh=fine,
        in_specs=(
            tokens, tokens, tokens, tokens, P(("x", "c"), SEQ), gain, rows, rows, rows, rows, gain, rows, rows, rows,
        ),
        out_specs=(
            tokens, P(), tokens, tokens, gain, rows, rows, rows, rows, gain, rows, rows, rows,
        ),
        check_vma=False,
    )
```

time: 504 us -> 486 us (0.964)
  Pallas kernels: 55.7 us -> 88.9 us
  other arithmetic: 58.3 us -> 27.7 us
  matrix products: 44.5 us -> 26.7 us
  blocking collectives: 13.6 us -> 0 us
  local copies, waits for them, and re-layouts: 24.2 us -> 36.8 us
  waiting for transfers between devices: 223 us -> 216 us
    pallas_call x4, Pallas kernels: 23.5 us -> 56.8 us  [the longest x1 21.7 us: mlp_backward(): pl.pallas_call(backward_kernel, grid=(parts * width // wide,), in_specs=[...]
    all_to_all x3, waiting for transfers between devices: 31.9 us -> 10.6 us  [exchange(): return lax.all_to_all(array, SEQ, split_axis=0, concat_axis=0, tiled=True)]
    all_to_all x1, waiting for transfers between devices: 0.01 us -> 19.4 us  [on_device(): lax.all_to_all(parcel, SEQ, split_axis=0, concat_axis=0, tiled=True)]
    all_to_all x1 -> x0, blocking collectives: 13.6 us -> none  [exchange(): return lax.all_to_all(array, SEQ, split_axis=0, concat_axis=0, tiled=True)]
    another operation x15 -> x9, other arithmetic: 20.4 us -> 8.41 us  [the longest x6 7.36 us: along_z(): return jnp.stack(arrange(pieces, lax.axis_index('z')), axis=0)]
    reshape x1 -> x15, local copies, waits for them, and re-layouts: 0.1 us -> 10 us  [the longest x4 2.24 us: unpack_columns(): grad.reshape(own_rows, -1, hidden_parts * own_rows)[:, :, :own_down]]
    ppermute x30 -> x29, waiting for transfers between devices: 191 us -> 181 us  [swap(): return lax.ppermute(array, name, [(i, i ^ distance) for i in range(size)])]
    concatenate x4 -> x2, other arithmetic: 9.52 us -> 1.03 us  [the longest x1 1.01 us: on_device(): parcel = jnp.concatenate([columns, firsts], axis=2).reshape(seqs, -1, PAIR)]
  transfers between devices with their start and end apart: 37 -> 38, of which waited for: 19 -> 25; matrix products, arithmetic and copies ran while one was open for 24% -> 11% of each run, Pallas kernels for 11% -> 10%
where the time goes in v3:
time: 486 us; the launch traced here: 479 us
  waiting for transfers between devices  216 us (44%)
  Pallas kernels  88.9 us (18%)
  starting transfers between devices  62.4 us (13%)
  local copies, waits for them, and re-layouts  36.8 us (8%)
  other arithmetic  27.7 us (6%)
  matrix products  26.7 us (5%)
  between operations  20 us (4%)
    ppermute x29, waiting for transfers between devices, swap(): return lax.ppermute(array, name, [(i, i ^ distance) for i in range(size)])  181 us
    ppermute x29, starting transfers between devices, swap(): return lax.ppermute(array, name, [(i, i ^ distance) for i in range(size)])  31.8 us
    dot_general x6, matrix products, dot(): return jnp.dot(left, right, preferred_element_type=F32)  21.8 us
    pallas_call x1, Pallas kernels, mlp_backward(): pl.pallas_call(backward_kernel, grid=(parts * width // wide,), in_specs=[...  21.7 us
    pallas_call x1, Pallas kernels, mlp_forward(): pl.pallas_call(forward_kernel, grid=(parts * width // wide,), in_specs=[w...  19.9 us
    all_to_all x1, waiting for transfers between devices, on_device(): lax.all_to_all(parcel, SEQ, split_axis=0, concat_axis=0, tiled=True)  19.4 us
    pallas_call x1, Pallas kernels, front(): pl.pallas_call(front_kernel, grid=(units,), in_specs=[pl.BlockSpec((parts...  17.8 us
    all_to_all x3, starting transfers between devices, exchange(): return lax.all_to_all(array, SEQ, split_axis=0, concat_axis=0, tiled=True)  17.2 us
  transfers between devices with their start and end apart: 38, of which 25 were waited for; matrix products, arithmetic and copies ran while one was open for 11% of the time, Pallas kernels for 10%

profile of v3, /device:TPU:8, one launch (start us, length us, event | category | flops | bytes accessed | tf_op | source)
XLA Modules:
  0.0 478.9 jit_solution(3703000377071401736)
XLA Ops:
  24.7 6.1 %collective-permute-done = bf16[32,4096]{1,0:T(8,128)(2,1)} collective-permute-done((bf16[32,4096]{1,0:T(8,128)(2,1)S(1)}, bf16[32,4096]{1,0:T(8,128)(2,1)}, u32[]{:S(2)}, u32[]{:S(2)}) %collective-permute-start) | collective-permute-done | bytes 262176 | tf_op jit(solution)/shard_map/ppermute | solution.py:140
  30.8 3.6 collective-permute-done.1
  37.4 4.4 collective-permute-start.4
  42.6 35.9 %collective-permute-done.3 = bf16[32,9216]{1,0:T(8,128)(2,1)S(1)} collective-permute-done((bf16[32,9216]{1,0:T(8,128)(2,1)S(1)}, bf16[32,9216]{1,0:T(8,128)(2,1)S(1)}, u32[]{:S(2)}, u32[]{:S(2)}) %collective-permute-start.3) | collective-permute-done | bytes 589856 | tf_op jit(solution)/shard_map/ppermute | solution.py:140
  78.4 8.7 %collective-permute-done.4 = bf16[32,9216]{1,0:T(8,128)(2,1)S(1)} collective-permute-done((bf16[32,9216]{1,0:T(8,128)(2,1)S(1)}, bf16[32,9216]{1,0:T(8,128)(2,1)S(1)}, u32[]{:S(2)}, u32[]{:S(2)}) %collective-permute-start.4) | collective-permute-done | bytes 589856 | tf_op jit(solution)/shard_map/ppermute | solution.py:140
  89.2 7.6 %all-to-all-start = ((bf16[8,480,128]{2,1,0:T(8,128)(2,1)}), bf16[8,480,128]{2,1,0:T(8,128)(2,1)S(1)}, u32[]{:S(2)}, u32[]{:S(2)}) async-start(bf16[8,480,128]{2,1,0:T(8,128)(2,1)} %pad_maximum_fusion.5), calls=%async_computation | async-start | bytes 1966080 | tf_op jit(solution)/shard_map/all_to_all | solution.py:588
  98.3 19.4 %all-to-all-done = bf16[8,480,128]{2,1,0:T(8,128)(2,1)S(1)} async-done(((bf16[8,480,128]{2,1,0:T(8,128)(2,1)}), bf16[8,480,128]{2,1,0:T(8,128)(2,1)S(1)}, u32[]{:S(2)}, u32[]{:S(2)}) %all-to-all-start) | async-done | bytes 983072 | tf_op jit(solution)/shard_map/all_to_all | solution.py:588
  120.4 4.2 collective-permute-start.8
  124.6 15.1 %collective-permute-done.10 = bf16[7,8,32,128]{3,2,0,1:T(8,128)(2,1)S(1)} collective-permute-done((bf16[7,8,32,128]{3,2,0,1:T(8,128)(2,1)S(1)}, bf16[7,8,32,128]{3,2,0,1:T(8,128)(2,1)S(1)}, u32[]{:S(2)}, u32[]{:S(2)}) %collective-permute-start.10) | collective-permute-done | bytes 458784 | tf_op jit(solution)/shard_map/ppermute | solution.py:140
  139.9 3.1 fusion.27
  143.0 13.6 %collective-permute-done.7 = bf16[2,128,1024]{2,1,0:T(8,128)(2,1)} collective-permute-done((bf16[2,128,1024]{2,1,0:T(8,128)(2,1)}, bf16[2,128,1024]{2,1,0:T(8,128)(2,1)}, u32[]{:S(2)}, u32[]{:S(2)}) %collective-permute-start.7) | collective-permute-done | bytes 524320 | tf_op jit(solution)/shard_map/ppermute | solution.py:140
  156.6 7.7 %collective-permute-done.8 = bf16[2,128,1024]{2,1,0:T(8,128)(2,1)} collective-permute-done((bf16[2,128,1024]{2,1,0:T(8,128)(2,1)}, bf16[2,128,1024]{2,1,0:T(8,128)(2,1)}, u32[]{:S(2)}, u32[]{:S(2)}) %collective-permute-start.8) | collective-permute-done | bytes 524320 | tf_op jit(solution)/shard_map/ppermute | solution.py:140
  172.9 17.8 %front.1 = (bf16[8,128,1024]{2,1,0:T(8,128)(2,1)}, bf16[8,3,2,128,128]{4,3,2,1,0:T(8,128)(2,1)}, bf16[8,2,128,128]{3,2,1,0:T(8,128)(2,1)}, f32[2,2,4,256]{3,2,1,0:T(4,128)}) custom-call(bf16[8,128,1024]{2,1,0:T(8,128)(2,1)} %bitcast.135, bf16[8,2,128,128]{3,2,1,0:T(8,128)(2,1)} %bitcast.149, f32[1,1024]{1,0:T(1,128)} %get-tuple-element.118.gain_ref, ...), custom_call_target="tpu_custom_call" | custom-call | tf_op jit(solution)/shard_map/front/pallas_call | solution.py:225
  190.8 6.7 %all-to-all-start.1 = ((bf16[8,2,128,128]{3,2,1,0:T(8,128)(2,1)}), bf16[8,2,128,128]{3,2,1,0:T(8,128)(2,1)S(1)}, u32[]{:S(2)}, u32[]{:S(2)}) async-start(bf16[8,2,128,128]{3,2,1,0:T(8,128)(2,1)} %get-tuple-element.52), calls=%async_computation.1 | async-start | bytes 1048576 | tf_op jit(solution)/shard_map/all_to_all | solution.py:613
  199.2 9.8 %all-to-all-done.1 = bf16[8,2,128,128]{3,2,1,0:T(8,128)(2,1)S(1)} async-done(((bf16[8,2,128,128]{3,2,1,0:T(8,128)(2,1)}), bf16[8,2,128,128]{3,2,1,0:T(8,128)(2,1)S(1)}, u32[]{:S(2)}, u32[]{:S(2)}) %all-to-all-start.1) | async-done | bytes 524320 | tf_op jit(solution)/shard_map/all_to_all | solution.py:613
  209.8 19.9 %mlp_forward.1 = (bf16[256,1024]{1,0:T(8,128)(2,1)}, f32[256,1024]{1,0:T(8,128)}, bf16[256,1024]{1,0:T(8,128)(2,1)}, f32[256,3072]{1,0:T(8,128)}, f32[256,3072]{...) custom-call(bf16[256,1024]{1,0:T(8,128)(2,1)} %bitcast.141, ...), custom_call_target="tpu_custom_call" | custom-call | tf_op jit(solution)/shard_map/mlp_forward/pallas_call | solution.py:335
  229.7 1.9 fusion.21
  236.3 4.9 %collective-permute-done.12 = bf16[1536,1024]{1,0:T(8,128)(2,1)S(1)} collective-permute-done((bf16[1536,1024]{1,0:T(8,128)(2,1)S(1)}, bf16[1536,1024]{1,0:T(8,128)(2,1)S(1)}, u32[]{:S(2)}, u32[]{:S(2)}) %collective-permute-start.12) | collective-permute-done | bytes 3145760 | tf_op jit(solution)/shard_map/ppermute | solution.py:140
  241.1 2.6 add_convert_fusion.1
  243.8 21.7 %mlp_backward.1 = (bf16[256,6144]{1,0:T(8,128)(2,1)}, f32[256,1024]{1,0:T(8,128)}, bf16[256,1024]{1,0:T(8,128)(2,1)}, bf16[4,2,2,128,128]{4,3,2,1,0:T(8,128)(2,1)}) custom-call(f32[256,1024]{1,0:T(8,128)} %get-tuple-element.58.grad_ref, bf16[256,1024]{1,0:T(8,128)(2,1)} %get-tuple-element.61.grad_low_ref, f32[256,1024]{1,0:T(8,128)} %get-tuple-element.62.hidden_ref, ...), custom_call_target="tpu_custom_call" | custom-call | tf_op jit(solution)/shard_map/mlp_backward/pallas_call | solution.py:407
  265.4 6.4 %convolution_convert_fusion = bf16[512,6144]{1,0:T(8,128)(2,1)} fusion(bf16[256,6144]{1,0:T(8,128)(2,1)} %get-tuple-element.67, bf16[1024,256]{1,0:T(8,128)(2,1)S(1)} %fusion.24), kind=kOutput, calls=%fused_computation.1 | convolution fusion | flops 1613758464 | bytes 9699328 | tf_op jit(solution)/shard_map/dot_general | solution.py:55
  275.4 5.6 %all-to-all-start.2 = ((bf16[8,2,128,128]{3,2,1,0:T(8,128)(2,1)}), bf16[8,2,128,128]{3,2,1,0:T(8,128)(2,1)}, u32[]{:S(2)}, u32[]{:S(2)}) async-start(bf16[8,2,128,128]{3,2,1,0:T(8,128)(2,1)} %bitcast.165), calls=%async_computation.2 | async-start | bytes 1048576 | tf_op jit(solution)/shard_map/all_to_all | solution.py:613
  281.4 2.3 collective-permute-done.14
  283.8 3.0 add_convert_fusion.2
  286.8 7.4 %add_convert_fusion = bf16[512,6144]{1,0:T(8,128)(2,1)} fusion(bf16[512,6144]{1,0:T(8,128)(2,1)} %collective-permute-done.13, bf16[256,6144]{1,0:T(8,128)(2,1)S(1)} %copy-done, bf16[1024,256]{1,0:T(8,128)(2,1)S(1)} %copy-done.19), kind=kOutput, calls=%fused_computation | convolution fusion | flops 1620049920 | bytes 15990784 | tf_op jit(solution)/shard_map/dot_general | solution.py:55
  295.1 14.3 %attend_backward.1.grads_ref = bf16[8,3,2,128,128]{4,3,2,1,0:T(8,128)(2,1)} custom-call(bf16[8,3,2,128,128]{4,3,2,1,0:T(8,128)(2,1)} %get-tuple-element.57.qkv_ref, bf16[8,2,128,128]{3,2,1,0:T(8,128)(2,1)} %all-to-all-done.2.grad_ref, f32[2,2,4,256]{3,2,1,0:T(4,128)} %get-tuple-element.71.total_ref, f32[1024,128]{1,0:T(8,128)} %get-tuple-element.124.cos_ref, ...), custom_call_target="tpu_custom_call" | custom-call | tf_op jit(solution)/shard_map/attend_backward/pallas_call | solution.py:120
  309.4 4.8 %all-to-all-start.3 = ((bf16[8,3,2,128,128]{4,3,2,1,0:T(8,128)(2,1)}), bf16[8,3,2,128,128]{4,3,2,1,0:T(8,128)(2,1)S(1)}, u32[]{:S(2)}, u32[]{:S(2)}) async-start(bf16[8,3,2,128,128]{4,3,2,1,0:T(8,128)(2,1)} %attend_backward.1.grads_ref), calls=%async_computation.3 | async-start | bytes 3145728 | tf_op jit(solution)/shard_map/all_to_all | solution.py:613
  316.0 7.6 %head_grads.1 = bf16[1024,896]{1,0:T(8,128)(2,1)} custom-call(bf16[8,128,1024]{2,1,0:T(8,128)(2,1)} %get-tuple-element.56.normed_ref, bf16[8,3,2,128,128]{4,3,2,1,0:T(8,128)(2,1)} %attend_backward.1.grads_ref, f32[1,128]{1,0:T(1,128)} %get-tuple-element.72.loss_ref, bf16[1024,1024]{1,0:T(8,128)(2,1)} %select_convert_fusion.pick_ref), custom_call_target="tpu_custom_call" | custom-call | tf_op jit(solution)/shard_map/head_grads/pallas_call | solution.py:448
  325.1 2.5 collective-permute-done.15
  330.1 2.8 collective-permute-start.19
  333.5 7.9 %collective-permute-done.16 = bf16[256,896]{1,0:T(8,128)(2,1)} collective-permute-done((bf16[256,896]{1,0:T(8,128)(2,1)}, bf16[256,896]{1,0:T(8,128)(2,1)}, u32[]{:S(2)}, u32[]{:S(2)}) %collective-permute-start.16) | collective-permute-done | bytes 458784 | tf_op jit(solution)/shard_map/ppermute | solution.py:140
  344.1 4.1 collective-permute-done.18
  348.2 17.8 %collective-permute-done.19 = bf16[128,1024]{1,0:T(8,128)(2,1)} collective-permute-done((bf16[128,1024]{1,0:T(8,128)(2,1)}, bf16[128,1024]{1,0:T(8,128)(2,1)}, u32[]{:S(2)}, u32[]{:S(2)}) %collective-permute-start.19) | collective-permute-done | bytes 262176 | tf_op jit(solution)/shard_map/ppermute | solution.py:140
  366.0 6.7 %collective-permute-done.20 = bf16[128,1024]{1,0:T(8,128)(2,1)} collective-permute-done((bf16[128,1024]{1,0:T(8,128)(2,1)}, bf16[128,1024]{1,0:T(8,128)(2,1)}, u32[]{:S(2)}, u32[]{:S(2)}) %collective-permute-start.20) | collective-permute-done | bytes 262176 | tf_op jit(solution)/shard_map/ppermute | solution.py:140
  376.3 7.0 %collective-permute-done.21 = bf16[64,1024]{1,0:T(8,128)(2,1)S(1)} collective-permute-done((bf16[64,1024]{1,0:T(8,128)(2,1)S(1)}, bf16[64,1024]{1,0:T(8,128)(2,1)S(1)}, u32[]{:S(2)}, u32[]{:S(2)}) %collective-permute-start.21) | collective-permute-done | bytes 131104 | tf_op jit(solution)/shard_map/ppermute | solution.py:140
  385.2 3.3 collective-permute-start.27
  388.7 5.1 %all-to-all-start.4 = ((bf16[4,32,896]{2,1,0:T(8,128)(2,1)}), bf16[4,32,896]{2,1,0:T(8,128)(2,1)S(1)}, u32[]{:S(2)}, u32[]{:S(2)}) async-start(bf16[4,32,896]{2,1,0:T(8,128)(2,1)} %bitcast.60), calls=%async_computation.4 | async-start | bytes 458752 | tf_op jit(solution)/shard_map/all_to_all | solution.py:674
  393.9 7.6 %last.1 = (f32[256,1024]{1,0:T(8,128)}, f32[256,1024]{1,0:T(8,128)}) custom-call(bf16[4,2,3,2,128,128]{5,4,3,2,1,0:T(8,128)(2,1)} %bitcast.137, bf16[256,1024]{1,0:T(8,128)(2,1)} %bitcast.142, f32[1,1024]{1,0:T(1,128)} %get-tuple-element.118.gain_ref, bf16[8,4,32,9216]{3,2,1,0:T(8,128)(2,1)} %bitcast.128, f32[256,1024]{1,0:T(8,128)} %get-tuple-element.77.grad_hidden_ref), custom_call_target="tpu_custom_call" | custom-call | tf_op jit(solution)/shard_map/last/pallas_call | solution.py:481
  403.2 4.7 collective-permute-done.28
  410.2 4.8 %reduce-scatter.9.cloned.1.call-done = bf16[1,128,6144]{2,1,0:T(8,128)(2,1)} async-done(((bf16[4,128,6144]{2,1,0:T(8,128)(2,1)}), bf16[1,128,6144]{2,1,0:T(8,128)(2,1)}) %reduce-scatter.9.cloned.1.call-update) | async-done | bytes 1572880
  415.0 2.1 slice_bitcast_fusion.2
  417.6 2.4 collective-permute-start.24
  422.7 11.4 %collective-permute-done.23 = bf16[32,6144]{1,0:T(8,128)(2,1)S(1)} collective-permute-done((bf16[32,6144]{1,0:T(8,128)(2,1)}, bf16[32,6144]{1,0:T(8,128)(2,1)S(1)}, u32[]{:S(2)}, u32[]{:S(2)}) %collective-permute-start.23) | collective-permute-done | bytes 393248 | tf_op jit(solution)/shard_map/ppermute | solution.py:140
  434.0 12.4 %collective-permute-done.24 = bf16[32,6144]{1,0:T(8,128)(2,1)S(1)} collective-permute-done((bf16[32,6144]{1,0:T(8,128)(2,1)S(1)}, bf16[32,6144]{1,0:T(8,128)(2,1)S(1)}, u32[]{:S(2)}, u32[]{:S(2)}) %collective-permute-start.24) | collective-permute-done | bytes 393248 | tf_op jit(solution)/shard_map/ppermute | solution.py:140
  446.4 8.0 %collective-permute-done.25 = bf16[32,6144]{1,0:T(8,128)(2,1)S(1)} collective-permute-done((bf16[32,6144]{1,0:T(8,128)(2,1)S(1)}, bf16[32,6144]{1,0:T(8,128)(2,1)S(1)}, u32[]{:S(2)}, u32[]{:S(2)}) %collective-permute-start.25) | collective-permute-done | bytes 393248 | tf_op jit(solution)/shard_map/ppermute | solution.py:140
  456.3 2.1 slice_reduce_fusion
  459.9 2.7 copy.117
  466.5 2.7 copy.116
  (224 shorter events, 75.0 us)
Async XLA Ops:
  7.2 201.8 %all-gather.5.cloned.1.call-start = ((), (), s32[]{:S(2)}) async-start(), calls=%async_computation.7 | async-start | bytes 9437184 | tf_op jit(solution)/shard_map/all_gather | solution.py:578
  8.9 9.4 %copy-start.12 = (bf16[32,1024]{1,0:T(8,128)(2,1)S(1)}, bf16[32,1024]{1,0:T(8,128)(2,1)}, u32[]{:S(2)}) copy-start(bf16[32,1024]{1,0:T(8,128)(2,1)} %param.22) | copy-start | bytes 196612
  9.5 10.7 %copy-start.10 = (bf16[32,2816]{1,0:T(8,128)(2,1)S(1)}, bf16[32,2816]{1,0:T(8,128)(2,1)}, u32[]{:S(2)}) copy-start(bf16[32,2816]{1,0:T(8,128)(2,1)} %param.26) | copy-start | bytes 540676
  10.4 20.4 %collective-permute-start = (bf16[32,4096]{1,0:T(8,128)(2,1)S(1)}, bf16[32,4096]{1,0:T(8,128)(2,1)}, u32[]{:S(2)}, u32[]{:S(2)}) collective-permute-start(bf16[32,4096]{1,0:T(8,128)(2,1)S(1)} %constant_dynamic-update-slice_fusion), channel_id=1, source_target_pairs={{0,24},{8,16},{16,8},{24,0},{1,25},{9,17},{17,9},{25,1},{2,26},{10... | collective-permute-start | bytes 786440 | tf_op jit(solution)/shard_map/ppermute | solution.py:140
  12.0 22.4 %collective-permute-start.1 = (bf16[32,4096]{1,0:T(8,128)(2,1)S(1)}, bf16[32,4096]{1,0:T(8,128)(2,1)}, u32[]{:S(2)}, u32[]{:S(2)}) collective-permute-start(bf16[32,4096]{1,0:T(8,128)(2,1)S(1)} %constant_dynamic-update-slice_fusion), channel_id=1, source_target_pairs={{0,16},{8,24},{16,0},{24,8},{1,17},{9,25},{17,1},{25,9},{2,18},{10... | collective-permute-start | bytes 786440 | tf_op jit(solution)/shard_map/ppermute | solution.py:140
  13.1 21.3 %collective-permute-start.2 = (bf16[32,4096]{1,0:T(8,128)(2,1)S(1)}, bf16[32,4096]{1,0:T(8,128)(2,1)}, u32[]{:S(2)}, u32[]{:S(2)}) collective-permute-start(bf16[32,4096]{1,0:T(8,128)(2,1)S(1)} %constant_dynamic-update-slice_fusion), channel_id=1, source_target_pairs={{0,8},{8,0},{16,24},{24,16},{1,9},{9,1},{17,25},{25,17},{2,10},{10... | collective-permute-start | bytes 786440 | tf_op jit(solution)/shard_map/ppermute | solution.py:140
  24.7 17.2 %copy-start.3 = (bf16[2,128,1024]{2,1,0:T(8,128)(2,1)S(1)}, bf16[2,128,1024]{2,1,0:T(8,128)(2,1)}, u32[]{:S(2)}) copy-start(bf16[2,128,1024]{2,1,0:T(8,128)(2,1)} %param.14) | copy-start | bytes 1572868
  36.8 172.2 %all-gather.7.cloned.1.call-start = ((), (), s32[]{:S(2)}) async-start(), calls=%async_computation.8 | async-start | bytes 21233664 | tf_op jit(solution)/shard_map/all_gather | solution.py:578
  36.8 41.6 %collective-permute-start.3 = (bf16[32,9216]{1,0:T(8,128)(2,1)S(1)}, bf16[32,9216]{1,0:T(8,128)(2,1)S(1)}, u32[]{:S(2)}, u32[]{:S(2)}) collective-permute-start(bf16[32,9216]{1,0:T(8,128)(2,1)S(1)} %constant_dynamic-update-slice_fusion.2), channel_id=1, source_target_pairs={{0,24},{8,16},{16,8},{24,0},{1,25},{9,17},{17,9},{25,1},{2,26},{10... | collective-permute-start | bytes 1769480 | tf_op jit(solution)/shard_map/ppermute | solution.py:140
  37.4 49.8 %collective-permute-start.4 = (bf16[32,9216]{1,0:T(8,128)(2,1)S(1)}, bf16[32,9216]{1,0:T(8,128)(2,1)S(1)}, u32[]{:S(2)}, u32[]{:S(2)}) collective-permute-start(bf16[32,9216]{1,0:T(8,128)(2,1)S(1)} %constant_dynamic-update-slice_fusion.2), channel_id=1, source_target_pairs={{0,16},{8,24},{16,0},{24,8},{1,17},{9,25},{17,1},{25,9},{2,18},{10... | collective-permute-start | bytes 1769480 | tf_op jit(solution)/shard_map/ppermute | solution.py:140
  41.7 45.4 %collective-permute-start.5 = (bf16[32,9216]{1,0:T(8,128)(2,1)S(1)}, bf16[32,9216]{1,0:T(8,128)(2,1)S(1)}, u32[]{:S(2)}, u32[]{:S(2)}) collective-permute-start(bf16[32,9216]{1,0:T(8,128)(2,1)S(1)} %constant_dynamic-update-slice_fusion.2), channel_id=1, source_target_pairs={{0,8},{8,0},{16,24},{24,16},{1,9},{9,1},{17,25},{25,17},{2,10},{10... | collective-permute-start | bytes 1769480 | tf_op jit(solution)/shard_map/ppermute | solution.py:140
  89.2 28.5 %all-to-all-start = ((bf16[8,480,128]{2,1,0:T(8,128)(2,1)}), bf16[8,480,128]{2,1,0:T(8,128)(2,1)S(1)}, u32[]{:S(2)}, u32[]{:S(2)}) async-start(bf16[8,480,128]{2,1,0:T(8,128)(2,1)} %pad_maximum_fusion.5), calls=%async_computation | async-start | bytes 1966080 | tf_op jit(solution)/shard_map/all_to_all | solution.py:588
  96.8 22.5 %collective-permute-start.6 = (bf16[128,1024]{1,0:T(8,128)(2,1)}, bf16[128,1024]{1,0:T(8,128)(2,1)S(1)}, u32[]{:S(2)}, u32[]{:S(2)}) collective-permute-start(bf16[128,1024]{1,0:T(8,128)(2,1)} %get-tuple-element.49), channel_id=1, source_target_pairs={{0,4},{4,0},{1,5},{5,1},{2,6},{6,2},{3,7},{7,3},{8,12},{12,8},{9,1... | collective-permute-start | bytes 786440 | tf_op jit(solution)/shard_map/ppermute | solution.py:140
  117.7 22.0 %collective-permute-start.10 = (bf16[7,8,32,128]{3,2,0,1:T(8,128)(2,1)S(1)}, bf16[7,8,32,128]{3,2,0,1:T(8,128)(2,1)S(1)}, u32[]{:S(2)}, u32[]{:S(2)}) collective-permute-start(bf16[7,8,32,128]{3,2,0,1:T(8,128)(2,1)S(1)} %bitcast.152), channel_id=1, source_target_pairs={{0,2},{2,0},{1,3},{3,1},{4,6},{6,4},{5,7},{7,5},{8,10},{10,8},{9,1... | collective-permute-start | bytes 1376264 | tf_op jit(solution)/shard_map/ppermute | solution.py:140
  120.1 36.4 %collective-permute-start.7 = (bf16[2,128,1024]{2,1,0:T(8,128)(2,1)}, bf16[2,128,1024]{2,1,0:T(8,128)(2,1)}, u32[]{:S(2)}, u32[]{:S(2)}) collective-permute-start(bf16[2,128,1024]{2,1,0:T(8,128)(2,1)} %pad_maximum_fusion.7), channel_id=1, source_target_pairs={{0,24},{8,16},{16,8},{24,0},{1,25},{9,17},{17,9},{25,1},{2,26},{10... | collective-permute-start | bytes 1572872 | tf_op jit(solution)/shard_map/ppermute | solution.py:140
  120.4 43.9 %collective-permute-start.8 = (bf16[2,128,1024]{2,1,0:T(8,128)(2,1)}, bf16[2,128,1024]{2,1,0:T(8,128)(2,1)}, u32[]{:S(2)}, u32[]{:S(2)}) collective-permute-start(bf16[2,128,1024]{2,1,0:T(8,128)(2,1)} %pad_maximum_fusion.7), channel_id=1, source_target_pairs={{0,16},{8,24},{16,0},{24,8},{1,17},{9,25},{17,1},{25,9},{2,18},{10... | collective-permute-start | bytes 1572872 | tf_op jit(solution)/shard_map/ppermute | solution.py:140
  124.6 39.7 %collective-permute-start.9 = (bf16[2,128,1024]{2,1,0:T(8,128)(2,1)}, bf16[2,128,1024]{2,1,0:T(8,128)(2,1)}, u32[]{:S(2)}, u32[]{:S(2)}) collective-permute-start(bf16[2,128,1024]{2,1,0:T(8,128)(2,1)} %pad_maximum_fusion.7), channel_id=1, source_target_pairs={{0,8},{8,0},{16,24},{24,16},{1,9},{9,1},{17,25},{25,17},{2,10},{10... | collective-permute-start | bytes 1572872 | tf_op jit(solution)/shard_map/ppermute | solution.py:140
  139.8 28.3 %collective-permute-start.11 = (bf16[7,8,2,32,128]{4,3,0,1,2:T(8,128)(2,1)S(1)}, bf16[7,8,2,32,128]{4,3,0,1,2:T(8,128)(2,1)}, u32[]{:S(2)}, u32[]{:S(2)}) collective-permute-start(bf16[7,8,2,32,128]{4,3,0,1,2:T(8,128)(2,1)S(1)} %pad_maximum_fusion.6), channel_id=1, source_target_pairs={{0,1},{1,0},{2,3},{3,2},{4,5},{5,4},{6,7},{7,6},{8,9},{9,8},{10,11... | collective-permute-start | bytes 2752520 | tf_op jit(solution)/shard_map/ppermute | solution.py:140
  190.8 18.2 %all-to-all-start.1 = ((bf16[8,2,128,128]{3,2,1,0:T(8,128)(2,1)}), bf16[8,2,128,128]{3,2,1,0:T(8,128)(2,1)S(1)}, u32[]{:S(2)}, u32[]{:S(2)}) async-start(bf16[8,2,128,128]{3,2,1,0:T(8,128)(2,1)} %get-tuple-element.52), calls=%async_computation.1 | async-start | bytes 1048576 | tf_op jit(solution)/shard_map/all_to_all | solution.py:613
  197.5 136.0 %reduce-scatter.7.cloned.1.call-start = ((), (), s32[]{:S(2)}) async-start(), calls=%async_computation.9 | async-start | bytes 3932160
  235.4 5.7 %collective-permute-start.12 = (bf16[1536,1024]{1,0:T(8,128)(2,1)S(1)}, bf16[1536,1024]{1,0:T(8,128)(2,1)S(1)}, u32[]{:S(2)}, u32[]{:S(2)}) collective-permute-start(bf16[1536,1024]{1,0:T(8,128)(2,1)S(1)} %convolution_convert_fusion.1), channel_id=1, source_target_pairs={{0,1},{1,0},{2,3},{3,2},{4,5},{5,4},{6,7},{7,6},{8,9},{9,8},{10,11... | collective-permute-start | bytes 9437192 | tf_op jit(solution)/shard_map/ppermute | solution.py:140
  236.2 29.2 %copy-start.18 = (bf16[1024,256]{1,0:T(8,128)(2,1)}, bf16[1024,256]{1,0:T(8,128)(2,1)S(1)}, u32[]{:S(2)}) copy-start(bf16[1024,256]{1,0:T(8,128)(2,1)S(1)} %fusion.24) | copy-start | bytes 1572868
  271.8 15.0 %collective-permute-start.13 = (bf16[512,6144]{1,0:T(8,128)(2,1)}, bf16[512,6144]{1,0:T(8,128)(2,1)}, u32[]{:S(2)}, u32[]{:S(2)}) collective-permute-start(bf16[512,6144]{1,0:T(8,128)(2,1)} %convolution_convert_fusion), channel_id=1, source_target_pairs={{0,1},{1,0},{2,3},{3,2},{4,5},{5,4},{6,7},{7,6},{8,9},{9,8},{10,11... | collective-permute-start | bytes 18874376 | tf_op jit(solution)/shard_map/ppermute | solution.py:140
  275.3 11.5 %copy-start = (bf16[256,6144]{1,0:T(8,128)(2,1)S(1)}, bf16[256,6144]{1,0:T(8,128)(2,1)}, u32[]{:S(2)}) copy-start(bf16[256,6144]{1,0:T(8,128)(2,1)} %get-tuple-element.67) | copy-start | bytes 9437188
  275.3 8.5 %collective-permute-start.14 = (bf16[512,1024]{1,0:T(8,128)(2,1)}, bf16[512,1024]{1,0:T(8,128)(2,1)}, u32[]{:S(2)}, u32[]{:S(2)}) collective-permute-start(bf16[512,1024]{1,0:T(8,128)(2,1)} %convolution_convert_fusion.2), channel_id=1, source_target_pairs={{0,1},{1,0},{2,3},{3,2},{4,5},{5,4},{6,7},{7,6},{8,9},{9,8},{10,11... | collective-permute-start | bytes 3145736 | tf_op jit(solution)/shard_map/ppermute | solution.py:140
  275.4 19.6 %all-to-all-start.2 = ((bf16[8,2,128,128]{3,2,1,0:T(8,128)(2,1)}), bf16[8,2,128,128]{3,2,1,0:T(8,128)(2,1)}, u32[]{:S(2)}, u32[]{:S(2)}) async-start(bf16[8,2,128,128]{3,2,1,0:T(8,128)(2,1)} %bitcast.165), calls=%async_computation.2 | async-start | bytes 1048576 | tf_op jit(solution)/shard_map/all_to_all | solution.py:613
  281.0 134.0 %reduce-scatter.9.cloned.1.call-start = ((), (), s32[]{:S(2)}) async-start(), calls=%async_computation.10 | async-start | bytes 7864320
  309.4 65.3 %all-to-all-start.3 = ((bf16[8,3,2,128,128]{4,3,2,1,0:T(8,128)(2,1)}), bf16[8,3,2,128,128]{4,3,2,1,0:T(8,128)(2,1)S(1)}, u32[]{:S(2)}, u32[]{:S(2)}) async-start(bf16[8,3,2,128,128]{4,3,2,1,0:T(8,128)(2,1)} %attend_backward.1.grads_ref), calls=%async_computation.3 | async-start | bytes 3145728 | tf_op jit(solution)/shard_map/all_to_all | solution.py:613
  325.0 2.5 collective-permute-start.15
  328.6 12.9 %collective-permute-start.16 = (bf16[256,896]{1,0:T(8,128)(2,1)}, bf16[256,896]{1,0:T(8,128)(2,1)}, u32[]{:S(2)}, u32[]{:S(2)}) collective-permute-start(bf16[256,896]{1,0:T(8,128)(2,1)} %slice.246), channel_id=1, source_target_pairs={{0,2},{2,0},{1,3},{3,1},{4,6},{6,4},{5,7},{7,5},{8,10},{10,8},{9,1... | collective-permute-start | bytes 1376264 | tf_op jit(solution)/shard_map/ppermute | solution.py:140
  330.0 18.2 %collective-permute-start.18 = (bf16[128,1024]{1,0:T(8,128)(2,1)}, bf16[128,1024]{1,0:T(8,128)(2,1)}, u32[]{:S(2)}, u32[]{:S(2)}) collective-permute-start(bf16[128,1024]{1,0:T(8,128)(2,1)} %get-tuple-element.100), channel_id=1, source_target_pairs={{0,8},{8,0},{16,24},{24,16},{1,9},{9,1},{17,25},{25,17},{2,10},{10... | collective-permute-start | bytes 786440 | tf_op jit(solution)/shard_map/ppermute | solution.py:140
  330.1 35.9 %collective-permute-start.19 = (bf16[128,1024]{1,0:T(8,128)(2,1)}, bf16[128,1024]{1,0:T(8,128)(2,1)}, u32[]{:S(2)}, u32[]{:S(2)}) collective-permute-start(bf16[128,1024]{1,0:T(8,128)(2,1)} %get-tuple-element.102), channel_id=1, source_target_pairs={{0,16},{8,24},{16,0},{24,8},{1,17},{9,25},{17,1},{25,9},{2,18},{10... | collective-permute-start | bytes 786440 | tf_op jit(solution)/shard_map/ppermute | solution.py:140
  332.9 39.7 %collective-permute-start.20 = (bf16[128,1024]{1,0:T(8,128)(2,1)}, bf16[128,1024]{1,0:T(8,128)(2,1)}, u32[]{:S(2)}, u32[]{:S(2)}) collective-permute-start(bf16[128,1024]{1,0:T(8,128)(2,1)} %get-tuple-element.101), channel_id=1, source_target_pairs={{0,24},{8,16},{16,8},{24,0},{1,25},{9,17},{17,9},{25,1},{2,26},{10... | collective-permute-start | bytes 786440 | tf_op jit(solution)/shard_map/ppermute | solution.py:140
  342.6 31.4 %collective-permute-start.17 = (bf16[128,896]{1,0:T(8,128)(2,1)S(1)}, bf16[128,896]{1,0:T(8,128)(2,1)S(1)}, u32[]{:S(2)}, u32[]{:S(2)}) collective-permute-start(bf16[128,896]{1,0:T(8,128)(2,1)S(1)} %slice.248), channel_id=1, source_target_pairs={{0,4},{4,0},{1,5},{5,1},{2,6},{6,2},{3,7},{7,3},{8,12},{12,8},{9,1... | collective-permute-start | bytes 688136 | tf_op jit(solution)/shard_map/ppermute | solution.py:140
  374.7 19.1 %copy-start.2 = (bf16[8,3,2,128,128]{4,3,2,1,0:T(8,128)(2,1)}, bf16[8,3,2,128,128]{4,3,2,1,0:T(8,128)(2,1)S(1)}, u32[]{:S(2)}) copy-start(bf16[8,3,2,128,128]{4,3,2,1,0:T(8,128)(2,1)S(1)} %all-to-all-done.3) | copy-start | bytes 4718596
  374.8 8.6 %collective-permute-start.21 = (bf16[64,1024]{1,0:T(8,128)(2,1)S(1)}, bf16[64,1024]{1,0:T(8,128)(2,1)S(1)}, u32[]{:S(2)}, u32[]{:S(2)}) collective-permute-start(bf16[64,1024]{1,0:T(8,128)(2,1)S(1)} %slice.213), channel_id=1, source_target_pairs={{0,4},{4,0},{1,5},{5,1},{2,6},{6,2},{3,7},{7,3},{8,12},{12,8},{9,1... | collective-permute-start | bytes 393224 | tf_op jit(solution)/shard_map/ppermute | solution.py:140
  383.4 18.1 %collective-permute-start.22 = (bf16[32,1024]{1,0:T(8,128)(2,1)S(1)}, bf16[32,1024]{1,0:T(8,128)(2,1)S(1)}, u32[]{:S(2)}, u32[]{:S(2)}) collective-permute-start(bf16[32,1024]{1,0:T(8,128)(2,1)S(1)} %slice.255), channel_id=1, source_target_pairs={{0,2},{2,0},{1,3},{3,1},{4,6},{6,4},{5,7},{7,5},{8,10},{10,8},{9,1... | collective-permute-start | bytes 196616 | tf_op jit(solution)/shard_map/ppermute | solution.py:140
  385.2 17.0 %collective-permute-start.26 = (bf16[96,1024]{1,0:T(8,128)(2,1)S(1)}, bf16[96,1024]{1,0:T(8,128)(2,1)S(1)}, u32[]{:S(2)}, u32[]{:S(2)}) collective-permute-start(bf16[96,1024]{1,0:T(8,128)(2,1)S(1)} %get-tuple-element.112), channel_id=1, source_target_pairs={{0,8},{8,0},{16,24},{24,16},{1,9},{9,1},{17,25},{25,17},{2,10},{10... | collective-permute-start | bytes 589832 | tf_op jit(solution)/shard_map/ppermute | solution.py:140
  385.2 18.0 %collective-permute-start.27 = (bf16[96,1024]{1,0:T(8,128)(2,1)S(1)}, bf16[96,1024]{1,0:T(8,128)(2,1)S(1)}, u32[]{:S(2)}, u32[]{:S(2)}) collective-permute-start(bf16[96,1024]{1,0:T(8,128)(2,1)S(1)} %get-tuple-element.111), channel_id=1, source_target_pairs={{0,16},{8,24},{16,0},{24,8},{1,17},{9,25},{17,1},{25,9},{2,18},{10... | collective-permute-start | bytes 589832 | tf_op jit(solution)/shard_map/ppermute | solution.py:140
  388.5 19.4 %collective-permute-start.28 = (bf16[96,1024]{1,0:T(8,128)(2,1)S(1)}, bf16[96,1024]{1,0:T(8,128)(2,1)S(1)}, u32[]{:S(2)}, u32[]{:S(2)}) collective-permute-start(bf16[96,1024]{1,0:T(8,128)(2,1)S(1)} %get-tuple-element.110), channel_id=1, source_target_pairs={{0,24},{8,16},{16,8},{24,0},{1,25},{9,17},{17,9},{25,1},{2,26},{10... | collective-permute-start | bytes 589832 | tf_op jit(solution)/shard_map/ppermute | solution.py:140
  388.7 20.3 %all-to-all-start.4 = ((bf16[4,32,896]{2,1,0:T(8,128)(2,1)}), bf16[4,32,896]{2,1,0:T(8,128)(2,1)S(1)}, u32[]{:S(2)}, u32[]{:S(2)}) async-start(bf16[4,32,896]{2,1,0:T(8,128)(2,1)} %bitcast.60), calls=%async_computation.4 | async-start | bytes 458752 | tf_op jit(solution)/shard_map/all_to_all | solution.py:674
  409.6 12.4 %copy-start.17 = (bf16[32,1024]{1,0:T(8,128)(2,1)S(1)}, bf16[32,1024]{1,0:T(8,128)(2,1)}, u32[]{:S(2)}) copy-start(bf16[32,1024]{1,0:T(8,128)(2,1)} %param.20) | copy-start | bytes 196612
  409.7 36.7 %copy-start.20 = (f32[32,1024]{1,0:T(8,128)}, f32[32,1024]{1,0:T(8,128)S(1)}, u32[]{:S(2)}) copy-start(f32[32,1024]{1,0:T(8,128)S(1)} %squeeze.26) | copy-start | bytes 393220
  409.9 36.5 %copy-start.21 = (f32[32,1024]{1,0:T(8,128)}, f32[32,1024]{1,0:T(8,128)S(1)}, u32[]{:S(2)}) copy-start(f32[32,1024]{1,0:T(8,128)S(1)} %squeeze.25) | copy-start | bytes 393220
  417.1 16.9 %collective-permute-start.23 = (bf16[32,6144]{1,0:T(8,128)(2,1)}, bf16[32,6144]{1,0:T(8,128)(2,1)S(1)}, u32[]{:S(2)}, u32[]{:S(2)}) collective-permute-start(bf16[32,6144]{1,0:T(8,128)(2,1)} %get-tuple-element.95), channel_id=1, source_target_pairs={{0,8},{8,0},{16,24},{24,16},{1,9},{9,1},{17,25},{25,17},{2,10},{10... | collective-permute-start | bytes 1179656 | tf_op jit(solution)/shard_map/ppermute | solution.py:140
  417.6 28.8 %collective-permute-start.24 = (bf16[32,6144]{1,0:T(8,128)(2,1)S(1)}, bf16[32,6144]{1,0:T(8,128)(2,1)S(1)}, u32[]{:S(2)}, u32[]{:S(2)}) collective-permute-start(bf16[32,6144]{1,0:T(8,128)(2,1)S(1)} %get-tuple-element.97), channel_id=1, source_target_pairs={{0,16},{8,24},{16,0},{24,8},{1,17},{9,25},{17,1},{25,9},{2,18},{10... | collective-permute-start | bytes 1179656 | tf_op jit(solution)/shard_map/ppermute | solution.py:140
  420.0 34.4 %collective-permute-start.25 = (bf16[32,6144]{1,0:T(8,128)(2,1)S(1)}, bf16[32,6144]{1,0:T(8,128)(2,1)S(1)}, u32[]{:S(2)}, u32[]{:S(2)}) collective-permute-start(bf16[32,6144]{1,0:T(8,128)(2,1)S(1)} %get-tuple-element.96), channel_id=1, source_target_pairs={{0,24},{8,16},{16,8},{24,0},{1,25},{9,17},{17,9},{25,1},{2,26},{10... | collective-permute-start | bytes 1179656 | tf_op jit(solution)/shard_map/ppermute | solution.py:140
  421.3 33.1 %copy-start.22 = (f32[32,1024]{1,0:T(8,128)}, f32[32,1024]{1,0:T(8,128)S(1)}, u32[]{:S(2)}) copy-start(f32[32,1024]{1,0:T(8,128)S(1)} %squeeze.24) | copy-start | bytes 393220
  (22 other events, 92.4 us)
Sparse Core Ops, SparseCore 0:
  36.9 56.4 all-gather.4
  95.3 112.3 all-gather.6
  272.1 58.3 reduce-scatter.6
  333.3 81.6 reduce-scatter.8

commit v4 on v3

--- a/solution.py
+++ b/solution.py
@@ -10,6 +10,7 @@
 
 HEAD_DIM = 64
 BLOCK = 256
+MLP_STEP = 512
 PAIR = 2 * HEAD_DIM
 
 EPSILON = 1e-06
@@ -66,13 +67,14 @@
             query = qkv_ref[lo:hi, 0, 0, :, lanes].reshape(BLOCK, HEAD_DIM)
             keys = qkv_ref[0:hi, 1, 0, :, lanes].reshape(hi * rows, HEAD_DIM)
             values = qkv_ref[0:hi, 2, 0, :, lanes].reshape(hi * rows, HEAD_DIM)
-            scores = dot_t(keys, query) * SCALE
+            scores = dot_t(keys, query * SCALE)
             top = jnp.max(scores, axis=0, keepdims=True)
-            total = top + jnp.log(jnp.sum(jnp.exp(scores - top), axis=0, keepdims=True))
-            probs = jnp.exp(scores - total).astype(BF16)
+            weights = jnp.exp(scores - top)
+            total = jnp.sum(weights, axis=0, keepdims=True)
+            probs = (weights * (1.0 / total)).astype(BF16)
             mixed = t_dot(values, probs)
             out_ref[lo:hi, 0, :, lanes] = mixed.T.astype(BF16).reshape(per_block, rows, HEAD_DIM)
-            total_ref[0, head, block : block + 1, :] = total
+            total_ref[0, head, block : block + 1, :] = top + jnp.log(total)
 
 
 def attend_backward_kernel(qkv_ref, grad_ref, total_ref, cos_ref, sin_ref, out_ref, dk_acc, dv_acc):
@@ -91,7 +93,7 @@
             grad = grad_ref[lo:hi, 0, :, lanes].reshape(BLOCK, HEAD_DIM)
             keys = qkv_ref[0:hi, 1, 0, :, lanes].reshape(keys_n, HEAD_DIM)
             values = qkv_ref[0:hi, 2, 0, :, lanes].reshape(keys_n, HEAD_DIM)
-            scores = dot_t(keys, query) * SCALE
+            scores = dot_t(keys, query * SCALE)
             probs = jnp.exp(scores - total_ref[0, head, block : block + 1, :])
             grad_probs = dot_t(values, grad)
             inner = jnp.sum(probs * grad_probs, axis=0, keepdims=True)
@@ -132,6 +134,7 @@
         scratch_shapes=[pltpu.VMEM((length, PAIR), F32), pltpu.VMEM((length, PAIR), F32)],
         compiler_params=pltpu.CompilerParams(vmem_limit_bytes=VMEM_LIMIT),
         name="attend_backward",
+        cost_estimate=cost(5 * units * length * length * PAIR, 8 * grad_att.size * 8, units * length * length),
     )(qkv, grad_att, totals, cos, sin)
 
 
@@ -184,6 +187,10 @@
     return lax.optimization_barrier(values)
 
 
+def cost(flops, moved, exps=0):
+    return pl.CostEstimate(flops=int(flops), bytes_accessed=int(moved), transcendentals=int(exps))
+
+
 def params():
     return pltpu.CompilerParams(vmem_limit_bytes=VMEM_LIMIT)
 
@@ -247,6 +254,7 @@
         ],
         compiler_params=params(),
         name="front",
+        cost_estimate=cost(6 * units * length * PAIR * width + 2 * units * length * length * PAIR, 6 * x.size, 2 * units * length * length),
     )(x, first, gain, cos, sin, weights)
 
 
@@ -292,7 +300,7 @@
     gate_ref[...] = gate
     up_ref[...] = up
     act_ref[...] = act
-    result_ref[...] += dot(act, sections(wd_ref)[0])
+    result_ref[...] += dot_sections(act, wd_ref)
 
     @pl.when(step == pl.num_programs(0) - 1)
     def _():
@@ -310,14 +318,14 @@
 
 def weight_specs(width, parts, gate_out, rest):
     outer, sides, rows, _ = rest.shape
-    wide = outer * rows
+    wide = MLP_STEP
     per = width // wide
     whole = (outer, sides, rows)
     return wide, [
         pl.BlockSpec(whole + (width,), lambda j: (0, 0, 0, parts)),
         pl.BlockSpec(whole + (wide,), lambda j: (0, 0, 0, j)),
         pl.BlockSpec(whole + (wide,), lambda j: (0, 0, 0, 3 * per + j)),
-        pl.BlockSpec((outer, 1, rows, width), lambda j: (0, j % per, 0, 3 + parts + j // per)),
+        pl.BlockSpec((outer, sides // per, rows, width), lambda j: (0, j % per, 0, 3 + parts + j // per)),
     ], (gate_out, gate_out, rest, rest)
 
 
@@ -352,6 +360,7 @@
         ],
         compiler_params=params(),
         name="mlp_forward",
+        cost_estimate=cost(2 * tokens * width * width * (3 * parts + 1), 2 * width * width * (3 * parts + 1) + 10 * tokens * width * parts, tokens * width * parts),
     )(x, heads, gain, teacher, cotangent, valid, rate, *weights)
 
 
@@ -364,7 +373,7 @@
     gate = gate_ref[...]
     up = up_ref[...]
     sigmoid = jax.nn.sigmoid(gate)
-    grad_act = dot_t(grad_low_ref[...], sections(wd_ref)[0])
+    grad_act = dot_t_sections(grad_low_ref[...], wd_ref)
     grad_gate = (grad_act * up * (sigmoid * (1.0 + gate * (1.0 - sigmoid)))).astype(BF16)
     grad_up = (grad_act * (gate * sigmoid)).astype(BF16)
     grads_ref[:, :wide] = grad_gate
@@ -418,6 +427,7 @@
         scratch_shapes=[pltpu.VMEM((tokens, width), F32)],
         compiler_params=params(),
         name="mlp_backward",
+        cost_estimate=cost(2 * tokens * width * width * (3 * parts + 1), 2 * width * width * (3 * parts + 1) + 12 * tokens * width * parts, tokens * width * parts),
     )(grad, grad_low, hidden, gain, gate, up, *weights)
 
 
@@ -451,6 +461,7 @@
         scratch_shapes=[pltpu.VMEM((columns, width), BF16)],
         compiler_params=params(),
         name="head_grads",
+        cost_estimate=cost(2 * normed.size * columns + 2 * width * width * columns, 2 * normed.size + 2 * width * width + 4 * width * columns),
     )(normed, grads, loss_row, pick)
 
 
@@ -496,7 +507,55 @@
         scratch_shapes=[pltpu.VMEM((tokens, 3 * width), BF16)],
         compiler_params=params(),
         name="last",
+        cost_estimate=cost(6 * tokens * width * width, 6 * width * width + 20 * tokens * width),
     )(heads, x, gain, weights, grad_hidden)
+
+
+def finish_kernel(*refs, own_down):
+    pieces, (gate_w_ref, up_w_ref), (gate_ref, up_ref, gain_ref) = refs[:-5], refs[-5:-3], refs[-3:]
+    rows, columns = pieces[0].shape
+    total = pieces[0][...].astype(F32)
+    for piece in pieces[1:]:
+        total = total + piece[...].astype(F32)
+    parts = -(-own_down // rows)
+    width = columns // (2 * parts)
+    gain = jnp.zeros((rows, 1), F32)
+    for side, (weight_ref, out_ref) in enumerate(((gate_w_ref, gate_ref), (up_w_ref, up_ref))):
+        values = []
+        for device in range(width // rows):
+            for part in range(parts):
+                step, lane = divmod(part * width + device * rows, MLP_STEP)
+                at = (2 * step + side) * MLP_STEP + lane
+                values.append(total[:, at : at + min(rows, own_down - part * rows)])
+        value = jnp.concatenate(values, axis=1)
+        out_ref[...] = value
+        gain = gain + jnp.sum(value * weight_ref[...].astype(F32), axis=1, keepdims=True)
+    gain_ref[...] = jnp.broadcast_to(gain, gain_ref.shape)
+
+
+def finish(pieces, w_gate, w_up, own_down):
+    rows, hidden = w_gate.shape
+    if rows % 8 == 0:
+        gate, up, gain = pl.pallas_call(
+            functools.partial(finish_kernel, own_down=own_down),
+            out_shape=[
+                jax.ShapeDtypeStruct((rows, hidden), F32),
+                jax.ShapeDtypeStruct((rows, hidden), F32),
+                jax.ShapeDtypeStruct((rows, PAIR), F32),
+            ],
+            compiler_params=params(),
+            name="finish",
+        )(*pieces, w_gate, w_up)
+        return gate, up, gain[:, 0]
+    total = sum(piece.astype(F32) for piece in pieces).reshape(rows, -1, 2, MLP_STEP)
+    parts = -(-own_down // rows)
+
+    def unpack(grad):
+        grad = grad.reshape(rows, parts, -1, rows).transpose(0, 2, 1, 3)
+        return grad.reshape(rows, -1, parts * rows)[:, :, :own_down].reshape(rows, hidden)
+
+    gate, up = unpack(total[:, :, 0]), unpack(total[:, :, 1])
+    return gate, up, jnp.sum(gate * w_gate.astype(F32) + up * w_up.astype(F32), axis=1)
 
 
 STAGES_NATIVE = ("c", "y", "x", "z")
@@ -564,10 +623,6 @@
         weight = weight.reshape(own_rows, -1, hidden_parts, own_rows)
         return weight.transpose(0, 2, 1, 3).reshape(own_rows, hidden_parts * width)
 
-    def unpack_columns(grad):
-        grad = grad.reshape(own_rows, hidden_parts, -1, own_rows).transpose(0, 2, 1, 3)
-        return grad.reshape(own_rows, -1, hidden_parts * own_rows)[:, :, :own_down].reshape(own_rows, -1)
-
     down_rows = jnp.pad(w_down, ((0, padded), (0, 0))).reshape(hidden_parts, own_rows, width)
     down_rows = down_rows.transpose(1, 0, 2).reshape(own_rows, hidden_parts * width)
     def along_z(rows):
@@ -656,7 +711,7 @@
     out_sent = swap(dot(turned_att[half:], grad_branch).astype(BF16), "c", 1)
     out_sum = (dot(turned_att[:half], grad_branch) + out_sent.astype(F32)).astype(BF16)
 
-    grad_heads, mlp_sum, out_sum = together(grad_heads, mlp_sum, out_sum)
+    grad_heads, mlp_sum, out_sum, down_sum = together(grad_heads, mlp_sum, out_sum, down_sum)
     mlp_sum = over_yx(mlp_sum)
     out_sum = add_stage(out_sum, "z").astype(BF16)
 
@@ -669,7 +724,8 @@
     value, grad_own, down_sum, out_sum = together(value.astype(BF16), grad_own, down_sum, out_sum)
     owned_down = add_stage(down_sum, "z")[:own_down]
     owned_output = add_stage(add_stage(out_sum, "y"), "x")
-    mlp_sum = add_stage(mlp_sum, "z")
+    mlp_sum = mlp_sum.reshape(zs, own_rows, -1)
+    mlp_sum = [mlp_sum[0]] + [swap(mlp_sum[k], "z", k) for k in range(1, zs)]
     value = value.reshape(zs, own_rows, value.shape[1])
     value = lax.all_to_all(value, "z", split_axis=0, concat_axis=0, tiled=True)
     columns = 3 * units * PAIR
@@ -684,12 +740,8 @@
         + jnp.sum(w_key.astype(F32) * owned_qkv[1], axis=1)
         + jnp.sum(w_value.astype(F32) * owned_qkv[2], axis=1)
     ) / attn_gain.astype(F32)
-    mlp_sum = mlp_sum.reshape(own_rows, -1, 2, BLOCK)
-    owned_gate = unpack_columns(mlp_sum[:, :, 0])
-    owned_up = unpack_columns(mlp_sum[:, :, 1])
-    gain_grad_m = (
-        jnp.sum(w_gate.astype(F32) * owned_gate, axis=1) + jnp.sum(w_up.astype(F32) * owned_up, axis=1)
-    ) / mlp_gain.astype(F32)
+    owned_gate, owned_up, gain_grad_m = finish(mlp_sum, w_gate, w_up, own_down)
+    gain_grad_m = gain_grad_m / mlp_gain.astype(F32)
     return (
         result.reshape(batch, local_len, width),
         loss_value,

time: 486 us -> 463 us (0.953)
  local copies, waits for them, and re-layouts: 36.8 us -> 20.9 us
  Pallas kernels: 88.9 us -> 83.7 us
    ppermute x29, waiting for transfers between devices: 181 us -> 174 us  [swap(): return lax.ppermute(array, name, [(i, i ^ distance) for i in range(size)])]
    unnamed x6, waiting for transfers between devices: 4.87 us -> 10.7 us
    transpose x2 -> x0, local copies, waits for them, and re-layouts: 5.37 us -> none  [unpack_columns(): grad.reshape(own_rows, hidden_parts, -1, own_rows).transpose(0, 2, 1, 3)]
  transfers between devices with their start and end apart: 38 -> 38, of which waited for: 25 -> 20; matrix products, arithmetic and copies ran while one was open for 11% -> 12% of each run, Pallas kernels for 10% -> 14%
where the time goes in v4:
time: 463 us; the launch traced here: 456 us
  waiting for transfers between devices  213 us (46%)
  Pallas kernels  83.7 us (18%)
  starting transfers between devices  64 us (14%)
  other arithmetic  27.2 us (6%)
  matrix products  26.9 us (6%)
  local copies, waits for them, and re-layouts  20.9 us (5%)
  between operations  20 us (4%)
    ppermute x29, waiting for transfers between devices, swap(): return lax.ppermute(array, name, [(i, i ^ distance) for i in range(size)])  174 us
    ppermute x29, starting transfers between devices, swap(): return lax.ppermute(array, name, [(i, i ^ distance) for i in range(size)])  34.3 us
    dot_general x6, matrix products, dot(): return jnp.dot(left, right, preferred_element_type=F32)  21.9 us
    all_to_all x1, waiting for transfers between devices, on_device(): lax.all_to_all(parcel, SEQ, split_axis=0, concat_axis=0, tiled=True)  19.3 us
    all_to_all x3, starting transfers between devices, exchange(): return lax.all_to_all(array, SEQ, split_axis=0, concat_axis=0, tiled=True)  17.8 us
    pallas_call x1, Pallas kernels, mlp_forward(): pl.pallas_call(forward_kernel, grid=(parts * width // wide,), in_specs=[w...  17.6 us
    pallas_call x1, Pallas kernels, mlp_backward(): pl.pallas_call(backward_kernel, grid=(parts * width // wide,), in_specs=[...  17.4 us
    pallas_call x1, Pallas kernels, front(): pl.pallas_call(front_kernel, grid=(units,), in_specs=[pl.BlockSpec((parts...  17.1 us
  transfers between devices with their start and end apart: 38, of which 20 were waited for; matrix products, arithmetic and copies ran while one was open for 12% of the time, Pallas kernels for 14%

profile of v4, /device:TPU:8, one launch (start us, length us, event | category | flops | bytes accessed | tf_op | source)
XLA Modules:
  0.0 456.0 jit_solution(11051008356267357706)
XLA Ops:
  23.7 7.1 %collective-permute-done = bf16[32,4096]{1,0:T(8,128)(2,1)} collective-permute-done((bf16[32,4096]{1,0:T(8,128)(2,1)S(1)}, bf16[32,4096]{1,0:T(8,128)(2,1)}, u32[]{:S(2)}, u32[]{:S(2)}) %collective-permute-start) | collective-permute-done | bytes 262176 | tf_op jit(solution)/shard_map/ppermute | solution.py:143
  30.8 3.6 collective-permute-done.1
  37.4 4.4 collective-permute-start.4
  42.6 35.9 %collective-permute-done.3 = bf16[32,9216]{1,0:T(8,128)(2,1)S(1)} collective-permute-done((bf16[32,9216]{1,0:T(8,128)(2,1)S(1)}, bf16[32,9216]{1,0:T(8,128)(2,1)S(1)}, u32[]{:S(2)}, u32[]{:S(2)}) %collective-permute-start.3) | collective-permute-done | bytes 589856 | tf_op jit(solution)/shard_map/ppermute | solution.py:143
  78.5 8.7 %collective-permute-done.4 = bf16[32,9216]{1,0:T(8,128)(2,1)S(1)} collective-permute-done((bf16[32,9216]{1,0:T(8,128)(2,1)S(1)}, bf16[32,9216]{1,0:T(8,128)(2,1)S(1)}, u32[]{:S(2)}, u32[]{:S(2)}) %collective-permute-start.4) | collective-permute-done | bytes 589856 | tf_op jit(solution)/shard_map/ppermute | solution.py:143
  90.2 7.4 %all-to-all-start = ((bf16[8,480,128]{2,1,0:T(8,128)(2,1)}), bf16[8,480,128]{2,1,0:T(8,128)(2,1)S(1)}, u32[]{:S(2)}, u32[]{:S(2)}) async-start(bf16[8,480,128]{2,1,0:T(8,128)(2,1)} %pad_maximum_fusion.5), calls=%async_computation | async-start | bytes 1966080 | tf_op jit(solution)/shard_map/all_to_all | solution.py:643
  99.1 19.3 %all-to-all-done = bf16[8,480,128]{2,1,0:T(8,128)(2,1)S(1)} async-done(((bf16[8,480,128]{2,1,0:T(8,128)(2,1)}), bf16[8,480,128]{2,1,0:T(8,128)(2,1)S(1)}, u32[]{:S(2)}, u32[]{:S(2)}) %all-to-all-start) | async-done | bytes 983072 | tf_op jit(solution)/shard_map/all_to_all | solution.py:643
  121.1 4.2 collective-permute-start.8
  125.3 15.1 %collective-permute-done.10 = bf16[7,8,32,128]{3,2,0,1:T(8,128)(2,1)S(1)} collective-permute-done((bf16[7,8,32,128]{3,2,0,1:T(8,128)(2,1)S(1)}, bf16[7,8,32,128]{3,2,0,1:T(8,128)(2,1)S(1)}, u32[]{:S(2)}, u32[]{:S(2)}) %collective-permute-start.10) | collective-permute-done | bytes 458784 | tf_op jit(solution)/shard_map/ppermute | solution.py:143
  140.7 3.1 fusion.25
  143.8 13.5 %collective-permute-done.7 = bf16[2,128,1024]{2,1,0:T(8,128)(2,1)} collective-permute-done((bf16[2,128,1024]{2,1,0:T(8,128)(2,1)}, bf16[2,128,1024]{2,1,0:T(8,128)(2,1)}, u32[]{:S(2)}, u32[]{:S(2)}) %collective-permute-start.7) | collective-permute-done | bytes 524320 | tf_op jit(solution)/shard_map/ppermute | solution.py:143
  157.3 7.6 %collective-permute-done.8 = bf16[2,128,1024]{2,1,0:T(8,128)(2,1)} collective-permute-done((bf16[2,128,1024]{2,1,0:T(8,128)(2,1)}, bf16[2,128,1024]{2,1,0:T(8,128)(2,1)}, u32[]{:S(2)}, u32[]{:S(2)}) %collective-permute-start.8) | collective-permute-done | bytes 524320 | tf_op jit(solution)/shard_map/ppermute | solution.py:143
  170.3 1.8 copy.82
  173.6 17.1 %front.1 = (bf16[8,128,1024]{2,1,0:T(8,128)(2,1)}, bf16[8,3,2,128,128]{4,3,2,1,0:T(8,128)(2,1)}, bf16[8,2,128,128]{3,2,1,0:T(8,128)(2,1)}, f32[2,2,4,256]{3,2,1,0:T(4,128)}) custom-call(bf16[8,128,1024]{2,1,0:T(8,128)(2,1)} %bitcast.136, bf16[8,2,128,128]{3,2,1,0:T(8,128)(2,1)} %bitcast.154, f32[1,1024]{1,0:T(1,128)} %get-tuple-element.125.gain_ref, ...), custom_call_target="tpu_custom_call" | custom-call | flops 2147483648 | bytes 6291456 | tf_op jit(solution)/shard_map/front/pallas_call | solution.py:232
  190.7 6.9 %all-to-all-start.1 = ((bf16[8,2,128,128]{3,2,1,0:T(8,128)(2,1)}), bf16[8,2,128,128]{3,2,1,0:T(8,128)(2,1)S(1)}, u32[]{:S(2)}, u32[]{:S(2)}) async-start(bf16[8,2,128,128]{3,2,1,0:T(8,128)(2,1)} %get-tuple-element.56), calls=%async_computation.1 | async-start | bytes 1048576 | tf_op jit(solution)/shard_map/all_to_all | solution.py:668
  199.1 9.7 %all-to-all-done.1 = bf16[8,2,128,128]{3,2,1,0:T(8,128)(2,1)S(1)} async-done(((bf16[8,2,128,128]{3,2,1,0:T(8,128)(2,1)}), bf16[8,2,128,128]{3,2,1,0:T(8,128)(2,1)S(1)}, u32[]{:S(2)}, u32[]{:S(2)}) %all-to-all-start.1) | async-done | bytes 524320 | tf_op jit(solution)/shard_map/all_to_all | solution.py:668
  209.7 17.6 %mlp_forward.1 = (bf16[256,1024]{1,0:T(8,128)(2,1)}, f32[256,1024]{1,0:T(8,128)}, bf16[256,1024]{1,0:T(8,128)(2,1)}, f32[256,3072]{1,0:T(8,128)}, f32[256,3072]{...) custom-call(bf16[256,1024]{1,0:T(8,128)(2,1)} %bitcast.130, ...), custom_call_target="tpu_custom_call" | custom-call | flops 5368709120 | bytes 28835840 | tf_op jit(solution)/shard_map/mlp_forward/pallas_call | solution.py:343
  227.3 1.9 fusion.21
  233.8 4.9 %collective-permute-done.12 = bf16[1536,1024]{1,0:T(8,128)(2,1)S(1)} collective-permute-done((bf16[1536,1024]{1,0:T(8,128)(2,1)S(1)}, bf16[1536,1024]{1,0:T(8,128)(2,1)S(1)}, u32[]{:S(2)}, u32[]{:S(2)}) %collective-permute-start.12) | collective-permute-done | bytes 3145760 | tf_op jit(solution)/shard_map/ppermute | solution.py:143
  238.7 2.7 add_convert_fusion.1
  241.3 17.4 %mlp_backward.1 = (bf16[256,6144]{1,0:T(8,128)(2,1)}, f32[256,1024]{1,0:T(8,128)}, bf16[256,1024]{1,0:T(8,128)(2,1)}, bf16[4,2,2,128,128]{4,3,2,1,0:T(8,128)(2,1)}) custom-call(f32[256,1024]{1,0:T(8,128)} %get-tuple-element.62.grad_ref, bf16[256,1024]{1,0:T(8,128)(2,1)} %get-tuple-element.65.grad_low_ref, f32[256,1024]{1,0:T(8,128)} %get-tuple-element.66.hidden_ref, ...), custom_call_target="tpu_custom_call" | custom-call | flops 5368709120 | bytes 30408704 | tf_op jit(solution)/shard_map/mlp_backward/pallas_call | solution.py:416
  258.7 6.6 %convolution_convert_fusion = bf16[512,6144]{1,0:T(8,128)(2,1)} fusion(bf16[256,6144]{1,0:T(8,128)(2,1)} %get-tuple-element.71, bf16[1024,256]{1,0:T(8,128)(2,1)S(1)} %fusion.24), kind=kOutput, calls=%fused_computation.1 | convolution fusion | flops 1613758464 | bytes 9699328 | tf_op jit(solution)/shard_map/dot_general | solution.py:56
  268.4 5.6 %all-to-all-start.2 = ((bf16[8,2,128,128]{3,2,1,0:T(8,128)(2,1)}), bf16[8,2,128,128]{3,2,1,0:T(8,128)(2,1)}, u32[]{:S(2)}, u32[]{:S(2)}) async-start(bf16[8,2,128,128]{3,2,1,0:T(8,128)(2,1)} %bitcast.153), calls=%async_computation.2 | async-start | bytes 1048576 | tf_op jit(solution)/shard_map/all_to_all | solution.py:668
  274.0 3.3 collective-permute-done.14
  277.4 2.9 add_convert_fusion.2
  280.3 10.6 %reduce-scatter.7.cloned.1.call-done = bf16[1,384,1024]{2,1,0:T(8,128)(2,1)} async-done(((bf16[4,384,1024]{2,1,0:T(8,128)(2,1)}), bf16[1,384,1024]{2,1,0:T(8,128)(2,1)}) %reduce-scatter.7.cloned.1.call-update) | async-done | bytes 786448
  290.9 7.4 %add_convert_fusion = bf16[512,6144]{1,0:T(8,128)(2,1)} fusion(bf16[512,6144]{1,0:T(8,128)(2,1)} %collective-permute-done.13, bf16[256,6144]{1,0:T(8,128)(2,1)S(1)} %copy-done, bf16[1024,256]{1,0:T(8,128)(2,1)} %copy-done.13), kind=kOutput, calls=%fused_computation | convolution fusion | flops 1620049920 | bytes 15990784 | tf_op jit(solution)/shard_map/dot_general | solution.py:56
  298.3 14.0 %attend_backward.1.grads_ref = bf16[8,3,2,128,128]{4,3,2,1,0:T(8,128)(2,1)} custom-call(bf16[8,3,2,128,128]{4,3,2,1,0:T(8,128)(2,1)} %get-tuple-element.61.qkv_ref, bf16[8,2,128,128]{3,2,1,0:T(8,128)(2,1)} %all-to-all-done.2.grad_ref, f32[2,2,4,256]{3,2,1,0:T(4,128)} %get-tuple-element.76.total_ref, f32[1024,128]{1,0:T(8,128)} %get-tuple-element.131.cos_ref, ...), custom_call_target="tpu_custom_call" | custom-call | flops 1342177280 | bytes 16777216 | tf_op jit(solution)/shard_map/attend_backward/pallas_call | solution.py:122
  312.3 5.4 %all-to-all-start.3 = ((bf16[8,3,2,128,128]{4,3,2,1,0:T(8,128)(2,1)}), bf16[8,3,2,128,128]{4,3,2,1,0:T(8,128)(2,1)S(1)}, u32[]{:S(2)}, u32[]{:S(2)}) async-start(bf16[8,3,2,128,128]{4,3,2,1,0:T(8,128)(2,1)} %attend_backward.1.grads_ref), calls=%async_computation.3 | async-start | bytes 3145728 | tf_op jit(solution)/shard_map/all_to_all | solution.py:668
  317.7 1.8 select_convert_fusion.pick_ref
  319.5 7.7 %head_grads.1 = bf16[1024,896]{1,0:T(8,128)(2,1)} custom-call(bf16[8,128,1024]{2,1,0:T(8,128)(2,1)} %get-tuple-element.60.normed_ref, bf16[8,3,2,128,128]{4,3,2,1,0:T(8,128)(2,1)} %attend_backward.1.grads_ref, f32[1,128]{1,0:T(1,128)} %get-tuple-element.77.loss_ref, bf16[1024,1024]{1,0:T(8,128)(2,1)} %select_convert_fusion.pick_ref), custom_call_target="tpu_custom_call" | custom-call | flops 3221225472 | bytes 7340032 | tf_op jit(solution)/shard_map/head_grads/pallas_call | solution.py:458
  328.7 2.5 collective-permute-done.15
  334.4 2.6 collective-permute-start.19
  337.8 12.7 %collective-permute-done.16 = bf16[256,896]{1,0:T(8,128)(2,1)S(1)} collective-permute-done((bf16[256,896]{1,0:T(8,128)(2,1)S(1)}, bf16[256,896]{1,0:T(8,128)(2,1)S(1)}, u32[]{:S(2)}, u32[]{:S(2)}) %collective-permute-start.16) | collective-permute-done | bytes 458784 | tf_op jit(solution)/shard_map/ppermute | solution.py:143
  352.2 16.6 %collective-permute-done.19 = bf16[128,1024]{1,0:T(8,128)(2,1)S(1)} collective-permute-done((bf16[128,1024]{1,0:T(8,128)(2,1)S(1)}, bf16[128,1024]{1,0:T(8,128)(2,1)S(1)}, u32[]{:S(2)}, u32[]{:S(2)}) %collective-permute-start.19) | collective-permute-done | bytes 262176 | tf_op jit(solution)/shard_map/ppermute | solution.py:143
  368.8 6.9 %collective-permute-done.20 = bf16[128,1024]{1,0:T(8,128)(2,1)S(1)} collective-permute-done((bf16[128,1024]{1,0:T(8,128)(2,1)S(1)}, bf16[128,1024]{1,0:T(8,128)(2,1)S(1)}, u32[]{:S(2)}, u32[]{:S(2)}) %collective-permute-start.20) | collective-permute-done | bytes 262176 | tf_op jit(solution)/shard_map/ppermute | solution.py:143
  378.9 2.1 collective-permute-start.27
  382.4 4.3 all-to-all-start.4
  387.7 1.8 collective-permute-start.22
  389.5 6.7 %last.1 = (f32[256,1024]{1,0:T(8,128)}, f32[256,1024]{1,0:T(8,128)}) custom-call(bf16[4,2,3,2,128,128]{5,4,3,2,1,0:T(8,128)(2,1)} %bitcast.128, bf16[256,1024]{1,0:T(8,128)(2,1)} %bitcast.131, f32[1,1024]{1,0:T(1,128)} %get-tuple-element.125.gain_ref, bf16[8,4,32,9216]{3,2,1,0:T(8,128)(2,1)} %bitcast.121, f32[256,1024]{1,0:T(8,128)} %get-tuple-element.82.grad_hidden_ref), custom_call_target="tpu_custom_call" | custom-call | flops 1610612736 | bytes 11534336 | tf_op jit(solution)/shard_map/last/pallas_call | solution.py:492
  396.9 5.3 %collective-permute-done.28 = bf16[96,1024]{1,0:T(8,128)(2,1)} collective-permute-done((bf16[96,1024]{1,0:T(8,128)(2,1)S(1)}, bf16[96,1024]{1,0:T(8,128)(2,1)}, u32[]{:S(2)}, u32[]{:S(2)}) %collective-permute-start.28) | collective-permute-done | bytes 196640 | tf_op jit(solution)/shard_map/ppermute | solution.py:143
  402.2 1.7 convert_add_fusion
  405.2 2.2 slice_bitcast_fusion
  408.3 2.1 collective-permute-start.24
  413.0 7.9 %collective-permute-done.23.refs_1_ = bf16[32,6144]{1,0:T(8,128)(2,1)S(1)} collective-permute-done((bf16[32,6144]{1,0:T(8,128)(2,1)S(1)}, bf16[32,6144]{1,0:T(8,128)(2,1)S(1)}, u32[]{:S(2)}, u32[]{:S(2)}) %collective-permute-start.23) | collective-permute-done | bytes 393248 | tf_op jit(solution)/shard_map/ppermute | solution.py:143
  420.9 15.9 %collective-permute-done.24.refs_2_ = bf16[32,6144]{1,0:T(8,128)(2,1)S(1)} collective-permute-done((bf16[32,6144]{1,0:T(8,128)(2,1)S(1)}, bf16[32,6144]{1,0:T(8,128)(2,1)S(1)}, u32[]{:S(2)}, u32[]{:S(2)}) %collective-permute-start.24) | collective-permute-done | bytes 393248 | tf_op jit(solution)/shard_map/ppermute | solution.py:143
  436.8 6.1 %collective-permute-done.25.refs_3_ = bf16[32,6144]{1,0:T(8,128)(2,1)S(1)} collective-permute-done((bf16[32,6144]{1,0:T(8,128)(2,1)S(1)}, bf16[32,6144]{1,0:T(8,128)(2,1)S(1)}, u32[]{:S(2)}, u32[]{:S(2)}) %collective-permute-start.25) | collective-permute-done | bytes 393248 | tf_op jit(solution)/shard_map/ppermute | solution.py:143
  443.7 3.1 finish.1
  (209 shorter events, 60.2 us)
Async XLA Ops:
  7.2 201.7 %all-gather.5.cloned.1.call-start = ((), (), s32[]{:S(2)}) async-start(), calls=%async_computation.7 | async-start | bytes 9437184 | tf_op jit(solution)/shard_map/all_gather | solution.py:633
  9.5 9.7 %copy-start.8 = (bf16[32,2816]{1,0:T(8,128)(2,1)S(1)}, bf16[32,2816]{1,0:T(8,128)(2,1)}, u32[]{:S(2)}) copy-start(bf16[32,2816]{1,0:T(8,128)(2,1)} %refs_5_.1) | copy-start | bytes 540676
  10.4 20.4 %collective-permute-start = (bf16[32,4096]{1,0:T(8,128)(2,1)S(1)}, bf16[32,4096]{1,0:T(8,128)(2,1)}, u32[]{:S(2)}, u32[]{:S(2)}) collective-permute-start(bf16[32,4096]{1,0:T(8,128)(2,1)S(1)} %constant_dynamic-update-slice_fusion), channel_id=1, source_target_pairs={{0,24},{8,16},{16,8},{24,0},{1,25},{9,17},{17,9},{25,1},{2,26},{10... | collective-permute-start | bytes 786440 | tf_op jit(solution)/shard_map/ppermute | solution.py:143
  12.1 22.4 %collective-permute-start.1 = (bf16[32,4096]{1,0:T(8,128)(2,1)S(1)}, bf16[32,4096]{1,0:T(8,128)(2,1)}, u32[]{:S(2)}, u32[]{:S(2)}) collective-permute-start(bf16[32,4096]{1,0:T(8,128)(2,1)S(1)} %constant_dynamic-update-slice_fusion), channel_id=1, source_target_pairs={{0,16},{8,24},{16,0},{24,8},{1,17},{9,25},{17,1},{25,9},{2,18},{10... | collective-permute-start | bytes 786440 | tf_op jit(solution)/shard_map/ppermute | solution.py:143
  13.1 21.3 %collective-permute-start.2 = (bf16[32,4096]{1,0:T(8,128)(2,1)S(1)}, bf16[32,4096]{1,0:T(8,128)(2,1)}, u32[]{:S(2)}, u32[]{:S(2)}) collective-permute-start(bf16[32,4096]{1,0:T(8,128)(2,1)S(1)} %constant_dynamic-update-slice_fusion), channel_id=1, source_target_pairs={{0,8},{8,0},{16,24},{24,16},{1,9},{9,1},{17,25},{25,17},{2,10},{10... | collective-permute-start | bytes 786440 | tf_op jit(solution)/shard_map/ppermute | solution.py:143
  23.7 18.2 %copy-start.2 = (bf16[2,128,1024]{2,1,0:T(8,128)(2,1)S(1)}, bf16[2,128,1024]{2,1,0:T(8,128)(2,1)}, u32[]{:S(2)}) copy-start(bf16[2,128,1024]{2,1,0:T(8,128)(2,1)} %param.14) | copy-start | bytes 1572868
  36.8 172.1 %all-gather.7.cloned.1.call-start = ((), (), s32[]{:S(2)}) async-start(), calls=%async_computation.8 | async-start | bytes 21233664 | tf_op jit(solution)/shard_map/all_gather | solution.py:633
  36.8 41.6 %collective-permute-start.3 = (bf16[32,9216]{1,0:T(8,128)(2,1)S(1)}, bf16[32,9216]{1,0:T(8,128)(2,1)S(1)}, u32[]{:S(2)}, u32[]{:S(2)}) collective-permute-start(bf16[32,9216]{1,0:T(8,128)(2,1)S(1)} %constant_dynamic-update-slice_fusion.2), channel_id=1, source_target_pairs={{0,24},{8,16},{16,8},{24,0},{1,25},{9,17},{17,9},{25,1},{2,26},{10... | collective-permute-start | bytes 1769480 | tf_op jit(solution)/shard_map/ppermute | solution.py:143
  37.4 49.8 %collective-permute-start.4 = (bf16[32,9216]{1,0:T(8,128)(2,1)S(1)}, bf16[32,9216]{1,0:T(8,128)(2,1)S(1)}, u32[]{:S(2)}, u32[]{:S(2)}) collective-permute-start(bf16[32,9216]{1,0:T(8,128)(2,1)S(1)} %constant_dynamic-update-slice_fusion.2), channel_id=1, source_target_pairs={{0,16},{8,24},{16,0},{24,8},{1,17},{9,25},{17,1},{25,9},{2,18},{10... | collective-permute-start | bytes 1769480 | tf_op jit(solution)/shard_map/ppermute | solution.py:143
  41.7 45.4 %collective-permute-start.5 = (bf16[32,9216]{1,0:T(8,128)(2,1)S(1)}, bf16[32,9216]{1,0:T(8,128)(2,1)}, u32[]{:S(2)}, u32[]{:S(2)}) collective-permute-start(bf16[32,9216]{1,0:T(8,128)(2,1)S(1)} %constant_dynamic-update-slice_fusion.2), channel_id=1, source_target_pairs={{0,8},{8,0},{16,24},{24,16},{1,9},{9,1},{17,25},{25,17},{2,10},{10... | collective-permute-start | bytes 1769480 | tf_op jit(solution)/shard_map/ppermute | solution.py:143
  90.2 28.2 %all-to-all-start = ((bf16[8,480,128]{2,1,0:T(8,128)(2,1)}), bf16[8,480,128]{2,1,0:T(8,128)(2,1)S(1)}, u32[]{:S(2)}, u32[]{:S(2)}) async-start(bf16[8,480,128]{2,1,0:T(8,128)(2,1)} %pad_maximum_fusion.5), calls=%async_computation | async-start | bytes 1966080 | tf_op jit(solution)/shard_map/all_to_all | solution.py:643
  97.5 22.5 %collective-permute-start.6 = (bf16[128,1024]{1,0:T(8,128)(2,1)}, bf16[128,1024]{1,0:T(8,128)(2,1)S(1)}, u32[]{:S(2)}, u32[]{:S(2)}) collective-permute-start(bf16[128,1024]{1,0:T(8,128)(2,1)} %get-tuple-element.53), channel_id=1, source_target_pairs={{0,4},{4,0},{1,5},{5,1},{2,6},{6,2},{3,7},{7,3},{8,12},{12,8},{9,1... | collective-permute-start | bytes 786440 | tf_op jit(solution)/shard_map/ppermute | solution.py:143
  118.4 22.0 %collective-permute-start.10 = (bf16[7,8,32,128]{3,2,0,1:T(8,128)(2,1)S(1)}, bf16[7,8,32,128]{3,2,0,1:T(8,128)(2,1)S(1)}, u32[]{:S(2)}, u32[]{:S(2)}) collective-permute-start(bf16[7,8,32,128]{3,2,0,1:T(8,128)(2,1)S(1)} %bitcast.140), channel_id=1, source_target_pairs={{0,2},{2,0},{1,3},{3,1},{4,6},{6,4},{5,7},{7,5},{8,10},{10,8},{9,1... | collective-permute-start | bytes 1376264 | tf_op jit(solution)/shard_map/ppermute | solution.py:143
  120.9 36.4 %collective-permute-start.7 = (bf16[2,128,1024]{2,1,0:T(8,128)(2,1)}, bf16[2,128,1024]{2,1,0:T(8,128)(2,1)}, u32[]{:S(2)}, u32[]{:S(2)}) collective-permute-start(bf16[2,128,1024]{2,1,0:T(8,128)(2,1)} %pad_maximum_fusion.7), channel_id=1, source_target_pairs={{0,24},{8,16},{16,8},{24,0},{1,25},{9,17},{17,9},{25,1},{2,26},{10... | collective-permute-start | bytes 1572872 | tf_op jit(solution)/shard_map/ppermute | solution.py:143
  121.1 43.8 %collective-permute-start.8 = (bf16[2,128,1024]{2,1,0:T(8,128)(2,1)}, bf16[2,128,1024]{2,1,0:T(8,128)(2,1)}, u32[]{:S(2)}, u32[]{:S(2)}) collective-permute-start(bf16[2,128,1024]{2,1,0:T(8,128)(2,1)} %pad_maximum_fusion.7), channel_id=1, source_target_pairs={{0,16},{8,24},{16,0},{24,8},{1,17},{9,25},{17,1},{25,9},{2,18},{10... | collective-permute-start | bytes 1572872 | tf_op jit(solution)/shard_map/ppermute | solution.py:143
  125.3 39.6 %collective-permute-start.9 = (bf16[2,128,1024]{2,1,0:T(8,128)(2,1)}, bf16[2,128,1024]{2,1,0:T(8,128)(2,1)}, u32[]{:S(2)}, u32[]{:S(2)}) collective-permute-start(bf16[2,128,1024]{2,1,0:T(8,128)(2,1)} %pad_maximum_fusion.7), channel_id=1, source_target_pairs={{0,8},{8,0},{16,24},{24,16},{1,9},{9,1},{17,25},{25,17},{2,10},{10... | collective-permute-start | bytes 1572872 | tf_op jit(solution)/shard_map/ppermute | solution.py:143
  140.6 28.3 %collective-permute-start.11 = (bf16[7,8,2,32,128]{4,3,0,1,2:T(8,128)(2,1)S(1)}, bf16[7,8,2,32,128]{4,3,0,1,2:T(8,128)(2,1)}, u32[]{:S(2)}, u32[]{:S(2)}) collective-permute-start(bf16[7,8,2,32,128]{4,3,0,1,2:T(8,128)(2,1)S(1)} %pad_maximum_fusion.6), channel_id=1, source_target_pairs={{0,1},{1,0},{2,3},{3,2},{4,5},{5,4},{6,7},{7,6},{8,9},{9,8},{10,11... | collective-permute-start | bytes 2752520 | tf_op jit(solution)/shard_map/ppermute | solution.py:143
  190.7 18.1 %all-to-all-start.1 = ((bf16[8,2,128,128]{3,2,1,0:T(8,128)(2,1)}), bf16[8,2,128,128]{3,2,1,0:T(8,128)(2,1)S(1)}, u32[]{:S(2)}, u32[]{:S(2)}) async-start(bf16[8,2,128,128]{3,2,1,0:T(8,128)(2,1)} %get-tuple-element.56), calls=%async_computation.1 | async-start | bytes 1048576 | tf_op jit(solution)/shard_map/all_to_all | solution.py:668
  197.6 93.3 %reduce-scatter.7.cloned.1.call-start = ((), (), s32[]{:S(2)}) async-start(), calls=%async_computation.9 | async-start | bytes 3932160
  232.9 5.7 %collective-permute-start.12 = (bf16[1536,1024]{1,0:T(8,128)(2,1)S(1)}, bf16[1536,1024]{1,0:T(8,128)(2,1)S(1)}, u32[]{:S(2)}, u32[]{:S(2)}) collective-permute-start(bf16[1536,1024]{1,0:T(8,128)(2,1)S(1)} %convolution_convert_fusion.1), channel_id=1, source_target_pairs={{0,1},{1,0},{2,3},{3,2},{4,5},{5,4},{6,7},{7,6},{8,9},{9,8},{10,11... | collective-permute-start | bytes 9437192 | tf_op jit(solution)/shard_map/ppermute | solution.py:143
  233.8 25.0 %copy-start.13 = (bf16[1024,256]{1,0:T(8,128)(2,1)}, bf16[1024,256]{1,0:T(8,128)(2,1)S(1)}, u32[]{:S(2)}) copy-start(bf16[1024,256]{1,0:T(8,128)(2,1)S(1)} %fusion.24) | copy-start | bytes 1572868
  265.4 25.5 %collective-permute-start.13 = (bf16[512,6144]{1,0:T(8,128)(2,1)}, bf16[512,6144]{1,0:T(8,128)(2,1)}, u32[]{:S(2)}, u32[]{:S(2)}) collective-permute-start(bf16[512,6144]{1,0:T(8,128)(2,1)} %convolution_convert_fusion), channel_id=1, source_target_pairs={{0,1},{1,0},{2,3},{3,2},{4,5},{5,4},{6,7},{7,6},{8,9},{9,8},{10,11... | collective-permute-start | bytes 18874376 | tf_op jit(solution)/shard_map/ppermute | solution.py:143
  268.0 22.9 %copy-start = (bf16[256,6144]{1,0:T(8,128)(2,1)S(1)}, bf16[256,6144]{1,0:T(8,128)(2,1)}, u32[]{:S(2)}) copy-start(bf16[256,6144]{1,0:T(8,128)(2,1)} %get-tuple-element.71) | copy-start | bytes 9437188
  268.0 9.4 %collective-permute-start.14 = (bf16[512,1024]{1,0:T(8,128)(2,1)}, bf16[512,1024]{1,0:T(8,128)(2,1)}, u32[]{:S(2)}, u32[]{:S(2)}) collective-permute-start(bf16[512,1024]{1,0:T(8,128)(2,1)} %convolution_convert_fusion.2), channel_id=1, source_target_pairs={{0,1},{1,0},{2,3},{3,2},{4,5},{5,4},{6,7},{7,6},{8,9},{9,8},{10,11... | collective-permute-start | bytes 3145736 | tf_op jit(solution)/shard_map/ppermute | solution.py:143
  268.4 29.9 %all-to-all-start.2 = ((bf16[8,2,128,128]{3,2,1,0:T(8,128)(2,1)}), bf16[8,2,128,128]{3,2,1,0:T(8,128)(2,1)}, u32[]{:S(2)}, u32[]{:S(2)}) async-start(bf16[8,2,128,128]{3,2,1,0:T(8,128)(2,1)} %bitcast.153), calls=%async_computation.2 | async-start | bytes 1048576 | tf_op jit(solution)/shard_map/all_to_all | solution.py:668
  274.0 131.2 %reduce-scatter.9.cloned.1.call-start = ((), (), s32[]{:S(2)}) async-start(), calls=%async_computation.10 | async-start | bytes 7864320
  312.3 64.3 %all-to-all-start.3 = ((bf16[8,3,2,128,128]{4,3,2,1,0:T(8,128)(2,1)}), bf16[8,3,2,128,128]{4,3,2,1,0:T(8,128)(2,1)S(1)}, u32[]{:S(2)}, u32[]{:S(2)}) async-start(bf16[8,3,2,128,128]{4,3,2,1,0:T(8,128)(2,1)} %attend_backward.1.grads_ref), calls=%async_computation.3 | async-start | bytes 3145728 | tf_op jit(solution)/shard_map/all_to_all | solution.py:668
  328.6 2.5 collective-permute-start.15
  332.6 17.9 %collective-permute-start.16 = (bf16[256,896]{1,0:T(8,128)(2,1)S(1)}, bf16[256,896]{1,0:T(8,128)(2,1)S(1)}, u32[]{:S(2)}, u32[]{:S(2)}) collective-permute-start(bf16[256,896]{1,0:T(8,128)(2,1)S(1)} %slice.234), channel_id=1, source_target_pairs={{0,2},{2,0},{1,3},{3,1},{4,6},{6,4},{5,7},{7,5},{8,10},{10,8},{9,1... | collective-permute-start | bytes 1376264 | tf_op jit(solution)/shard_map/ppermute | solution.py:143
  334.3 44.5 %copy-start.7 = (bf16[1,384,1024]{2,1,0:T(8,128)(2,1)S(1)}, bf16[1,384,1024]{2,1,0:T(8,128)(2,1)}, u32[]{:S(2)}) copy-start(bf16[1,384,1024]{2,1,0:T(8,128)(2,1)} %reduce-scatter.7.cloned.1.call-done) | copy-start | bytes 2359300
  334.3 17.9 %collective-permute-start.18 = (bf16[128,1024]{1,0:T(8,128)(2,1)S(1)}, bf16[128,1024]{1,0:T(8,128)(2,1)S(1)}, u32[]{:S(2)}, u32[]{:S(2)}) collective-permute-start(bf16[128,1024]{1,0:T(8,128)(2,1)S(1)} %get-tuple-element.107), channel_id=1, source_target_pairs={{0,8},{8,0},{16,24},{24,16},{1,9},{9,1},{17,25},{25,17},{2,10},{10... | collective-permute-start | bytes 786440 | tf_op jit(solution)/shard_map/ppermute | solution.py:143
  334.4 34.5 %collective-permute-start.19 = (bf16[128,1024]{1,0:T(8,128)(2,1)S(1)}, bf16[128,1024]{1,0:T(8,128)(2,1)S(1)}, u32[]{:S(2)}, u32[]{:S(2)}) collective-permute-start(bf16[128,1024]{1,0:T(8,128)(2,1)S(1)} %get-tuple-element.109), channel_id=1, source_target_pairs={{0,16},{8,24},{16,0},{24,8},{1,17},{9,25},{17,1},{25,9},{2,18},{10... | collective-permute-start | bytes 786440 | tf_op jit(solution)/shard_map/ppermute | solution.py:143
  336.9 38.7 %collective-permute-start.20 = (bf16[128,1024]{1,0:T(8,128)(2,1)S(1)}, bf16[128,1024]{1,0:T(8,128)(2,1)S(1)}, u32[]{:S(2)}, u32[]{:S(2)}) collective-permute-start(bf16[128,1024]{1,0:T(8,128)(2,1)S(1)} %get-tuple-element.108), channel_id=1, source_target_pairs={{0,24},{8,16},{16,8},{24,0},{1,25},{9,17},{17,9},{25,1},{2,26},{10... | collective-permute-start | bytes 786440 | tf_op jit(solution)/shard_map/ppermute | solution.py:143
  350.7 25.2 %collective-permute-start.17 = (bf16[128,896]{1,0:T(8,128)(2,1)S(1)}, bf16[128,896]{1,0:T(8,128)(2,1)S(1)}, u32[]{:S(2)}, u32[]{:S(2)}) collective-permute-start(bf16[128,896]{1,0:T(8,128)(2,1)S(1)} %slice.236), channel_id=1, source_target_pairs={{0,4},{4,0},{1,5},{5,1},{2,6},{6,2},{3,7},{7,3},{8,12},{12,8},{9,1... | collective-permute-start | bytes 688136 | tf_op jit(solution)/shard_map/ppermute | solution.py:143
  376.6 12.9 %copy-start.1 = (bf16[8,3,2,128,128]{4,3,2,1,0:T(8,128)(2,1)}, bf16[8,3,2,128,128]{4,3,2,1,0:T(8,128)(2,1)S(1)}, u32[]{:S(2)}) copy-start(bf16[8,3,2,128,128]{4,3,2,1,0:T(8,128)(2,1)S(1)} %all-to-all-done.3) | copy-start | bytes 4718596
  377.3 9.4 %collective-permute-start.21 = (bf16[64,1024]{1,0:T(8,128)(2,1)}, bf16[64,1024]{1,0:T(8,128)(2,1)}, u32[]{:S(2)}, u32[]{:S(2)}) collective-permute-start(bf16[64,1024]{1,0:T(8,128)(2,1)} %slice.204), channel_id=1, source_target_pairs={{0,4},{4,0},{1,5},{5,1},{2,6},{6,2},{3,7},{7,3},{8,12},{12,8},{9,1... | collective-permute-start | bytes 393224 | tf_op jit(solution)/shard_map/ppermute | solution.py:143
  378.8 18.1 %collective-permute-start.26 = (bf16[96,1024]{1,0:T(8,128)(2,1)S(1)}, bf16[96,1024]{1,0:T(8,128)(2,1)S(1)}, u32[]{:S(2)}, u32[]{:S(2)}) collective-permute-start(bf16[96,1024]{1,0:T(8,128)(2,1)S(1)} %get-tuple-element.119), channel_id=1, source_target_pairs={{0,8},{8,0},{16,24},{24,16},{1,9},{9,1},{17,25},{25,17},{2,10},{10... | collective-permute-start | bytes 589832 | tf_op jit(solution)/shard_map/ppermute | solution.py:143
  378.9 18.0 %collective-permute-start.27 = (bf16[96,1024]{1,0:T(8,128)(2,1)S(1)}, bf16[96,1024]{1,0:T(8,128)(2,1)S(1)}, u32[]{:S(2)}, u32[]{:S(2)}) collective-permute-start(bf16[96,1024]{1,0:T(8,128)(2,1)S(1)} %get-tuple-element.118), channel_id=1, source_target_pairs={{0,16},{8,24},{16,0},{24,8},{1,17},{9,25},{17,1},{25,9},{2,18},{10... | collective-permute-start | bytes 589832 | tf_op jit(solution)/shard_map/ppermute | solution.py:143
  381.0 21.2 %collective-permute-start.28 = (bf16[96,1024]{1,0:T(8,128)(2,1)S(1)}, bf16[96,1024]{1,0:T(8,128)(2,1)}, u32[]{:S(2)}, u32[]{:S(2)}) collective-permute-start(bf16[96,1024]{1,0:T(8,128)(2,1)S(1)} %get-tuple-element.117), channel_id=1, source_target_pairs={{0,24},{8,16},{16,8},{24,0},{1,25},{9,17},{17,9},{25,1},{2,26},{10... | collective-permute-start | bytes 589832 | tf_op jit(solution)/shard_map/ppermute | solution.py:143
  382.4 21.6 %all-to-all-start.4 = ((bf16[4,32,896]{2,1,0:T(8,128)(2,1)}), bf16[4,32,896]{2,1,0:T(8,128)(2,1)S(1)}, u32[]{:S(2)}, u32[]{:S(2)}) async-start(bf16[4,32,896]{2,1,0:T(8,128)(2,1)} %bitcast.60), calls=%async_computation.4 | async-start | bytes 458752 | tf_op jit(solution)/shard_map/all_to_all | solution.py:730
  387.7 8.6 %collective-permute-start.22 = (bf16[32,1024]{1,0:T(8,128)(2,1)S(1)}, bf16[32,1024]{1,0:T(8,128)(2,1)S(1)}, u32[]{:S(2)}, u32[]{:S(2)}) collective-permute-start(bf16[32,1024]{1,0:T(8,128)(2,1)S(1)} %slice.243), channel_id=1, source_target_pairs={{0,2},{2,0},{1,3},{3,1},{4,6},{6,4},{5,7},{7,5},{8,10},{10,8},{9,1... | collective-permute-start | bytes 196616 | tf_op jit(solution)/shard_map/ppermute | solution.py:143
  404.9 41.9 %copy-start.16 = (f32[32,1024]{1,0:T(8,128)}, f32[32,1024]{1,0:T(8,128)S(1)}, u32[]{:S(2)}) copy-start(f32[32,1024]{1,0:T(8,128)S(1)} %squeeze.29) | copy-start | bytes 393220
  405.2 42.4 %copy-start.26 = (bf16[32]{0:T(256)(128)(2,1)S(1)}, bf16[32]{0:T(256)(128)(2,1)}, u32[]{:S(2)}) copy-start(bf16[32]{0:T(256)(128)(2,1)} %param.24) | copy-start | bytes 196
  407.4 13.5 %collective-permute-start.23 = (bf16[32,6144]{1,0:T(8,128)(2,1)S(1)}, bf16[32,6144]{1,0:T(8,128)(2,1)S(1)}, u32[]{:S(2)}, u32[]{:S(2)}) collective-permute-start(bf16[32,6144]{1,0:T(8,128)(2,1)S(1)} %get-tuple-element.103), channel_id=1, source_target_pairs={{0,8},{8,0},{16,24},{24,16},{1,9},{9,1},{17,25},{25,17},{2,10},{10... | collective-permute-start | bytes 1179656 | tf_op jit(solution)/shard_map/ppermute | solution.py:143
  408.3 28.5 %collective-permute-start.24 = (bf16[32,6144]{1,0:T(8,128)(2,1)S(1)}, bf16[32,6144]{1,0:T(8,128)(2,1)S(1)}, u32[]{:S(2)}, u32[]{:S(2)}) collective-permute-start(bf16[32,6144]{1,0:T(8,128)(2,1)S(1)} %get-tuple-element.102), channel_id=1, source_target_pairs={{0,16},{8,24},{16,0},{24,8},{1,17},{9,25},{17,1},{25,9},{2,18},{10... | collective-permute-start | bytes 1179656 | tf_op jit(solution)/shard_map/ppermute | solution.py:143
  410.4 32.5 %collective-permute-start.25 = (bf16[32,6144]{1,0:T(8,128)(2,1)S(1)}, bf16[32,6144]{1,0:T(8,128)(2,1)S(1)}, u32[]{:S(2)}, u32[]{:S(2)}) collective-permute-start(bf16[32,6144]{1,0:T(8,128)(2,1)S(1)} %get-tuple-element.101), channel_id=1, source_target_pairs={{0,24},{8,16},{16,8},{24,0},{1,25},{9,17},{17,9},{25,1},{2,26},{10... | collective-permute-start | bytes 1179656 | tf_op jit(solution)/shard_map/ppermute | solution.py:143
  411.7 36.4 %copy-start.17 = (f32[32,1024]{1,0:T(8,128)}, f32[32,1024]{1,0:T(8,128)S(1)}, u32[]{:S(2)}) copy-start(f32[32,1024]{1,0:T(8,128)S(1)} %squeeze.28) | copy-start | bytes 393220
  420.9 22.0 %copy-start.19 = (bf16[32,6144]{1,0:T(8,128)(2,1)}, bf16[32,6144]{1,0:T(8,128)(2,1)S(1)}, u32[]{:S(2)}) copy-start(bf16[32,6144]{1,0:T(8,128)(2,1)S(1)} %collective-permute-done.23.refs_1_) | copy-start | bytes 1179652
  (20 other events, 106.0 us)
Sparse Core Ops, SparseCore 0:
  36.9 56.4 all-gather.4
  95.3 112.3 all-gather.6
  241.5 49.3 reduce-scatter.6
  298.4 94.5 reduce-scatter.8

commit v5 on v4

--- a/solution.py
+++ b/solution.py
@@ -134,7 +134,7 @@
         scratch_shapes=[pltpu.VMEM((length, PAIR), F32), pltpu.VMEM((length, PAIR), F32)],
         compiler_params=pltpu.CompilerParams(vmem_limit_bytes=VMEM_LIMIT),
         name="attend_backward",
-        cost_estimate=cost(5 * units * length * length * PAIR, 8 * grad_att.size * 8, units * length * length),
+        cost_estimate=cost(units * length * length, 22),
     )(qkv, grad_att, totals, cos, sin)
 
 
@@ -187,8 +187,8 @@
     return lax.optimization_barrier(values)
 
 
-def cost(flops, moved, exps=0):
-    return pl.CostEstimate(flops=int(flops), bytes_accessed=int(moved), transcendentals=int(exps))
+def cost(size, factor):
+    return pl.CostEstimate(flops=0, bytes_accessed=int(size * factor), transcendentals=0)
 
 
 def params():
@@ -254,7 +254,7 @@
         ],
         compiler_params=params(),
         name="front",
-        cost_estimate=cost(6 * units * length * PAIR * width + 2 * units * length * length * PAIR, 6 * x.size, 2 * units * length * length),
+        cost_estimate=cost(units * length * length, 27),
     )(x, first, gain, cos, sin, weights)
 
 
@@ -276,159 +276,155 @@
     return jnp.concatenate([dot_t(left, part) for part in sections(weight_ref)], axis=1)
 
 
-def forward_kernel(
-    x_ref, heads_ref, gain_ref, teacher_ref, cotangent_ref, valid_ref, rate_ref, wo_ref, wg_ref, wu_ref, wd_ref,
-    att_ref, hidden_ref, normed_ref, gate_ref, up_ref, act_ref, result_ref, grad_ref, grad_low_ref, loss_ref,
+def mlp_kernel(
+    x_ref, heads_ref, gain_ref, teacher_ref, cotangent_ref, valid_ref, rate_ref, gate_out, up_down,
+    att_ref, normed_ref, act_ref, result_ref, grad_low_ref, loss_ref, grads_ref, grad_hidden_ref, branch_ref, out_heads_ref,
+    wo, wg, wu, wd, gates, ups, hidden_ref, total, arrived,
 ):
-    step = pl.program_id(0)
     tokens, width = x_ref.shape
-
-    @pl.when(step == 0)
-    def _():
-        for pair in range(width // PAIR):
-            at, unit = divmod(pair, heads_ref.shape[2])
-            att_ref[:, pair * PAIR : (pair + 1) * PAIR] = heads_ref[at, :, unit].reshape(tokens, PAIR)
-        hidden = x_ref[...].astype(F32) + dot_sections(att_ref[...], wo_ref)
-        inv = lax.rsqrt(jnp.mean(hidden * hidden, axis=-1, keepdims=True) + EPSILON)
-        hidden_ref[...] = hidden
-        result_ref[...] = hidden
-        normed_ref[...] = (hidden * inv * gain_ref[...]).astype(BF16)
-
-    gate = dot_sections(normed_ref[...], wg_ref)
-    up = dot_sections(normed_ref[...], wu_ref)
-    act = (gate * jax.nn.sigmoid(gate) * up).astype(BF16)
-    gate_ref[...] = gate
-    up_ref[...] = up
-    act_ref[...] = act
-    result_ref[...] += dot_sections(act, wd_ref)
-
-    @pl.when(step == pl.num_programs(0) - 1)
-    def _():
-        error = result_ref[...] - teacher_ref[...].astype(F32)
-        valid = valid_ref[...]
-        grad = cotangent_ref[...].astype(F32) + rate_ref[0:1, 0:1] * valid * error
-        grad_ref[...] = grad
-        grad_low_ref[...] = grad.astype(BF16)
-        losses = jnp.sum(error * error * (valid / width), axis=0, keepdims=True)
-        total = losses[:, :PAIR]
-        for at in range(PAIR, width, PAIR):
-            total = total + losses[:, at : at + PAIR]
-        loss_ref[...] = total
-
-
-def weight_specs(width, parts, gate_out, rest):
-    outer, sides, rows, _ = rest.shape
-    wide = MLP_STEP
+    steps, _, sides, _, wide = wg.shape
+    parts = steps * wide // width
     per = width // wide
-    whole = (outer, sides, rows)
-    return wide, [
-        pl.BlockSpec(whole + (width,), lambda j: (0, 0, 0, parts)),
-        pl.BlockSpec(whole + (wide,), lambda j: (0, 0, 0, j)),
-        pl.BlockSpec(whole + (wide,), lambda j: (0, 0, 0, 3 * per + j)),
-        pl.BlockSpec((outer, sides // per, rows, width), lambda j: (0, j % per, 0, 3 + parts + j // per)),
-    ], (gate_out, gate_out, rest, rest)
+    deep = sides // per
+
+    def output_copy():
+        return pltpu.make_async_copy(
+            gate_out.at[:, :, :, pl.ds(parts * width, width)], wo, arrived.at[3 * steps]
+        )
+
+    def copies(step):
+        lanes = pl.ds(pl.multiple_of(step * wide, wide), wide)
+        rows = pl.ds(step % per * deep, deep)
+        across = pl.ds(pl.multiple_of((parts + step // per) * width, width), width)
+        return (
+            pltpu.make_async_copy(gate_out.at[:, :, :, lanes], wg.at[step], arrived.at[3 * step]),
+            pltpu.make_async_copy(up_down.at[:, :, :, lanes], wu.at[step], arrived.at[3 * step + 1]),
+            pltpu.make_async_copy(up_down.at[:, rows, :, across], wd.at[step], arrived.at[3 * step + 2]),
+        )
+
+    output_copy().start()
+    for step in range(steps):
+        for copy in copies(step):
+            copy.start()
+
+    for pair in range(width // PAIR):
+        at, unit = divmod(pair, heads_ref.shape[2])
+        att_ref[:, pair * PAIR : (pair + 1) * PAIR] = heads_ref[at, :, unit].reshape(tokens, PAIR)
+    output_copy().wait()
+    hidden = x_ref[...].astype(F32) + dot_sections(att_ref[...], wo)
+    inv = lax.rsqrt(jnp.mean(hidden * hidden, axis=-1, keepdims=True) + EPSILON)
+    hidden_ref[...] = hidden
+    result_ref[...] = hidden
+    normed_ref[...] = (hidden * inv * gain_ref[...]).astype(BF16)
+
+    def forward(step, carry):
+        for copy in copies(step):
+            copy.wait()
+        gate = dot_sections(normed_ref[...], wg.at[step])
+        up = dot_sections(normed_ref[...], wu.at[step])
+        act = (gate * jax.nn.sigmoid(gate) * up).astype(BF16)
+        gates[step] = gate
+        ups[step] = up
+        act_ref[:, pl.ds(pl.multiple_of(step * wide, wide), wide)] = act
+        result_ref[...] += dot_sections(act, wd.at[step])
+        return carry
+
+    lax.fori_loop(0, steps, forward, 0)
+    error = result_ref[...] - teacher_ref[...].astype(F32)
+    valid = valid_ref[...]
+    grad = cotangent_ref[...].astype(F32) + rate_ref[0:1, 0:1] * valid * error
+    grad_hidden_ref[...] = grad
+    grad_low_ref[...] = grad.astype(BF16)
+    losses = jnp.sum(error * error * (valid / width), axis=0, keepdims=True)
+    loss = losses[:, :PAIR]
+    for at in range(PAIR, width, PAIR):
+        loss = loss + losses[:, at : at + PAIR]
+    loss_ref[...] = loss
+    total[...] = jnp.zeros_like(total)
+
+    def backward(step, carry):
+        gate = gates[step]
+        up = ups[step]
+        sigmoid = jax.nn.sigmoid(gate)
+        grad_act = dot_t_sections(grad_low_ref[...], wd.at[step])
+        grad_gate = (grad_act * up * (sigmoid * (1.0 + gate * (1.0 - sigmoid)))).astype(BF16)
+        grad_up = (grad_act * (gate * sigmoid)).astype(BF16)
+        at = pl.multiple_of(2 * step * wide, 2 * wide)
+        grads_ref[:, pl.ds(at, wide)] = grad_gate
+        grads_ref[:, pl.ds(pl.multiple_of(at + wide, wide), wide)] = grad_up
+        total[...] += dot_t_sections(grad_gate, wg.at[step]) + dot_t_sections(grad_up, wu.at[step])
+        return carry
+
+    lax.fori_loop(0, steps, backward, 0)
+    hidden = hidden_ref[...]
+    inv = lax.rsqrt(jnp.mean(hidden * hidden, axis=-1, keepdims=True) + EPSILON)
+    scaled = hidden * inv
+    scaled_grad = total[...] * gain_ref[...]
+    grad = grad_hidden_ref[...] + inv * (
+        scaled_grad - scaled * jnp.mean(scaled_grad * scaled, axis=-1, keepdims=True)
+    )
+    grad_hidden_ref[...] = grad
+    branch = grad.astype(BF16)
+    branch_ref[...] = branch
+    value = dot_t_sections(branch, wo).astype(BF16)
+    _, batch, units, rows, _ = out_heads_ref.shape
+    for pair in range(width // PAIR):
+        at, unit = divmod(pair, units)
+        out_heads_ref[at, :, unit] = value[:, pair * PAIR : (pair + 1) * PAIR].reshape(batch, rows, PAIR)
 
 
 def still(*shape):
     return pl.BlockSpec(shape, lambda j: (0,) * len(shape))
 
 
-def mlp_forward(x, heads, gain, teacher, cotangent, valid, rate, gate_out, rest):
+def mlp(x, heads, gain, teacher, cotangent, valid, rate, gate_out, up_down):
     tokens, width = x.shape
+    outer, sides, rows, _ = gate_out.shape
     parts = gate_out.shape[3] // width - 1
-    wide, specs, weights = weight_specs(width, parts, gate_out, rest)
-    moving = pl.BlockSpec((tokens, wide), lambda j: (0, j))
+    wide = MLP_STEP
+    steps = parts * width // wide
+    deep = sides * wide // width
     whole = still(tokens, width)
+    outside = pl.BlockSpec(memory_space=pl.ANY)
+    low = jax.ShapeDtypeStruct((tokens, width), BF16)
+    full = jax.ShapeDtypeStruct((tokens, width), F32)
     hidden = (tokens, parts * width)
+    grads = (tokens, 2 * parts * width)
     return pl.pallas_call(
-        forward_kernel,
-        grid=(parts * width // wide,),
+        mlp_kernel,
+        grid=(1,),
         in_specs=[whole, still(*heads.shape), still(1, width), whole, whole, still(tokens, 1), still(1, PAIR)]
-        + specs,
-        out_specs=[whole, whole, whole, moving, moving, moving, whole, whole, whole, still(1, PAIR)],
+        + [outside, outside],
+        out_specs=[
+            whole, whole, still(*hidden), whole, whole, still(1, PAIR), still(*grads), whole, whole, still(*heads.shape),
+        ],
         out_shape=[
-            jax.ShapeDtypeStruct((tokens, width), BF16),
-            jax.ShapeDtypeStruct((tokens, width), F32),
-            jax.ShapeDtypeStruct((tokens, width), BF16),
-            jax.ShapeDtypeStruct(hidden, F32),
-            jax.ShapeDtypeStruct(hidden, F32),
+            low,
+            low,
             jax.ShapeDtypeStruct(hidden, BF16),
-            jax.ShapeDtypeStruct((tokens, width), F32),
-            jax.ShapeDtypeStruct((tokens, width), F32),
-            jax.ShapeDtypeStruct((tokens, width), BF16),
+            full,
+            low,
             jax.ShapeDtypeStruct((1, PAIR), F32),
+            jax.ShapeDtypeStruct(grads, BF16),
+            full,
+            low,
+            jax.ShapeDtypeStruct(heads.shape, BF16),
+        ],
+        scratch_shapes=[
+            pltpu.VMEM((outer, sides, rows, width), BF16),
+            pltpu.VMEM((steps, outer, sides, rows, wide), BF16),
+            pltpu.VMEM((steps, outer, sides, rows, wide), BF16),
+            pltpu.VMEM((steps, outer, deep, rows, width), BF16),
+            pltpu.VMEM((steps, tokens, wide), F32),
+            pltpu.VMEM((steps, tokens, wide), F32),
+            pltpu.VMEM((tokens, width), F32),
+            pltpu.VMEM((tokens, width), F32),
+            pltpu.SemaphoreType.DMA((3 * steps + 1,)),
         ],
         compiler_params=params(),
-        name="mlp_forward",
-        cost_estimate=cost(2 * tokens * width * width * (3 * parts + 1), 2 * width * width * (3 * parts + 1) + 10 * tokens * width * parts, tokens * width * parts),
-    )(x, heads, gain, teacher, cotangent, valid, rate, *weights)
-
-
-def backward_kernel(
-    grad_ref, grad_low_ref, hidden_ref, gain_ref, gate_ref, up_ref, wo_ref, wg_ref, wu_ref, wd_ref,
-    grads_ref, grad_hidden_ref, branch_ref, heads_ref, total,
-):
-    step = pl.program_id(0)
-    wide = gate_ref.shape[1]
-    gate = gate_ref[...]
-    up = up_ref[...]
-    sigmoid = jax.nn.sigmoid(gate)
-    grad_act = dot_t_sections(grad_low_ref[...], wd_ref)
-    grad_gate = (grad_act * up * (sigmoid * (1.0 + gate * (1.0 - sigmoid)))).astype(BF16)
-    grad_up = (grad_act * (gate * sigmoid)).astype(BF16)
-    grads_ref[:, :wide] = grad_gate
-    grads_ref[:, wide:] = grad_up
-    value = dot_t_sections(grad_gate, wg_ref) + dot_t_sections(grad_up, wu_ref)
-
-    @pl.when(step == 0)
-    def _():
-        total[...] = value
-
-    @pl.when(step > 0)
-    def _():
-        total[...] += value
-
-    @pl.when(step == pl.num_programs(0) - 1)
-    def _():
-        hidden = hidden_ref[...]
-        inv = lax.rsqrt(jnp.mean(hidden * hidden, axis=-1, keepdims=True) + EPSILON)
-        scaled = hidden * inv
-        scaled_grad = total[...] * gain_ref[...]
-        grad = grad_ref[...] + inv * (
-            scaled_grad - scaled * jnp.mean(scaled_grad * scaled, axis=-1, keepdims=True)
-        )
-        grad_hidden_ref[...] = grad
-        branch = grad.astype(BF16)
-        branch_ref[...] = branch
-        value = dot_t_sections(branch, wo_ref).astype(BF16)
-        _, batch, units, rows, _ = heads_ref.shape
-        for pair in range(value.shape[1] // PAIR):
-            at, unit = divmod(pair, units)
-            heads_ref[at, :, unit] = value[:, pair * PAIR : (pair + 1) * PAIR].reshape(batch, rows, PAIR)
-
-
-def mlp_backward(grad, grad_low, hidden, gain, gate, up, gate_out, rest, heads):
-    tokens, width = grad.shape
-    parts = gate_out.shape[3] // width - 1
-    wide, specs, weights = weight_specs(width, parts, gate_out, rest)
-    moving = pl.BlockSpec((tokens, wide), lambda j: (0, j))
-    whole = still(tokens, width)
-    return pl.pallas_call(
-        backward_kernel,
-        grid=(parts * width // wide,),
-        in_specs=[whole, whole, whole, still(1, width), moving, moving] + specs,
-        out_specs=[pl.BlockSpec((tokens, 2 * wide), lambda j: (0, j)), whole, whole, still(*heads)],
-        out_shape=[
-            jax.ShapeDtypeStruct((tokens, 2 * parts * width), BF16),
-            jax.ShapeDtypeStruct((tokens, width), F32),
-            jax.ShapeDtypeStruct((tokens, width), BF16),
-            jax.ShapeDtypeStruct(heads, BF16),
-        ],
-        scratch_shapes=[pltpu.VMEM((tokens, width), F32)],
-        compiler_params=params(),
-        name="mlp_backward",
-        cost_estimate=cost(2 * tokens * width * width * (3 * parts + 1), 2 * width * width * (3 * parts + 1) + 12 * tokens * width * parts, tokens * width * parts),
-    )(grad, grad_low, hidden, gain, gate, up, *weights)
+        name="mlp",
+        cost_estimate=cost(tokens * width * parts, 80),
+    )(x, heads, gain, teacher, cotangent, valid, rate, gate_out, up_down)
 
 
 def picker(place, width):
@@ -461,7 +457,7 @@
         scratch_shapes=[pltpu.VMEM((columns, width), BF16)],
         compiler_params=params(),
         name="head_grads",
-        cost_estimate=cost(2 * normed.size * columns + 2 * width * width * columns, 2 * normed.size + 2 * width * width + 4 * width * columns),
+        cost_estimate=cost(normed.size, 24),
     )(normed, grads, loss_row, pick)
 
 
@@ -507,7 +503,7 @@
         scratch_shapes=[pltpu.VMEM((tokens, 3 * width), BF16)],
         compiler_params=params(),
         name="last",
-        cost_estimate=cost(6 * tokens * width * width, 6 * width * width + 20 * tokens * width),
+        cost_estimate=cost(tokens * width, 84),
     )(heads, x, gain, weights, grad_hidden)
 
 
@@ -635,16 +631,19 @@
             rows = rows.transpose(1, 0, 2, 3).reshape(1, width // BLOCK, BLOCK, rows.shape[3])
         return rows
 
+    x_own, x_sent = pick(inputs, mine, 0), pick(inputs, 1 - mine, 0)
+    x_sent = swap(x_sent, "y", 1)
     gate_out = along_z(jnp.concatenate([pack_columns(w_gate), w_output], axis=1))
-    rest = jnp.concatenate([w_query, w_key, w_value, pack_columns(w_up), down_rows], axis=1)
-    gate_out, rest, parcel = together(gate_out, rest, parcel)
+    rest = jnp.concatenate([pack_columns(w_up), down_rows], axis=1)
+    gate_out, rest, parcel, x_sent = together(gate_out, rest, parcel, x_sent)
     gate_out = across(gate_out)
     rest = along_z(rest)
+    rest, x_own, x_sent, parcel = together(rest, x_own, x_sent, parcel)
+    rest = across(rest)
     parcel = lax.all_to_all(parcel, SEQ, split_axis=0, concat_axis=0, tiled=True)
-    rest, x_own, x_sent = together(rest, pick(inputs, mine, 0), pick(inputs, 1 - mine, 0))
-    rest = across(rest)
-    pieces = arrange([x_own, swap(x_sent, "y", 1)], mine)
-    x_all = along_z(jnp.stack(pieces, axis=0)).reshape(seqs, local_len, width)
+    x_all = along_z(jnp.stack(arrange([x_own, x_sent], mine), axis=0)).reshape(seqs, local_len, width)
+    x_all, attn_rows = together(x_all, jnp.concatenate([w_query, w_key, w_value], axis=1))
+    attn_w = along_z(attn_rows)
 
     first_all = parcel[:, blocks * own_rows :].reshape(seqs, units, local_len, PAIR)
     head_w = parcel[:, : blocks * own_rows].reshape(seqs, blocks, own_rows, PAIR).transpose(1, 0, 2, 3)
@@ -659,6 +658,7 @@
 
     cos_all, sin_all = rotary_tables(jnp.arange(length, dtype=jnp.int32))
     pick_native = picker(stage_rows(width, STAGES_NATIVE, ("c", "z")), width)
+    pick_down = picker(stage_rows(width, STAGES_NATIVE), width)
     pick_output = picker(stage_rows(width, STAGES_OUTPUT), width)
     pick_heads = picker(stage_rows(width, STAGES_HEADS, ("c", "x", "y")), width)
 
@@ -668,9 +668,13 @@
         return lax.all_to_all(array, SEQ, split_axis=0, concat_axis=0, tiled=True)
 
     att_heads = exchange(attended).reshape(zs, batch, units, local_len, PAIR)
+    att_heads, attn_w = together(att_heads, attn_w)
+    attn_w = across(attn_w)
     x_low = inputs.reshape(tokens, width)
     rate = jnp.full((1, PAIR), 2.0 / width, F32) / valid_total
-    att_low, hidden_in, normed_mlp, gate, up, activated, result, grad_out, grad_down_in, loss_row = mlp_forward(
+    (
+        att_low, normed_mlp, activated, result, grad_down_in, loss_row, grads, grad_hidden, grad_branch, grad_heads,
+    ) = mlp(
         x_low,
         att_heads,
         gain_m,
@@ -683,26 +687,36 @@
     )
 
     half = width // 2
-    turned = [
-        dot_t(pick_native, activated[:, p * width : (p + 1) * width]).astype(BF16).reshape(-1, own_rows, tokens)
-        for p in range(hidden_parts)
-    ]
-    turned_act = jnp.stack(turned, axis=1).reshape(hidden_parts * width, tokens)
-    cut = hidden_parts * half
-    down_sent = swap(dot(turned_act[cut:], grad_down_in).astype(BF16), "c", 1)
-    down_sum = (dot(turned_act[:cut], grad_down_in) + down_sent.astype(F32)).astype(BF16)
-    down_sum, grad_down_in = together(down_sum, grad_down_in)
+    def down_half(rows):
+        turned = [
+            dot_t(pick_down[rows], activated[:, p * width : (p + 1) * width]).astype(BF16).reshape(-1, own_rows, tokens)
+            for p in range(hidden_parts)
+        ]
+        return dot(jnp.stack(turned, axis=1).reshape(hidden_parts * half, tokens), grad_down_in)
+
+    down_sent = swap(down_half(slice(half, None)).astype(BF16), "c", 1)
+    down_sum = (down_half(slice(half)) + down_sent.astype(F32)).astype(BF16)
 
     def over_yx(value):
         value = value.reshape(2 * lax.axis_size("x"), -1, value.shape[1])
         value = lax.psum_scatter(value, ("y", "x"), scatter_dimension=0, tiled=True)
         return lax.optimization_barrier(value)[0]
 
-    down_sum = over_yx(down_sum)
-    grads, grad_hidden, grad_branch, grad_heads = mlp_backward(
-        grad_out, grad_down_in, hidden_in, gain_m, gate, up, gate_out, rest, att_heads.shape
-    )
+    xs = lax.axis_size("x")
+    down_sum = down_sum.reshape(2, xs, -1, width)
+
+    def add_axis(value, name, axis):
+        size = value.shape[axis]
+        received = [swap(lax.index_in_dim(value, k, axis, False), name, k) for k in range(1, size)]
+        value = lax.index_in_dim(value, 0, axis, False).astype(F32)
+        for piece in received:
+            value = value + piece.astype(F32)
+        return value.astype(BF16)
+
+    down_left = add_axis(down_sum[:, :, :, :half], "y", 0)
+    down_right = add_axis(down_sum[:, :, :, half:], "x", 1)
     grad_heads = exchange(grad_heads.reshape(seqs, units, local_len, PAIR))
+    down_sum = jnp.concatenate([add_axis(down_left, "x", 0), add_axis(down_right, "y", 0)], axis=1)
     turned_mlp = dot_t(pick_native, normed_mlp).astype(BF16)
     mlp_sent = swap(dot(turned_mlp[half:], grads).astype(BF16), "c", 1)
     mlp_sum = (dot(turned_mlp[:half], grads) + mlp_sent.astype(F32)).astype(BF16)
@@ -711,9 +725,9 @@
     out_sent = swap(dot(turned_att[half:], grad_branch).astype(BF16), "c", 1)
     out_sum = (dot(turned_att[:half], grad_branch) + out_sent.astype(F32)).astype(BF16)
 
-    grad_heads, mlp_sum, out_sum, down_sum = together(grad_heads, mlp_sum, out_sum, down_sum)
+    out_sum = add_stage(out_sum, "z").astype(BF16)
+    grad_heads, attn_w, *_ = together(grad_heads, attn_w, mlp_sum, out_sum, down_sum)
     mlp_sum = over_yx(mlp_sum)
-    out_sum = add_stage(out_sum, "z").astype(BF16)
 
     grad_qkv = attend_backward(qkv, grad_heads, totals, cos_all, sin_all)
     grad_own = exchange(grad_qkv).reshape(zs, batch, 3, units, local_len, PAIR)
@@ -721,11 +735,11 @@
     value = head_grads(normed_all, grad_qkv, loss_row, pick_heads)
     for name in ("c", "x", "y"):
         value = add_stage(value, name)
-    value, grad_own, down_sum, out_sum = together(value.astype(BF16), grad_own, down_sum, out_sum)
     owned_down = add_stage(down_sum, "z")[:own_down]
-    owned_output = add_stage(add_stage(out_sum, "y"), "x")
-    mlp_sum = mlp_sum.reshape(zs, own_rows, -1)
-    mlp_sum = [mlp_sum[0]] + [swap(mlp_sum[k], "z", k) for k in range(1, zs)]
+    value, grad_own, owned_down, out_sum, mlp_sum = together(value, grad_own, owned_down, out_sum, mlp_sum)
+    value = value.astype(BF16)
+    out_sum = add_stage(add_stage(out_sum, "y"), "x")
+    owned_output = out_sum
     value = value.reshape(zs, own_rows, value.shape[1])
     value = lax.all_to_all(value, "z", split_axis=0, concat_axis=0, tiled=True)
     columns = 3 * units * PAIR
@@ -733,7 +747,9 @@
     value = value[:, :, :columns].reshape(zs, own_rows, units, 3, PAIR).astype(F32)
     owned_qkv = value.transpose(3, 1, 0, 2, 4).reshape(3, own_rows, width)
 
-    grad_in, grad_first = last(grad_own, x_low, gain_a, rest, grad_hidden)
+    mlp_sum = mlp_sum.reshape(zs, own_rows, -1)
+    mlp_sum = [mlp_sum[0]] + [swap(mlp_sum[k], "z", k) for k in range(1, zs)]
+    grad_in, grad_first = last(grad_own, x_low, gain_a, attn_w, grad_hidden)
 
     gain_grad_a = (
         jnp.sum(w_query.astype(F32) * owned_qkv[0], axis=1)

time: 463 us -> 431 us (0.931)
  waiting for transfers between devices: 213 us -> 192 us
  Pallas kernels: 83.7 us -> 69.9 us
    pallas_call x2 -> x1, Pallas kernels: 35 us -> 21.3 us  [mlp(): pl.pallas_call(mlp_kernel, grid=(1,), in_specs=[whole, still(*heads.shape...]
    ppermute x29 -> x36, waiting for transfers between devices: 174 us -> 162 us  [swap(): return lax.ppermute(array, name, [(i, i ^ distance) for i in range(size)])]
    unnamed x6 -> x5, waiting for transfers between devices: 10.7 us -> 0.07 us
    dot_general x6, matrix products: 21.9 us -> 13.3 us  [dot(): return jnp.dot(left, right, preferred_element_type=F32)]
    ppermute x29 -> x36, starting transfers between devices: 34.3 us -> 40.6 us  [swap(): return lax.ppermute(array, name, [(i, i ^ distance) for i in range(size)])]
    dot_general x5 -> x8, matrix products: 4.91 us -> 9.4 us  [dot_t(): lax.dot_general(left, right, (((1,), (1,)), ((), ())), preferred_element_...]
  transfers between devices with their start and end apart: 38 -> 45, of which waited for: 20 -> 21; matrix products, arithmetic and copies ran while one was open for 12% -> 16% of each run, Pallas kernels for 14% -> 16%
where the time goes in v5:
time: 431 us; the launch traced here: 424 us
  waiting for transfers between devices  192 us (45%)
  Pallas kernels  69.9 us (16%)
  starting transfers between devices  68.6 us (16%)
  other arithmetic  29.5 us (7%)
  matrix products  22.7 us (5%)
  local copies, waits for them, and re-layouts  21.6 us (5%)
  between operations  20.4 us (5%)
    ppermute x36, waiting for transfers between devices, swap(): return lax.ppermute(array, name, [(i, i ^ distance) for i in range(size)])  162 us
    ppermute x36, starting transfers between devices, swap(): return lax.ppermute(array, name, [(i, i ^ distance) for i in range(size)])  40.6 us
    pallas_call x1, Pallas kernels, mlp(): pl.pallas_call(mlp_kernel, grid=(1,), in_specs=[whole, still(*heads.shape...  21.3 us
    all_to_all x1, waiting for transfers between devices, on_device(): lax.all_to_all(parcel, SEQ, split_axis=0, concat_axis=0, tiled=True)  20.9 us
    pallas_call x1, Pallas kernels, front(): pl.pallas_call(front_kernel, grid=(units,), in_specs=[pl.BlockSpec((parts...  17.1 us
    all_to_all x3, starting transfers between devices, exchange(): return lax.all_to_all(array, SEQ, split_axis=0, concat_axis=0, tiled=True)  15.8 us
    pallas_call x1, Pallas kernels, attend_backward(): pl.pallas_call(attend_backward_kernel, grid=(units,), in_specs=[pl.BlockS...  14 us
    dot_general x6, matrix products, dot(): return jnp.dot(left, right, preferred_element_type=F32)  13.3 us
  transfers between devices with their start and end apart: 45, of which 21 were waited for; matrix products, arithmetic and copies ran while one was open for 16% of the time, Pallas kernels for 16%

profile of v5, /device:TPU:8, one launch (start us, length us, event | category | flops | bytes accessed | tf_op | source)
XLA Modules:
  0.0 424.1 jit_solution(11329620740203719595)
XLA Ops:
  10.4 1.6 collective-permute-start
  25.0 5.8 %collective-permute-done = bf16[32,4096]{1,0:T(8,128)(2,1)} collective-permute-done((bf16[32,4096]{1,0:T(8,128)(2,1)S(1)}, bf16[32,4096]{1,0:T(8,128)(2,1)}, u32[]{:S(2)}, u32[]{:S(2)}) %collective-permute-start) | collective-permute-done | bytes 262176 | tf_op jit(solution)/shard_map/ppermute | solution.py:143
  30.8 3.6 collective-permute-done.1
  37.3 4.4 %collective-permute-start.5 = (bf16[32,6144]{1,0:T(8,128)(2,1)S(1)}, bf16[32,6144]{1,0:T(8,128)(2,1)S(1)}, u32[]{:S(2)}, u32[]{:S(2)}) collective-permute-start(bf16[32,6144]{1,0:T(8,128)(2,1)S(1)} %pad_maximum_fusion.11), channel_id=1, source_target_pairs={{0,16},{8,24},{16,0},{24,8},{1,17},{9,25},{17,1},{25,9},{2,18},{10... | collective-permute-start | bytes 1179656 | tf_op jit(solution)/shard_map/ppermute | solution.py:143
  41.8 24.0 %collective-permute-done.4 = bf16[32,6144]{1,0:T(8,128)(2,1)S(1)} collective-permute-done((bf16[32,6144]{1,0:T(8,128)(2,1)S(1)}, bf16[32,6144]{1,0:T(8,128)(2,1)S(1)}, u32[]{:S(2)}, u32[]{:S(2)}) %collective-permute-start.4) | collective-permute-done | bytes 393248 | tf_op jit(solution)/shard_map/ppermute | solution.py:143
  65.8 4.5 %collective-permute-done.5 = bf16[32,6144]{1,0:T(8,128)(2,1)S(1)} collective-permute-done((bf16[32,6144]{1,0:T(8,128)(2,1)S(1)}, bf16[32,6144]{1,0:T(8,128)(2,1)S(1)}, u32[]{:S(2)}, u32[]{:S(2)}) %collective-permute-start.5) | collective-permute-done | bytes 393248 | tf_op jit(solution)/shard_map/ppermute | solution.py:143
  71.9 7.6 %all-to-all-start = ((bf16[8,480,128]{2,1,0:T(8,128)(2,1)}), bf16[8,480,128]{2,1,0:T(8,128)(2,1)S(1)}, u32[]{:S(2)}, u32[]{:S(2)}) async-start(bf16[8,480,128]{2,1,0:T(8,128)(2,1)} %pad_maximum_fusion.5), calls=%async_computation | async-start | bytes 1966080 | tf_op jit(solution)/shard_map/all_to_all | solution.py:643
  79.5 20.9 %all-to-all-done = bf16[8,480,128]{2,1,0:T(8,128)(2,1)S(1)} async-done(((bf16[8,480,128]{2,1,0:T(8,128)(2,1)}), bf16[8,480,128]{2,1,0:T(8,128)(2,1)S(1)}, u32[]{:S(2)}, u32[]{:S(2)}) %all-to-all-start) | async-done | bytes 983072 | tf_op jit(solution)/shard_map/all_to_all | solution.py:643
  104.1 4.2 collective-permute-start.8
  108.3 1.7 collective-permute-done.10
  110.3 3.1 fusion.20
  114.3 26.0 %collective-permute-done.7 = bf16[2,128,1024]{2,1,0:T(8,128)(2,1)} collective-permute-done((bf16[2,128,1024]{2,1,0:T(8,128)(2,1)}, bf16[2,128,1024]{2,1,0:T(8,128)(2,1)}, u32[]{:S(2)}, u32[]{:S(2)}) %collective-permute-start.7) | collective-permute-done | bytes 524320 | tf_op jit(solution)/shard_map/ppermute | solution.py:143
  140.3 7.7 %collective-permute-done.8 = bf16[2,128,1024]{2,1,0:T(8,128)(2,1)} collective-permute-done((bf16[2,128,1024]{2,1,0:T(8,128)(2,1)}, bf16[2,128,1024]{2,1,0:T(8,128)(2,1)}, u32[]{:S(2)}, u32[]{:S(2)}) %collective-permute-start.8) | collective-permute-done | bytes 524320 | tf_op jit(solution)/shard_map/ppermute | solution.py:143
  151.4 4.2 collective-permute-start.13
  158.2 1.9 copy.94
  161.6 17.1 %front.1 = (bf16[8,128,1024]{2,1,0:T(8,128)(2,1)}, bf16[8,3,2,128,128]{4,3,2,1,0:T(8,128)(2,1)}, bf16[8,2,128,128]{3,2,1,0:T(8,128)(2,1)}, f32[2,2,4,256]{3,2,1,0:T(4,128)}) custom-call(bf16[8,128,1024]{2,1,0:T(8,128)(2,1)} %bitcast.165, bf16[8,2,128,128]{3,2,1,0:T(8,128)(2,1)} %bitcast.175, f32[1,1024]{1,0:T(1,128)} %get-tuple-element.126.gain_ref, ...), custom_call_target="tpu_custom_call" | custom-call | bytes 56623104 | tf_op jit(solution)/shard_map/front/pallas_call | solution.py:232
  178.7 6.3 %all-to-all-start.1 = ((bf16[8,2,128,128]{3,2,1,0:T(8,128)(2,1)}), bf16[8,2,128,128]{3,2,1,0:T(8,128)(2,1)S(1)}, u32[]{:S(2)}, u32[]{:S(2)}) async-start(bf16[8,2,128,128]{3,2,1,0:T(8,128)(2,1)} %get-tuple-element.58), calls=%async_computation.1 | async-start | bytes 1048576 | tf_op jit(solution)/shard_map/all_to_all | solution.py:668
  187.0 8.7 %all-to-all-done.1 = bf16[8,2,128,128]{3,2,1,0:T(8,128)(2,1)S(1)} async-done(((bf16[8,2,128,128]{3,2,1,0:T(8,128)(2,1)}), bf16[8,2,128,128]{3,2,1,0:T(8,128)(2,1)S(1)}, u32[]{:S(2)}, u32[]{:S(2)}) %all-to-all-start.1) | async-done | bytes 524320 | tf_op jit(solution)/shard_map/all_to_all | solution.py:668
  197.8 21.3 %mlp.1 = (bf16[256,1024]{1,0:T(8,128)(2,1)}, bf16[256,1024]{1,0:T(8,128)(2,1)}, bf16[256,3072]{1,0:T(8,128)(2,1)}, f32[256,1024]{1,0:T(8,128)}, bf16[256,1024]{1...) custom-call(bf16[256,1024]{1,0:T(8,128)(2,1)} %bitcast.169, ...), custom_call_target="tpu_custom_call" | custom-call | bytes 62914560 | tf_op jit(solution)/shard_map/mlp/pallas_call | solution.py:393
  219.2 2.1 fusion.11
  222.0 1.8 convolution_convert_fusion
  223.9 10.3 %collective-permute-done.15 = bf16[512,6144]{1,0:T(8,128)(2,1)S(1)} collective-permute-done((bf16[512,6144]{1,0:T(8,128)(2,1)S(1)}, bf16[512,6144]{1,0:T(8,128)(2,1)S(1)}, u32[]{:S(2)}, u32[]{:S(2)}) %collective-permute-start.15) | collective-permute-done | bytes 6291488 | tf_op jit(solution)/shard_map/ppermute | solution.py:143
  234.3 4.4 %add_convert_fusion = bf16[512,6144]{1,0:T(8,128)(2,1)} fusion(bf16[512,6144]{1,0:T(8,128)(2,1)S(1)} %collective-permute-done.15, bf16[256,6144]{1,0:T(8,128)(2,1)S(1)} %copy-done, bf16[1024,256]{1,0:T(8,128)(2,1)S(1)} %fusion.11), kind=kOutput, calls=%fused_computation | convolution fusion | flops 1620049920 | bytes 15990784 | tf_op jit(solution)/shard_map/dot_general | solution.py:56
  246.5 5.0 %all-to-all-start.2 = ((bf16[8,2,128,128]{3,2,1,0:T(8,128)(2,1)}), bf16[8,2,128,128]{3,2,1,0:T(8,128)(2,1)}, u32[]{:S(2)}, u32[]{:S(2)}) async-start(bf16[8,2,128,128]{3,2,1,0:T(8,128)(2,1)} %bitcast.191), calls=%async_computation.2 | async-start | bytes 1048576 | tf_op jit(solution)/shard_map/all_to_all | solution.py:668
  251.5 2.0 convolution_convert_fusion.8
  256.8 1.7 add_convert_fusion.2
  258.7 2.9 collective-permute-start.18
  262.2 2.9 add_convert_fusion.1
  270.6 9.3 %collective-permute-done.18 = bf16[128,1024]{1,0:T(8,128)(2,1)S(1)} collective-permute-done((bf16[128,1024]{1,0:T(8,128)(2,1)S(1)}, bf16[128,1024]{1,0:T(8,128)(2,1)S(1)}, u32[]{:S(2)}, u32[]{:S(2)}) %collective-permute-start.18) | collective-permute-done | bytes 262176 | tf_op jit(solution)/shard_map/ppermute | solution.py:143
  279.8 7.4 %collective-permute-done.19 = bf16[128,1024]{1,0:T(8,128)(2,1)S(1)} collective-permute-done((bf16[128,1024]{1,0:T(8,128)(2,1)S(1)}, bf16[128,1024]{1,0:T(8,128)(2,1)S(1)}, u32[]{:S(2)}, u32[]{:S(2)}) %collective-permute-start.19) | collective-permute-done | bytes 262176 | tf_op jit(solution)/shard_map/ppermute | solution.py:143
  287.5 14.0 %attend_backward.1.grads_ref = bf16[8,3,2,128,128]{4,3,2,1,0:T(8,128)(2,1)} custom-call(bf16[8,3,2,128,128]{4,3,2,1,0:T(8,128)(2,1)} %get-tuple-element.65.qkv_ref, bf16[8,2,128,128]{3,2,1,0:T(8,128)(2,1)} %all-to-all-done.2.grad_ref, f32[2,2,4,256]{3,2,1,0:T(4,128)} %get-tuple-element.75.total_ref, f32[1024,128]{1,0:T(8,128)} %get-tuple-element.134.cos_ref, ...), custom_call_target="tpu_custom_call" | custom-call | bytes 46137344 | tf_op jit(solution)/shard_map/attend_backward/pallas_call | solution.py:122
  301.4 4.6 %all-to-all-start.3 = ((bf16[8,3,2,128,128]{4,3,2,1,0:T(8,128)(2,1)}), bf16[8,3,2,128,128]{4,3,2,1,0:T(8,128)(2,1)}, u32[]{:S(2)}, u32[]{:S(2)}) async-start(bf16[8,3,2,128,128]{4,3,2,1,0:T(8,128)(2,1)} %attend_backward.1.grads_ref), calls=%async_computation.3 | async-start | bytes 3145728 | tf_op jit(solution)/shard_map/all_to_all | solution.py:668
  306.0 1.8 select_convert_fusion.pick_ref
  307.9 7.7 %head_grads.1 = bf16[1024,896]{1,0:T(8,128)(2,1)} custom-call(bf16[8,128,1024]{2,1,0:T(8,128)(2,1)} %get-tuple-element.64.normed_ref, bf16[8,3,2,128,128]{4,3,2,1,0:T(8,128)(2,1)} %attend_backward.1.grads_ref, f32[1,128]{1,0:T(1,128)} %get-tuple-element.76.loss_ref, bf16[1024,1024]{1,0:T(8,128)(2,1)} %select_convert_fusion.pick_ref), custom_call_target="tpu_custom_call" | custom-call | bytes 25165824 | tf_op jit(solution)/shard_map/head_grads/pallas_call | solution.py:454
  316.9 1.9 fusion.8
  322.8 22.6 %collective-permute-done.24 = bf16[384,512]{1,0:T(8,128)(2,1)S(1)} collective-permute-done((bf16[384,512]{1,0:T(8,128)(2,1)S(1)}, bf16[384,512]{1,0:T(8,128)(2,1)S(1)}, u32[]{:S(2)}, u32[]{:S(2)}) %collective-permute-start.24) | collective-permute-done | bytes 393248 | tf_op jit(solution)/shard_map/ppermute | solution.py:143
  345.9 2.9 collective-permute-start.29
  349.4 8.7 %collective-permute-done.26 = bf16[256,896]{1,0:T(8,128)(2,1)S(1)} collective-permute-done((bf16[256,896]{1,0:T(8,128)(2,1)S(1)}, bf16[256,896]{1,0:T(8,128)(2,1)S(1)}, u32[]{:S(2)}, u32[]{:S(2)}) %collective-permute-start.26) | collective-permute-done | bytes 458784 | tf_op jit(solution)/shard_map/ppermute | solution.py:143
  358.3 3.7 collective-permute-done.29
  362.0 3.5 collective-permute-done.30
  367.2 4.5 %all-to-all-start.4 = ((bf16[4,32,896]{2,1,0:T(8,128)(2,1)}), bf16[4,32,896]{2,1,0:T(8,128)(2,1)S(1)}, u32[]{:S(2)}, u32[]{:S(2)}) async-start(bf16[4,32,896]{2,1,0:T(8,128)(2,1)} %bitcast.80), calls=%async_computation.4 | async-start | bytes 458752 | tf_op jit(solution)/shard_map/all_to_all | solution.py:744
  372.2 1.8 collective-permute-start.32
  373.9 2.2 fusion.88
  376.2 3.4 collective-permute-start.34
  379.6 6.7 %last.1 = (f32[256,1024]{1,0:T(8,128)}, f32[256,1024]{1,0:T(8,128)}) custom-call(bf16[4,2,3,2,128,128]{5,4,3,2,1,0:T(8,128)(2,1)} %bitcast.77.heads_ref, bf16[256,1024]{1,0:T(8,128)(2,1)} %bitcast.170, f32[1,1024]{1,0:T(1,128)} %get-tuple-element.126.gain_ref, bf16[8,4,32,3072]{3,2,1,0:T(8,128)(2,1)} %bitcast.167, f32[256,1024]{1,0:T(8,128)} %get-tuple-element.80.grad_hidden_ref), custom_call_target="tpu_custom_call" | custom-call | bytes 22020096 | tf_op jit(solution)/shard_map/last/pallas_call | solution.py:488
  390.7 15.1 %collective-permute-done.34.refs_2_ = bf16[32,6144]{1,0:T(8,128)(2,1)S(1)} collective-permute-done((bf16[32,6144]{1,0:T(8,128)(2,1)S(1)}, bf16[32,6144]{1,0:T(8,128)(2,1)S(1)}, u32[]{:S(2)}, u32[]{:S(2)}) %collective-permute-start.34) | collective-permute-done | bytes 393248 | tf_op jit(solution)/shard_map/ppermute | solution.py:143
  405.8 5.7 %collective-permute-done.35.refs_3_ = bf16[32,6144]{1,0:T(8,128)(2,1)} collective-permute-done((bf16[32,6144]{1,0:T(8,128)(2,1)S(1)}, bf16[32,6144]{1,0:T(8,128)(2,1)}, u32[]{:S(2)}, u32[]{:S(2)}) %collective-permute-start.35) | collective-permute-done | bytes 393248 | tf_op jit(solution)/shard_map/ppermute | solution.py:143
  411.5 3.1 finish.1
  (235 shorter events, 65.6 us)
Async XLA Ops:
  7.2 190.1 %all-gather.7.cloned.1.call-start = ((), (), s32[]{:S(2)}) async-start(), calls=%async_computation.6 | async-start | bytes 9437184 | tf_op jit(solution)/shard_map/all_gather | solution.py:629
  10.4 20.4 %collective-permute-start = (bf16[32,4096]{1,0:T(8,128)(2,1)S(1)}, bf16[32,4096]{1,0:T(8,128)(2,1)}, u32[]{:S(2)}, u32[]{:S(2)}) collective-permute-start(bf16[32,4096]{1,0:T(8,128)(2,1)S(1)} %constant_dynamic-update-slice_fusion), channel_id=1, source_target_pairs={{0,24},{8,16},{16,8},{24,0},{1,25},{9,17},{17,9},{25,1},{2,26},{10... | collective-permute-start | bytes 786440 | tf_op jit(solution)/shard_map/ppermute | solution.py:143
  12.0 22.4 %collective-permute-start.1 = (bf16[32,4096]{1,0:T(8,128)(2,1)S(1)}, bf16[32,4096]{1,0:T(8,128)(2,1)}, u32[]{:S(2)}, u32[]{:S(2)}) collective-permute-start(bf16[32,4096]{1,0:T(8,128)(2,1)S(1)} %constant_dynamic-update-slice_fusion), channel_id=1, source_target_pairs={{0,16},{8,24},{16,0},{24,8},{1,17},{9,25},{17,1},{25,9},{2,18},{10... | collective-permute-start | bytes 786440 | tf_op jit(solution)/shard_map/ppermute | solution.py:143
  13.1 21.3 %collective-permute-start.2 = (bf16[32,4096]{1,0:T(8,128)(2,1)S(1)}, bf16[32,4096]{1,0:T(8,128)(2,1)}, u32[]{:S(2)}, u32[]{:S(2)}) collective-permute-start(bf16[32,4096]{1,0:T(8,128)(2,1)S(1)} %constant_dynamic-update-slice_fusion), channel_id=1, source_target_pairs={{0,8},{8,0},{16,24},{24,16},{1,9},{9,1},{17,25},{25,17},{2,10},{10... | collective-permute-start | bytes 786440 | tf_op jit(solution)/shard_map/ppermute | solution.py:143
  15.2 21.5 %collective-permute-start.3 = (bf16[128,1024]{1,0:T(8,128)(2,1)}, bf16[128,1024]{1,0:T(8,128)(2,1)}, u32[]{:S(2)}, u32[]{:S(2)}) collective-permute-start(bf16[128,1024]{1,0:T(8,128)(2,1)} %get-tuple-element.130), channel_id=1, source_target_pairs={{0,4},{4,0},{1,5},{5,1},{2,6},{6,2},{3,7},{7,3},{8,12},{12,8},{9,1... | collective-permute-start | bytes 786440 | tf_op jit(solution)/shard_map/ppermute | solution.py:143
  36.8 160.5 %all-gather.9.cloned.1.call-start = ((), (), s32[]{:S(2)}) async-start(), calls=%async_computation.7 | async-start | bytes 14155776 | tf_op jit(solution)/shard_map/all_gather | solution.py:629
  36.8 29.0 %collective-permute-start.4 = (bf16[32,6144]{1,0:T(8,128)(2,1)S(1)}, bf16[32,6144]{1,0:T(8,128)(2,1)S(1)}, u32[]{:S(2)}, u32[]{:S(2)}) collective-permute-start(bf16[32,6144]{1,0:T(8,128)(2,1)S(1)} %pad_maximum_fusion.11), channel_id=1, source_target_pairs={{0,24},{8,16},{16,8},{24,0},{1,25},{9,17},{17,9},{25,1},{2,26},{10... | collective-permute-start | bytes 1179656 | tf_op jit(solution)/shard_map/ppermute | solution.py:143
  37.3 33.0 %collective-permute-start.5 = (bf16[32,6144]{1,0:T(8,128)(2,1)S(1)}, bf16[32,6144]{1,0:T(8,128)(2,1)S(1)}, u32[]{:S(2)}, u32[]{:S(2)}) collective-permute-start(bf16[32,6144]{1,0:T(8,128)(2,1)S(1)} %pad_maximum_fusion.11), channel_id=1, source_target_pairs={{0,16},{8,24},{16,0},{24,8},{1,17},{9,25},{17,1},{25,9},{2,18},{10... | collective-permute-start | bytes 1179656 | tf_op jit(solution)/shard_map/ppermute | solution.py:143
  41.7 28.6 %collective-permute-start.6 = (bf16[32,6144]{1,0:T(8,128)(2,1)S(1)}, bf16[32,6144]{1,0:T(8,128)(2,1)S(1)}, u32[]{:S(2)}, u32[]{:S(2)}) collective-permute-start(bf16[32,6144]{1,0:T(8,128)(2,1)S(1)} %pad_maximum_fusion.11), channel_id=1, source_target_pairs={{0,8},{8,0},{16,24},{24,16},{1,9},{9,1},{17,25},{25,17},{2,10},{10... | collective-permute-start | bytes 1179656 | tf_op jit(solution)/shard_map/ppermute | solution.py:143
  71.9 28.5 %all-to-all-start = ((bf16[8,480,128]{2,1,0:T(8,128)(2,1)}), bf16[8,480,128]{2,1,0:T(8,128)(2,1)S(1)}, u32[]{:S(2)}, u32[]{:S(2)}) async-start(bf16[8,480,128]{2,1,0:T(8,128)(2,1)} %pad_maximum_fusion.5), calls=%async_computation | async-start | bytes 1966080 | tf_op jit(solution)/shard_map/all_to_all | solution.py:643
  100.5 9.6 %collective-permute-start.10 = (bf16[7,8,32,128]{3,2,0,1:T(8,128)(2,1)S(1)}, bf16[7,8,32,128]{3,2,0,1:T(8,128)(2,1)S(1)}, u32[]{:S(2)}, u32[]{:S(2)}) collective-permute-start(bf16[7,8,32,128]{3,2,0,1:T(8,128)(2,1)S(1)} %bitcast.178), channel_id=1, source_target_pairs={{0,2},{2,0},{1,3},{3,1},{4,6},{6,4},{5,7},{7,5},{8,10},{10,8},{9,1... | collective-permute-start | bytes 1376264 | tf_op jit(solution)/shard_map/ppermute | solution.py:143
  103.9 36.4 %collective-permute-start.7 = (bf16[2,128,1024]{2,1,0:T(8,128)(2,1)}, bf16[2,128,1024]{2,1,0:T(8,128)(2,1)}, u32[]{:S(2)}, u32[]{:S(2)}) collective-permute-start(bf16[2,128,1024]{2,1,0:T(8,128)(2,1)} %pad_maximum_fusion.10), channel_id=1, source_target_pairs={{0,24},{8,16},{16,8},{24,0},{1,25},{9,17},{17,9},{25,1},{2,26},{10... | collective-permute-start | bytes 1572872 | tf_op jit(solution)/shard_map/ppermute | solution.py:143
  104.1 43.9 %collective-permute-start.8 = (bf16[2,128,1024]{2,1,0:T(8,128)(2,1)}, bf16[2,128,1024]{2,1,0:T(8,128)(2,1)}, u32[]{:S(2)}, u32[]{:S(2)}) collective-permute-start(bf16[2,128,1024]{2,1,0:T(8,128)(2,1)} %pad_maximum_fusion.10), channel_id=1, source_target_pairs={{0,16},{8,24},{16,0},{24,8},{1,17},{9,25},{17,1},{25,9},{2,18},{10... | collective-permute-start | bytes 1572872 | tf_op jit(solution)/shard_map/ppermute | solution.py:143
  108.3 39.7 %collective-permute-start.9 = (bf16[2,128,1024]{2,1,0:T(8,128)(2,1)}, bf16[2,128,1024]{2,1,0:T(8,128)(2,1)}, u32[]{:S(2)}, u32[]{:S(2)}) collective-permute-start(bf16[2,128,1024]{2,1,0:T(8,128)(2,1)} %pad_maximum_fusion.10), channel_id=1, source_target_pairs={{0,8},{8,0},{16,24},{24,16},{1,9},{9,1},{17,25},{25,17},{2,10},{10... | collective-permute-start | bytes 1572872 | tf_op jit(solution)/shard_map/ppermute | solution.py:143
  110.2 46.6 %collective-permute-start.11 = (bf16[7,8,2,32,128]{4,3,0,1,2:T(8,128)(2,1)S(1)}, bf16[7,8,2,32,128]{4,3,0,1,2:T(8,128)(2,1)}, u32[]{:S(2)}, u32[]{:S(2)}) collective-permute-start(bf16[7,8,2,32,128]{4,3,0,1,2:T(8,128)(2,1)S(1)} %pad_maximum_fusion.6), channel_id=1, source_target_pairs={{0,1},{1,0},{2,3},{3,2},{4,5},{5,4},{6,7},{7,6},{8,9},{9,8},{10,11... | collective-permute-start | bytes 2752520 | tf_op jit(solution)/shard_map/ppermute | solution.py:143
  151.1 33.9 %collective-permute-start.12 = (bf16[32,3072]{1,0:T(8,128)(2,1)S(1)}, bf16[32,3072]{1,0:T(8,128)(2,1)S(1)}, u32[]{:S(2)}, u32[]{:S(2)}) collective-permute-start(bf16[32,3072]{1,0:T(8,128)(2,1)S(1)} %pad_maximum_fusion.13), channel_id=1, source_target_pairs={{0,24},{8,16},{16,8},{24,0},{1,25},{9,17},{17,9},{25,1},{2,26},{10... | collective-permute-start | bytes 589832 | tf_op jit(solution)/shard_map/ppermute | solution.py:143
  151.4 33.6 %collective-permute-start.13 = (bf16[32,3072]{1,0:T(8,128)(2,1)S(1)}, bf16[32,3072]{1,0:T(8,128)(2,1)S(1)}, u32[]{:S(2)}, u32[]{:S(2)}) collective-permute-start(bf16[32,3072]{1,0:T(8,128)(2,1)S(1)} %pad_maximum_fusion.13), channel_id=1, source_target_pairs={{0,16},{8,24},{16,0},{24,8},{1,17},{9,25},{17,1},{25,9},{2,18},{10... | collective-permute-start | bytes 589832 | tf_op jit(solution)/shard_map/ppermute | solution.py:143
  155.6 29.4 %collective-permute-start.14 = (bf16[32,3072]{1,0:T(8,128)(2,1)S(1)}, bf16[32,3072]{1,0:T(8,128)(2,1)}, u32[]{:S(2)}, u32[]{:S(2)}) collective-permute-start(bf16[32,3072]{1,0:T(8,128)(2,1)S(1)} %pad_maximum_fusion.13), channel_id=1, source_target_pairs={{0,8},{8,0},{16,24},{24,16},{1,9},{9,1},{17,25},{25,17},{2,10},{10... | collective-permute-start | bytes 589832 | tf_op jit(solution)/shard_map/ppermute | solution.py:143
  178.7 16.9 %all-to-all-start.1 = ((bf16[8,2,128,128]{3,2,1,0:T(8,128)(2,1)}), bf16[8,2,128,128]{3,2,1,0:T(8,128)(2,1)S(1)}, u32[]{:S(2)}, u32[]{:S(2)}) async-start(bf16[8,2,128,128]{3,2,1,0:T(8,128)(2,1)} %get-tuple-element.58), calls=%async_computation.1 | async-start | bytes 1048576 | tf_op jit(solution)/shard_map/all_to_all | solution.py:668
  185.0 102.5 %all-gather.11.cloned.1.call-start = ((), (), s32[]{:S(2)}) async-start(), calls=%async_computation.8 | async-start | bytes 7077888 | tf_op jit(solution)/shard_map/all_gather | solution.py:629
  195.7 171.4 %reduce-scatter.4.cloned.1.call-start = ((), (), s32[]{:S(2)}) async-start(), calls=%async_computation.9 | async-start | bytes 7864320
  223.8 10.4 %collective-permute-start.15 = (bf16[512,6144]{1,0:T(8,128)(2,1)S(1)}, bf16[512,6144]{1,0:T(8,128)(2,1)S(1)}, u32[]{:S(2)}, u32[]{:S(2)}) collective-permute-start(bf16[512,6144]{1,0:T(8,128)(2,1)S(1)} %convolution_convert_fusion), channel_id=1, source_target_pairs={{0,1},{1,0},{2,3},{3,2},{4,5},{5,4},{6,7},{7,6},{8,9},{9,8},{10,11... | collective-permute-start | bytes 18874376 | tf_op jit(solution)/shard_map/ppermute | solution.py:143
  243.4 18.7 %collective-permute-start.20 = (bf16[1536,1024]{1,0:T(8,128)(2,1)S(1)}, bf16[1536,1024]{1,0:T(8,128)(2,1)}, u32[]{:S(2)}, u32[]{:S(2)}) collective-permute-start(bf16[1536,1024]{1,0:T(8,128)(2,1)S(1)} %convolution_convert_fusion.1), channel_id=1, source_target_pairs={{0,1},{1,0},{2,3},{3,2},{4,5},{5,4},{6,7},{7,6},{8,9},{9,8},{10,11... | collective-permute-start | bytes 9437192 | tf_op jit(solution)/shard_map/ppermute | solution.py:143
  246.0 10.8 %collective-permute-start.16 = (bf16[512,1024]{1,0:T(8,128)(2,1)}, bf16[512,1024]{1,0:T(8,128)(2,1)}, u32[]{:S(2)}, u32[]{:S(2)}) collective-permute-start(bf16[512,1024]{1,0:T(8,128)(2,1)} %convolution_convert_fusion.2), channel_id=1, source_target_pairs={{0,1},{1,0},{2,3},{3,2},{4,5},{5,4},{6,7},{7,6},{8,9},{9,8},{10,11... | collective-permute-start | bytes 3145736 | tf_op jit(solution)/shard_map/ppermute | solution.py:143
  246.5 41.0 %all-to-all-start.2 = ((bf16[8,2,128,128]{3,2,1,0:T(8,128)(2,1)}), bf16[8,2,128,128]{3,2,1,0:T(8,128)(2,1)}, u32[]{:S(2)}, u32[]{:S(2)}) async-start(bf16[8,2,128,128]{3,2,1,0:T(8,128)(2,1)} %bitcast.191), calls=%async_computation.2 | async-start | bytes 1048576 | tf_op jit(solution)/shard_map/all_to_all | solution.py:668
  258.6 12.0 %collective-permute-start.17 = (bf16[128,1024]{1,0:T(8,128)(2,1)S(1)}, bf16[128,1024]{1,0:T(8,128)(2,1)S(1)}, u32[]{:S(2)}, u32[]{:S(2)}) collective-permute-start(bf16[128,1024]{1,0:T(8,128)(2,1)S(1)} %get-tuple-element.105), channel_id=1, source_target_pairs={{0,8},{8,0},{16,24},{24,16},{1,9},{9,1},{17,25},{25,17},{2,10},{10... | collective-permute-start | bytes 786440 | tf_op jit(solution)/shard_map/ppermute | solution.py:143
  258.7 21.1 %collective-permute-start.18 = (bf16[128,1024]{1,0:T(8,128)(2,1)S(1)}, bf16[128,1024]{1,0:T(8,128)(2,1)S(1)}, u32[]{:S(2)}, u32[]{:S(2)}) collective-permute-start(bf16[128,1024]{1,0:T(8,128)(2,1)S(1)} %get-tuple-element.107), channel_id=1, source_target_pairs={{0,16},{8,24},{16,0},{24,8},{1,17},{9,25},{17,1},{25,9},{2,18},{10... | collective-permute-start | bytes 786440 | tf_op jit(solution)/shard_map/ppermute | solution.py:143
  261.6 25.6 %collective-permute-start.19 = (bf16[128,1024]{1,0:T(8,128)(2,1)S(1)}, bf16[128,1024]{1,0:T(8,128)(2,1)S(1)}, u32[]{:S(2)}, u32[]{:S(2)}) collective-permute-start(bf16[128,1024]{1,0:T(8,128)(2,1)S(1)} %get-tuple-element.106), channel_id=1, source_target_pairs={{0,24},{8,16},{16,8},{24,0},{1,25},{9,17},{17,9},{25,1},{2,26},{10... | collective-permute-start | bytes 786440 | tf_op jit(solution)/shard_map/ppermute | solution.py:143
  267.0 49.9 %collective-permute-start.21 = (bf16[2,384,512]{2,1,0:T(8,128)(2,1)}, bf16[2,384,512]{2,1,0:T(8,128)(2,1)}, u32[]{:S(2)}, u32[]{:S(2)}) collective-permute-start(bf16[2,384,512]{2,1,0:T(8,128)(2,1)} %slice_bitcast_fusion.2), channel_id=1, source_target_pairs={{0,4},{4,0},{1,5},{5,1},{2,6},{6,2},{3,7},{7,3},{8,12},{12,8},{9,1... | collective-permute-start | bytes 2359304 | tf_op jit(solution)/shard_map/ppermute | solution.py:143
  268.5 48.5 %collective-permute-start.23 = (bf16[2,384,512]{2,1,0:T(8,128)(2,1)}, bf16[2,384,512]{2,1,0:T(8,128)(2,1)}, u32[]{:S(2)}, u32[]{:S(2)}) collective-permute-start(bf16[2,384,512]{2,1,0:T(8,128)(2,1)} %slice_bitcast_fusion), channel_id=1, source_target_pairs={{0,2},{2,0},{1,3},{3,1},{4,6},{6,4},{5,7},{7,5},{8,10},{10,8},{9,1... | collective-permute-start | bytes 2359304 | tf_op jit(solution)/shard_map/ppermute | solution.py:143
  301.4 65.6 %all-to-all-start.3 = ((bf16[8,3,2,128,128]{4,3,2,1,0:T(8,128)(2,1)}), bf16[8,3,2,128,128]{4,3,2,1,0:T(8,128)(2,1)}, u32[]{:S(2)}, u32[]{:S(2)}) async-start(bf16[8,3,2,128,128]{4,3,2,1,0:T(8,128)(2,1)} %attend_backward.1.grads_ref), calls=%async_computation.3 | async-start | bytes 3145728 | tf_op jit(solution)/shard_map/all_to_all | solution.py:668
  316.8 5.0 %collective-permute-start.25 = (bf16[512,896]{1,0:T(8,128)(2,1)S(1)}, bf16[512,896]{1,0:T(8,128)(2,1)S(1)}, u32[]{:S(2)}, u32[]{:S(2)}) collective-permute-start(bf16[512,896]{1,0:T(8,128)(2,1)S(1)} %slice.281), channel_id=1, source_target_pairs={{0,1},{1,0},{2,3},{3,2},{4,5},{5,4},{6,7},{7,6},{8,9},{9,8},{10,11... | collective-permute-start | bytes 2752520 | tf_op jit(solution)/shard_map/ppermute | solution.py:143
  318.9 26.6 %collective-permute-start.24 = (bf16[384,512]{1,0:T(8,128)(2,1)S(1)}, bf16[384,512]{1,0:T(8,128)(2,1)S(1)}, u32[]{:S(2)}, u32[]{:S(2)}) collective-permute-start(bf16[384,512]{1,0:T(8,128)(2,1)S(1)} %slice_bitcast_fusion.4), channel_id=1, source_target_pairs={{0,4},{4,0},{1,5},{5,1},{2,6},{6,2},{3,7},{7,3},{8,12},{12,8},{9,1... | collective-permute-start | bytes 1179656 | tf_op jit(solution)/shard_map/ppermute | solution.py:143
  320.4 25.2 %collective-permute-start.22 = (bf16[384,512]{1,0:T(8,128)(2,1)S(1)}, bf16[384,512]{1,0:T(8,128)(2,1)S(1)}, u32[]{:S(2)}, u32[]{:S(2)}) collective-permute-start(bf16[384,512]{1,0:T(8,128)(2,1)S(1)} %slice_bitcast_fusion.6), channel_id=1, source_target_pairs={{0,2},{2,0},{1,3},{3,1},{4,6},{6,4},{5,7},{7,5},{8,10},{10,8},{9,1... | collective-permute-start | bytes 1179656 | tf_op jit(solution)/shard_map/ppermute | solution.py:143
  322.1 35.9 %collective-permute-start.26 = (bf16[256,896]{1,0:T(8,128)(2,1)S(1)}, bf16[256,896]{1,0:T(8,128)(2,1)S(1)}, u32[]{:S(2)}, u32[]{:S(2)}) collective-permute-start(bf16[256,896]{1,0:T(8,128)(2,1)S(1)} %slice.283), channel_id=1, source_target_pairs={{0,2},{2,0},{1,3},{3,1},{4,6},{6,4},{5,7},{7,5},{8,10},{10,8},{9,1... | collective-permute-start | bytes 1376264 | tf_op jit(solution)/shard_map/ppermute | solution.py:143
  345.8 12.5 %collective-permute-start.28 = (bf16[96,1024]{1,0:T(8,128)(2,1)S(1)}, bf16[96,1024]{1,0:T(8,128)(2,1)S(1)}, u32[]{:S(2)}, u32[]{:S(2)}) collective-permute-start(bf16[96,1024]{1,0:T(8,128)(2,1)S(1)} %get-tuple-element.114), channel_id=1, source_target_pairs={{0,8},{8,0},{16,24},{24,16},{1,9},{9,1},{17,25},{25,17},{2,10},{10... | collective-permute-start | bytes 589832 | tf_op jit(solution)/shard_map/ppermute | solution.py:143
  345.9 16.1 %collective-permute-start.29 = (bf16[96,1024]{1,0:T(8,128)(2,1)S(1)}, bf16[96,1024]{1,0:T(8,128)(2,1)S(1)}, u32[]{:S(2)}, u32[]{:S(2)}) collective-permute-start(bf16[96,1024]{1,0:T(8,128)(2,1)S(1)} %get-tuple-element.115), channel_id=1, source_target_pairs={{0,16},{8,24},{16,0},{24,8},{1,17},{9,25},{17,1},{25,9},{2,18},{10... | collective-permute-start | bytes 589832 | tf_op jit(solution)/shard_map/ppermute | solution.py:143
  348.8 16.7 %collective-permute-start.30 = (bf16[96,1024]{1,0:T(8,128)(2,1)S(1)}, bf16[96,1024]{1,0:T(8,128)(2,1)S(1)}, u32[]{:S(2)}, u32[]{:S(2)}) collective-permute-start(bf16[96,1024]{1,0:T(8,128)(2,1)S(1)} %get-tuple-element.116), channel_id=1, source_target_pairs={{0,24},{8,16},{16,8},{24,0},{1,25},{9,17},{17,9},{25,1},{2,26},{10... | collective-permute-start | bytes 589832 | tf_op jit(solution)/shard_map/ppermute | solution.py:143
  358.2 8.1 %collective-permute-start.27 = (bf16[128,896]{1,0:T(8,128)(2,1)S(1)}, bf16[128,896]{1,0:T(8,128)(2,1)S(1)}, u32[]{:S(2)}, u32[]{:S(2)}) collective-permute-start(bf16[128,896]{1,0:T(8,128)(2,1)S(1)} %slice.285), channel_id=1, source_target_pairs={{0,4},{4,0},{1,5},{5,1},{2,6},{6,2},{3,7},{7,3},{8,12},{12,8},{9,1... | collective-permute-start | bytes 688136 | tf_op jit(solution)/shard_map/ppermute | solution.py:143
  367.1 5.0 %collective-permute-start.31 = (bf16[64,1024]{1,0:T(8,128)(2,1)S(1)}, bf16[64,1024]{1,0:T(8,128)(2,1)S(1)}, u32[]{:S(2)}, u32[]{:S(2)}) collective-permute-start(bf16[64,1024]{1,0:T(8,128)(2,1)S(1)} %slice.246), channel_id=1, source_target_pairs={{0,4},{4,0},{1,5},{5,1},{2,6},{6,2},{3,7},{7,3},{8,12},{12,8},{9,1... | collective-permute-start | bytes 393224 | tf_op jit(solution)/shard_map/ppermute | solution.py:143
  367.2 19.8 %all-to-all-start.4 = ((bf16[4,32,896]{2,1,0:T(8,128)(2,1)}), bf16[4,32,896]{2,1,0:T(8,128)(2,1)S(1)}, u32[]{:S(2)}, u32[]{:S(2)}) async-start(bf16[4,32,896]{2,1,0:T(8,128)(2,1)} %bitcast.80), calls=%async_computation.4 | async-start | bytes 458752 | tf_op jit(solution)/shard_map/all_to_all | solution.py:744
  372.2 14.2 %collective-permute-start.32 = (bf16[32,1024]{1,0:T(8,128)(2,1)S(1)}, bf16[32,1024]{1,0:T(8,128)(2,1)S(1)}, u32[]{:S(2)}, u32[]{:S(2)}) collective-permute-start(bf16[32,1024]{1,0:T(8,128)(2,1)S(1)} %slice.305), channel_id=1, source_target_pairs={{0,2},{2,0},{1,3},{3,1},{4,6},{6,4},{5,7},{7,5},{8,10},{10,8},{9,1... | collective-permute-start | bytes 196616 | tf_op jit(solution)/shard_map/ppermute | solution.py:143
  376.2 14.6 %collective-permute-start.33 = (bf16[32,6144]{1,0:T(8,128)(2,1)S(1)}, bf16[32,6144]{1,0:T(8,128)(2,1)S(1)}, u32[]{:S(2)}, u32[]{:S(2)}) collective-permute-start(bf16[32,6144]{1,0:T(8,128)(2,1)S(1)} %get-tuple-element.99), channel_id=1, source_target_pairs={{0,8},{8,0},{16,24},{24,16},{1,9},{9,1},{17,25},{25,17},{2,10},{10... | collective-permute-start | bytes 1179656 | tf_op jit(solution)/shard_map/ppermute | solution.py:143
  376.2 29.7 %collective-permute-start.34 = (bf16[32,6144]{1,0:T(8,128)(2,1)S(1)}, bf16[32,6144]{1,0:T(8,128)(2,1)S(1)}, u32[]{:S(2)}, u32[]{:S(2)}) collective-permute-start(bf16[32,6144]{1,0:T(8,128)(2,1)S(1)} %get-tuple-element.98), channel_id=1, source_target_pairs={{0,16},{8,24},{16,0},{24,8},{1,17},{9,25},{17,1},{25,9},{2,18},{10... | collective-permute-start | bytes 1179656 | tf_op jit(solution)/shard_map/ppermute | solution.py:143
  379.5 32.0 %collective-permute-start.35 = (bf16[32,6144]{1,0:T(8,128)(2,1)S(1)}, bf16[32,6144]{1,0:T(8,128)(2,1)}, u32[]{:S(2)}, u32[]{:S(2)}) collective-permute-start(bf16[32,6144]{1,0:T(8,128)(2,1)S(1)} %get-tuple-element.97), channel_id=1, source_target_pairs={{0,24},{8,16},{16,8},{24,0},{1,25},{9,17},{17,9},{25,1},{2,26},{10... | collective-permute-start | bytes 1179656 | tf_op jit(solution)/shard_map/ppermute | solution.py:143
  387.7 28.2 %copy-start.18 = (f32[32,1024]{1,0:T(8,128)}, f32[32,1024]{1,0:T(8,128)S(1)}, u32[]{:S(2)}) copy-start(f32[32,1024]{1,0:T(8,128)S(1)} %squeeze.34) | copy-start | bytes 393220
  388.1 27.9 %copy-start.19 = (f32[32,1024]{1,0:T(8,128)}, f32[32,1024]{1,0:T(8,128)S(1)}, u32[]{:S(2)}) copy-start(f32[32,1024]{1,0:T(8,128)S(1)} %squeeze.33) | copy-start | bytes 393220
  389.0 27.0 %copy-start.20 = (f32[32,1024]{1,0:T(8,128)}, f32[32,1024]{1,0:T(8,128)S(1)}, u32[]{:S(2)}) copy-start(f32[32,1024]{1,0:T(8,128)S(1)} %squeeze.32) | copy-start | bytes 393220
  (29 other events, 126.4 us)
Sparse Core Ops, SparseCore 0:
  36.9 66.9 all-gather.6
  105.8 72.1 all-gather.8
  195.8 44.3 all-gather.10
  243.0 116.9 reduce-scatter.3

commit v6 on v5

--- a/solution.py
+++ b/solution.py
@@ -196,32 +196,48 @@
 
 
 def front_kernel(
-    x_ref, first_ref, gain_ref, cos_ref, sin_ref, weight_ref, normed_ref, qkv_ref, att_ref, total_ref
+    x_ref, first_ref, gain_ref, cos_ref, sin_ref, weight_ref, normed_out, qkv_out, att_ref, total_ref, weights, normed_ref,
+    qkv_ref, left,
 ):
     parts, rows, width = x_ref.shape
+    units = first_ref.shape[1]
     per_block = BLOCK // rows
     blocks = parts // per_block
     gain = gain_ref[...]
+    for kind in range(3):
+        for unit in range(units):
+            at = (kind * units + unit) * PAIR
+            weights[:, at : at + PAIR] = weight_ref[3 * unit + kind]
+    wide = units * PAIR
     for block in range(blocks):
         lo, hi = block * per_block, (block + 1) * per_block
-
-        @pl.when(pl.program_id(0) == 0)
-        def _(lo=lo, hi=hi):
-            x = x_ref[lo:hi].reshape(BLOCK, width).astype(F32)
-            inv = lax.rsqrt(jnp.mean(x * x, axis=-1, keepdims=True) + EPSILON)
-            normed_ref[lo:hi] = (x * inv * gain).astype(BF16).reshape(per_block, rows, width)
-
-        normed = normed_ref[lo:hi].reshape(BLOCK, width)
-        cos = cos_ref[block * BLOCK : (block + 1) * BLOCK, :]
-        sin = sin_ref[block * BLOCK : (block + 1) * BLOCK, :]
-        for kind in range(2):
-            value = dot(normed, weight_ref[kind])
-            value = (value * cos + partner(value) * sin).astype(BF16)
-            qkv_ref[lo:hi, kind, 0] = value.reshape(per_block, rows, PAIR)
-        first = first_ref[lo:hi, 0].reshape(BLOCK, PAIR).astype(F32)
-        mixed = (0.5 * dot(normed, weight_ref[2]) + 0.5 * first).astype(BF16)
-        qkv_ref[lo:hi, 2, 0] = mixed.reshape(per_block, rows, PAIR)
-    attend_forward_kernel(qkv_ref, att_ref, total_ref)
+        x = x_ref[lo:hi].reshape(BLOCK, width).astype(F32)
+        inv = lax.rsqrt(jnp.mean(x * x, axis=-1, keepdims=True) + EPSILON)
+        normed = (x * inv * gain).astype(BF16)
+        normed_ref[lo:hi] = normed.reshape(per_block, rows, width)
+        values = dot(normed, weights[...])
+        cos = jnp.concatenate([cos_ref[block * BLOCK : (block + 1) * BLOCK, :]] * (2 * units), axis=1)
+        sin = jnp.concatenate([sin_ref[block * BLOCK : (block + 1) * BLOCK, :]] * (2 * units), axis=1)
+        turning = values[:, : 2 * wide]
+        turned = (turning * cos + partner(turning) * sin).astype(BF16)
+        for unit in range(units):
+            lanes = slice(unit * PAIR, (unit + 1) * PAIR)
+            qkv_ref[lo:hi, 0, unit] = turned[:, :wide][:, lanes].reshape(per_block, rows, PAIR)
+            qkv_ref[lo:hi, 1, unit] = turned[:, wide:][:, lanes].reshape(per_block, rows, PAIR)
+            first = first_ref[lo:hi, unit].reshape(BLOCK, PAIR).astype(F32)
+            mixed = (0.5 * values[:, 2 * wide :][:, lanes] + 0.5 * first).astype(BF16)
+            qkv_ref[lo:hi, 2, unit] = mixed.reshape(per_block, rows, PAIR)
+    sent = [
+        pltpu.make_async_copy(normed_ref, normed_out, left.at[0]),
+        pltpu.make_async_copy(qkv_ref, qkv_out, left.at[1]),
+    ]
+    for copy in sent:
+        copy.start()
+    for unit in range(units):
+        one = pl.ds(unit, 1)
+        attend_forward_kernel(qkv_ref.at[:, :, one], att_ref.at[:, one], total_ref.at[one])
+    for copy in sent:
+        copy.wait()
 
 
 def front(x, first, gain, cos, sin, weights):
@@ -229,28 +245,27 @@
     units = first.shape[1]
     length = parts * rows
     blocks = length // BLOCK
+    outside = pl.BlockSpec(memory_space=pl.ANY)
+    normed = (parts, rows, width)
+    qkv = (parts, 3, units, rows, PAIR)
     return pl.pallas_call(
         front_kernel,
-        grid=(units,),
+        grid=(1,),
         in_specs=[
-            pl.BlockSpec((parts, rows, width), lambda u: (0, 0, 0)),
-            pl.BlockSpec((parts, 1, rows, PAIR), lambda u: (0, u, 0, 0)),
-            pl.BlockSpec((1, width), lambda u: (0, 0)),
-            pl.BlockSpec((length, PAIR), lambda u: (0, 0)),
-            pl.BlockSpec((length, PAIR), lambda u: (0, 0)),
-            pl.BlockSpec((3, width, PAIR), lambda u: (u, 0, 0)),
+            still(*normed), still(*first.shape), still(1, width), still(length, PAIR), still(length, PAIR), still(*weights.shape),
         ],
-        out_specs=[
-            pl.BlockSpec((parts, rows, width), lambda u: (0, 0, 0)),
-            pl.BlockSpec((parts, 3, 1, rows, PAIR), lambda u: (0, 0, u, 0, 0)),
-            pl.BlockSpec((parts, 1, rows, PAIR), lambda u: (0, u, 0, 0)),
-            pl.BlockSpec((1, 2, blocks, BLOCK), lambda u: (u, 0, 0, 0)),
+        out_specs=[outside, outside, still(*first.shape), still(units, 2, blocks, BLOCK)],
+        out_shape=[
+            jax.ShapeDtypeStruct(normed, BF16),
+            jax.ShapeDtypeStruct(qkv, BF16),
+            jax.ShapeDtypeStruct(first.shape, BF16),
+            jax.ShapeDtypeStruct((units, 2, blocks, BLOCK), F32),
         ],
-        out_shape=[
-            jax.ShapeDtypeStruct((parts, rows, width), BF16),
-            jax.ShapeDtypeStruct((parts, 3, units, rows, PAIR), BF16),
-            jax.ShapeDtypeStruct((parts, units, rows, PAIR), BF16),
-            jax.ShapeDtypeStruct((units, 2, blocks, BLOCK), F32),
+        scratch_shapes=[
+            pltpu.VMEM((width, 3 * units * PAIR), BF16),
+            pltpu.VMEM(normed, BF16),
+            pltpu.VMEM(qkv, BF16),
+            pltpu.SemaphoreType.DMA((2,)),
         ],
         compiler_params=params(),
         name="front",
@@ -278,8 +293,9 @@
 
 def mlp_kernel(
     x_ref, heads_ref, gain_ref, teacher_ref, cotangent_ref, valid_ref, rate_ref, gate_out, up_down,
-    att_ref, normed_ref, act_ref, result_ref, grad_low_ref, loss_ref, grads_ref, grad_hidden_ref, branch_ref, out_heads_ref,
-    wo, wg, wu, wd, gates, ups, hidden_ref, total, arrived,
+    att_out, normed_out, act_out, result_out, grad_low_out, grads_out, loss_ref, grad_hidden_ref, branch_ref, out_heads_ref,
+    wo, wg, wu, wd, gates, ups, hidden_ref, total, att_ref, normed_ref, act_ref, result_ref, grad_low_ref, grads_ref,
+    arrived, left,
 ):
     tokens, width = x_ref.shape
     steps, _, sides, _, wide = wg.shape
@@ -293,14 +309,33 @@
         )
 
     def copies(step):
-        lanes = pl.ds(pl.multiple_of(step * wide, wide), wide)
+        lanes = pl.ds(step * wide, wide)
         rows = pl.ds(step % per * deep, deep)
-        across = pl.ds(pl.multiple_of((parts + step // per) * width, width), width)
+        across = pl.ds((parts + step // per) * width, width)
         return (
             pltpu.make_async_copy(gate_out.at[:, :, :, lanes], wg.at[step], arrived.at[3 * step]),
             pltpu.make_async_copy(up_down.at[:, :, :, lanes], wu.at[step], arrived.at[3 * step + 1]),
             pltpu.make_async_copy(up_down.at[:, rows, :, across], wd.at[step], arrived.at[3 * step + 2]),
         )
+
+    sent = [
+        pltpu.make_async_copy(source, target, left.at[at])
+        for at, (source, target) in enumerate(
+            (
+                (att_ref, att_out),
+                (normed_ref, normed_out),
+                (act_ref, act_out),
+                (result_ref, result_out),
+                (grad_low_ref, grad_low_out),
+            )
+        )
+    ]
+    sent += [
+        pltpu.make_async_copy(
+            grads_ref.at[step], grads_out.at[:, pl.ds(2 * step * wide, 2 * wide)], left.at[5 + step]
+        )
+        for step in range(steps)
+    ]
 
     output_copy().start()
     for step in range(steps):
@@ -316,8 +351,10 @@
     hidden_ref[...] = hidden
     result_ref[...] = hidden
     normed_ref[...] = (hidden * inv * gain_ref[...]).astype(BF16)
-
-    def forward(step, carry):
+    sent[0].start()
+    sent[1].start()
+
+    for step in range(steps):
         for copy in copies(step):
             copy.wait()
         gate = dot_sections(normed_ref[...], wg.at[step])
@@ -325,16 +362,17 @@
         act = (gate * jax.nn.sigmoid(gate) * up).astype(BF16)
         gates[step] = gate
         ups[step] = up
-        act_ref[:, pl.ds(pl.multiple_of(step * wide, wide), wide)] = act
+        act_ref[:, step * wide : (step + 1) * wide] = act
         result_ref[...] += dot_sections(act, wd.at[step])
-        return carry
-
-    lax.fori_loop(0, steps, forward, 0)
+
+    sent[2].start()
+    sent[3].start()
     error = result_ref[...] - teacher_ref[...].astype(F32)
     valid = valid_ref[...]
     grad = cotangent_ref[...].astype(F32) + rate_ref[0:1, 0:1] * valid * error
     grad_hidden_ref[...] = grad
     grad_low_ref[...] = grad.astype(BF16)
+    sent[4].start()
     losses = jnp.sum(error * error * (valid / width), axis=0, keepdims=True)
     loss = losses[:, :PAIR]
     for at in range(PAIR, width, PAIR):
@@ -342,20 +380,18 @@
     loss_ref[...] = loss
     total[...] = jnp.zeros_like(total)
 
-    def backward(step, carry):
+    for step in range(steps):
         gate = gates[step]
         up = ups[step]
         sigmoid = jax.nn.sigmoid(gate)
         grad_act = dot_t_sections(grad_low_ref[...], wd.at[step])
         grad_gate = (grad_act * up * (sigmoid * (1.0 + gate * (1.0 - sigmoid)))).astype(BF16)
         grad_up = (grad_act * (gate * sigmoid)).astype(BF16)
-        at = pl.multiple_of(2 * step * wide, 2 * wide)
-        grads_ref[:, pl.ds(at, wide)] = grad_gate
-        grads_ref[:, pl.ds(pl.multiple_of(at + wide, wide), wide)] = grad_up
+        grads_ref[step, :, :wide] = grad_gate
+        grads_ref[step, :, wide:] = grad_up
+        sent[5 + step].start()
         total[...] += dot_t_sections(grad_gate, wg.at[step]) + dot_t_sections(grad_up, wu.at[step])
-        return carry
-
-    lax.fori_loop(0, steps, backward, 0)
+
     hidden = hidden_ref[...]
     inv = lax.rsqrt(jnp.mean(hidden * hidden, axis=-1, keepdims=True) + EPSILON)
     scaled = hidden * inv
@@ -371,6 +407,8 @@
     for pair in range(width // PAIR):
         at, unit = divmod(pair, units)
         out_heads_ref[at, :, unit] = value[:, pair * PAIR : (pair + 1) * PAIR].reshape(batch, rows, PAIR)
+    for copy in sent:
+        copy.wait()
 
 
 def still(*shape):
@@ -395,17 +433,15 @@
         grid=(1,),
         in_specs=[whole, still(*heads.shape), still(1, width), whole, whole, still(tokens, 1), still(1, PAIR)]
         + [outside, outside],
-        out_specs=[
-            whole, whole, still(*hidden), whole, whole, still(1, PAIR), still(*grads), whole, whole, still(*heads.shape),
-        ],
+        out_specs=[outside] * 6 + [still(1, PAIR), whole, whole, still(*heads.shape)],
         out_shape=[
             low,
             low,
             jax.ShapeDtypeStruct(hidden, BF16),
             full,
             low,
+            jax.ShapeDtypeStruct(grads, BF16),
             jax.ShapeDtypeStruct((1, PAIR), F32),
-            jax.ShapeDtypeStruct(grads, BF16),
             full,
             low,
             jax.ShapeDtypeStruct(heads.shape, BF16),
@@ -419,7 +455,14 @@
             pltpu.VMEM((steps, tokens, wide), F32),
             pltpu.VMEM((tokens, width), F32),
             pltpu.VMEM((tokens, width), F32),
+            pltpu.VMEM((tokens, width), BF16),
+            pltpu.VMEM((tokens, width), BF16),
+            pltpu.VMEM(hidden, BF16),
+            pltpu.VMEM((tokens, width), F32),
+            pltpu.VMEM((tokens, width), BF16),
+            pltpu.VMEM((steps, tokens, 2 * wide), BF16),
             pltpu.SemaphoreType.DMA((3 * steps + 1,)),
+            pltpu.SemaphoreType.DMA((5 + steps,)),
         ],
         compiler_params=params(),
         name="mlp",
@@ -673,7 +716,7 @@
     x_low = inputs.reshape(tokens, width)
     rate = jnp.full((1, PAIR), 2.0 / width, F32) / valid_total
     (
-        att_low, normed_mlp, activated, result, grad_down_in, loss_row, grads, grad_hidden, grad_branch, grad_heads,
+        att_low, normed_mlp, activated, result, grad_down_in, grads, loss_row, grad_hidden, grad_branch, grad_heads,
     ) = mlp(
         x_low,
         att_heads,

time: 431 us -> 428 us (level)
  Pallas kernels: 69.9 us -> 64.8 us
  transfers between devices with their start and end apart: 45 -> 45, of which waited for: 21 -> 21; matrix products, arithmetic and copies ran while one was open for 16% -> 16% of each run, Pallas kernels for 16% -> 15%
where the time goes in v6:
time: 428 us; the launch traced here: 420 us
  waiting for transfers between devices  193 us (45%)
  starting transfers between devices  68.6 us (16%)
  Pallas kernels  64.8 us (15%)
  other arithmetic  29.6 us (7%)
  matrix products  23.1 us (5%)
  local copies, waits for them, and re-layouts  20.7 us (5%)
  between operations  20.2 us (5%)
    ppermute x36, waiting for transfers between devices, swap(): return lax.ppermute(array, name, [(i, i ^ distance) for i in range(size)])  164 us
    ppermute x36, starting transfers between devices, swap(): return lax.ppermute(array, name, [(i, i ^ distance) for i in range(size)])  39.5 us
    all_to_all x1, waiting for transfers between devices, on_device(): lax.all_to_all(parcel, SEQ, split_axis=0, concat_axis=0, tiled=True)  20.9 us
    pallas_call x1, Pallas kernels, mlp(): pl.pallas_call(mlp_kernel, grid=(1,), in_specs=[whole, still(*heads.shape...  19.3 us
    all_to_all x3, starting transfers between devices, exchange(): return lax.all_to_all(array, SEQ, split_axis=0, concat_axis=0, tiled=True)  17.5 us
    pallas_call x1, Pallas kernels, front(): pl.pallas_call(front_kernel, grid=(1,), in_specs=[still(*normed), still(*...  14 us
    pallas_call x1, Pallas kernels, attend_backward(): pl.pallas_call(attend_backward_kernel, grid=(units,), in_specs=[pl.BlockS...  14 us
    dot_general x6, matrix products, dot(): return jnp.dot(left, right, preferred_element_type=F32)  13.8 us
  transfers between devices with their start and end apart: 45, of which 21 were waited for; matrix products, arithmetic and copies ran while one was open for 16% of the time, Pallas kernels for 15%

profile of v6, /device:TPU:8, one launch (start us, length us, event | category | flops | bytes accessed | tf_op | source)
XLA Modules:
  0.0 420.3 jit_solution(13986904718922508168)
XLA Ops:
  25.0 5.8 %collective-permute-done = bf16[32,4096]{1,0:T(8,128)(2,1)} collective-permute-done((bf16[32,4096]{1,0:T(8,128)(2,1)S(1)}, bf16[32,4096]{1,0:T(8,128)(2,1)}, u32[]{:S(2)}, u32[]{:S(2)}) %collective-permute-start) | collective-permute-done | bytes 262176 | tf_op jit(solution)/shard_map/ppermute | solution.py:143
  30.8 3.6 collective-permute-done.1
  37.3 4.4 %collective-permute-start.5 = (bf16[32,6144]{1,0:T(8,128)(2,1)S(1)}, bf16[32,6144]{1,0:T(8,128)(2,1)S(1)}, u32[]{:S(2)}, u32[]{:S(2)}) collective-permute-start(bf16[32,6144]{1,0:T(8,128)(2,1)S(1)} %pad_maximum_fusion.11), channel_id=1, source_target_pairs={{0,16},{8,24},{16,0},{24,8},{1,17},{9,25},{17,1},{25,9},{2,18},{10... | collective-permute-start | bytes 1179656 | tf_op jit(solution)/shard_map/ppermute | solution.py:143
  41.8 24.0 %collective-permute-done.4 = bf16[32,6144]{1,0:T(8,128)(2,1)S(1)} collective-permute-done((bf16[32,6144]{1,0:T(8,128)(2,1)S(1)}, bf16[32,6144]{1,0:T(8,128)(2,1)S(1)}, u32[]{:S(2)}, u32[]{:S(2)}) %collective-permute-start.4) | collective-permute-done | bytes 393248 | tf_op jit(solution)/shard_map/ppermute | solution.py:143
  65.8 4.5 %collective-permute-done.5 = bf16[32,6144]{1,0:T(8,128)(2,1)S(1)} collective-permute-done((bf16[32,6144]{1,0:T(8,128)(2,1)S(1)}, bf16[32,6144]{1,0:T(8,128)(2,1)S(1)}, u32[]{:S(2)}, u32[]{:S(2)}) %collective-permute-start.5) | collective-permute-done | bytes 393248 | tf_op jit(solution)/shard_map/ppermute | solution.py:143
  71.9 7.1 %all-to-all-start = ((bf16[8,480,128]{2,1,0:T(8,128)(2,1)}), bf16[8,480,128]{2,1,0:T(8,128)(2,1)S(1)}, u32[]{:S(2)}, u32[]{:S(2)}) async-start(bf16[8,480,128]{2,1,0:T(8,128)(2,1)} %pad_maximum_fusion.5), calls=%async_computation | async-start | bytes 1966080 | tf_op jit(solution)/shard_map/all_to_all | solution.py:686
  79.0 20.9 %all-to-all-done = bf16[8,480,128]{2,1,0:T(8,128)(2,1)S(1)} async-done(((bf16[8,480,128]{2,1,0:T(8,128)(2,1)}), bf16[8,480,128]{2,1,0:T(8,128)(2,1)S(1)}, u32[]{:S(2)}, u32[]{:S(2)}) %all-to-all-start) | async-done | bytes 983072 | tf_op jit(solution)/shard_map/all_to_all | solution.py:686
  103.6 4.2 %collective-permute-start.8 = (bf16[2,128,1024]{2,1,0:T(8,128)(2,1)}, bf16[2,128,1024]{2,1,0:T(8,128)(2,1)}, u32[]{:S(2)}, u32[]{:S(2)}) collective-permute-start(bf16[2,128,1024]{2,1,0:T(8,128)(2,1)} %pad_maximum_fusion.10), channel_id=1, source_target_pairs={{0,16},{8,24},{16,0},{24,8},{1,17},{9,25},{17,1},{25,9},{2,18},{10... | collective-permute-start | bytes 1572872 | tf_op jit(solution)/shard_map/ppermute | solution.py:143
  107.8 1.7 collective-permute-done.10
  109.8 3.2 fusion.20
  114.0 25.8 %collective-permute-done.7 = bf16[2,128,1024]{2,1,0:T(8,128)(2,1)} collective-permute-done((bf16[2,128,1024]{2,1,0:T(8,128)(2,1)}, bf16[2,128,1024]{2,1,0:T(8,128)(2,1)}, u32[]{:S(2)}, u32[]{:S(2)}) %collective-permute-start.7) | collective-permute-done | bytes 524320 | tf_op jit(solution)/shard_map/ppermute | solution.py:143
  139.8 7.6 %collective-permute-done.8 = bf16[2,128,1024]{2,1,0:T(8,128)(2,1)} collective-permute-done((bf16[2,128,1024]{2,1,0:T(8,128)(2,1)}, bf16[2,128,1024]{2,1,0:T(8,128)(2,1)}, u32[]{:S(2)}, u32[]{:S(2)}) %collective-permute-start.8) | collective-permute-done | bytes 524320 | tf_op jit(solution)/shard_map/ppermute | solution.py:143
  150.9 4.3 %collective-permute-start.13 = (bf16[32,3072]{1,0:T(8,128)(2,1)S(1)}, bf16[32,3072]{1,0:T(8,128)(2,1)S(1)}, u32[]{:S(2)}, u32[]{:S(2)}) collective-permute-start(bf16[32,3072]{1,0:T(8,128)(2,1)S(1)} %pad_maximum_fusion.13), channel_id=1, source_target_pairs={{0,16},{8,24},{16,0},{24,8},{1,17},{9,25},{17,1},{25,9},{2,18},{10... | collective-permute-start | bytes 589832 | tf_op jit(solution)/shard_map/ppermute | solution.py:143
  157.8 1.9 copy.94
  161.2 14.0 %front.1 = (bf16[8,128,1024]{2,1,0:T(8,128)(2,1)}, bf16[8,3,2,128,128]{4,3,2,1,0:T(8,128)(2,1)}, bf16[8,2,128,128]{3,2,1,0:T(8,128)(2,1)}, f32[2,2,4,256]{3,2,1,0:T(4,128)}) custom-call(bf16[8,128,1024]{2,1,0:T(8,128)(2,1)} %bitcast.165, bf16[8,2,128,128]{3,2,1,0:T(8,128)(2,1)} %bitcast.175, f32[1,1024]{1,0:T(1,128)} %get-tuple-element.126.gain_ref, ...), custom_call_target="tpu_custom_call" | custom-call | bytes 56623104 | tf_op jit(solution)/shard_map/front/pallas_call | solution.py:251
  175.2 6.3 %all-to-all-start.1 = ((bf16[8,2,128,128]{3,2,1,0:T(8,128)(2,1)}), bf16[8,2,128,128]{3,2,1,0:T(8,128)(2,1)S(1)}, u32[]{:S(2)}, u32[]{:S(2)}) async-start(bf16[8,2,128,128]{3,2,1,0:T(8,128)(2,1)} %get-tuple-element.58), calls=%async_computation.1 | async-start | bytes 1048576 | tf_op jit(solution)/shard_map/all_to_all | solution.py:711
  183.5 8.5 %all-to-all-done.1 = bf16[8,2,128,128]{3,2,1,0:T(8,128)(2,1)S(1)} async-done(((bf16[8,2,128,128]{3,2,1,0:T(8,128)(2,1)}), bf16[8,2,128,128]{3,2,1,0:T(8,128)(2,1)S(1)}, u32[]{:S(2)}, u32[]{:S(2)}) %all-to-all-start.1) | async-done | bytes 524320 | tf_op jit(solution)/shard_map/all_to_all | solution.py:711
  194.4 19.3 %mlp.1 = (bf16[256,1024]{1,0:T(8,128)(2,1)}, bf16[256,1024]{1,0:T(8,128)(2,1)}, bf16[256,3072]{1,0:T(8,128)(2,1)}, f32[256,1024]{1,0:T(8,128)}, bf16[256,1024]{1...) custom-call(bf16[256,1024]{1,0:T(8,128)(2,1)} %bitcast.169, ...), custom_call_target="tpu_custom_call" | custom-call | bytes 62914560 | tf_op jit(solution)/shard_map/mlp/pallas_call | solution.py:431
  213.7 1.9 fusion.11
  215.8 2.2 convolution_convert_fusion
  218.1 10.1 %collective-permute-done.15 = bf16[512,6144]{1,0:T(8,128)(2,1)S(1)} collective-permute-done((bf16[512,6144]{1,0:T(8,128)(2,1)S(1)}, bf16[512,6144]{1,0:T(8,128)(2,1)S(1)}, u32[]{:S(2)}, u32[]{:S(2)}) %collective-permute-start.15) | collective-permute-done | bytes 6291488 | tf_op jit(solution)/shard_map/ppermute | solution.py:143
  228.2 4.4 %add_convert_fusion = bf16[512,6144]{1,0:T(8,128)(2,1)} fusion(bf16[512,6144]{1,0:T(8,128)(2,1)S(1)} %collective-permute-done.15, bf16[256,6144]{1,0:T(8,128)(2,1)S(1)} %copy-done, bf16[1024,256]{1,0:T(8,128)(2,1)S(1)} %fusion.11), kind=kOutput, calls=%fused_computation | convolution fusion | flops 1620049920 | bytes 15990784 | tf_op jit(solution)/shard_map/dot_general | solution.py:56
  240.2 6.6 %all-to-all-start.2 = ((bf16[8,2,128,128]{3,2,1,0:T(8,128)(2,1)}), bf16[8,2,128,128]{3,2,1,0:T(8,128)(2,1)}, u32[]{:S(2)}, u32[]{:S(2)}) async-start(bf16[8,2,128,128]{3,2,1,0:T(8,128)(2,1)} %bitcast.191), calls=%async_computation.2 | async-start | bytes 1048576 | tf_op jit(solution)/shard_map/all_to_all | solution.py:711
  246.9 2.0 convolution_convert_fusion.8
  252.3 1.7 add_convert_fusion.2
  254.2 2.9 collective-permute-start.18
  257.6 3.1 add_convert_fusion.1
  266.4 9.3 %collective-permute-done.18 = bf16[128,1024]{1,0:T(8,128)(2,1)S(1)} collective-permute-done((bf16[128,1024]{1,0:T(8,128)(2,1)S(1)}, bf16[128,1024]{1,0:T(8,128)(2,1)S(1)}, u32[]{:S(2)}, u32[]{:S(2)}) %collective-permute-start.18) | collective-permute-done | bytes 262176 | tf_op jit(solution)/shard_map/ppermute | solution.py:143
  275.8 7.5 %collective-permute-done.19 = bf16[128,1024]{1,0:T(8,128)(2,1)S(1)} collective-permute-done((bf16[128,1024]{1,0:T(8,128)(2,1)S(1)}, bf16[128,1024]{1,0:T(8,128)(2,1)S(1)}, u32[]{:S(2)}, u32[]{:S(2)}) %collective-permute-start.19) | collective-permute-done | bytes 262176 | tf_op jit(solution)/shard_map/ppermute | solution.py:143
  283.5 14.0 %attend_backward.1.grads_ref = bf16[8,3,2,128,128]{4,3,2,1,0:T(8,128)(2,1)} custom-call(bf16[8,3,2,128,128]{4,3,2,1,0:T(8,128)(2,1)} %get-tuple-element.65.qkv_ref, bf16[8,2,128,128]{3,2,1,0:T(8,128)(2,1)} %all-to-all-done.2.grad_ref, f32[2,2,4,256]{3,2,1,0:T(4,128)} %get-tuple-element.75.total_ref, f32[1024,128]{1,0:T(8,128)} %get-tuple-element.134.cos_ref, ...), custom_call_target="tpu_custom_call" | custom-call | bytes 46137344 | tf_op jit(solution)/shard_map/attend_backward/pallas_call | solution.py:122
  297.5 4.5 %all-to-all-start.3 = ((bf16[8,3,2,128,128]{4,3,2,1,0:T(8,128)(2,1)}), bf16[8,3,2,128,128]{4,3,2,1,0:T(8,128)(2,1)}, u32[]{:S(2)}, u32[]{:S(2)}) async-start(bf16[8,3,2,128,128]{4,3,2,1,0:T(8,128)(2,1)} %attend_backward.1.grads_ref), calls=%async_computation.3 | async-start | bytes 3145728 | tf_op jit(solution)/shard_map/all_to_all | solution.py:711
  302.0 1.8 select_convert_fusion.pick_ref
  303.9 7.7 %head_grads.1 = bf16[1024,896]{1,0:T(8,128)(2,1)} custom-call(bf16[8,128,1024]{2,1,0:T(8,128)(2,1)} %get-tuple-element.64.normed_ref, bf16[8,3,2,128,128]{4,3,2,1,0:T(8,128)(2,1)} %attend_backward.1.grads_ref, f32[1,128]{1,0:T(1,128)} %get-tuple-element.76.loss_ref, bf16[1024,1024]{1,0:T(8,128)(2,1)} %select_convert_fusion.pick_ref), custom_call_target="tpu_custom_call" | custom-call | bytes 25165824 | tf_op jit(solution)/shard_map/head_grads/pallas_call | solution.py:497
  312.9 1.9 fusion.8
  316.8 2.1 collective-permute-start.26
  318.9 22.1 %collective-permute-done.24 = bf16[384,512]{1,0:T(8,128)(2,1)S(1)} collective-permute-done((bf16[384,512]{1,0:T(8,128)(2,1)S(1)}, bf16[384,512]{1,0:T(8,128)(2,1)S(1)}, u32[]{:S(2)}, u32[]{:S(2)}) %collective-permute-start.24) | collective-permute-done | bytes 393248 | tf_op jit(solution)/shard_map/ppermute | solution.py:143
  341.4 2.8 collective-permute-start.29
  344.9 7.5 %collective-permute-done.26 = bf16[256,896]{1,0:T(8,128)(2,1)S(1)} collective-permute-done((bf16[256,896]{1,0:T(8,128)(2,1)S(1)}, bf16[256,896]{1,0:T(8,128)(2,1)S(1)}, u32[]{:S(2)}, u32[]{:S(2)}) %collective-permute-start.26) | collective-permute-done | bytes 458784 | tf_op jit(solution)/shard_map/ppermute | solution.py:143
  352.6 5.3 %collective-permute-done.29 = bf16[96,1024]{1,0:T(8,128)(2,1)S(1)} collective-permute-done((bf16[96,1024]{1,0:T(8,128)(2,1)S(1)}, bf16[96,1024]{1,0:T(8,128)(2,1)S(1)}, u32[]{:S(2)}, u32[]{:S(2)}) %collective-permute-start.29) | collective-permute-done | bytes 196640 | tf_op jit(solution)/shard_map/ppermute | solution.py:143
  357.9 4.0 collective-permute-done.30
  363.7 4.3 %all-to-all-start.4 = ((bf16[4,32,896]{2,1,0:T(8,128)(2,1)}), bf16[4,32,896]{2,1,0:T(8,128)(2,1)S(1)}, u32[]{:S(2)}, u32[]{:S(2)}) async-start(bf16[4,32,896]{2,1,0:T(8,128)(2,1)} %bitcast.80), calls=%async_computation.4 | async-start | bytes 458752 | tf_op jit(solution)/shard_map/all_to_all | solution.py:787
  368.8 2.2 fusion.88
  371.0 3.0 collective-permute-start.34
  374.5 6.7 %last.1 = (f32[256,1024]{1,0:T(8,128)}, f32[256,1024]{1,0:T(8,128)}) custom-call(bf16[4,2,3,2,128,128]{5,4,3,2,1,0:T(8,128)(2,1)} %bitcast.77.heads_ref, bf16[256,1024]{1,0:T(8,128)(2,1)} %bitcast.170, f32[1,1024]{1,0:T(1,128)} %get-tuple-element.126.gain_ref, bf16[8,4,32,3072]{3,2,1,0:T(8,128)(2,1)} %bitcast.167, f32[256,1024]{1,0:T(8,128)} %get-tuple-element.80.grad_hidden_ref), custom_call_target="tpu_custom_call" | custom-call | bytes 22020096 | tf_op jit(solution)/shard_map/last/pallas_call | solution.py:531
  385.1 2.3 collective-permute-done.33.refs_1_
  387.4 13.0 %collective-permute-done.34.refs_2_ = bf16[32,6144]{1,0:T(8,128)(2,1)S(1)} collective-permute-done((bf16[32,6144]{1,0:T(8,128)(2,1)S(1)}, bf16[32,6144]{1,0:T(8,128)(2,1)S(1)}, u32[]{:S(2)}, u32[]{:S(2)}) %collective-permute-start.34) | collective-permute-done | bytes 393248 | tf_op jit(solution)/shard_map/ppermute | solution.py:143
  400.4 7.5 %collective-permute-done.35.refs_3_ = bf16[32,6144]{1,0:T(8,128)(2,1)} collective-permute-done((bf16[32,6144]{1,0:T(8,128)(2,1)S(1)}, bf16[32,6144]{1,0:T(8,128)(2,1)}, u32[]{:S(2)}, u32[]{:S(2)}) %collective-permute-start.35) | collective-permute-done | bytes 393248 | tf_op jit(solution)/shard_map/ppermute | solution.py:143
  407.9 3.1 finish.1
  (235 shorter events, 65.1 us)
Async XLA Ops:
  7.2 186.7 %all-gather.7.cloned.1.call-start = ((), (), s32[]{:S(2)}) async-start(), calls=%async_computation.6 | async-start | bytes 9437184 | tf_op jit(solution)/shard_map/all_gather | solution.py:672
  10.4 20.4 %collective-permute-start = (bf16[32,4096]{1,0:T(8,128)(2,1)S(1)}, bf16[32,4096]{1,0:T(8,128)(2,1)}, u32[]{:S(2)}, u32[]{:S(2)}) collective-permute-start(bf16[32,4096]{1,0:T(8,128)(2,1)S(1)} %constant_dynamic-update-slice_fusion), channel_id=1, source_target_pairs={{0,24},{8,16},{16,8},{24,0},{1,25},{9,17},{17,9},{25,1},{2,26},{10... | collective-permute-start | bytes 786440 | tf_op jit(solution)/shard_map/ppermute | solution.py:143
  12.0 22.4 %collective-permute-start.1 = (bf16[32,4096]{1,0:T(8,128)(2,1)S(1)}, bf16[32,4096]{1,0:T(8,128)(2,1)}, u32[]{:S(2)}, u32[]{:S(2)}) collective-permute-start(bf16[32,4096]{1,0:T(8,128)(2,1)S(1)} %constant_dynamic-update-slice_fusion), channel_id=1, source_target_pairs={{0,16},{8,24},{16,0},{24,8},{1,17},{9,25},{17,1},{25,9},{2,18},{10... | collective-permute-start | bytes 786440 | tf_op jit(solution)/shard_map/ppermute | solution.py:143
  13.1 21.3 %collective-permute-start.2 = (bf16[32,4096]{1,0:T(8,128)(2,1)S(1)}, bf16[32,4096]{1,0:T(8,128)(2,1)}, u32[]{:S(2)}, u32[]{:S(2)}) collective-permute-start(bf16[32,4096]{1,0:T(8,128)(2,1)S(1)} %constant_dynamic-update-slice_fusion), channel_id=1, source_target_pairs={{0,8},{8,0},{16,24},{24,16},{1,9},{9,1},{17,25},{25,17},{2,10},{10... | collective-permute-start | bytes 786440 | tf_op jit(solution)/shard_map/ppermute | solution.py:143
  15.2 21.5 %collective-permute-start.3 = (bf16[128,1024]{1,0:T(8,128)(2,1)}, bf16[128,1024]{1,0:T(8,128)(2,1)}, u32[]{:S(2)}, u32[]{:S(2)}) collective-permute-start(bf16[128,1024]{1,0:T(8,128)(2,1)} %get-tuple-element.130), channel_id=1, source_target_pairs={{0,4},{4,0},{1,5},{5,1},{2,6},{6,2},{3,7},{7,3},{8,12},{12,8},{9,1... | collective-permute-start | bytes 786440 | tf_op jit(solution)/shard_map/ppermute | solution.py:143
  36.8 157.1 %all-gather.9.cloned.1.call-start = ((), (), s32[]{:S(2)}) async-start(), calls=%async_computation.7 | async-start | bytes 14155776 | tf_op jit(solution)/shard_map/all_gather | solution.py:672
  36.8 29.0 %collective-permute-start.4 = (bf16[32,6144]{1,0:T(8,128)(2,1)S(1)}, bf16[32,6144]{1,0:T(8,128)(2,1)S(1)}, u32[]{:S(2)}, u32[]{:S(2)}) collective-permute-start(bf16[32,6144]{1,0:T(8,128)(2,1)S(1)} %pad_maximum_fusion.11), channel_id=1, source_target_pairs={{0,24},{8,16},{16,8},{24,0},{1,25},{9,17},{17,9},{25,1},{2,26},{10... | collective-permute-start | bytes 1179656 | tf_op jit(solution)/shard_map/ppermute | solution.py:143
  37.3 33.0 %collective-permute-start.5 = (bf16[32,6144]{1,0:T(8,128)(2,1)S(1)}, bf16[32,6144]{1,0:T(8,128)(2,1)S(1)}, u32[]{:S(2)}, u32[]{:S(2)}) collective-permute-start(bf16[32,6144]{1,0:T(8,128)(2,1)S(1)} %pad_maximum_fusion.11), channel_id=1, source_target_pairs={{0,16},{8,24},{16,0},{24,8},{1,17},{9,25},{17,1},{25,9},{2,18},{10... | collective-permute-start | bytes 1179656 | tf_op jit(solution)/shard_map/ppermute | solution.py:143
  41.7 28.6 %collective-permute-start.6 = (bf16[32,6144]{1,0:T(8,128)(2,1)S(1)}, bf16[32,6144]{1,0:T(8,128)(2,1)S(1)}, u32[]{:S(2)}, u32[]{:S(2)}) collective-permute-start(bf16[32,6144]{1,0:T(8,128)(2,1)S(1)} %pad_maximum_fusion.11), channel_id=1, source_target_pairs={{0,8},{8,0},{16,24},{24,16},{1,9},{9,1},{17,25},{25,17},{2,10},{10... | collective-permute-start | bytes 1179656 | tf_op jit(solution)/shard_map/ppermute | solution.py:143
  71.9 28.0 %all-to-all-start = ((bf16[8,480,128]{2,1,0:T(8,128)(2,1)}), bf16[8,480,128]{2,1,0:T(8,128)(2,1)S(1)}, u32[]{:S(2)}, u32[]{:S(2)}) async-start(bf16[8,480,128]{2,1,0:T(8,128)(2,1)} %pad_maximum_fusion.5), calls=%async_computation | async-start | bytes 1966080 | tf_op jit(solution)/shard_map/all_to_all | solution.py:686
  100.0 9.6 %collective-permute-start.10 = (bf16[7,8,32,128]{3,2,0,1:T(8,128)(2,1)S(1)}, bf16[7,8,32,128]{3,2,0,1:T(8,128)(2,1)S(1)}, u32[]{:S(2)}, u32[]{:S(2)}) collective-permute-start(bf16[7,8,32,128]{3,2,0,1:T(8,128)(2,1)S(1)} %bitcast.178), channel_id=1, source_target_pairs={{0,2},{2,0},{1,3},{3,1},{4,6},{6,4},{5,7},{7,5},{8,10},{10,8},{9,1... | collective-permute-start | bytes 1376264 | tf_op jit(solution)/shard_map/ppermute | solution.py:143
  103.4 36.4 %collective-permute-start.7 = (bf16[2,128,1024]{2,1,0:T(8,128)(2,1)}, bf16[2,128,1024]{2,1,0:T(8,128)(2,1)}, u32[]{:S(2)}, u32[]{:S(2)}) collective-permute-start(bf16[2,128,1024]{2,1,0:T(8,128)(2,1)} %pad_maximum_fusion.10), channel_id=1, source_target_pairs={{0,24},{8,16},{16,8},{24,0},{1,25},{9,17},{17,9},{25,1},{2,26},{10... | collective-permute-start | bytes 1572872 | tf_op jit(solution)/shard_map/ppermute | solution.py:143
  103.6 43.9 %collective-permute-start.8 = (bf16[2,128,1024]{2,1,0:T(8,128)(2,1)}, bf16[2,128,1024]{2,1,0:T(8,128)(2,1)}, u32[]{:S(2)}, u32[]{:S(2)}) collective-permute-start(bf16[2,128,1024]{2,1,0:T(8,128)(2,1)} %pad_maximum_fusion.10), channel_id=1, source_target_pairs={{0,16},{8,24},{16,0},{24,8},{1,17},{9,25},{17,1},{25,9},{2,18},{10... | collective-permute-start | bytes 1572872 | tf_op jit(solution)/shard_map/ppermute | solution.py:143
  107.8 39.6 %collective-permute-start.9 = (bf16[2,128,1024]{2,1,0:T(8,128)(2,1)}, bf16[2,128,1024]{2,1,0:T(8,128)(2,1)}, u32[]{:S(2)}, u32[]{:S(2)}) collective-permute-start(bf16[2,128,1024]{2,1,0:T(8,128)(2,1)} %pad_maximum_fusion.10), channel_id=1, source_target_pairs={{0,8},{8,0},{16,24},{24,16},{1,9},{9,1},{17,25},{25,17},{2,10},{10... | collective-permute-start | bytes 1572872 | tf_op jit(solution)/shard_map/ppermute | solution.py:143
  109.7 46.6 %collective-permute-start.11 = (bf16[7,8,2,32,128]{4,3,0,1,2:T(8,128)(2,1)S(1)}, bf16[7,8,2,32,128]{4,3,0,1,2:T(8,128)(2,1)}, u32[]{:S(2)}, u32[]{:S(2)}) collective-permute-start(bf16[7,8,2,32,128]{4,3,0,1,2:T(8,128)(2,1)S(1)} %pad_maximum_fusion.6), channel_id=1, source_target_pairs={{0,1},{1,0},{2,3},{3,2},{4,5},{5,4},{6,7},{7,6},{8,9},{9,8},{10,11... | collective-permute-start | bytes 2752520 | tf_op jit(solution)/shard_map/ppermute | solution.py:143
  150.6 30.9 %collective-permute-start.12 = (bf16[32,3072]{1,0:T(8,128)(2,1)S(1)}, bf16[32,3072]{1,0:T(8,128)(2,1)S(1)}, u32[]{:S(2)}, u32[]{:S(2)}) collective-permute-start(bf16[32,3072]{1,0:T(8,128)(2,1)S(1)} %pad_maximum_fusion.13), channel_id=1, source_target_pairs={{0,24},{8,16},{16,8},{24,0},{1,25},{9,17},{17,9},{25,1},{2,26},{10... | collective-permute-start | bytes 589832 | tf_op jit(solution)/shard_map/ppermute | solution.py:143
  150.9 30.6 %collective-permute-start.13 = (bf16[32,3072]{1,0:T(8,128)(2,1)S(1)}, bf16[32,3072]{1,0:T(8,128)(2,1)S(1)}, u32[]{:S(2)}, u32[]{:S(2)}) collective-permute-start(bf16[32,3072]{1,0:T(8,128)(2,1)S(1)} %pad_maximum_fusion.13), channel_id=1, source_target_pairs={{0,16},{8,24},{16,0},{24,8},{1,17},{9,25},{17,1},{25,9},{2,18},{10... | collective-permute-start | bytes 589832 | tf_op jit(solution)/shard_map/ppermute | solution.py:143
  155.2 26.3 %collective-permute-start.14 = (bf16[32,3072]{1,0:T(8,128)(2,1)S(1)}, bf16[32,3072]{1,0:T(8,128)(2,1)}, u32[]{:S(2)}, u32[]{:S(2)}) collective-permute-start(bf16[32,3072]{1,0:T(8,128)(2,1)S(1)} %pad_maximum_fusion.13), channel_id=1, source_target_pairs={{0,8},{8,0},{16,24},{24,16},{1,9},{9,1},{17,25},{25,17},{2,10},{10... | collective-permute-start | bytes 589832 | tf_op jit(solution)/shard_map/ppermute | solution.py:143
  175.2 16.8 %all-to-all-start.1 = ((bf16[8,2,128,128]{3,2,1,0:T(8,128)(2,1)}), bf16[8,2,128,128]{3,2,1,0:T(8,128)(2,1)S(1)}, u32[]{:S(2)}, u32[]{:S(2)}) async-start(bf16[8,2,128,128]{3,2,1,0:T(8,128)(2,1)} %get-tuple-element.58), calls=%async_computation.1 | async-start | bytes 1048576 | tf_op jit(solution)/shard_map/all_to_all | solution.py:711
  181.5 102.0 %all-gather.11.cloned.1.call-start = ((), (), s32[]{:S(2)}) async-start(), calls=%async_computation.8 | async-start | bytes 7077888 | tf_op jit(solution)/shard_map/all_gather | solution.py:672
  192.1 171.5 %reduce-scatter.4.cloned.1.call-start = ((), (), s32[]{:S(2)}) async-start(), calls=%async_computation.9 | async-start | bytes 7864320
  218.0 10.2 %collective-permute-start.15 = (bf16[512,6144]{1,0:T(8,128)(2,1)S(1)}, bf16[512,6144]{1,0:T(8,128)(2,1)S(1)}, u32[]{:S(2)}, u32[]{:S(2)}) collective-permute-start(bf16[512,6144]{1,0:T(8,128)(2,1)S(1)} %convolution_convert_fusion), channel_id=1, source_target_pairs={{0,1},{1,0},{2,3},{3,2},{4,5},{5,4},{6,7},{7,6},{8,9},{9,8},{10,11... | collective-permute-start | bytes 18874376 | tf_op jit(solution)/shard_map/ppermute | solution.py:143
  237.2 20.4 %collective-permute-start.20 = (bf16[1536,1024]{1,0:T(8,128)(2,1)S(1)}, bf16[1536,1024]{1,0:T(8,128)(2,1)}, u32[]{:S(2)}, u32[]{:S(2)}) collective-permute-start(bf16[1536,1024]{1,0:T(8,128)(2,1)S(1)} %convolution_convert_fusion.1), channel_id=1, source_target_pairs={{0,1},{1,0},{2,3},{3,2},{4,5},{5,4},{6,7},{7,6},{8,9},{9,8},{10,11... | collective-permute-start | bytes 9437192 | tf_op jit(solution)/shard_map/ppermute | solution.py:143
  239.9 12.4 %collective-permute-start.16 = (bf16[512,1024]{1,0:T(8,128)(2,1)}, bf16[512,1024]{1,0:T(8,128)(2,1)}, u32[]{:S(2)}, u32[]{:S(2)}) collective-permute-start(bf16[512,1024]{1,0:T(8,128)(2,1)} %convolution_convert_fusion.2), channel_id=1, source_target_pairs={{0,1},{1,0},{2,3},{3,2},{4,5},{5,4},{6,7},{7,6},{8,9},{9,8},{10,11... | collective-permute-start | bytes 3145736 | tf_op jit(solution)/shard_map/ppermute | solution.py:143
  240.2 43.3 %all-to-all-start.2 = ((bf16[8,2,128,128]{3,2,1,0:T(8,128)(2,1)}), bf16[8,2,128,128]{3,2,1,0:T(8,128)(2,1)}, u32[]{:S(2)}, u32[]{:S(2)}) async-start(bf16[8,2,128,128]{3,2,1,0:T(8,128)(2,1)} %bitcast.191), calls=%async_computation.2 | async-start | bytes 1048576 | tf_op jit(solution)/shard_map/all_to_all | solution.py:711
  254.1 12.4 %collective-permute-start.17 = (bf16[128,1024]{1,0:T(8,128)(2,1)S(1)}, bf16[128,1024]{1,0:T(8,128)(2,1)S(1)}, u32[]{:S(2)}, u32[]{:S(2)}) collective-permute-start(bf16[128,1024]{1,0:T(8,128)(2,1)S(1)} %get-tuple-element.105), channel_id=1, source_target_pairs={{0,8},{8,0},{16,24},{24,16},{1,9},{9,1},{17,25},{25,17},{2,10},{10... | collective-permute-start | bytes 786440 | tf_op jit(solution)/shard_map/ppermute | solution.py:143
  254.2 21.6 %collective-permute-start.18 = (bf16[128,1024]{1,0:T(8,128)(2,1)S(1)}, bf16[128,1024]{1,0:T(8,128)(2,1)S(1)}, u32[]{:S(2)}, u32[]{:S(2)}) collective-permute-start(bf16[128,1024]{1,0:T(8,128)(2,1)S(1)} %get-tuple-element.107), channel_id=1, source_target_pairs={{0,16},{8,24},{16,0},{24,8},{1,17},{9,25},{17,1},{25,9},{2,18},{10... | collective-permute-start | bytes 786440 | tf_op jit(solution)/shard_map/ppermute | solution.py:143
  257.1 26.2 %collective-permute-start.19 = (bf16[128,1024]{1,0:T(8,128)(2,1)S(1)}, bf16[128,1024]{1,0:T(8,128)(2,1)S(1)}, u32[]{:S(2)}, u32[]{:S(2)}) collective-permute-start(bf16[128,1024]{1,0:T(8,128)(2,1)S(1)} %get-tuple-element.106), channel_id=1, source_target_pairs={{0,24},{8,16},{16,8},{24,0},{1,25},{9,17},{17,9},{25,1},{2,26},{10... | collective-permute-start | bytes 786440 | tf_op jit(solution)/shard_map/ppermute | solution.py:143
  262.6 50.3 %collective-permute-start.21 = (bf16[2,384,512]{2,1,0:T(8,128)(2,1)}, bf16[2,384,512]{2,1,0:T(8,128)(2,1)}, u32[]{:S(2)}, u32[]{:S(2)}) collective-permute-start(bf16[2,384,512]{2,1,0:T(8,128)(2,1)} %slice_bitcast_fusion.2), channel_id=1, source_target_pairs={{0,4},{4,0},{1,5},{5,1},{2,6},{6,2},{3,7},{7,3},{8,12},{12,8},{9,1... | collective-permute-start | bytes 2359304 | tf_op jit(solution)/shard_map/ppermute | solution.py:143
  263.9 49.0 %collective-permute-start.23 = (bf16[2,384,512]{2,1,0:T(8,128)(2,1)}, bf16[2,384,512]{2,1,0:T(8,128)(2,1)}, u32[]{:S(2)}, u32[]{:S(2)}) collective-permute-start(bf16[2,384,512]{2,1,0:T(8,128)(2,1)} %slice_bitcast_fusion), channel_id=1, source_target_pairs={{0,2},{2,0},{1,3},{3,1},{4,6},{6,4},{5,7},{7,5},{8,10},{10,8},{9,1... | collective-permute-start | bytes 2359304 | tf_op jit(solution)/shard_map/ppermute | solution.py:143
  297.5 66.1 %all-to-all-start.3 = ((bf16[8,3,2,128,128]{4,3,2,1,0:T(8,128)(2,1)}), bf16[8,3,2,128,128]{4,3,2,1,0:T(8,128)(2,1)}, u32[]{:S(2)}, u32[]{:S(2)}) async-start(bf16[8,3,2,128,128]{4,3,2,1,0:T(8,128)(2,1)} %attend_backward.1.grads_ref), calls=%async_computation.3 | async-start | bytes 3145728 | tf_op jit(solution)/shard_map/all_to_all | solution.py:711
  312.8 3.7 collective-permute-start.25
  314.9 26.1 %collective-permute-start.24 = (bf16[384,512]{1,0:T(8,128)(2,1)S(1)}, bf16[384,512]{1,0:T(8,128)(2,1)S(1)}, u32[]{:S(2)}, u32[]{:S(2)}) collective-permute-start(bf16[384,512]{1,0:T(8,128)(2,1)S(1)} %slice_bitcast_fusion.4), channel_id=1, source_target_pairs={{0,4},{4,0},{1,5},{5,1},{2,6},{6,2},{3,7},{7,3},{8,12},{12,8},{9,1... | collective-permute-start | bytes 1179656 | tf_op jit(solution)/shard_map/ppermute | solution.py:143
  316.5 24.6 %collective-permute-start.22 = (bf16[384,512]{1,0:T(8,128)(2,1)S(1)}, bf16[384,512]{1,0:T(8,128)(2,1)S(1)}, u32[]{:S(2)}, u32[]{:S(2)}) collective-permute-start(bf16[384,512]{1,0:T(8,128)(2,1)S(1)} %slice_bitcast_fusion.6), channel_id=1, source_target_pairs={{0,2},{2,0},{1,3},{3,1},{4,6},{6,4},{5,7},{7,5},{8,10},{10,8},{9,1... | collective-permute-start | bytes 1179656 | tf_op jit(solution)/shard_map/ppermute | solution.py:143
  316.8 35.5 %collective-permute-start.26 = (bf16[256,896]{1,0:T(8,128)(2,1)S(1)}, bf16[256,896]{1,0:T(8,128)(2,1)S(1)}, u32[]{:S(2)}, u32[]{:S(2)}) collective-permute-start(bf16[256,896]{1,0:T(8,128)(2,1)S(1)} %slice.283), channel_id=1, source_target_pairs={{0,2},{2,0},{1,3},{3,1},{4,6},{6,4},{5,7},{7,5},{8,10},{10,8},{9,1... | collective-permute-start | bytes 1376264 | tf_op jit(solution)/shard_map/ppermute | solution.py:143
  341.3 11.2 %collective-permute-start.28 = (bf16[96,1024]{1,0:T(8,128)(2,1)S(1)}, bf16[96,1024]{1,0:T(8,128)(2,1)S(1)}, u32[]{:S(2)}, u32[]{:S(2)}) collective-permute-start(bf16[96,1024]{1,0:T(8,128)(2,1)S(1)} %get-tuple-element.114), channel_id=1, source_target_pairs={{0,8},{8,0},{16,24},{24,16},{1,9},{9,1},{17,25},{25,17},{2,10},{10... | collective-permute-start | bytes 589832 | tf_op jit(solution)/shard_map/ppermute | solution.py:143
  341.4 16.5 %collective-permute-start.29 = (bf16[96,1024]{1,0:T(8,128)(2,1)S(1)}, bf16[96,1024]{1,0:T(8,128)(2,1)S(1)}, u32[]{:S(2)}, u32[]{:S(2)}) collective-permute-start(bf16[96,1024]{1,0:T(8,128)(2,1)S(1)} %get-tuple-element.115), channel_id=1, source_target_pairs={{0,16},{8,24},{16,0},{24,8},{1,17},{9,25},{17,1},{25,9},{2,18},{10... | collective-permute-start | bytes 589832 | tf_op jit(solution)/shard_map/ppermute | solution.py:143
  344.2 17.8 %collective-permute-start.30 = (bf16[96,1024]{1,0:T(8,128)(2,1)S(1)}, bf16[96,1024]{1,0:T(8,128)(2,1)S(1)}, u32[]{:S(2)}, u32[]{:S(2)}) collective-permute-start(bf16[96,1024]{1,0:T(8,128)(2,1)S(1)} %get-tuple-element.116), channel_id=1, source_target_pairs={{0,24},{8,16},{16,8},{24,0},{1,25},{9,17},{17,9},{25,1},{2,26},{10... | collective-permute-start | bytes 589832 | tf_op jit(solution)/shard_map/ppermute | solution.py:143
  352.5 10.4 %collective-permute-start.27 = (bf16[128,896]{1,0:T(8,128)(2,1)S(1)}, bf16[128,896]{1,0:T(8,128)(2,1)S(1)}, u32[]{:S(2)}, u32[]{:S(2)}) collective-permute-start(bf16[128,896]{1,0:T(8,128)(2,1)S(1)} %slice.285), channel_id=1, source_target_pairs={{0,4},{4,0},{1,5},{5,1},{2,6},{6,2},{3,7},{7,3},{8,12},{12,8},{9,1... | collective-permute-start | bytes 688136 | tf_op jit(solution)/shard_map/ppermute | solution.py:143
  363.6 5.0 %collective-permute-start.31 = (bf16[64,1024]{1,0:T(8,128)(2,1)S(1)}, bf16[64,1024]{1,0:T(8,128)(2,1)S(1)}, u32[]{:S(2)}, u32[]{:S(2)}) collective-permute-start(bf16[64,1024]{1,0:T(8,128)(2,1)S(1)} %slice.246), channel_id=1, source_target_pairs={{0,4},{4,0},{1,5},{5,1},{2,6},{6,2},{3,7},{7,3},{8,12},{12,8},{9,1... | collective-permute-start | bytes 393224 | tf_op jit(solution)/shard_map/ppermute | solution.py:143
  363.7 18.2 %all-to-all-start.4 = ((bf16[4,32,896]{2,1,0:T(8,128)(2,1)}), bf16[4,32,896]{2,1,0:T(8,128)(2,1)S(1)}, u32[]{:S(2)}, u32[]{:S(2)}) async-start(bf16[4,32,896]{2,1,0:T(8,128)(2,1)} %bitcast.80), calls=%async_computation.4 | async-start | bytes 458752 | tf_op jit(solution)/shard_map/all_to_all | solution.py:787
  368.7 12.5 %collective-permute-start.32 = (bf16[32,1024]{1,0:T(8,128)(2,1)S(1)}, bf16[32,1024]{1,0:T(8,128)(2,1)S(1)}, u32[]{:S(2)}, u32[]{:S(2)}) collective-permute-start(bf16[32,1024]{1,0:T(8,128)(2,1)S(1)} %slice.305), channel_id=1, source_target_pairs={{0,2},{2,0},{1,3},{3,1},{4,6},{6,4},{5,7},{7,5},{8,10},{10,8},{9,1... | collective-permute-start | bytes 196616 | tf_op jit(solution)/shard_map/ppermute | solution.py:143
  371.0 16.4 %collective-permute-start.33 = (bf16[32,6144]{1,0:T(8,128)(2,1)S(1)}, bf16[32,6144]{1,0:T(8,128)(2,1)S(1)}, u32[]{:S(2)}, u32[]{:S(2)}) collective-permute-start(bf16[32,6144]{1,0:T(8,128)(2,1)S(1)} %get-tuple-element.99), channel_id=1, source_target_pairs={{0,8},{8,0},{16,24},{24,16},{1,9},{9,1},{17,25},{25,17},{2,10},{10... | collective-permute-start | bytes 1179656 | tf_op jit(solution)/shard_map/ppermute | solution.py:143
  371.0 29.4 %collective-permute-start.34 = (bf16[32,6144]{1,0:T(8,128)(2,1)S(1)}, bf16[32,6144]{1,0:T(8,128)(2,1)S(1)}, u32[]{:S(2)}, u32[]{:S(2)}) collective-permute-start(bf16[32,6144]{1,0:T(8,128)(2,1)S(1)} %get-tuple-element.98), channel_id=1, source_target_pairs={{0,16},{8,24},{16,0},{24,8},{1,17},{9,25},{17,1},{25,9},{2,18},{10... | collective-permute-start | bytes 1179656 | tf_op jit(solution)/shard_map/ppermute | solution.py:143
  374.0 33.9 %collective-permute-start.35 = (bf16[32,6144]{1,0:T(8,128)(2,1)S(1)}, bf16[32,6144]{1,0:T(8,128)(2,1)}, u32[]{:S(2)}, u32[]{:S(2)}) collective-permute-start(bf16[32,6144]{1,0:T(8,128)(2,1)S(1)} %get-tuple-element.97), channel_id=1, source_target_pairs={{0,24},{8,16},{16,8},{24,0},{1,25},{9,17},{17,9},{25,1},{2,26},{10... | collective-permute-start | bytes 1179656 | tf_op jit(solution)/shard_map/ppermute | solution.py:143
  382.6 29.8 %copy-start.18 = (f32[32,1024]{1,0:T(8,128)}, f32[32,1024]{1,0:T(8,128)S(1)}, u32[]{:S(2)}) copy-start(f32[32,1024]{1,0:T(8,128)S(1)} %squeeze.34) | copy-start | bytes 393220
  382.9 29.5 %copy-start.19 = (f32[32,1024]{1,0:T(8,128)}, f32[32,1024]{1,0:T(8,128)S(1)}, u32[]{:S(2)}) copy-start(f32[32,1024]{1,0:T(8,128)S(1)} %squeeze.33) | copy-start | bytes 393220
  383.8 28.6 %copy-start.20 = (f32[32,1024]{1,0:T(8,128)}, f32[32,1024]{1,0:T(8,128)S(1)}, u32[]{:S(2)}) copy-start(f32[32,1024]{1,0:T(8,128)S(1)} %squeeze.32) | copy-start | bytes 393220
  (29 other events, 125.7 us)
Sparse Core Ops, SparseCore 0:
  36.9 66.9 all-gather.6
  105.8 72.1 all-gather.8
  192.2 44.3 all-gather.10
  239.4 116.5 reduce-scatter.3

commit v7 on v6

--- a/solution.py
+++ b/solution.py
@@ -737,8 +737,13 @@
         ]
         return dot(jnp.stack(turned, axis=1).reshape(hidden_parts * half, tokens), grad_down_in)
 
-    down_sent = swap(down_half(slice(half, None)).astype(BF16), "c", 1)
-    down_sum = (down_half(slice(half)) + down_sent.astype(F32)).astype(BF16)
+    down_first = down_half(slice(half, None)).astype(BF16)
+    turned_mlp = dot_t(pick_native, normed_mlp).astype(BF16)
+    turned_att = dot_t(pick_output, att_low).astype(BF16)
+    out_first = dot(turned_att[half:], grad_branch).astype(BF16)
+    mlp_first = dot(turned_mlp[half:], grads).astype(BF16)
+    turned_kept, down_first, out_first = together(turned_mlp[:half], down_first, out_first)
+    down_sum = (down_half(slice(half)) + swap(down_first, "c", 1).astype(F32)).astype(BF16)
 
     def over_yx(value):
         value = value.reshape(2 * lax.axis_size("x"), -1, value.shape[1])
@@ -760,12 +765,10 @@
     down_right = add_axis(down_sum[:, :, :, half:], "x", 1)
     grad_heads = exchange(grad_heads.reshape(seqs, units, local_len, PAIR))
     down_sum = jnp.concatenate([add_axis(down_left, "x", 0), add_axis(down_right, "y", 0)], axis=1)
-    turned_mlp = dot_t(pick_native, normed_mlp).astype(BF16)
-    mlp_sent = swap(dot(turned_mlp[half:], grads).astype(BF16), "c", 1)
-    mlp_sum = (dot(turned_mlp[:half], grads) + mlp_sent.astype(F32)).astype(BF16)
-
-    turned_att = dot_t(pick_output, att_low).astype(BF16)
-    out_sent = swap(dot(turned_att[half:], grad_branch).astype(BF16), "c", 1)
+    mlp_sent = swap(mlp_first, "c", 1)
+    mlp_sum = (dot(turned_kept, grads) + mlp_sent.astype(F32)).astype(BF16)
+
+    out_sent = swap(out_first, "c", 1)
     out_sum = (dot(turned_att[:half], grad_branch) + out_sent.astype(F32)).astype(BF16)
 
     out_sum = add_stage(out_sum, "z").astype(BF16)

time: 428 us -> 420 us (0.981)
  waiting for transfers between devices: 193 us -> 184 us
    ppermute x36, waiting for transfers between devices: 164 us -> 151 us  [swap(): return lax.ppermute(array, name, [(i, i ^ distance) for i in range(size)])]
where the time goes in v7:
time: 420 us; the launch traced here: 413 us
  waiting for transfers between devices  184 us (44%)
  starting transfers between devices  71.3 us (17%)
  Pallas kernels  64.6 us (15%)
  other arithmetic  29.6 us (7%)
  matrix products  23 us (5%)
  local copies, waits for them, and re-layouts  20.5 us (5%)
  between operations  20.2 us (5%)
    ppermute x36, waiting for transfers between devices, swap(): return lax.ppermute(array, name, [(i, i ^ distance) for i in range(size)])  151 us
    ppermute x36, starting transfers between devices, swap(): return lax.ppermute(array, name, [(i, i ^ distance) for i in range(size)])  41.3 us
    all_to_all x1, waiting for transfers between devices, on_device(): lax.all_to_all(parcel, SEQ, split_axis=0, concat_axis=0, tiled=True)  20.9 us
    pallas_call x1, Pallas kernels, mlp(): pl.pallas_call(mlp_kernel, grid=(1,), in_specs=[whole, still(*heads.shape...  19.3 us
    all_to_all x3, starting transfers between devices, exchange(): return lax.all_to_all(array, SEQ, split_axis=0, concat_axis=0, tiled=True)  17.4 us
    pallas_call x1, Pallas kernels, front(): pl.pallas_call(front_kernel, grid=(1,), in_specs=[still(*normed), still(*...  14 us
    pallas_call x1, Pallas kernels, attend_backward(): pl.pallas_call(attend_backward_kernel, grid=(units,), in_specs=[pl.BlockS...  14 us
    dot_general x6, matrix products, dot(): return jnp.dot(left, right, preferred_element_type=F32)  13.8 us
  transfers between devices with their start and end apart: 45, of which 21 were waited for; matrix products, arithmetic and copies ran while one was open for 16% of the time, Pallas kernels for 15%

profile of v7, /device:TPU:8, one launch (start us, length us, event | category | flops | bytes accessed | tf_op | source)
XLA Modules:
  0.0 413.3 jit_solution(4279478121518347980)
XLA Ops:
  25.0 5.8 %collective-permute-done = bf16[32,4096]{1,0:T(8,128)(2,1)} collective-permute-done((bf16[32,4096]{1,0:T(8,128)(2,1)S(1)}, bf16[32,4096]{1,0:T(8,128)(2,1)}, u32[]{:S(2)}, u32[]{:S(2)}) %collective-permute-start) | collective-permute-done | bytes 262176 | tf_op jit(solution)/shard_map/ppermute | solution.py:143
  30.8 3.6 collective-permute-done.1
  37.3 4.4 %collective-permute-start.5 = (bf16[32,6144]{1,0:T(8,128)(2,1)S(1)}, bf16[32,6144]{1,0:T(8,128)(2,1)S(1)}, u32[]{:S(2)}, u32[]{:S(2)}) collective-permute-start(bf16[32,6144]{1,0:T(8,128)(2,1)S(1)} %pad_maximum_fusion.11), channel_id=1, source_target_pairs={{0,16},{8,24},{16,0},{24,8},{1,17},{9,25},{17,1},{25,9},{2,18},{10... | collective-permute-start | bytes 1179656 | tf_op jit(solution)/shard_map/ppermute | solution.py:143
  41.8 24.0 %collective-permute-done.4 = bf16[32,6144]{1,0:T(8,128)(2,1)S(1)} collective-permute-done((bf16[32,6144]{1,0:T(8,128)(2,1)S(1)}, bf16[32,6144]{1,0:T(8,128)(2,1)S(1)}, u32[]{:S(2)}, u32[]{:S(2)}) %collective-permute-start.4) | collective-permute-done | bytes 393248 | tf_op jit(solution)/shard_map/ppermute | solution.py:143
  65.8 4.5 %collective-permute-done.5 = bf16[32,6144]{1,0:T(8,128)(2,1)S(1)} collective-permute-done((bf16[32,6144]{1,0:T(8,128)(2,1)S(1)}, bf16[32,6144]{1,0:T(8,128)(2,1)S(1)}, u32[]{:S(2)}, u32[]{:S(2)}) %collective-permute-start.5) | collective-permute-done | bytes 393248 | tf_op jit(solution)/shard_map/ppermute | solution.py:143
  71.9 7.1 %all-to-all-start = ((bf16[8,480,128]{2,1,0:T(8,128)(2,1)}), bf16[8,480,128]{2,1,0:T(8,128)(2,1)S(1)}, u32[]{:S(2)}, u32[]{:S(2)}) async-start(bf16[8,480,128]{2,1,0:T(8,128)(2,1)} %pad_maximum_fusion.5), calls=%async_computation | async-start | bytes 1966080 | tf_op jit(solution)/shard_map/all_to_all | solution.py:686
  79.0 20.9 %all-to-all-done = bf16[8,480,128]{2,1,0:T(8,128)(2,1)S(1)} async-done(((bf16[8,480,128]{2,1,0:T(8,128)(2,1)}), bf16[8,480,128]{2,1,0:T(8,128)(2,1)S(1)}, u32[]{:S(2)}, u32[]{:S(2)}) %all-to-all-start) | async-done | bytes 983072 | tf_op jit(solution)/shard_map/all_to_all | solution.py:686
  103.6 4.2 %collective-permute-start.8 = (bf16[2,128,1024]{2,1,0:T(8,128)(2,1)}, bf16[2,128,1024]{2,1,0:T(8,128)(2,1)}, u32[]{:S(2)}, u32[]{:S(2)}) collective-permute-start(bf16[2,128,1024]{2,1,0:T(8,128)(2,1)} %pad_maximum_fusion.10), channel_id=1, source_target_pairs={{0,16},{8,24},{16,0},{24,8},{1,17},{9,25},{17,1},{25,9},{2,18},{10... | collective-permute-start | bytes 1572872 | tf_op jit(solution)/shard_map/ppermute | solution.py:143
  107.8 1.7 collective-permute-done.10
  109.8 3.2 fusion.20
  114.0 25.8 %collective-permute-done.7 = bf16[2,128,1024]{2,1,0:T(8,128)(2,1)} collective-permute-done((bf16[2,128,1024]{2,1,0:T(8,128)(2,1)}, bf16[2,128,1024]{2,1,0:T(8,128)(2,1)}, u32[]{:S(2)}, u32[]{:S(2)}) %collective-permute-start.7) | collective-permute-done | bytes 524320 | tf_op jit(solution)/shard_map/ppermute | solution.py:143
  139.8 7.6 %collective-permute-done.8 = bf16[2,128,1024]{2,1,0:T(8,128)(2,1)} collective-permute-done((bf16[2,128,1024]{2,1,0:T(8,128)(2,1)}, bf16[2,128,1024]{2,1,0:T(8,128)(2,1)}, u32[]{:S(2)}, u32[]{:S(2)}) %collective-permute-start.8) | collective-permute-done | bytes 524320 | tf_op jit(solution)/shard_map/ppermute | solution.py:143
  150.9 4.3 %collective-permute-start.13 = (bf16[32,3072]{1,0:T(8,128)(2,1)S(1)}, bf16[32,3072]{1,0:T(8,128)(2,1)S(1)}, u32[]{:S(2)}, u32[]{:S(2)}) collective-permute-start(bf16[32,3072]{1,0:T(8,128)(2,1)S(1)} %pad_maximum_fusion.13), channel_id=1, source_target_pairs={{0,16},{8,24},{16,0},{24,8},{1,17},{9,25},{17,1},{25,9},{2,18},{10... | collective-permute-start | bytes 589832 | tf_op jit(solution)/shard_map/ppermute | solution.py:143
  157.8 1.9 copy.94
  161.2 14.0 %front.1 = (bf16[8,128,1024]{2,1,0:T(8,128)(2,1)}, bf16[8,3,2,128,128]{4,3,2,1,0:T(8,128)(2,1)}, bf16[8,2,128,128]{3,2,1,0:T(8,128)(2,1)}, f32[2,2,4,256]{3,2,1,0:T(4,128)}) custom-call(bf16[8,128,1024]{2,1,0:T(8,128)(2,1)} %bitcast.166, bf16[8,2,128,128]{3,2,1,0:T(8,128)(2,1)} %bitcast.176, f32[1,1024]{1,0:T(1,128)} %get-tuple-element.132.gain_ref, ...), custom_call_target="tpu_custom_call" | custom-call | bytes 56623104 | tf_op jit(solution)/shard_map/front/pallas_call | solution.py:251
  175.2 6.3 %all-to-all-start.1 = ((bf16[8,2,128,128]{3,2,1,0:T(8,128)(2,1)}), bf16[8,2,128,128]{3,2,1,0:T(8,128)(2,1)S(1)}, u32[]{:S(2)}, u32[]{:S(2)}) async-start(bf16[8,2,128,128]{3,2,1,0:T(8,128)(2,1)} %get-tuple-element.61), calls=%async_computation.1 | async-start | bytes 1048576 | tf_op jit(solution)/shard_map/all_to_all | solution.py:711
  183.5 8.5 %all-to-all-done.1 = bf16[8,2,128,128]{3,2,1,0:T(8,128)(2,1)S(1)} async-done(((bf16[8,2,128,128]{3,2,1,0:T(8,128)(2,1)}), bf16[8,2,128,128]{3,2,1,0:T(8,128)(2,1)S(1)}, u32[]{:S(2)}, u32[]{:S(2)}) %all-to-all-start.1) | async-done | bytes 524320 | tf_op jit(solution)/shard_map/all_to_all | solution.py:711
  194.4 19.3 %mlp.1 = (bf16[256,1024]{1,0:T(8,128)(2,1)}, bf16[256,1024]{1,0:T(8,128)(2,1)}, bf16[256,3072]{1,0:T(8,128)(2,1)}, f32[256,1024]{1,0:T(8,128)}, bf16[256,1024]{1...) custom-call(bf16[256,1024]{1,0:T(8,128)(2,1)} %bitcast.170, ...), custom_call_target="tpu_custom_call" | custom-call | bytes 62914560 | tf_op jit(solution)/shard_map/mlp/pallas_call | solution.py:431
  213.7 1.9 fusion.11
  215.8 2.2 convolution_convert_fusion
  224.9 3.3 collective-permute-done.15
  228.2 4.4 %add_convert_fusion = bf16[512,6144]{1,0:T(8,128)(2,1)} fusion(bf16[512,6144]{1,0:T(8,128)(2,1)S(1)} %collective-permute-done.15, bf16[512,256]{1,0:T(8,128)(2,1)S(1)} %slice-done, bf16[256,6144]{1,0:T(8,128)(2,1)S(1)} %copy-done), kind=kOutput, calls=%fused_computation | convolution fusion | flops 1620049920 | bytes 15990784 | tf_op jit(solution)/shard_map/dot_general | solution.py:56
  233.3 6.7 %all-to-all-start.2 = ((bf16[8,2,128,128]{3,2,1,0:T(8,128)(2,1)}), bf16[8,2,128,128]{3,2,1,0:T(8,128)(2,1)}, u32[]{:S(2)}, u32[]{:S(2)}) async-start(bf16[8,2,128,128]{3,2,1,0:T(8,128)(2,1)} %bitcast.192), calls=%async_computation.2 | async-start | bytes 1048576 | tf_op jit(solution)/shard_map/all_to_all | solution.py:711
  240.0 2.0 convolution_convert_fusion.5
  247.2 2.9 collective-permute-start.18
  250.7 3.0 add_convert_fusion.1
  259.3 9.0 %collective-permute-done.18 = bf16[128,1024]{1,0:T(8,128)(2,1)S(1)} collective-permute-done((bf16[128,1024]{1,0:T(8,128)(2,1)S(1)}, bf16[128,1024]{1,0:T(8,128)(2,1)S(1)}, u32[]{:S(2)}, u32[]{:S(2)}) %collective-permute-start.18) | collective-permute-done | bytes 262176 | tf_op jit(solution)/shard_map/ppermute | solution.py:143
  268.3 7.7 %collective-permute-done.19 = bf16[128,1024]{1,0:T(8,128)(2,1)S(1)} collective-permute-done((bf16[128,1024]{1,0:T(8,128)(2,1)S(1)}, bf16[128,1024]{1,0:T(8,128)(2,1)S(1)}, u32[]{:S(2)}, u32[]{:S(2)}) %collective-permute-start.19) | collective-permute-done | bytes 262176 | tf_op jit(solution)/shard_map/ppermute | solution.py:143
  276.2 14.0 %attend_backward.1.grads_ref = bf16[8,3,2,128,128]{4,3,2,1,0:T(8,128)(2,1)} custom-call(bf16[8,3,2,128,128]{4,3,2,1,0:T(8,128)(2,1)} %get-tuple-element.68.qkv_ref, bf16[8,2,128,128]{3,2,1,0:T(8,128)(2,1)} %all-to-all-done.2.grad_ref, f32[2,2,4,256]{3,2,1,0:T(4,128)} %get-tuple-element.81.total_ref, f32[1024,128]{1,0:T(8,128)} %get-tuple-element.140.cos_ref, ...), custom_call_target="tpu_custom_call" | custom-call | bytes 46137344 | tf_op jit(solution)/shard_map/attend_backward/pallas_call | solution.py:122
  290.2 4.5 %all-to-all-start.3 = ((bf16[8,3,2,128,128]{4,3,2,1,0:T(8,128)(2,1)}), bf16[8,3,2,128,128]{4,3,2,1,0:T(8,128)(2,1)}, u32[]{:S(2)}, u32[]{:S(2)}) async-start(bf16[8,3,2,128,128]{4,3,2,1,0:T(8,128)(2,1)} %attend_backward.1.grads_ref), calls=%async_computation.3 | async-start | bytes 3145728 | tf_op jit(solution)/shard_map/all_to_all | solution.py:711
  294.7 1.8 select_convert_fusion.pick_ref
  296.5 7.6 %head_grads.1 = bf16[1024,896]{1,0:T(8,128)(2,1)} custom-call(bf16[8,128,1024]{2,1,0:T(8,128)(2,1)} %get-tuple-element.67.normed_ref, bf16[8,3,2,128,128]{4,3,2,1,0:T(8,128)(2,1)} %attend_backward.1.grads_ref, f32[1,128]{1,0:T(1,128)} %get-tuple-element.82.loss_ref, bf16[1024,1024]{1,0:T(8,128)(2,1)} %select_convert_fusion.pick_ref), custom_call_target="tpu_custom_call" | custom-call | bytes 25165824 | tf_op jit(solution)/shard_map/head_grads/pallas_call | solution.py:497
  305.5 2.0 fusion.8
  309.5 2.0 collective-permute-start.26
  311.4 17.0 %collective-permute-done.24 = bf16[384,512]{1,0:T(8,128)(2,1)S(1)} collective-permute-done((bf16[384,512]{1,0:T(8,128)(2,1)S(1)}, bf16[384,512]{1,0:T(8,128)(2,1)S(1)}, u32[]{:S(2)}, u32[]{:S(2)}) %collective-permute-start.24) | collective-permute-done | bytes 393248 | tf_op jit(solution)/shard_map/ppermute | solution.py:143
  329.2 2.1 collective-permute-start.29
  332.5 4.4 %collective-permute-done.28 = bf16[96,1024]{1,0:T(8,128)(2,1)S(1)} collective-permute-done((bf16[96,1024]{1,0:T(8,128)(2,1)S(1)}, bf16[96,1024]{1,0:T(8,128)(2,1)S(1)}, u32[]{:S(2)}, u32[]{:S(2)}) %collective-permute-start.28) | collective-permute-done | bytes 196640 | tf_op jit(solution)/shard_map/ppermute | solution.py:143
  336.9 8.1 %collective-permute-done.29 = bf16[96,1024]{1,0:T(8,128)(2,1)S(1)} collective-permute-done((bf16[96,1024]{1,0:T(8,128)(2,1)S(1)}, bf16[96,1024]{1,0:T(8,128)(2,1)S(1)}, u32[]{:S(2)}, u32[]{:S(2)}) %collective-permute-start.29) | collective-permute-done | bytes 196640 | tf_op jit(solution)/shard_map/ppermute | solution.py:143
  345.0 4.5 %collective-permute-done.30 = bf16[96,1024]{1,0:T(8,128)(2,1)S(1)} collective-permute-done((bf16[96,1024]{1,0:T(8,128)(2,1)S(1)}, bf16[96,1024]{1,0:T(8,128)(2,1)S(1)}, u32[]{:S(2)}, u32[]{:S(2)}) %collective-permute-start.30) | collective-permute-done | bytes 196640 | tf_op jit(solution)/shard_map/ppermute | solution.py:143
  351.1 3.8 reduce-scatter.4.cloned.1.call-done
  355.5 5.1 %all-to-all-start.4 = ((bf16[4,32,896]{2,1,0:T(8,128)(2,1)}), bf16[4,32,896]{2,1,0:T(8,128)(2,1)S(1)}, u32[]{:S(2)}, u32[]{:S(2)}) async-start(bf16[4,32,896]{2,1,0:T(8,128)(2,1)} %bitcast.80), calls=%async_computation.4 | async-start | bytes 458752 | tf_op jit(solution)/shard_map/all_to_all | solution.py:790
  362.3 2.2 fusion.84
  364.6 2.8 collective-permute-start.34
  368.0 6.7 %last.1 = (f32[256,1024]{1,0:T(8,128)}, f32[256,1024]{1,0:T(8,128)}) custom-call(bf16[4,2,3,2,128,128]{5,4,3,2,1,0:T(8,128)(2,1)} %bitcast.77.heads_ref, bf16[256,1024]{1,0:T(8,128)(2,1)} %bitcast.171, f32[1,1024]{1,0:T(1,128)} %get-tuple-element.132.gain_ref, bf16[8,4,32,3072]{3,2,1,0:T(8,128)(2,1)} %bitcast.168, f32[256,1024]{1,0:T(8,128)} %get-tuple-element.86.grad_hidden_ref), custom_call_target="tpu_custom_call" | custom-call | bytes 22020096 | tf_op jit(solution)/shard_map/last/pallas_call | solution.py:531
  378.6 1.8 collective-permute-done.33.refs_1_
  380.4 13.5 %collective-permute-done.34.refs_2_ = bf16[32,6144]{1,0:T(8,128)(2,1)S(1)} collective-permute-done((bf16[32,6144]{1,0:T(8,128)(2,1)S(1)}, bf16[32,6144]{1,0:T(8,128)(2,1)S(1)}, u32[]{:S(2)}, u32[]{:S(2)}) %collective-permute-start.34) | collective-permute-done | bytes 393248 | tf_op jit(solution)/shard_map/ppermute | solution.py:143
  393.8 7.1 %collective-permute-done.35.refs_3_ = bf16[32,6144]{1,0:T(8,128)(2,1)} collective-permute-done((bf16[32,6144]{1,0:T(8,128)(2,1)S(1)}, bf16[32,6144]{1,0:T(8,128)(2,1)}, u32[]{:S(2)}, u32[]{:S(2)}) %collective-permute-start.35) | collective-permute-done | bytes 393248 | tf_op jit(solution)/shard_map/ppermute | solution.py:143
  401.0 3.1 finish.1
  (240 shorter events, 68.8 us)
Async XLA Ops:
  7.2 186.7 %all-gather.7.cloned.1.call-start = ((), (), s32[]{:S(2)}) async-start(), calls=%async_computation.6 | async-start | bytes 9437184 | tf_op jit(solution)/shard_map/all_gather | solution.py:672
  10.4 20.4 %collective-permute-start = (bf16[32,4096]{1,0:T(8,128)(2,1)S(1)}, bf16[32,4096]{1,0:T(8,128)(2,1)}, u32[]{:S(2)}, u32[]{:S(2)}) collective-permute-start(bf16[32,4096]{1,0:T(8,128)(2,1)S(1)} %constant_dynamic-update-slice_fusion), channel_id=1, source_target_pairs={{0,24},{8,16},{16,8},{24,0},{1,25},{9,17},{17,9},{25,1},{2,26},{10... | collective-permute-start | bytes 786440 | tf_op jit(solution)/shard_map/ppermute | solution.py:143
  12.0 22.4 %collective-permute-start.1 = (bf16[32,4096]{1,0:T(8,128)(2,1)S(1)}, bf16[32,4096]{1,0:T(8,128)(2,1)}, u32[]{:S(2)}, u32[]{:S(2)}) collective-permute-start(bf16[32,4096]{1,0:T(8,128)(2,1)S(1)} %constant_dynamic-update-slice_fusion), channel_id=1, source_target_pairs={{0,16},{8,24},{16,0},{24,8},{1,17},{9,25},{17,1},{25,9},{2,18},{10... | collective-permute-start | bytes 786440 | tf_op jit(solution)/shard_map/ppermute | solution.py:143
  13.1 21.3 %collective-permute-start.2 = (bf16[32,4096]{1,0:T(8,128)(2,1)S(1)}, bf16[32,4096]{1,0:T(8,128)(2,1)}, u32[]{:S(2)}, u32[]{:S(2)}) collective-permute-start(bf16[32,4096]{1,0:T(8,128)(2,1)S(1)} %constant_dynamic-update-slice_fusion), channel_id=1, source_target_pairs={{0,8},{8,0},{16,24},{24,16},{1,9},{9,1},{17,25},{25,17},{2,10},{10... | collective-permute-start | bytes 786440 | tf_op jit(solution)/shard_map/ppermute | solution.py:143
  15.2 21.5 %collective-permute-start.3 = (bf16[128,1024]{1,0:T(8,128)(2,1)}, bf16[128,1024]{1,0:T(8,128)(2,1)}, u32[]{:S(2)}, u32[]{:S(2)}) collective-permute-start(bf16[128,1024]{1,0:T(8,128)(2,1)} %get-tuple-element.136), channel_id=1, source_target_pairs={{0,4},{4,0},{1,5},{5,1},{2,6},{6,2},{3,7},{7,3},{8,12},{12,8},{9,1... | collective-permute-start | bytes 786440 | tf_op jit(solution)/shard_map/ppermute | solution.py:143
  36.8 157.1 %all-gather.9.cloned.1.call-start = ((), (), s32[]{:S(2)}) async-start(), calls=%async_computation.7 | async-start | bytes 14155776 | tf_op jit(solution)/shard_map/all_gather | solution.py:672
  36.8 29.0 %collective-permute-start.4 = (bf16[32,6144]{1,0:T(8,128)(2,1)S(1)}, bf16[32,6144]{1,0:T(8,128)(2,1)S(1)}, u32[]{:S(2)}, u32[]{:S(2)}) collective-permute-start(bf16[32,6144]{1,0:T(8,128)(2,1)S(1)} %pad_maximum_fusion.11), channel_id=1, source_target_pairs={{0,24},{8,16},{16,8},{24,0},{1,25},{9,17},{17,9},{25,1},{2,26},{10... | collective-permute-start | bytes 1179656 | tf_op jit(solution)/shard_map/ppermute | solution.py:143
  37.3 33.0 %collective-permute-start.5 = (bf16[32,6144]{1,0:T(8,128)(2,1)S(1)}, bf16[32,6144]{1,0:T(8,128)(2,1)S(1)}, u32[]{:S(2)}, u32[]{:S(2)}) collective-permute-start(bf16[32,6144]{1,0:T(8,128)(2,1)S(1)} %pad_maximum_fusion.11), channel_id=1, source_target_pairs={{0,16},{8,24},{16,0},{24,8},{1,17},{9,25},{17,1},{25,9},{2,18},{10... | collective-permute-start | bytes 1179656 | tf_op jit(solution)/shard_map/ppermute | solution.py:143
  41.7 28.6 %collective-permute-start.6 = (bf16[32,6144]{1,0:T(8,128)(2,1)S(1)}, bf16[32,6144]{1,0:T(8,128)(2,1)S(1)}, u32[]{:S(2)}, u32[]{:S(2)}) collective-permute-start(bf16[32,6144]{1,0:T(8,128)(2,1)S(1)} %pad_maximum_fusion.11), channel_id=1, source_target_pairs={{0,8},{8,0},{16,24},{24,16},{1,9},{9,1},{17,25},{25,17},{2,10},{10... | collective-permute-start | bytes 1179656 | tf_op jit(solution)/shard_map/ppermute | solution.py:143
  71.9 28.0 %all-to-all-start = ((bf16[8,480,128]{2,1,0:T(8,128)(2,1)}), bf16[8,480,128]{2,1,0:T(8,128)(2,1)S(1)}, u32[]{:S(2)}, u32[]{:S(2)}) async-start(bf16[8,480,128]{2,1,0:T(8,128)(2,1)} %pad_maximum_fusion.5), calls=%async_computation | async-start | bytes 1966080 | tf_op jit(solution)/shard_map/all_to_all | solution.py:686
  100.0 9.6 %collective-permute-start.10 = (bf16[7,8,32,128]{3,2,0,1:T(8,128)(2,1)S(1)}, bf16[7,8,32,128]{3,2,0,1:T(8,128)(2,1)S(1)}, u32[]{:S(2)}, u32[]{:S(2)}) collective-permute-start(bf16[7,8,32,128]{3,2,0,1:T(8,128)(2,1)S(1)} %bitcast.179), channel_id=1, source_target_pairs={{0,2},{2,0},{1,3},{3,1},{4,6},{6,4},{5,7},{7,5},{8,10},{10,8},{9,1... | collective-permute-start | bytes 1376264 | tf_op jit(solution)/shard_map/ppermute | solution.py:143
  103.4 36.4 %collective-permute-start.7 = (bf16[2,128,1024]{2,1,0:T(8,128)(2,1)}, bf16[2,128,1024]{2,1,0:T(8,128)(2,1)}, u32[]{:S(2)}, u32[]{:S(2)}) collective-permute-start(bf16[2,128,1024]{2,1,0:T(8,128)(2,1)} %pad_maximum_fusion.10), channel_id=1, source_target_pairs={{0,24},{8,16},{16,8},{24,0},{1,25},{9,17},{17,9},{25,1},{2,26},{10... | collective-permute-start | bytes 1572872 | tf_op jit(solution)/shard_map/ppermute | solution.py:143
  103.6 43.9 %collective-permute-start.8 = (bf16[2,128,1024]{2,1,0:T(8,128)(2,1)}, bf16[2,128,1024]{2,1,0:T(8,128)(2,1)}, u32[]{:S(2)}, u32[]{:S(2)}) collective-permute-start(bf16[2,128,1024]{2,1,0:T(8,128)(2,1)} %pad_maximum_fusion.10), channel_id=1, source_target_pairs={{0,16},{8,24},{16,0},{24,8},{1,17},{9,25},{17,1},{25,9},{2,18},{10... | collective-permute-start | bytes 1572872 | tf_op jit(solution)/shard_map/ppermute | solution.py:143
  107.8 39.6 %collective-permute-start.9 = (bf16[2,128,1024]{2,1,0:T(8,128)(2,1)}, bf16[2,128,1024]{2,1,0:T(8,128)(2,1)}, u32[]{:S(2)}, u32[]{:S(2)}) collective-permute-start(bf16[2,128,1024]{2,1,0:T(8,128)(2,1)} %pad_maximum_fusion.10), channel_id=1, source_target_pairs={{0,8},{8,0},{16,24},{24,16},{1,9},{9,1},{17,25},{25,17},{2,10},{10... | collective-permute-start | bytes 1572872 | tf_op jit(solution)/shard_map/ppermute | solution.py:143
  109.7 46.5 %collective-permute-start.11 = (bf16[7,8,2,32,128]{4,3,0,1,2:T(8,128)(2,1)S(1)}, bf16[7,8,2,32,128]{4,3,0,1,2:T(8,128)(2,1)}, u32[]{:S(2)}, u32[]{:S(2)}) collective-permute-start(bf16[7,8,2,32,128]{4,3,0,1,2:T(8,128)(2,1)S(1)} %pad_maximum_fusion.6), channel_id=1, source_target_pairs={{0,1},{1,0},{2,3},{3,2},{4,5},{5,4},{6,7},{7,6},{8,9},{9,8},{10,11... | collective-permute-start | bytes 2752520 | tf_op jit(solution)/shard_map/ppermute | solution.py:143
  150.6 30.9 %collective-permute-start.12 = (bf16[32,3072]{1,0:T(8,128)(2,1)S(1)}, bf16[32,3072]{1,0:T(8,128)(2,1)S(1)}, u32[]{:S(2)}, u32[]{:S(2)}) collective-permute-start(bf16[32,3072]{1,0:T(8,128)(2,1)S(1)} %pad_maximum_fusion.13), channel_id=1, source_target_pairs={{0,24},{8,16},{16,8},{24,0},{1,25},{9,17},{17,9},{25,1},{2,26},{10... | collective-permute-start | bytes 589832 | tf_op jit(solution)/shard_map/ppermute | solution.py:143
  150.9 30.6 %collective-permute-start.13 = (bf16[32,3072]{1,0:T(8,128)(2,1)S(1)}, bf16[32,3072]{1,0:T(8,128)(2,1)S(1)}, u32[]{:S(2)}, u32[]{:S(2)}) collective-permute-start(bf16[32,3072]{1,0:T(8,128)(2,1)S(1)} %pad_maximum_fusion.13), channel_id=1, source_target_pairs={{0,16},{8,24},{16,0},{24,8},{1,17},{9,25},{17,1},{25,9},{2,18},{10... | collective-permute-start | bytes 589832 | tf_op jit(solution)/shard_map/ppermute | solution.py:143
  155.2 26.3 %collective-permute-start.14 = (bf16[32,3072]{1,0:T(8,128)(2,1)S(1)}, bf16[32,3072]{1,0:T(8,128)(2,1)}, u32[]{:S(2)}, u32[]{:S(2)}) collective-permute-start(bf16[32,3072]{1,0:T(8,128)(2,1)S(1)} %pad_maximum_fusion.13), channel_id=1, source_target_pairs={{0,8},{8,0},{16,24},{24,16},{1,9},{9,1},{17,25},{25,17},{2,10},{10... | collective-permute-start | bytes 589832 | tf_op jit(solution)/shard_map/ppermute | solution.py:143
  175.2 16.8 %all-to-all-start.1 = ((bf16[8,2,128,128]{3,2,1,0:T(8,128)(2,1)}), bf16[8,2,128,128]{3,2,1,0:T(8,128)(2,1)S(1)}, u32[]{:S(2)}, u32[]{:S(2)}) async-start(bf16[8,2,128,128]{3,2,1,0:T(8,128)(2,1)} %get-tuple-element.61), calls=%async_computation.1 | async-start | bytes 1048576 | tf_op jit(solution)/shard_map/all_to_all | solution.py:711
  181.5 94.8 %all-gather.11.cloned.1.call-start = ((), (), s32[]{:S(2)}) async-start(), calls=%async_computation.8 | async-start | bytes 7077888 | tf_op jit(solution)/shard_map/all_gather | solution.py:672
  192.1 162.9 %reduce-scatter.4.cloned.1.call-start = ((), (), s32[]{:S(2)}) async-start(), calls=%async_computation.9 | async-start | bytes 7864320
  218.0 10.2 %collective-permute-start.15 = (bf16[512,6144]{1,0:T(8,128)(2,1)S(1)}, bf16[512,6144]{1,0:T(8,128)(2,1)S(1)}, u32[]{:S(2)}, u32[]{:S(2)}) collective-permute-start(bf16[512,6144]{1,0:T(8,128)(2,1)S(1)} %convolution_convert_fusion), channel_id=1, source_target_pairs={{0,1},{1,0},{2,3},{3,2},{4,5},{5,4},{6,7},{7,6},{8,9},{9,8},{10,11... | collective-permute-start | bytes 18874376 | tf_op jit(solution)/shard_map/ppermute | solution.py:143
  232.7 18.0 %collective-permute-start.20 = (bf16[1536,1024]{1,0:T(8,128)(2,1)S(1)}, bf16[1536,1024]{1,0:T(8,128)(2,1)}, u32[]{:S(2)}, u32[]{:S(2)}) collective-permute-start(bf16[1536,1024]{1,0:T(8,128)(2,1)S(1)} %convolution_convert_fusion.1), channel_id=1, source_target_pairs={{0,1},{1,0},{2,3},{3,2},{4,5},{5,4},{6,7},{7,6},{8,9},{9,8},{10,11... | collective-permute-start | bytes 9437192 | tf_op jit(solution)/shard_map/ppermute | solution.py:143
  232.9 12.4 %collective-permute-start.16 = (bf16[512,1024]{1,0:T(8,128)(2,1)}, bf16[512,1024]{1,0:T(8,128)(2,1)}, u32[]{:S(2)}, u32[]{:S(2)}) collective-permute-start(bf16[512,1024]{1,0:T(8,128)(2,1)} %convolution_convert_fusion.2), channel_id=1, source_target_pairs={{0,1},{1,0},{2,3},{3,2},{4,5},{5,4},{6,7},{7,6},{8,9},{9,8},{10,11... | collective-permute-start | bytes 3145736 | tf_op jit(solution)/shard_map/ppermute | solution.py:143
  233.3 43.0 %all-to-all-start.2 = ((bf16[8,2,128,128]{3,2,1,0:T(8,128)(2,1)}), bf16[8,2,128,128]{3,2,1,0:T(8,128)(2,1)}, u32[]{:S(2)}, u32[]{:S(2)}) async-start(bf16[8,2,128,128]{3,2,1,0:T(8,128)(2,1)} %bitcast.192), calls=%async_computation.2 | async-start | bytes 1048576 | tf_op jit(solution)/shard_map/all_to_all | solution.py:711
  247.1 12.2 %collective-permute-start.17 = (bf16[128,1024]{1,0:T(8,128)(2,1)S(1)}, bf16[128,1024]{1,0:T(8,128)(2,1)S(1)}, u32[]{:S(2)}, u32[]{:S(2)}) collective-permute-start(bf16[128,1024]{1,0:T(8,128)(2,1)S(1)} %get-tuple-element.111), channel_id=1, source_target_pairs={{0,8},{8,0},{16,24},{24,16},{1,9},{9,1},{17,25},{25,17},{2,10},{10... | collective-permute-start | bytes 786440 | tf_op jit(solution)/shard_map/ppermute | solution.py:143
  247.2 21.1 %collective-permute-start.18 = (bf16[128,1024]{1,0:T(8,128)(2,1)S(1)}, bf16[128,1024]{1,0:T(8,128)(2,1)S(1)}, u32[]{:S(2)}, u32[]{:S(2)}) collective-permute-start(bf16[128,1024]{1,0:T(8,128)(2,1)S(1)} %get-tuple-element.113), channel_id=1, source_target_pairs={{0,16},{8,24},{16,0},{24,8},{1,17},{9,25},{17,1},{25,9},{2,18},{10... | collective-permute-start | bytes 786440 | tf_op jit(solution)/shard_map/ppermute | solution.py:143
  250.1 25.9 %collective-permute-start.19 = (bf16[128,1024]{1,0:T(8,128)(2,1)S(1)}, bf16[128,1024]{1,0:T(8,128)(2,1)S(1)}, u32[]{:S(2)}, u32[]{:S(2)}) collective-permute-start(bf16[128,1024]{1,0:T(8,128)(2,1)S(1)} %get-tuple-element.112), channel_id=1, source_target_pairs={{0,24},{8,16},{16,8},{24,0},{1,25},{9,17},{17,9},{25,1},{2,26},{10... | collective-permute-start | bytes 786440 | tf_op jit(solution)/shard_map/ppermute | solution.py:143
  255.6 49.8 %collective-permute-start.21 = (bf16[2,384,512]{2,1,0:T(8,128)(2,1)}, bf16[2,384,512]{2,1,0:T(8,128)(2,1)}, u32[]{:S(2)}, u32[]{:S(2)}) collective-permute-start(bf16[2,384,512]{2,1,0:T(8,128)(2,1)} %slice_bitcast_fusion.2), channel_id=1, source_target_pairs={{0,4},{4,0},{1,5},{5,1},{2,6},{6,2},{3,7},{7,3},{8,12},{12,8},{9,1... | collective-permute-start | bytes 2359304 | tf_op jit(solution)/shard_map/ppermute | solution.py:143
  257.1 48.4 %collective-permute-start.23 = (bf16[2,384,512]{2,1,0:T(8,128)(2,1)}, bf16[2,384,512]{2,1,0:T(8,128)(2,1)}, u32[]{:S(2)}, u32[]{:S(2)}) collective-permute-start(bf16[2,384,512]{2,1,0:T(8,128)(2,1)} %slice_bitcast_fusion), channel_id=1, source_target_pairs={{0,2},{2,0},{1,3},{3,1},{4,6},{6,4},{5,7},{7,5},{8,10},{10,8},{9,1... | collective-permute-start | bytes 2359304 | tf_op jit(solution)/shard_map/ppermute | solution.py:143
  290.2 64.7 %all-to-all-start.3 = ((bf16[8,3,2,128,128]{4,3,2,1,0:T(8,128)(2,1)}), bf16[8,3,2,128,128]{4,3,2,1,0:T(8,128)(2,1)}, u32[]{:S(2)}, u32[]{:S(2)}) async-start(bf16[8,3,2,128,128]{4,3,2,1,0:T(8,128)(2,1)} %attend_backward.1.grads_ref), calls=%async_computation.3 | async-start | bytes 3145728 | tf_op jit(solution)/shard_map/all_to_all | solution.py:711
  305.4 3.8 collective-permute-start.25
  307.5 20.9 %collective-permute-start.24 = (bf16[384,512]{1,0:T(8,128)(2,1)S(1)}, bf16[384,512]{1,0:T(8,128)(2,1)S(1)}, u32[]{:S(2)}, u32[]{:S(2)}) collective-permute-start(bf16[384,512]{1,0:T(8,128)(2,1)S(1)} %slice_bitcast_fusion.4), channel_id=1, source_target_pairs={{0,4},{4,0},{1,5},{5,1},{2,6},{6,2},{3,7},{7,3},{8,12},{12,8},{9,1... | collective-permute-start | bytes 1179656 | tf_op jit(solution)/shard_map/ppermute | solution.py:143
  309.0 19.5 %collective-permute-start.22 = (bf16[384,512]{1,0:T(8,128)(2,1)S(1)}, bf16[384,512]{1,0:T(8,128)(2,1)S(1)}, u32[]{:S(2)}, u32[]{:S(2)}) collective-permute-start(bf16[384,512]{1,0:T(8,128)(2,1)S(1)} %slice_bitcast_fusion.6), channel_id=1, source_target_pairs={{0,2},{2,0},{1,3},{3,1},{4,6},{6,4},{5,7},{7,5},{8,10},{10,8},{9,1... | collective-permute-start | bytes 1179656 | tf_op jit(solution)/shard_map/ppermute | solution.py:143
  309.5 22.8 %collective-permute-start.26 = (bf16[256,896]{1,0:T(8,128)(2,1)S(1)}, bf16[256,896]{1,0:T(8,128)(2,1)S(1)}, u32[]{:S(2)}, u32[]{:S(2)}) collective-permute-start(bf16[256,896]{1,0:T(8,128)(2,1)S(1)} %slice.283), channel_id=1, source_target_pairs={{0,2},{2,0},{1,3},{3,1},{4,6},{6,4},{5,7},{7,5},{8,10},{10,8},{9,1... | collective-permute-start | bytes 1376264 | tf_op jit(solution)/shard_map/ppermute | solution.py:143
  328.7 8.2 %collective-permute-start.28 = (bf16[96,1024]{1,0:T(8,128)(2,1)S(1)}, bf16[96,1024]{1,0:T(8,128)(2,1)S(1)}, u32[]{:S(2)}, u32[]{:S(2)}) collective-permute-start(bf16[96,1024]{1,0:T(8,128)(2,1)S(1)} %get-tuple-element.120), channel_id=1, source_target_pairs={{0,8},{8,0},{16,24},{24,16},{1,9},{9,1},{17,25},{25,17},{2,10},{10... | collective-permute-start | bytes 589832 | tf_op jit(solution)/shard_map/ppermute | solution.py:143
  329.2 15.8 %collective-permute-start.29 = (bf16[96,1024]{1,0:T(8,128)(2,1)S(1)}, bf16[96,1024]{1,0:T(8,128)(2,1)S(1)}, u32[]{:S(2)}, u32[]{:S(2)}) collective-permute-start(bf16[96,1024]{1,0:T(8,128)(2,1)S(1)} %get-tuple-element.121), channel_id=1, source_target_pairs={{0,16},{8,24},{16,0},{24,8},{1,17},{9,25},{17,1},{25,9},{2,18},{10... | collective-permute-start | bytes 589832 | tf_op jit(solution)/shard_map/ppermute | solution.py:143
  331.3 18.2 %collective-permute-start.30 = (bf16[96,1024]{1,0:T(8,128)(2,1)S(1)}, bf16[96,1024]{1,0:T(8,128)(2,1)S(1)}, u32[]{:S(2)}, u32[]{:S(2)}) collective-permute-start(bf16[96,1024]{1,0:T(8,128)(2,1)S(1)} %get-tuple-element.122), channel_id=1, source_target_pairs={{0,24},{8,16},{16,8},{24,0},{1,25},{9,17},{17,9},{25,1},{2,26},{10... | collective-permute-start | bytes 589832 | tf_op jit(solution)/shard_map/ppermute | solution.py:143
  332.4 17.9 %collective-permute-start.27 = (bf16[128,896]{1,0:T(8,128)(2,1)S(1)}, bf16[128,896]{1,0:T(8,128)(2,1)S(1)}, u32[]{:S(2)}, u32[]{:S(2)}) collective-permute-start(bf16[128,896]{1,0:T(8,128)(2,1)S(1)} %slice.285), channel_id=1, source_target_pairs={{0,4},{4,0},{1,5},{5,1},{2,6},{6,2},{3,7},{7,3},{8,12},{12,8},{9,1... | collective-permute-start | bytes 688136 | tf_op jit(solution)/shard_map/ppermute | solution.py:143
  354.9 5.8 %collective-permute-start.31 = (bf16[64,1024]{1,0:T(8,128)(2,1)S(1)}, bf16[64,1024]{1,0:T(8,128)(2,1)S(1)}, u32[]{:S(2)}, u32[]{:S(2)}) collective-permute-start(bf16[64,1024]{1,0:T(8,128)(2,1)S(1)} %slice.246), channel_id=1, source_target_pairs={{0,4},{4,0},{1,5},{5,1},{2,6},{6,2},{3,7},{7,3},{8,12},{12,8},{9,1... | collective-permute-start | bytes 393224 | tf_op jit(solution)/shard_map/ppermute | solution.py:143
  355.5 19.8 %all-to-all-start.4 = ((bf16[4,32,896]{2,1,0:T(8,128)(2,1)}), bf16[4,32,896]{2,1,0:T(8,128)(2,1)S(1)}, u32[]{:S(2)}, u32[]{:S(2)}) async-start(bf16[4,32,896]{2,1,0:T(8,128)(2,1)} %bitcast.80), calls=%async_computation.4 | async-start | bytes 458752 | tf_op jit(solution)/shard_map/all_to_all | solution.py:790
  360.7 13.9 %collective-permute-start.32 = (bf16[32,1024]{1,0:T(8,128)(2,1)S(1)}, bf16[32,1024]{1,0:T(8,128)(2,1)S(1)}, u32[]{:S(2)}, u32[]{:S(2)}) collective-permute-start(bf16[32,1024]{1,0:T(8,128)(2,1)S(1)} %slice.305), channel_id=1, source_target_pairs={{0,2},{2,0},{1,3},{3,1},{4,6},{6,4},{5,7},{7,5},{8,10},{10,8},{9,1... | collective-permute-start | bytes 196616 | tf_op jit(solution)/shard_map/ppermute | solution.py:143
  364.5 15.9 %collective-permute-start.33 = (bf16[32,6144]{1,0:T(8,128)(2,1)S(1)}, bf16[32,6144]{1,0:T(8,128)(2,1)S(1)}, u32[]{:S(2)}, u32[]{:S(2)}) collective-permute-start(bf16[32,6144]{1,0:T(8,128)(2,1)S(1)} %get-tuple-element.105), channel_id=1, source_target_pairs={{0,8},{8,0},{16,24},{24,16},{1,9},{9,1},{17,25},{25,17},{2,10},{10... | collective-permute-start | bytes 1179656 | tf_op jit(solution)/shard_map/ppermute | solution.py:143
  364.6 29.3 %collective-permute-start.34 = (bf16[32,6144]{1,0:T(8,128)(2,1)S(1)}, bf16[32,6144]{1,0:T(8,128)(2,1)S(1)}, u32[]{:S(2)}, u32[]{:S(2)}) collective-permute-start(bf16[32,6144]{1,0:T(8,128)(2,1)S(1)} %get-tuple-element.104), channel_id=1, source_target_pairs={{0,16},{8,24},{16,0},{24,8},{1,17},{9,25},{17,1},{25,9},{2,18},{10... | collective-permute-start | bytes 1179656 | tf_op jit(solution)/shard_map/ppermute | solution.py:143
  367.4 33.5 %collective-permute-start.35 = (bf16[32,6144]{1,0:T(8,128)(2,1)S(1)}, bf16[32,6144]{1,0:T(8,128)(2,1)}, u32[]{:S(2)}, u32[]{:S(2)}) collective-permute-start(bf16[32,6144]{1,0:T(8,128)(2,1)S(1)} %get-tuple-element.103), channel_id=1, source_target_pairs={{0,24},{8,16},{16,8},{24,0},{1,25},{9,17},{17,9},{25,1},{2,26},{10... | collective-permute-start | bytes 1179656 | tf_op jit(solution)/shard_map/ppermute | solution.py:143
  376.1 29.4 %copy-start.19 = (f32[32,1024]{1,0:T(8,128)}, f32[32,1024]{1,0:T(8,128)S(1)}, u32[]{:S(2)}) copy-start(f32[32,1024]{1,0:T(8,128)S(1)} %squeeze.34) | copy-start | bytes 393220
  376.4 29.0 %copy-start.20 = (f32[32,1024]{1,0:T(8,128)}, f32[32,1024]{1,0:T(8,128)S(1)}, u32[]{:S(2)}) copy-start(f32[32,1024]{1,0:T(8,128)S(1)} %squeeze.33) | copy-start | bytes 393220
  377.3 28.1 %copy-start.21 = (f32[32,1024]{1,0:T(8,128)}, f32[32,1024]{1,0:T(8,128)S(1)}, u32[]{:S(2)}) copy-start(f32[32,1024]{1,0:T(8,128)S(1)} %squeeze.32) | copy-start | bytes 393220
  (31 other events, 132.9 us)
Sparse Core Ops, SparseCore 0:
  36.9 66.9 all-gather.6
  105.8 72.1 all-gather.8
  192.2 47.0 all-gather.10
  242.1 112.7 reduce-scatter.3

commit v8 on v7

--- a/solution.py
+++ b/solution.py
@@ -730,20 +730,22 @@
     )
 
     half = width // 2
-    def down_half(rows):
+    def turned_down(rows):
         turned = [
             dot_t(pick_down[rows], activated[:, p * width : (p + 1) * width]).astype(BF16).reshape(-1, own_rows, tokens)
             for p in range(hidden_parts)
         ]
-        return dot(jnp.stack(turned, axis=1).reshape(hidden_parts * half, tokens), grad_down_in)
-
-    down_first = down_half(slice(half, None)).astype(BF16)
+        return jnp.stack(turned, axis=1).reshape(hidden_parts * half, tokens)
+
+    down_first = dot(turned_down(slice(half, None)), grad_down_in).astype(BF16)
     turned_mlp = dot_t(pick_native, normed_mlp).astype(BF16)
     turned_att = dot_t(pick_output, att_low).astype(BF16)
     out_first = dot(turned_att[half:], grad_branch).astype(BF16)
     mlp_first = dot(turned_mlp[half:], grads).astype(BF16)
-    turned_kept, down_first, out_first = together(turned_mlp[:half], down_first, out_first)
-    down_sum = (down_half(slice(half)) + swap(down_first, "c", 1).astype(F32)).astype(BF16)
+    turned_kept, down_first, out_first, down_kept = together(
+        turned_mlp[:half], down_first, out_first, turned_down(slice(half))
+    )
+    down_sum = (dot(down_kept, grad_down_in) + swap(down_first, "c", 1).astype(F32)).astype(BF16)
 
     def over_yx(value):
         value = value.reshape(2 * lax.axis_size("x"), -1, value.shape[1])

time: 420 us -> 420 us (level)
  transfers between devices with their start and end apart: 45 -> 45, of which waited for: 21 -> 22; matrix products, arithmetic and copies ran while one was open for 16% -> 16% of each run, Pallas kernels for 15% -> 15%
where the time goes in v8:
time: 420 us; the launch traced here: 413 us
  waiting for transfers between devices  187 us (45%)
  starting transfers between devices  70.9 us (17%)
  Pallas kernels  64.7 us (15%)
  other arithmetic  30.7 us (7%)
  local copies, waits for them, and re-layouts  20.4 us (5%)
  between operations  20.1 us (5%)
  matrix products  19.4 us (5%)
    ppermute x36, waiting for transfers between devices, swap(): return lax.ppermute(array, name, [(i, i ^ distance) for i in range(size)])  154 us
    ppermute x36, starting transfers between devices, swap(): return lax.ppermute(array, name, [(i, i ^ distance) for i in range(size)])  40.8 us
    all_to_all x1, waiting for transfers between devices, on_device(): lax.all_to_all(parcel, SEQ, split_axis=0, concat_axis=0, tiled=True)  20.9 us
    pallas_call x1, Pallas kernels, mlp(): pl.pallas_call(mlp_kernel, grid=(1,), in_specs=[whole, still(*heads.shape...  19.3 us
    all_to_all x3, starting transfers between devices, exchange(): return lax.all_to_all(array, SEQ, split_axis=0, concat_axis=0, tiled=True)  17.6 us
    pallas_call x1, Pallas kernels, front(): pl.pallas_call(front_kernel, grid=(1,), in_specs=[still(*normed), still(*...  14 us
    pallas_call x1, Pallas kernels, attend_backward(): pl.pallas_call(attend_backward_kernel, grid=(units,), in_specs=[pl.BlockS...  14 us
    dot_general x6, matrix products, dot(): return jnp.dot(left, right, preferred_element_type=F32)  13.9 us
  transfers between devices with their start and end apart: 45, of which 22 were waited for; matrix products, arithmetic and copies ran while one was open for 16% of the time, Pallas kernels for 15%

profile of v8, /device:TPU:8, one launch (start us, length us, event | category | flops | bytes accessed | tf_op | source)
XLA Modules:
  0.0 413.3 jit_solution(4678258480866146168)
XLA Ops:
  25.0 5.8 %collective-permute-done = bf16[32,4096]{1,0:T(8,128)(2,1)} collective-permute-done((bf16[32,4096]{1,0:T(8,128)(2,1)S(1)}, bf16[32,4096]{1,0:T(8,128)(2,1)}, u32[]{:S(2)}, u32[]{:S(2)}) %collective-permute-start) | collective-permute-done | bytes 262176 | tf_op jit(solution)/shard_map/ppermute | solution.py:143
  30.8 3.6 collective-permute-done.1
  37.3 4.4 %collective-permute-start.5 = (bf16[32,6144]{1,0:T(8,128)(2,1)S(1)}, bf16[32,6144]{1,0:T(8,128)(2,1)S(1)}, u32[]{:S(2)}, u32[]{:S(2)}) collective-permute-start(bf16[32,6144]{1,0:T(8,128)(2,1)S(1)} %pad_maximum_fusion.11), channel_id=1, source_target_pairs={{0,16},{8,24},{16,0},{24,8},{1,17},{9,25},{17,1},{25,9},{2,18},{10... | collective-permute-start | bytes 1179656 | tf_op jit(solution)/shard_map/ppermute | solution.py:143
  41.8 24.0 %collective-permute-done.4 = bf16[32,6144]{1,0:T(8,128)(2,1)S(1)} collective-permute-done((bf16[32,6144]{1,0:T(8,128)(2,1)S(1)}, bf16[32,6144]{1,0:T(8,128)(2,1)S(1)}, u32[]{:S(2)}, u32[]{:S(2)}) %collective-permute-start.4) | collective-permute-done | bytes 393248 | tf_op jit(solution)/shard_map/ppermute | solution.py:143
  65.8 4.5 %collective-permute-done.5 = bf16[32,6144]{1,0:T(8,128)(2,1)S(1)} collective-permute-done((bf16[32,6144]{1,0:T(8,128)(2,1)S(1)}, bf16[32,6144]{1,0:T(8,128)(2,1)S(1)}, u32[]{:S(2)}, u32[]{:S(2)}) %collective-permute-start.5) | collective-permute-done | bytes 393248 | tf_op jit(solution)/shard_map/ppermute | solution.py:143
  71.9 7.1 %all-to-all-start = ((bf16[8,480,128]{2,1,0:T(8,128)(2,1)}), bf16[8,480,128]{2,1,0:T(8,128)(2,1)S(1)}, u32[]{:S(2)}, u32[]{:S(2)}) async-start(bf16[8,480,128]{2,1,0:T(8,128)(2,1)} %pad_maximum_fusion.5), calls=%async_computation | async-start | bytes 1966080 | tf_op jit(solution)/shard_map/all_to_all | solution.py:686
  79.0 20.9 %all-to-all-done = bf16[8,480,128]{2,1,0:T(8,128)(2,1)S(1)} async-done(((bf16[8,480,128]{2,1,0:T(8,128)(2,1)}), bf16[8,480,128]{2,1,0:T(8,128)(2,1)S(1)}, u32[]{:S(2)}, u32[]{:S(2)}) %all-to-all-start) | async-done | bytes 983072 | tf_op jit(solution)/shard_map/all_to_all | solution.py:686
  103.6 4.2 %collective-permute-start.8 = (bf16[2,128,1024]{2,1,0:T(8,128)(2,1)}, bf16[2,128,1024]{2,1,0:T(8,128)(2,1)}, u32[]{:S(2)}, u32[]{:S(2)}) collective-permute-start(bf16[2,128,1024]{2,1,0:T(8,128)(2,1)} %pad_maximum_fusion.10), channel_id=1, source_target_pairs={{0,16},{8,24},{16,0},{24,8},{1,17},{9,25},{17,1},{25,9},{2,18},{10... | collective-permute-start | bytes 1572872 | tf_op jit(solution)/shard_map/ppermute | solution.py:143
  107.9 1.7 collective-permute-done.10
  109.8 3.2 fusion.20
  114.1 25.8 %collective-permute-done.7 = bf16[2,128,1024]{2,1,0:T(8,128)(2,1)} collective-permute-done((bf16[2,128,1024]{2,1,0:T(8,128)(2,1)}, bf16[2,128,1024]{2,1,0:T(8,128)(2,1)}, u32[]{:S(2)}, u32[]{:S(2)}) %collective-permute-start.7) | collective-permute-done | bytes 524320 | tf_op jit(solution)/shard_map/ppermute | solution.py:143
  139.8 7.6 %collective-permute-done.8 = bf16[2,128,1024]{2,1,0:T(8,128)(2,1)} collective-permute-done((bf16[2,128,1024]{2,1,0:T(8,128)(2,1)}, bf16[2,128,1024]{2,1,0:T(8,128)(2,1)}, u32[]{:S(2)}, u32[]{:S(2)}) %collective-permute-start.8) | collective-permute-done | bytes 524320 | tf_op jit(solution)/shard_map/ppermute | solution.py:143
  150.9 4.3 %collective-permute-start.13 = (bf16[32,3072]{1,0:T(8,128)(2,1)S(1)}, bf16[32,3072]{1,0:T(8,128)(2,1)S(1)}, u32[]{:S(2)}, u32[]{:S(2)}) collective-permute-start(bf16[32,3072]{1,0:T(8,128)(2,1)S(1)} %pad_maximum_fusion.13), channel_id=1, source_target_pairs={{0,16},{8,24},{16,0},{24,8},{1,17},{9,25},{17,1},{25,9},{2,18},{10... | collective-permute-start | bytes 589832 | tf_op jit(solution)/shard_map/ppermute | solution.py:143
  157.8 1.9 copy.94
  161.2 14.0 %front.1 = (bf16[8,128,1024]{2,1,0:T(8,128)(2,1)}, bf16[8,3,2,128,128]{4,3,2,1,0:T(8,128)(2,1)}, bf16[8,2,128,128]{3,2,1,0:T(8,128)(2,1)}, f32[2,2,4,256]{3,2,1,0:T(4,128)}) custom-call(bf16[8,128,1024]{2,1,0:T(8,128)(2,1)} %bitcast.166, bf16[8,2,128,128]{3,2,1,0:T(8,128)(2,1)} %bitcast.176, f32[1,1024]{1,0:T(1,128)} %get-tuple-element.134.gain_ref, ...), custom_call_target="tpu_custom_call" | custom-call | bytes 56623104 | tf_op jit(solution)/shard_map/front/pallas_call | solution.py:251
  175.2 6.3 %all-to-all-start.1 = ((bf16[8,2,128,128]{3,2,1,0:T(8,128)(2,1)}), bf16[8,2,128,128]{3,2,1,0:T(8,128)(2,1)S(1)}, u32[]{:S(2)}, u32[]{:S(2)}) async-start(bf16[8,2,128,128]{3,2,1,0:T(8,128)(2,1)} %get-tuple-element.62), calls=%async_computation.1 | async-start | bytes 1048576 | tf_op jit(solution)/shard_map/all_to_all | solution.py:711
  183.5 8.5 %all-to-all-done.1 = bf16[8,2,128,128]{3,2,1,0:T(8,128)(2,1)S(1)} async-done(((bf16[8,2,128,128]{3,2,1,0:T(8,128)(2,1)}), bf16[8,2,128,128]{3,2,1,0:T(8,128)(2,1)S(1)}, u32[]{:S(2)}, u32[]{:S(2)}) %all-to-all-start.1) | async-done | bytes 524320 | tf_op jit(solution)/shard_map/all_to_all | solution.py:711
  194.4 19.3 %mlp.1 = (bf16[256,1024]{1,0:T(8,128)(2,1)}, bf16[256,1024]{1,0:T(8,128)(2,1)}, bf16[256,3072]{1,0:T(8,128)(2,1)}, f32[256,1024]{1,0:T(8,128)}, bf16[256,1024]{1...) custom-call(bf16[256,1024]{1,0:T(8,128)(2,1)} %bitcast.170, ...), custom_call_target="tpu_custom_call" | custom-call | bytes 62914560 | tf_op jit(solution)/shard_map/mlp/pallas_call | solution.py:431
  213.8 1.9 fusion.11
  215.8 2.2 convolution_convert_fusion
  228.3 4.4 %add_convert_fusion = bf16[512,6144]{1,0:T(8,128)(2,1)} fusion(bf16[512,6144]{1,0:T(8,128)(2,1)S(1)} %collective-permute-done.15, bf16[512,256]{1,0:T(8,128)(2,1)S(1)} %slice-done, bf16[256,6144]{1,0:T(8,128)(2,1)S(1)} %copy-done), kind=kOutput, calls=%fused_computation | convolution fusion | flops 1620049920 | bytes 15990784 | tf_op jit(solution)/shard_map/dot_general | solution.py:56
  233.3 6.6 %all-to-all-start.2 = ((bf16[8,2,128,128]{3,2,1,0:T(8,128)(2,1)}), bf16[8,2,128,128]{3,2,1,0:T(8,128)(2,1)}, u32[]{:S(2)}, u32[]{:S(2)}) async-start(bf16[8,2,128,128]{3,2,1,0:T(8,128)(2,1)} %bitcast.192), calls=%async_computation.2 | async-start | bytes 1048576 | tf_op jit(solution)/shard_map/all_to_all | solution.py:711
  240.6 1.9 add_convert_fusion.2
  242.6 2.3 collective-permute-start.17
  246.4 2.9 add_convert_fusion.1
  253.1 5.5 %collective-permute-done.17 = bf16[128,1024]{1,0:T(8,128)(2,1)S(1)} collective-permute-done((bf16[128,1024]{1,0:T(8,128)(2,1)S(1)}, bf16[128,1024]{1,0:T(8,128)(2,1)S(1)}, u32[]{:S(2)}, u32[]{:S(2)}) %collective-permute-start.17) | collective-permute-done | bytes 262176 | tf_op jit(solution)/shard_map/ppermute | solution.py:143
  258.7 9.6 %collective-permute-done.18 = bf16[128,1024]{1,0:T(8,128)(2,1)S(1)} collective-permute-done((bf16[128,1024]{1,0:T(8,128)(2,1)S(1)}, bf16[128,1024]{1,0:T(8,128)(2,1)S(1)}, u32[]{:S(2)}, u32[]{:S(2)}) %collective-permute-start.18) | collective-permute-done | bytes 262176 | tf_op jit(solution)/shard_map/ppermute | solution.py:143
  268.3 7.7 %collective-permute-done.19 = bf16[128,1024]{1,0:T(8,128)(2,1)S(1)} collective-permute-done((bf16[128,1024]{1,0:T(8,128)(2,1)S(1)}, bf16[128,1024]{1,0:T(8,128)(2,1)S(1)}, u32[]{:S(2)}, u32[]{:S(2)}) %collective-permute-start.19) | collective-permute-done | bytes 262176 | tf_op jit(solution)/shard_map/ppermute | solution.py:143
  276.1 14.0 %attend_backward.1.grads_ref = bf16[8,3,2,128,128]{4,3,2,1,0:T(8,128)(2,1)} custom-call(bf16[8,3,2,128,128]{4,3,2,1,0:T(8,128)(2,1)} %get-tuple-element.69.qkv_ref, bf16[8,2,128,128]{3,2,1,0:T(8,128)(2,1)} %all-to-all-done.2.grad_ref, f32[2,2,4,256]{3,2,1,0:T(4,128)} %get-tuple-element.83.total_ref, f32[1024,128]{1,0:T(8,128)} %get-tuple-element.142.cos_ref, ...), custom_call_target="tpu_custom_call" | custom-call | bytes 46137344 | tf_op jit(solution)/shard_map/attend_backward/pallas_call | solution.py:122
  290.2 4.7 %all-to-all-start.3 = ((bf16[8,3,2,128,128]{4,3,2,1,0:T(8,128)(2,1)}), bf16[8,3,2,128,128]{4,3,2,1,0:T(8,128)(2,1)}, u32[]{:S(2)}, u32[]{:S(2)}) async-start(bf16[8,3,2,128,128]{4,3,2,1,0:T(8,128)(2,1)} %attend_backward.1.grads_ref), calls=%async_computation.3 | async-start | bytes 3145728 | tf_op jit(solution)/shard_map/all_to_all | solution.py:711
  294.9 1.9 select_convert_fusion.pick_ref
  296.7 7.6 %head_grads.1 = bf16[1024,896]{1,0:T(8,128)(2,1)} custom-call(bf16[8,128,1024]{2,1,0:T(8,128)(2,1)} %get-tuple-element.68.normed_ref, bf16[8,3,2,128,128]{4,3,2,1,0:T(8,128)(2,1)} %attend_backward.1.grads_ref, f32[1,128]{1,0:T(1,128)} %get-tuple-element.84.loss_ref, bf16[1024,1024]{1,0:T(8,128)(2,1)} %select_convert_fusion.pick_ref), custom_call_target="tpu_custom_call" | custom-call | bytes 25165824 | tf_op jit(solution)/shard_map/head_grads/pallas_call | solution.py:497
  305.7 2.0 fusion.8
  309.6 2.1 collective-permute-start.26
  311.6 16.8 %collective-permute-done.24 = bf16[384,512]{1,0:T(8,128)(2,1)S(1)} collective-permute-done((bf16[384,512]{1,0:T(8,128)(2,1)S(1)}, bf16[384,512]{1,0:T(8,128)(2,1)S(1)}, u32[]{:S(2)}, u32[]{:S(2)}) %collective-permute-start.24) | collective-permute-done | bytes 393248 | tf_op jit(solution)/shard_map/ppermute | solution.py:143
  329.2 2.1 collective-permute-start.29
  332.5 4.3 %collective-permute-done.28 = bf16[96,1024]{1,0:T(8,128)(2,1)S(1)} collective-permute-done((bf16[96,1024]{1,0:T(8,128)(2,1)S(1)}, bf16[96,1024]{1,0:T(8,128)(2,1)S(1)}, u32[]{:S(2)}, u32[]{:S(2)}) %collective-permute-start.28) | collective-permute-done | bytes 196640 | tf_op jit(solution)/shard_map/ppermute | solution.py:143
  336.9 8.1 %collective-permute-done.29 = bf16[96,1024]{1,0:T(8,128)(2,1)S(1)} collective-permute-done((bf16[96,1024]{1,0:T(8,128)(2,1)S(1)}, bf16[96,1024]{1,0:T(8,128)(2,1)S(1)}, u32[]{:S(2)}, u32[]{:S(2)}) %collective-permute-start.29) | collective-permute-done | bytes 196640 | tf_op jit(solution)/shard_map/ppermute | solution.py:143
  345.0 4.5 %collective-permute-done.30 = bf16[96,1024]{1,0:T(8,128)(2,1)S(1)} collective-permute-done((bf16[96,1024]{1,0:T(8,128)(2,1)S(1)}, bf16[96,1024]{1,0:T(8,128)(2,1)S(1)}, u32[]{:S(2)}, u32[]{:S(2)}) %collective-permute-start.30) | collective-permute-done | bytes 196640 | tf_op jit(solution)/shard_map/ppermute | solution.py:143
  351.1 3.8 reduce-scatter.4.cloned.1.call-done
  355.5 5.1 %all-to-all-start.4 = ((bf16[4,32,896]{2,1,0:T(8,128)(2,1)}), bf16[4,32,896]{2,1,0:T(8,128)(2,1)S(1)}, u32[]{:S(2)}, u32[]{:S(2)}) async-start(bf16[4,32,896]{2,1,0:T(8,128)(2,1)} %bitcast.80), calls=%async_computation.4 | async-start | bytes 458752 | tf_op jit(solution)/shard_map/all_to_all | solution.py:792
  362.3 2.2 fusion.84
  364.6 2.8 collective-permute-start.34
  368.0 6.7 %last.1 = (f32[256,1024]{1,0:T(8,128)}, f32[256,1024]{1,0:T(8,128)}) custom-call(bf16[4,2,3,2,128,128]{5,4,3,2,1,0:T(8,128)(2,1)} %bitcast.77.heads_ref, bf16[256,1024]{1,0:T(8,128)(2,1)} %bitcast.171, f32[1,1024]{1,0:T(1,128)} %get-tuple-element.134.gain_ref, bf16[8,4,32,3072]{3,2,1,0:T(8,128)(2,1)} %bitcast.168, f32[256,1024]{1,0:T(8,128)} %get-tuple-element.88.grad_hidden_ref), custom_call_target="tpu_custom_call" | custom-call | bytes 22020096 | tf_op jit(solution)/shard_map/last/pallas_call | solution.py:531
  378.6 1.8 collective-permute-done.33.refs_1_
  380.4 13.4 %collective-permute-done.34.refs_2_ = bf16[32,6144]{1,0:T(8,128)(2,1)S(1)} collective-permute-done((bf16[32,6144]{1,0:T(8,128)(2,1)S(1)}, bf16[32,6144]{1,0:T(8,128)(2,1)S(1)}, u32[]{:S(2)}, u32[]{:S(2)}) %collective-permute-start.34) | collective-permute-done | bytes 393248 | tf_op jit(solution)/shard_map/ppermute | solution.py:143
  393.8 7.1 %collective-permute-done.35.refs_3_ = bf16[32,6144]{1,0:T(8,128)(2,1)} collective-permute-done((bf16[32,6144]{1,0:T(8,128)(2,1)S(1)}, bf16[32,6144]{1,0:T(8,128)(2,1)}, u32[]{:S(2)}, u32[]{:S(2)}) %collective-permute-start.35) | collective-permute-done | bytes 393248 | tf_op jit(solution)/shard_map/ppermute | solution.py:143
  401.0 3.1 finish.1
  (234 shorter events, 66.8 us)
Async XLA Ops:
  7.2 186.7 %all-gather.7.cloned.1.call-start = ((), (), s32[]{:S(2)}) async-start(), calls=%async_computation.6 | async-start | bytes 9437184 | tf_op jit(solution)/shard_map/all_gather | solution.py:672
  10.4 20.4 %collective-permute-start = (bf16[32,4096]{1,0:T(8,128)(2,1)S(1)}, bf16[32,4096]{1,0:T(8,128)(2,1)}, u32[]{:S(2)}, u32[]{:S(2)}) collective-permute-start(bf16[32,4096]{1,0:T(8,128)(2,1)S(1)} %constant_dynamic-update-slice_fusion), channel_id=1, source_target_pairs={{0,24},{8,16},{16,8},{24,0},{1,25},{9,17},{17,9},{25,1},{2,26},{10... | collective-permute-start | bytes 786440 | tf_op jit(solution)/shard_map/ppermute | solution.py:143
  12.0 22.4 %collective-permute-start.1 = (bf16[32,4096]{1,0:T(8,128)(2,1)S(1)}, bf16[32,4096]{1,0:T(8,128)(2,1)}, u32[]{:S(2)}, u32[]{:S(2)}) collective-permute-start(bf16[32,4096]{1,0:T(8,128)(2,1)S(1)} %constant_dynamic-update-slice_fusion), channel_id=1, source_target_pairs={{0,16},{8,24},{16,0},{24,8},{1,17},{9,25},{17,1},{25,9},{2,18},{10... | collective-permute-start | bytes 786440 | tf_op jit(solution)/shard_map/ppermute | solution.py:143
  13.1 21.3 %collective-permute-start.2 = (bf16[32,4096]{1,0:T(8,128)(2,1)S(1)}, bf16[32,4096]{1,0:T(8,128)(2,1)}, u32[]{:S(2)}, u32[]{:S(2)}) collective-permute-start(bf16[32,4096]{1,0:T(8,128)(2,1)S(1)} %constant_dynamic-update-slice_fusion), channel_id=1, source_target_pairs={{0,8},{8,0},{16,24},{24,16},{1,9},{9,1},{17,25},{25,17},{2,10},{10... | collective-permute-start | bytes 786440 | tf_op jit(solution)/shard_map/ppermute | solution.py:143
  15.2 21.5 %collective-permute-start.3 = (bf16[128,1024]{1,0:T(8,128)(2,1)}, bf16[128,1024]{1,0:T(8,128)(2,1)}, u32[]{:S(2)}, u32[]{:S(2)}) collective-permute-start(bf16[128,1024]{1,0:T(8,128)(2,1)} %get-tuple-element.138), channel_id=1, source_target_pairs={{0,4},{4,0},{1,5},{5,1},{2,6},{6,2},{3,7},{7,3},{8,12},{12,8},{9,1... | collective-permute-start | bytes 786440 | tf_op jit(solution)/shard_map/ppermute | solution.py:143
  36.8 157.1 %all-gather.9.cloned.1.call-start = ((), (), s32[]{:S(2)}) async-start(), calls=%async_computation.7 | async-start | bytes 14155776 | tf_op jit(solution)/shard_map/all_gather | solution.py:672
  36.8 29.0 %collective-permute-start.4 = (bf16[32,6144]{1,0:T(8,128)(2,1)S(1)}, bf16[32,6144]{1,0:T(8,128)(2,1)S(1)}, u32[]{:S(2)}, u32[]{:S(2)}) collective-permute-start(bf16[32,6144]{1,0:T(8,128)(2,1)S(1)} %pad_maximum_fusion.11), channel_id=1, source_target_pairs={{0,24},{8,16},{16,8},{24,0},{1,25},{9,17},{17,9},{25,1},{2,26},{10... | collective-permute-start | bytes 1179656 | tf_op jit(solution)/shard_map/ppermute | solution.py:143
  37.3 33.0 %collective-permute-start.5 = (bf16[32,6144]{1,0:T(8,128)(2,1)S(1)}, bf16[32,6144]{1,0:T(8,128)(2,1)S(1)}, u32[]{:S(2)}, u32[]{:S(2)}) collective-permute-start(bf16[32,6144]{1,0:T(8,128)(2,1)S(1)} %pad_maximum_fusion.11), channel_id=1, source_target_pairs={{0,16},{8,24},{16,0},{24,8},{1,17},{9,25},{17,1},{25,9},{2,18},{10... | collective-permute-start | bytes 1179656 | tf_op jit(solution)/shard_map/ppermute | solution.py:143
  41.7 28.6 %collective-permute-start.6 = (bf16[32,6144]{1,0:T(8,128)(2,1)S(1)}, bf16[32,6144]{1,0:T(8,128)(2,1)S(1)}, u32[]{:S(2)}, u32[]{:S(2)}) collective-permute-start(bf16[32,6144]{1,0:T(8,128)(2,1)S(1)} %pad_maximum_fusion.11), channel_id=1, source_target_pairs={{0,8},{8,0},{16,24},{24,16},{1,9},{9,1},{17,25},{25,17},{2,10},{10... | collective-permute-start | bytes 1179656 | tf_op jit(solution)/shard_map/ppermute | solution.py:143
  71.9 28.0 %all-to-all-start = ((bf16[8,480,128]{2,1,0:T(8,128)(2,1)}), bf16[8,480,128]{2,1,0:T(8,128)(2,1)S(1)}, u32[]{:S(2)}, u32[]{:S(2)}) async-start(bf16[8,480,128]{2,1,0:T(8,128)(2,1)} %pad_maximum_fusion.5), calls=%async_computation | async-start | bytes 1966080 | tf_op jit(solution)/shard_map/all_to_all | solution.py:686
  100.0 9.6 %collective-permute-start.10 = (bf16[7,8,32,128]{3,2,0,1:T(8,128)(2,1)S(1)}, bf16[7,8,32,128]{3,2,0,1:T(8,128)(2,1)S(1)}, u32[]{:S(2)}, u32[]{:S(2)}) collective-permute-start(bf16[7,8,32,128]{3,2,0,1:T(8,128)(2,1)S(1)} %bitcast.179), channel_id=1, source_target_pairs={{0,2},{2,0},{1,3},{3,1},{4,6},{6,4},{5,7},{7,5},{8,10},{10,8},{9,1... | collective-permute-start | bytes 1376264 | tf_op jit(solution)/shard_map/ppermute | solution.py:143
  103.4 36.4 %collective-permute-start.7 = (bf16[2,128,1024]{2,1,0:T(8,128)(2,1)}, bf16[2,128,1024]{2,1,0:T(8,128)(2,1)}, u32[]{:S(2)}, u32[]{:S(2)}) collective-permute-start(bf16[2,128,1024]{2,1,0:T(8,128)(2,1)} %pad_maximum_fusion.10), channel_id=1, source_target_pairs={{0,24},{8,16},{16,8},{24,0},{1,25},{9,17},{17,9},{25,1},{2,26},{10... | collective-permute-start | bytes 1572872 | tf_op jit(solution)/shard_map/ppermute | solution.py:143
  103.6 43.9 %collective-permute-start.8 = (bf16[2,128,1024]{2,1,0:T(8,128)(2,1)}, bf16[2,128,1024]{2,1,0:T(8,128)(2,1)}, u32[]{:S(2)}, u32[]{:S(2)}) collective-permute-start(bf16[2,128,1024]{2,1,0:T(8,128)(2,1)} %pad_maximum_fusion.10), channel_id=1, source_target_pairs={{0,16},{8,24},{16,0},{24,8},{1,17},{9,25},{17,1},{25,9},{2,18},{10... | collective-permute-start | bytes 1572872 | tf_op jit(solution)/shard_map/ppermute | solution.py:143
  107.8 39.6 %collective-permute-start.9 = (bf16[2,128,1024]{2,1,0:T(8,128)(2,1)}, bf16[2,128,1024]{2,1,0:T(8,128)(2,1)}, u32[]{:S(2)}, u32[]{:S(2)}) collective-permute-start(bf16[2,128,1024]{2,1,0:T(8,128)(2,1)} %pad_maximum_fusion.10), channel_id=1, source_target_pairs={{0,8},{8,0},{16,24},{24,16},{1,9},{9,1},{17,25},{25,17},{2,10},{10... | collective-permute-start | bytes 1572872 | tf_op jit(solution)/shard_map/ppermute | solution.py:143
  109.7 46.6 %collective-permute-start.11 = (bf16[7,8,2,32,128]{4,3,0,1,2:T(8,128)(2,1)S(1)}, bf16[7,8,2,32,128]{4,3,0,1,2:T(8,128)(2,1)}, u32[]{:S(2)}, u32[]{:S(2)}) collective-permute-start(bf16[7,8,2,32,128]{4,3,0,1,2:T(8,128)(2,1)S(1)} %pad_maximum_fusion.6), channel_id=1, source_target_pairs={{0,1},{1,0},{2,3},{3,2},{4,5},{5,4},{6,7},{7,6},{8,9},{9,8},{10,11... | collective-permute-start | bytes 2752520 | tf_op jit(solution)/shard_map/ppermute | solution.py:143
  150.6 30.9 %collective-permute-start.12 = (bf16[32,3072]{1,0:T(8,128)(2,1)S(1)}, bf16[32,3072]{1,0:T(8,128)(2,1)S(1)}, u32[]{:S(2)}, u32[]{:S(2)}) collective-permute-start(bf16[32,3072]{1,0:T(8,128)(2,1)S(1)} %pad_maximum_fusion.13), channel_id=1, source_target_pairs={{0,24},{8,16},{16,8},{24,0},{1,25},{9,17},{17,9},{25,1},{2,26},{10... | collective-permute-start | bytes 589832 | tf_op jit(solution)/shard_map/ppermute | solution.py:143
  150.9 30.6 %collective-permute-start.13 = (bf16[32,3072]{1,0:T(8,128)(2,1)S(1)}, bf16[32,3072]{1,0:T(8,128)(2,1)S(1)}, u32[]{:S(2)}, u32[]{:S(2)}) collective-permute-start(bf16[32,3072]{1,0:T(8,128)(2,1)S(1)} %pad_maximum_fusion.13), channel_id=1, source_target_pairs={{0,16},{8,24},{16,0},{24,8},{1,17},{9,25},{17,1},{25,9},{2,18},{10... | collective-permute-start | bytes 589832 | tf_op jit(solution)/shard_map/ppermute | solution.py:143
  155.2 26.3 %collective-permute-start.14 = (bf16[32,3072]{1,0:T(8,128)(2,1)S(1)}, bf16[32,3072]{1,0:T(8,128)(2,1)}, u32[]{:S(2)}, u32[]{:S(2)}) collective-permute-start(bf16[32,3072]{1,0:T(8,128)(2,1)S(1)} %pad_maximum_fusion.13), channel_id=1, source_target_pairs={{0,8},{8,0},{16,24},{24,16},{1,9},{9,1},{17,25},{25,17},{2,10},{10... | collective-permute-start | bytes 589832 | tf_op jit(solution)/shard_map/ppermute | solution.py:143
  175.2 16.8 %all-to-all-start.1 = ((bf16[8,2,128,128]{3,2,1,0:T(8,128)(2,1)}), bf16[8,2,128,128]{3,2,1,0:T(8,128)(2,1)S(1)}, u32[]{:S(2)}, u32[]{:S(2)}) async-start(bf16[8,2,128,128]{3,2,1,0:T(8,128)(2,1)} %get-tuple-element.62), calls=%async_computation.1 | async-start | bytes 1048576 | tf_op jit(solution)/shard_map/all_to_all | solution.py:711
  181.5 94.6 %all-gather.11.cloned.1.call-start = ((), (), s32[]{:S(2)}) async-start(), calls=%async_computation.8 | async-start | bytes 7077888 | tf_op jit(solution)/shard_map/all_gather | solution.py:672
  192.1 162.8 %reduce-scatter.4.cloned.1.call-start = ((), (), s32[]{:S(2)}) async-start(), calls=%async_computation.9 | async-start | bytes 7864320
  218.0 10.2 %collective-permute-start.15 = (bf16[512,6144]{1,0:T(8,128)(2,1)S(1)}, bf16[512,6144]{1,0:T(8,128)(2,1)S(1)}, u32[]{:S(2)}, u32[]{:S(2)}) collective-permute-start(bf16[512,6144]{1,0:T(8,128)(2,1)S(1)} %convolution_convert_fusion), channel_id=1, source_target_pairs={{0,1},{1,0},{2,3},{3,2},{4,5},{5,4},{6,7},{7,6},{8,9},{9,8},{10,11... | collective-permute-start | bytes 18874376 | tf_op jit(solution)/shard_map/ppermute | solution.py:143
  232.7 13.7 %collective-permute-start.20 = (bf16[1536,1024]{1,0:T(8,128)(2,1)S(1)}, bf16[1536,1024]{1,0:T(8,128)(2,1)}, u32[]{:S(2)}, u32[]{:S(2)}) collective-permute-start(bf16[1536,1024]{1,0:T(8,128)(2,1)S(1)} %convolution_convert_fusion.1), channel_id=1, source_target_pairs={{0,1},{1,0},{2,3},{3,2},{4,5},{5,4},{6,7},{7,6},{8,9},{9,8},{10,11... | collective-permute-start | bytes 9437192 | tf_op jit(solution)/shard_map/ppermute | solution.py:143
  232.9 7.7 %collective-permute-start.16 = (bf16[512,1024]{1,0:T(8,128)(2,1)}, bf16[512,1024]{1,0:T(8,128)(2,1)}, u32[]{:S(2)}, u32[]{:S(2)}) collective-permute-start(bf16[512,1024]{1,0:T(8,128)(2,1)} %convolution_convert_fusion.2), channel_id=1, source_target_pairs={{0,1},{1,0},{2,3},{3,2},{4,5},{5,4},{6,7},{7,6},{8,9},{9,8},{10,11... | collective-permute-start | bytes 3145736 | tf_op jit(solution)/shard_map/ppermute | solution.py:143
  233.3 42.8 %all-to-all-start.2 = ((bf16[8,2,128,128]{3,2,1,0:T(8,128)(2,1)}), bf16[8,2,128,128]{3,2,1,0:T(8,128)(2,1)}, u32[]{:S(2)}, u32[]{:S(2)}) async-start(bf16[8,2,128,128]{3,2,1,0:T(8,128)(2,1)} %bitcast.192), calls=%async_computation.2 | async-start | bytes 1048576 | tf_op jit(solution)/shard_map/all_to_all | solution.py:711
  242.6 16.1 %collective-permute-start.17 = (bf16[128,1024]{1,0:T(8,128)(2,1)S(1)}, bf16[128,1024]{1,0:T(8,128)(2,1)S(1)}, u32[]{:S(2)}, u32[]{:S(2)}) collective-permute-start(bf16[128,1024]{1,0:T(8,128)(2,1)S(1)} %get-tuple-element.113), channel_id=1, source_target_pairs={{0,8},{8,0},{16,24},{24,16},{1,9},{9,1},{17,25},{25,17},{2,10},{10... | collective-permute-start | bytes 786440 | tf_op jit(solution)/shard_map/ppermute | solution.py:143
  244.8 23.4 %collective-permute-start.18 = (bf16[128,1024]{1,0:T(8,128)(2,1)S(1)}, bf16[128,1024]{1,0:T(8,128)(2,1)S(1)}, u32[]{:S(2)}, u32[]{:S(2)}) collective-permute-start(bf16[128,1024]{1,0:T(8,128)(2,1)S(1)} %get-tuple-element.115), channel_id=1, source_target_pairs={{0,16},{8,24},{16,0},{24,8},{1,17},{9,25},{17,1},{25,9},{2,18},{10... | collective-permute-start | bytes 786440 | tf_op jit(solution)/shard_map/ppermute | solution.py:143
  245.1 30.9 %collective-permute-start.19 = (bf16[128,1024]{1,0:T(8,128)(2,1)S(1)}, bf16[128,1024]{1,0:T(8,128)(2,1)S(1)}, u32[]{:S(2)}, u32[]{:S(2)}) collective-permute-start(bf16[128,1024]{1,0:T(8,128)(2,1)S(1)} %get-tuple-element.114), channel_id=1, source_target_pairs={{0,24},{8,16},{16,8},{24,0},{1,25},{9,17},{17,9},{25,1},{2,26},{10... | collective-permute-start | bytes 786440 | tf_op jit(solution)/shard_map/ppermute | solution.py:143
  251.2 54.4 %collective-permute-start.21 = (bf16[2,384,512]{2,1,0:T(8,128)(2,1)}, bf16[2,384,512]{2,1,0:T(8,128)(2,1)}, u32[]{:S(2)}, u32[]{:S(2)}) collective-permute-start(bf16[2,384,512]{2,1,0:T(8,128)(2,1)} %slice_bitcast_fusion.2), channel_id=1, source_target_pairs={{0,4},{4,0},{1,5},{5,1},{2,6},{6,2},{3,7},{7,3},{8,12},{12,8},{9,1... | collective-permute-start | bytes 2359304 | tf_op jit(solution)/shard_map/ppermute | solution.py:143
  251.8 53.8 %collective-permute-start.23 = (bf16[2,384,512]{2,1,0:T(8,128)(2,1)}, bf16[2,384,512]{2,1,0:T(8,128)(2,1)}, u32[]{:S(2)}, u32[]{:S(2)}) collective-permute-start(bf16[2,384,512]{2,1,0:T(8,128)(2,1)} %slice_bitcast_fusion), channel_id=1, source_target_pairs={{0,2},{2,0},{1,3},{3,1},{4,6},{6,4},{5,7},{7,5},{8,10},{10,8},{9,1... | collective-permute-start | bytes 2359304 | tf_op jit(solution)/shard_map/ppermute | solution.py:143
  290.2 64.8 %all-to-all-start.3 = ((bf16[8,3,2,128,128]{4,3,2,1,0:T(8,128)(2,1)}), bf16[8,3,2,128,128]{4,3,2,1,0:T(8,128)(2,1)}, u32[]{:S(2)}, u32[]{:S(2)}) async-start(bf16[8,3,2,128,128]{4,3,2,1,0:T(8,128)(2,1)} %attend_backward.1.grads_ref), calls=%async_computation.3 | async-start | bytes 3145728 | tf_op jit(solution)/shard_map/all_to_all | solution.py:711
  305.6 3.7 collective-permute-start.25
  307.7 20.7 %collective-permute-start.24 = (bf16[384,512]{1,0:T(8,128)(2,1)S(1)}, bf16[384,512]{1,0:T(8,128)(2,1)S(1)}, u32[]{:S(2)}, u32[]{:S(2)}) collective-permute-start(bf16[384,512]{1,0:T(8,128)(2,1)S(1)} %slice_bitcast_fusion.4), channel_id=1, source_target_pairs={{0,4},{4,0},{1,5},{5,1},{2,6},{6,2},{3,7},{7,3},{8,12},{12,8},{9,1... | collective-permute-start | bytes 1179656 | tf_op jit(solution)/shard_map/ppermute | solution.py:143
  309.2 19.3 %collective-permute-start.22 = (bf16[384,512]{1,0:T(8,128)(2,1)S(1)}, bf16[384,512]{1,0:T(8,128)(2,1)S(1)}, u32[]{:S(2)}, u32[]{:S(2)}) collective-permute-start(bf16[384,512]{1,0:T(8,128)(2,1)S(1)} %slice_bitcast_fusion.6), channel_id=1, source_target_pairs={{0,2},{2,0},{1,3},{3,1},{4,6},{6,4},{5,7},{7,5},{8,10},{10,8},{9,1... | collective-permute-start | bytes 1179656 | tf_op jit(solution)/shard_map/ppermute | solution.py:143
  309.6 22.7 %collective-permute-start.26 = (bf16[256,896]{1,0:T(8,128)(2,1)S(1)}, bf16[256,896]{1,0:T(8,128)(2,1)S(1)}, u32[]{:S(2)}, u32[]{:S(2)}) collective-permute-start(bf16[256,896]{1,0:T(8,128)(2,1)S(1)} %slice.283), channel_id=1, source_target_pairs={{0,2},{2,0},{1,3},{3,1},{4,6},{6,4},{5,7},{7,5},{8,10},{10,8},{9,1... | collective-permute-start | bytes 1376264 | tf_op jit(solution)/shard_map/ppermute | solution.py:143
  328.7 8.1 %collective-permute-start.28 = (bf16[96,1024]{1,0:T(8,128)(2,1)S(1)}, bf16[96,1024]{1,0:T(8,128)(2,1)S(1)}, u32[]{:S(2)}, u32[]{:S(2)}) collective-permute-start(bf16[96,1024]{1,0:T(8,128)(2,1)S(1)} %get-tuple-element.122), channel_id=1, source_target_pairs={{0,8},{8,0},{16,24},{24,16},{1,9},{9,1},{17,25},{25,17},{2,10},{10... | collective-permute-start | bytes 589832 | tf_op jit(solution)/shard_map/ppermute | solution.py:143
  329.2 15.8 %collective-permute-start.29 = (bf16[96,1024]{1,0:T(8,128)(2,1)S(1)}, bf16[96,1024]{1,0:T(8,128)(2,1)S(1)}, u32[]{:S(2)}, u32[]{:S(2)}) collective-permute-start(bf16[96,1024]{1,0:T(8,128)(2,1)S(1)} %get-tuple-element.123), channel_id=1, source_target_pairs={{0,16},{8,24},{16,0},{24,8},{1,17},{9,25},{17,1},{25,9},{2,18},{10... | collective-permute-start | bytes 589832 | tf_op jit(solution)/shard_map/ppermute | solution.py:143
  331.2 18.2 %collective-permute-start.30 = (bf16[96,1024]{1,0:T(8,128)(2,1)S(1)}, bf16[96,1024]{1,0:T(8,128)(2,1)S(1)}, u32[]{:S(2)}, u32[]{:S(2)}) collective-permute-start(bf16[96,1024]{1,0:T(8,128)(2,1)S(1)} %get-tuple-element.124), channel_id=1, source_target_pairs={{0,24},{8,16},{16,8},{24,0},{1,25},{9,17},{17,9},{25,1},{2,26},{10... | collective-permute-start | bytes 589832 | tf_op jit(solution)/shard_map/ppermute | solution.py:143
  332.4 17.9 %collective-permute-start.27 = (bf16[128,896]{1,0:T(8,128)(2,1)S(1)}, bf16[128,896]{1,0:T(8,128)(2,1)S(1)}, u32[]{:S(2)}, u32[]{:S(2)}) collective-permute-start(bf16[128,896]{1,0:T(8,128)(2,1)S(1)} %slice.285), channel_id=1, source_target_pairs={{0,4},{4,0},{1,5},{5,1},{2,6},{6,2},{3,7},{7,3},{8,12},{12,8},{9,1... | collective-permute-start | bytes 688136 | tf_op jit(solution)/shard_map/ppermute | solution.py:143
  354.9 5.8 %collective-permute-start.31 = (bf16[64,1024]{1,0:T(8,128)(2,1)S(1)}, bf16[64,1024]{1,0:T(8,128)(2,1)S(1)}, u32[]{:S(2)}, u32[]{:S(2)}) collective-permute-start(bf16[64,1024]{1,0:T(8,128)(2,1)S(1)} %slice.246), channel_id=1, source_target_pairs={{0,4},{4,0},{1,5},{5,1},{2,6},{6,2},{3,7},{7,3},{8,12},{12,8},{9,1... | collective-permute-start | bytes 393224 | tf_op jit(solution)/shard_map/ppermute | solution.py:143
  355.5 19.8 %all-to-all-start.4 = ((bf16[4,32,896]{2,1,0:T(8,128)(2,1)}), bf16[4,32,896]{2,1,0:T(8,128)(2,1)S(1)}, u32[]{:S(2)}, u32[]{:S(2)}) async-start(bf16[4,32,896]{2,1,0:T(8,128)(2,1)} %bitcast.80), calls=%async_computation.4 | async-start | bytes 458752 | tf_op jit(solution)/shard_map/all_to_all | solution.py:792
  360.7 13.9 %collective-permute-start.32 = (bf16[32,1024]{1,0:T(8,128)(2,1)S(1)}, bf16[32,1024]{1,0:T(8,128)(2,1)S(1)}, u32[]{:S(2)}, u32[]{:S(2)}) collective-permute-start(bf16[32,1024]{1,0:T(8,128)(2,1)S(1)} %slice.305), channel_id=1, source_target_pairs={{0,2},{2,0},{1,3},{3,1},{4,6},{6,4},{5,7},{7,5},{8,10},{10,8},{9,1... | collective-permute-start | bytes 196616 | tf_op jit(solution)/shard_map/ppermute | solution.py:143
  364.5 15.9 %collective-permute-start.33 = (bf16[32,6144]{1,0:T(8,128)(2,1)S(1)}, bf16[32,6144]{1,0:T(8,128)(2,1)S(1)}, u32[]{:S(2)}, u32[]{:S(2)}) collective-permute-start(bf16[32,6144]{1,0:T(8,128)(2,1)S(1)} %get-tuple-element.107), channel_id=1, source_target_pairs={{0,8},{8,0},{16,24},{24,16},{1,9},{9,1},{17,25},{25,17},{2,10},{10... | collective-permute-start | bytes 1179656 | tf_op jit(solution)/shard_map/ppermute | solution.py:143
  364.6 29.3 %collective-permute-start.34 = (bf16[32,6144]{1,0:T(8,128)(2,1)S(1)}, bf16[32,6144]{1,0:T(8,128)(2,1)S(1)}, u32[]{:S(2)}, u32[]{:S(2)}) collective-permute-start(bf16[32,6144]{1,0:T(8,128)(2,1)S(1)} %get-tuple-element.106), channel_id=1, source_target_pairs={{0,16},{8,24},{16,0},{24,8},{1,17},{9,25},{17,1},{25,9},{2,18},{10... | collective-permute-start | bytes 1179656 | tf_op jit(solution)/shard_map/ppermute | solution.py:143
  367.4 33.6 %collective-permute-start.35 = (bf16[32,6144]{1,0:T(8,128)(2,1)S(1)}, bf16[32,6144]{1,0:T(8,128)(2,1)}, u32[]{:S(2)}, u32[]{:S(2)}) collective-permute-start(bf16[32,6144]{1,0:T(8,128)(2,1)S(1)} %get-tuple-element.105), channel_id=1, source_target_pairs={{0,24},{8,16},{16,8},{24,0},{1,25},{9,17},{17,9},{25,1},{2,26},{10... | collective-permute-start | bytes 1179656 | tf_op jit(solution)/shard_map/ppermute | solution.py:143
  376.1 29.4 %copy-start.17 = (f32[32,1024]{1,0:T(8,128)}, f32[32,1024]{1,0:T(8,128)S(1)}, u32[]{:S(2)}) copy-start(f32[32,1024]{1,0:T(8,128)S(1)} %squeeze.34) | copy-start | bytes 393220
  376.4 29.1 %copy-start.18 = (f32[32,1024]{1,0:T(8,128)}, f32[32,1024]{1,0:T(8,128)S(1)}, u32[]{:S(2)}) copy-start(f32[32,1024]{1,0:T(8,128)S(1)} %squeeze.33) | copy-start | bytes 393220
  377.3 28.2 %copy-start.19 = (f32[32,1024]{1,0:T(8,128)}, f32[32,1024]{1,0:T(8,128)S(1)}, u32[]{:S(2)}) copy-start(f32[32,1024]{1,0:T(8,128)S(1)} %squeeze.32) | copy-start | bytes 393220
  (28 other events, 130.6 us)
Sparse Core Ops, SparseCore 0:
  36.9 66.9 all-gather.6
  105.8 72.1 all-gather.8
  192.2 47.0 all-gather.10
  242.1 112.7 reduce-scatter.3
